TPU v7x, 256 devices: a whole 4x4x8 slice. The times are simulated.
256 devices in a mesh: tm: 8 (over z_hi, y), aux: 32 (over z_lo, x, core).
Axes of the slice: x: 4, y: 4, z: 8 (z_hi: 2, z_lo: 4; z = z_hi * 4 + z_lo), core: 2. Of those that a mesh axis runs over, the one named last changes fastest.
Arguments:
- green: bfloat16 [16, 1024, 1024], P('tm'), may hold values from -4 to 4
- factors: bfloat16 [4096, 1024], P('aux'), may hold values from -0.1875 to 0.1875
- pattern: int32 [32, 8], P('aux'), may hold values 0 or 1
- coulomb: float32 [4096], P('aux'), may hold values from 0.5 to 2
Outputs:
- sigma: float32 [1024, 16, 1024], P('aux', 'tm')
All inputs are finite; a program needn't handle non-finite values. No bound on the sum of `pattern` on one device may be relied on, other than what follows from the above.
Results may differ from a plain program's by a relative error of at most 0.006.
Values may be sent and summed in bfloat16 or wider, within the bound.
No kernel may reach another device: no remote copies, remote signals or barrier semaphores. Data moves between devices by JAX's collectives and lax.ppermute only.
A program may use at most 64 MiB of HBM per device.

v0:
```python
import jax
import jax.numpy as jnp
from jax import lax
from jax.sharding import PartitionSpec as P

BLOCK = 128


def swapped(value, axis, distance):
    return lax.ppermute(value, axis, [(i, i ^ 1 << distance) for i in range(lax.axis_size(axis))])


def mirrored_times(values):
    top_bit = lax.axis_size("tm").bit_length() - 2
    return swapped(values, "tm", top_bit)


def local(green, factors, pattern, coulomb):
    mask = jnp.repeat(jnp.repeat(pattern, BLOCK, axis=0), BLOCK, axis=1)
    masked = factors * mask.astype(factors.dtype)
    left = jnp.einsum("po,tok->tpk", masked, green, preferred_element_type=jnp.float32).astype(
        jnp.bfloat16
    )
    partner_green = mirrored_times(green)
    right = jnp.einsum(
        "po,tko->tpk", masked, partner_green, preferred_element_type=jnp.float32
    ).astype(jnp.bfloat16)
    rows = lax.all_gather(masked, "aux", axis=0, tiled=True)
    weights = lax.all_gather(coulomb.astype(jnp.bfloat16), "aux", axis=0, tiled=True).astype(
        jnp.float32
    )
    aux_green = jnp.einsum("tpo,qo->tpq", left, rows, preferred_element_type=jnp.float32)
    mirror = jnp.einsum("tpo,qo->tpq", right, rows, preferred_element_type=jnp.float32)
    chi = -aux_green * mirror
    kernel = (aux_green * coulomb[None, :, None] * chi * weights[None, None, :]).astype(
        jnp.bfloat16
    )
    summed = jnp.einsum("tpq,qo->tpo", kernel, rows, preferred_element_type=jnp.float32)
    carried = summed.astype(jnp.bfloat16)
    return lax.psum_scatter(
        -jnp.einsum("pi,tpj->itj", masked, carried, preferred_element_type=jnp.float32),
        "aux",
        scatter_dimension=0,
        tiled=True,
    )


def solution(mesh):
    in_specs = (P("tm", None, None), P("aux", None), P("aux", None), P("aux"))
    out_specs = P("aux", "tm", None)
    return jax.shard_map(local, mesh=mesh, in_specs=in_specs, out_specs=out_specs, check_vma=False)
```

profile of v0, /device:TPU:1, one launch (start us, length us, event | category | flops | bytes accessed | tf_op | source)
XLA Modules:
  0.0 438.9 jit_solution(6494498491092852017)
XLA Ops:
  6.5 0.0 all-gather.3.cloned.1.call-start
  6.5 0.7 convert_bitcast_fusion.1
  7.2 0.1 broadcast_bitcast_fusion
  7.3 1.7 broadcast_multiply_fusion
  8.9 0.0 copy-start
  8.9 0.0 all-gather.3.cloned.1.call-update
  9.0 0.0 reduce-scatter.2.cloned.1.call-start
  9.0 7.8 %collective-permute-start = (bf16[2,1024,1024]{2,1,0:T(8,128)(2,1)}, bf16[2,1024,1024]{2,1,0:T(8,128)(2,1)S(1)}, u32[]{:S(2)}, u32[]{:S(2)}) collective-permute-start(bf16[2,1024,1024]{2,1,0:T(8,128)(2,1)} %param.4), channel_id=1, source_target_pairs={{0,128},{32,160},{64,192},{96,224},{128,0},{160,32},{192,64},{224,... | collective-permute-start | bytes 12582920 | tf_op jit(solution)/shard_map/ppermute | solution.py:10
  16.8 0.7 convert_bitcast_fusion
  17.5 232.1 %all-gather = bf16[32,1,128]{2,1,0:T(2,128)(2,1)S(1)} all-gather(bf16[1,1,128]{2,1,0:T(2,128)(2,1)S(1)} %convert_bitcast_fusion), channel_id=1, replica_groups=mesh['tm'=8,'aux'=32] {'aux'}, dimensions={0}, use_global_device_ids=true | all-gather | bytes 8448 | tf_op jit(solution)/shard_map/all_gather | solution.py:29
  249.6 0.0 collective-permute-done
  249.6 2.5 convolution_convert_fusion
  252.1 0.5 copy.18
  252.6 0.0 copy-start.1
  252.6 2.1 all-gather.3.cloned.1.call-done
  254.8 0.0 copy-done
  254.8 9.6 %fusion.4 = f32[2,128,4096]{2,1,0:T(8,128)} fusion(bf16[4096,1024]{1,0:T(8,128)(2,1)} %all-gather.3.cloned.1.call-done, bf16[2,1024,1024]{2,1,0:T(8,128)(2,1)} %param.4, bf16[128,1024]{1,0:T(8,128)(2,1)S(1)} %copy-done), kind=kOutput, calls=%fused_computation.4 | convolution fusion | flops 2684616704 | bytes 17039360 | tf_op jit(solution)/shard_map/tpo,qo->tpq/dot_general | solution.py:32
  264.4 0.0 copy-done.1
  264.4 12.1 %fusion.22 = bf16[2,128,1024]{2,1,0:T(8,128)(2,1)S(1)} fusion(bf16[4096,1024]{1,0:T(8,128)(2,1)} %all-gather.3.cloned.1.call-done, f32[2,128,4096]{2,1,0:T(8,128)} %fusion.4, f32[4096]{0:T(1024)S(1)} %bitcast.48, f32[128]{0:T(128)S(1)} %copy-done.1, bf16[2,128,1024]{2,0,1:T(2,128)(2,1)S(1)} %bitcast.47), kind=kOutput, calls=%fused_computation.13 | convolution fusion | flops 4301520896 | bytes 13648384 | tf_op jit(solution)/shard_map/tpq,qo->tpo/dot_general | solution.py:38
  276.4 4.5 %convolution_negate_fusion = f32[1024,2,1024]{2,0,1:T(8,128)} fusion(bf16[2,128,1024]{2,1,0:T(8,128)(2,1)S(1)} %fusion.22, bf16[128,1024]{1,0:T(8,128)(2,1)S(1)} %copy-done), kind=kOutput, calls=%fused_computation.10 | convolution fusion | flops 538968064 | bytes 9175040 | tf_op jit(solution)/shard_map/pi,tpj->itj/dot_general | solution.py:41
  281.0 0.0 reduce-scatter.2.cloned.1.call-update
  281.0 149.3 %reduce-scatter.2.cloned.1.call-done = f32[32,2,1024]{2,0,1:T(8,128)} async-done(((f32[1024,2,1024]{2,0,1:T(8,128)}), f32[32,2,1024]{2,0,1:T(8,128)}) %reduce-scatter.2.cloned.1.call-update) | async-done | bytes 262160 | tf_op jit(solution)/shard_map/reduce_scatter | solution.py:40
  430.2 1.9 copy.8
  (1 shorter events, 0.0 us)
Async XLA Ops:
  6.5 248.2 %all-gather.3.cloned.1.call-start = ((), (), s32[]{:S(2)}) async-start(), calls=%async_computation.1 | async-start | bytes 8650752 | tf_op jit(solution)/shard_map/all_gather | solution.py:28
  8.9 245.8 %copy-start = (bf16[128,1024]{1,0:T(8,128)(2,1)S(1)}, bf16[128,1024]{1,0:T(8,128)(2,1)}, u32[]{:S(2)}) copy-start(bf16[128,1024]{1,0:T(8,128)(2,1)} %broadcast_multiply_fusion) | copy-start | bytes 786436
  9.0 421.3 %reduce-scatter.2.cloned.1.call-start = ((), (), s32[]{:S(2)}) async-start(), calls=%async_computation.2 | async-start | bytes 8650752 | tf_op jit(solution)/shard_map/reduce_scatter | solution.py:40
  9.0 240.6 %collective-permute-start = (bf16[2,1024,1024]{2,1,0:T(8,128)(2,1)}, bf16[2,1024,1024]{2,1,0:T(8,128)(2,1)S(1)}, u32[]{:S(2)}, u32[]{:S(2)}) collective-permute-start(bf16[2,1024,1024]{2,1,0:T(8,128)(2,1)} %param.4), channel_id=1, source_target_pairs={{0,128},{32,160},{64,192},{96,224},{128,0},{160,32},{192,64},{224,... | collective-permute-start | bytes 12582920 | tf_op jit(solution)/shard_map/ppermute | solution.py:10
  252.6 11.7 %copy-start.1 = (f32[128]{0:T(128)S(1)}, f32[128]{0:T(128)}, u32[]{:S(2)}) copy-start(f32[128]{0:T(128)} %param.7) | copy-start | bytes 1540
Sparse Core Ops, SparseCore 0:
  9.2 245.5 all-gather.2
  281.1 149.0 reduce-scatter.1
where the time goes:
time: 444 us; the launch traced here: 439 us
  blocking collectives  232 us (52%)
  waiting for transfers between devices  151 us (34%)
  matrix products  28.6 us (6%)
  between operations  13.4 us (3%)
  starting transfers between devices  7.87 us (2%)
    all_gather x1, blocking collectives, local(): lax.all_gather(coulomb.astype(jnp.bfloat16), 'aux', axis=0, tiled=True)  232 us
    reduce_scatter x1, waiting for transfers between devices, local(): lax.psum_scatter(-jnp.einsum('pi,tpj->itj', masked, carried, preferred_el...  149 us
    dot_general x1, matrix products, local(): jnp.einsum('tpq,qo->tpo', kernel, rows, preferred_element_type=jnp.float32)  12.1 us
    dot_general x1, matrix products, local(): jnp.einsum('tpo,qo->tpq', left, rows, preferred_element_type=jnp.float32)  9.6 us
  transfers between devices with their start and end apart: 3, of which 2 were waited for; matrix products, arithmetic and copies ran while one was open for 1% of the time, Pallas kernels for 0%

commit v1 on v0

v1 whole, which is shorter than its diff:
```python
import jax
import jax.numpy as jnp
from jax import lax
from jax.sharding import PartitionSpec as P

BLOCK = 128


def local(green, factors, pattern, coulomb):
    f32, bf16 = jnp.float32, jnp.bfloat16
    devices = lax.axis_size("aux")
    own = factors.shape[0]
    mask = jnp.repeat(jnp.repeat(pattern, BLOCK, axis=0), BLOCK, axis=1)
    masked = factors * mask.astype(factors.dtype)
    rows = lax.all_gather(masked, "aux", axis=0, tiled=True)
    left = jnp.einsum("qo,tok->tqk", masked, green, preferred_element_type=f32).astype(bf16)
    half = lax.axis_size("tm") // 2
    left = lax.ppermute(left, "tm", [(i, (i + half) % (2 * half)) for i in range(2 * half)])
    right = jnp.einsum("qo,tko->tqk", masked, green, preferred_element_type=f32).astype(bf16)
    weights = lax.all_gather(coulomb, "aux", axis=0, tiled=True)
    aux_green = jnp.einsum("tqo,po->tqp", right, rows, preferred_element_type=f32)
    mirror = jnp.einsum("tqo,po->tqp", left, rows, preferred_element_type=f32)
    kernel = aux_green * weights[None, None, :] * (aux_green * mirror) * coulomb[None, :, None]
    kernel = kernel.astype(bf16)
    part = jnp.einsum("tqp,pi->tqi", kernel, rows, preferred_element_type=f32).astype(bf16)
    times, orb = green.shape[0], green.shape[1]
    part = part.reshape(times, own, devices, orb // devices).transpose(2, 0, 1, 3)
    part = lax.all_to_all(part, "aux", split_axis=0, concat_axis=0, tiled=True)
    rows = rows.reshape(devices, own, orb)
    return jnp.einsum("dtqi,dqj->itj", part, rows, preferred_element_type=f32)


def solution(mesh):
    in_specs = (P("tm", None, None), P("aux", None), P("aux", None), P("aux"))
    out_specs = P("aux", "tm", None)
    return jax.shard_map(local, mesh=mesh, in_specs=in_specs, out_specs=out_specs, check_vma=False)
```

time: 444 us -> 155 us (0.35); the launches traced: 439 us -> 155 us
  blocking collectives: 232 us -> 86.9 us
  waiting for transfers between devices: 151 us -> 12.6 us
    all_gather x1, blocking collectives: 232 us -> 65 us  [local(): weights = lax.all_gather(coulomb, 'aux', axis=0, tiled=True)]
    reduce_scatter x1 -> x0, waiting for transfers between devices: 149 us -> none  [local(): lax.psum_scatter(-jnp.einsum('pi,tpj->itj', masked, carried, preferred_el...]
    all_to_all x0 -> x1, blocking collectives: none -> 21.9 us  [local(): part = lax.all_to_all(part, 'aux', split_axis=0, concat_axis=0, tiled=True)]
    all_gather x1, waiting for transfers between devices: 2.13 us -> 12.6 us  [local(): rows = lax.all_gather(masked, 'aux', axis=0, tiled=True)]
  transfers between devices with their start and end apart: 3 -> 2, of which waited for: 2 -> 1; matrix products, arithmetic and copies ran while one was open for 1% -> 9% of each run, Pallas kernels for 0% -> 0%
where the time goes in v1:
time: 155 us
  blocking collectives  86.9 us (56%)
  matrix products  30.2 us (19%)
  between operations  13.4 us (9%)
  waiting for transfers between devices  12.6 us (8%)
  starting transfers between devices  7.83 us (5%)
  other arithmetic  2.34 us (2%)
    all_gather x1, blocking collectives, local(): weights = lax.all_gather(coulomb, 'aux', axis=0, tiled=True)  65 us
    all_to_all x1, blocking collectives, local(): part = lax.all_to_all(part, 'aux', split_axis=0, concat_axis=0, tiled=True)  21.9 us
    all_gather x1, waiting for transfers between devices, local(): rows = lax.all_gather(masked, 'aux', axis=0, tiled=True)  12.6 us
    dot_general x1, matrix products, local(): jnp.einsum('tqp,pi->tqi', kernel, rows, preferred_element_type=f32)  11.9 us
    dot_general x1, matrix products, local(): jnp.einsum('tqo,po->tqp', right, rows, preferred_element_type=f32)  10.4 us
    ppermute x1, starting transfers between devices, local(): lax.ppermute(left, 'tm', [(i, (i + half) % (2 * half)) for i in range(2 *...  7.83 us
    dot_general x1, matrix products, local(): return jnp.einsum('dtqi,dqj->itj', part, rows, preferred_element_type=f32)  4.96 us
  transfers between devices with their start and end apart: 2, of which 1 were waited for; matrix products, arithmetic and copies ran while one was open for 9% of the time, Pallas kernels for 0%

profile of v1, /device:TPU:1, one launch (start us, length us, event | category | flops | bytes accessed | tf_op | source)
XLA Modules:
  0.0 154.6 jit_solution(5889969668802881452)
XLA Ops:
  6.5 0.0 copy-start.1
  6.5 0.0 all-gather.3.cloned.1.call-start
  6.5 0.7 convert_bitcast_fusion
  7.2 0.1 broadcast_bitcast_fusion
  7.3 1.7 %broadcast_multiply_fusion = bf16[128,1024]{1,0:T(8,128)(2,1)} fusion(bf16[128,1024]{1,0:T(8,128)(2,1)} %param.5, bf16[1024]{0:T(1024)(128)(2,1)S(1)} %broadcast_bitcast_fusion), kind=kLoop, calls=%fused_computation.20 | loop fusion | flops 131072 | bytes 526336 | tf_op jit(solution)/shard_map/mul | solution.py:14
  9.0 0.0 copy-start
  9.0 0.0 all-gather.3.cloned.1.call-update
  9.0 3.0 %fusion.28 = bf16[2,128,1024]{2,1,0:T(8,128)(2,1)S(1)} fusion(bf16[2,1024,1024]{2,1,0:T(8,128)(2,1)} %param.4, bf16[128,1024]{1,0:T(8,128)(2,1)} %broadcast_multiply_fusion), kind=kOutput, calls=%fused_computation.16 | convolution fusion | flops 537133056 | bytes 4980736 | tf_op jit(solution)/shard_map/qo,tok->tqk/dot_general | solution.py:16
  12.0 7.8 %collective-permute-start = (bf16[2,128,1024]{2,1,0:T(8,128)(2,1)S(1)}, bf16[2,128,1024]{2,1,0:T(8,128)(2,1)S(1)}, u32[]{:S(2)}, u32[]{:S(2)}) collective-permute-start(bf16[2,128,1024]{2,1,0:T(8,128)(2,1)S(1)} %fusion.28), channel_id=1, source_target_pairs={{0,128},{32,160},{64,192},{96,224},{128,0},{160,32},{192,64},{224,... | collective-permute-start | bytes 1572872 | tf_op jit(solution)/shard_map/ppermute | solution.py:18
  19.8 0.0 copy-done.1
  19.8 65.0 %all-gather = f32[32,1,128]{2,1,0:T(1,128)S(1)} all-gather(f32[1,1,128]{2,1,0:T(1,128)S(1)} %bitcast.62), channel_id=1, replica_groups=mesh['tm'=8,'aux'=32] {'aux'}, dimensions={0}, use_global_device_ids=true | all-gather | bytes 16896 | tf_op jit(solution)/shard_map/all_gather | solution.py:20
  84.8 12.6 %all-gather.3.cloned.1.call-done = bf16[4096,1024]{1,0:T(8,128)(2,1)} async-done(((bf16[128,1024]{1,0:T(8,128)(2,1)}), bf16[4096,1024]{1,0:T(8,128)(2,1)}) %all-gather.3.cloned.1.call-update) | async-done | bytes 8388624 | tf_op jit(solution)/shard_map/all_gather | solution.py:15
  97.4 0.0 copy-done
  97.4 10.4 %fusion.4 = f32[2,128,4096]{2,1,0:T(8,128)} fusion(bf16[4096,1024]{1,0:T(8,128)(2,1)} %all-gather.3.cloned.1.call-done, bf16[2,1024,1024]{2,1,0:T(8,128)(2,1)} %param.4, bf16[128,1024]{1,0:T(8,128)(2,1)S(1)} %copy-done), kind=kOutput, calls=%fused_computation.4 | convolution fusion | flops 2684616704 | bytes 17039360 | tf_op jit(solution)/shard_map/tqo,po->tqp/dot_general | solution.py:21
  107.8 0.0 collective-permute-done
  107.8 11.9 %fusion.22 = bf16[2,128,1024]{2,1,0:T(8,128)(2,1)S(1)} fusion(bf16[4096,1024]{1,0:T(8,128)(2,1)} %all-gather.3.cloned.1.call-done, f32[2,128,4096]{2,1,0:T(8,128)} %fusion.4, bf16[2,128,1024]{2,1,0:T(8,128)(2,1)S(1)} %collective-permute-done, f32[128]{0:T(128)S(1)} %copy-done.1, f32[4096]{0:T(1024)S(1)} %bitcast.61), kind=kOutput, calls=%fused_computation.12 | convolution fusion | flops 4300472320 | bytes 13648384 | tf_op jit(solution)/shard_map/tqp,pi->tqi/dot_general | solution.py:25
  119.6 0.3 copy.9
  119.9 0.1 copy.10
  120.0 21.9 %all_to_all.5 = bf16[32,2,128,32]{2,3,1,0:T(8,128)(2,1)S(1)} all-to-all(bf16[32,2,128,32]{2,3,1,0:T(8,128)(2,1)S(1)} %copy.10), channel_id=1, replica_groups=mesh['tm'=8,'aux'=32] {'aux'}, dimensions={0} | all-to-all | bytes 1048576 | tf_op jit(solution)/shard_map/all_to_all | solution.py:28
  141.9 5.0 %convolution_bitcast_fusion = f32[32,2,1024]{2,0,1:T(8,128)S(1)} fusion(bf16[32,128,1024,1]{2,1,3,0:T(8,128)(2,1)} %bitcast.63, bf16[32,2,128,32]{2,3,1,0:T(8,128)(2,1)S(1)} %all_to_all.5), kind=kOutput, calls=%fused_computation.17 | convolution fusion | flops 536870912 | bytes 9175040 | tf_op jit(solution)/shard_map/dtqi,dqj->itj/dot_general | solution.py:30
  146.9 0.9 copy.12
Async XLA Ops:
  6.5 13.3 %copy-start.1 = (f32[128]{0:T(128)S(1)}, f32[128]{0:T(128)}, u32[]{:S(2)}) copy-start(f32[128]{0:T(128)} %param.7) | copy-start | bytes 1540
  6.5 90.9 %all-gather.3.cloned.1.call-start = ((), (), s32[]{:S(2)}) async-start(), calls=%async_computation.1 | async-start | bytes 8650752 | tf_op jit(solution)/shard_map/all_gather | solution.py:15
  9.0 88.4 %copy-start = (bf16[128,1024]{1,0:T(8,128)(2,1)S(1)}, bf16[128,1024]{1,0:T(8,128)(2,1)}, u32[]{:S(2)}) copy-start(bf16[128,1024]{1,0:T(8,128)(2,1)} %broadcast_multiply_fusion) | copy-start | bytes 786436
  12.0 95.8 %collective-permute-start = (bf16[2,128,1024]{2,1,0:T(8,128)(2,1)S(1)}, bf16[2,128,1024]{2,1,0:T(8,128)(2,1)S(1)}, u32[]{:S(2)}, u32[]{:S(2)}) collective-permute-start(bf16[2,128,1024]{2,1,0:T(8,128)(2,1)S(1)} %fusion.28), channel_id=1, source_target_pairs={{0,128},{32,160},{64,192},{96,224},{128,0},{160,32},{192,64},{224,... | collective-permute-start | bytes 1572872 | tf_op jit(solution)/shard_map/ppermute | solution.py:18
Sparse Core Ops, SparseCore 0:
  9.2 88.1 all-gather.2

commit v2 on v1

v2 whole, which is shorter than its diff:
```python
import functools

import jax
import jax.numpy as jnp
from jax import lax
from jax.experimental import pallas as pl
from jax.experimental.pallas import tpu as pltpu
from jax.sharding import PartitionSpec as P

BLOCK = 128
ORB = 1024
F32, BF16 = jnp.float32, jnp.bfloat16
BOTH = ("tm", "aux")
NT = (((1,), (1,)), ((), ()))
NN = (((1,), (0,)), ((), ()))


def device_at(x, y, z, core):
    return (z // 4 * 4 + y % 4) * 32 + (z % 4 * 4 + x % 4) * 2 + core


def hop(value, dx=0, dz=0, flip=0):
    pairs = []
    for x in range(4):
        for y in range(4):
            for z in range(8):
                for core in range(2):
                    to = device_at((x + dx) % 4, y, (z + dz) % 8, core ^ flip)
                    pairs.append((device_at(x, y, z, core), to))
    return lax.ppermute(value, BOTH, sorted(pairs))


def params(mib):
    return pltpu.CompilerParams(vmem_limit_bytes=mib << 20)


def weights_of(ref, row, block):
    parts = [ref[pl.ds(row + block, 1), pl.ds(k * BLOCK, BLOCK)].astype(F32) for k in range(3)]
    return parts[0] + (parts[1] + parts[2])


def chunk_kernel(spans, first, *refs):
    count = len({span[0] for span in spans})
    right_own, right_other, left_own, left_other = refs[:4]
    rows = refs[4 : 4 + count]
    rest = refs[4 + count :]
    if not first:
        acc_own, acc_other = rest[:2]
        rest = rest[2:]
    out_own, out_other = rest
    for t in range(out_own.shape[0]):
        right = jnp.concatenate([right_own[t], right_other[t]], axis=0)
        left = jnp.concatenate([left_own[t], left_other[t]], axis=0)
        total = None
        for at, start, size, weight_at, weight_row, block in spans:
            part = rows[at][pl.ds(start, size), :]
            weight = jnp.concatenate(
                [weights_of(rows[weight_at], weight_row, block + k) for k in range(size // BLOCK)],
                axis=1,
            )
            a = lax.dot_general(right, part, NT, preferred_element_type=F32)
            m = lax.dot_general(left, part, NT, preferred_element_type=F32)
            k = (a * weight * (a * m)).astype(BF16)
            d = lax.dot_general(k, part, NN, preferred_element_type=F32)
            total = d if total is None else total + d
        own = out_own.shape[1]
        if first:
            out_own[t] = total[:own]
            out_other[t] = total[own:]
        else:
            out_own[t] = acc_own[t] + total[:own]
            out_other[t] = acc_other[t] + total[own:]


def chunk(sides, rows, spans, acc=None):
    times, own, orb = sides[0].shape
    shape = jax.ShapeDtypeStruct((times, own, orb), F32)
    n = sum(span[2] for span in spans)
    extra = () if acc is None else tuple(acc)
    aliases = {} if acc is None else {4 + len(rows): 0, 5 + len(rows): 1}
    return pl.pallas_call(
        functools.partial(chunk_kernel, tuple(spans), acc is None),
        out_shape=(shape, shape),
        input_output_aliases=aliases,
        compiler_params=params(40),
        cost_estimate=pl.CostEstimate(
            flops=times * 3 * 2 * (2 * own) * n * orb, bytes_accessed=2 << 20, transcendentals=0
        ),
    )(*sides, *rows, *extra)


def finish_kernel(own_ref, got_ref, coulomb_ref, out_ref):
    chips, times, rows, _ = out_ref.shape
    for t in range(times):
        d = jnp.transpose(own_ref[t] + got_ref[t]) * coulomb_ref[...]
        d = d.astype(BF16)
        for chip in range(chips):
            out_ref[chip, t] = d[chip * rows : (chip + 1) * rows]


def sigma_kernel(spans, where_ref, part_ref, *refs):
    rows = refs[:-4]
    keep_ref, send_ref, lhs, total_ref = refs[-4:]
    chips, times, i_rows, width = part_ref.shape
    for b in range(chips):
        for t in range(times):
            lhs[pl.ds(t * i_rows, i_rows), pl.ds(b * width, width)] = part_ref[where_ref[b], t]
    total = None
    offset = 0
    for at, start, size in spans:
        d = lax.dot_general(
            lhs[:, pl.ds(offset, size)],
            rows[at][pl.ds(start, size), :],
            NN,
            preferred_element_type=F32,
        )
        total = d if total is None else total + d
        offset += size
    total_ref[...] = total
    half = i_rows // 2
    core = where_ref[chips]
    for t in range(times):
        keep = pl.multiple_of(t * i_rows + core * half, half)
        send = pl.multiple_of(t * i_rows + (1 - core) * half, half)
        keep_ref[t] = total_ref[pl.ds(keep, half), :]
        send_ref[t] = total_ref[pl.ds(send, half), :]


def add_kernel(keep_ref, got_ref, out_ref):
    for t in range(keep_ref.shape[0]):
        out_ref[:, t, :] = keep_ref[t] + got_ref[t]


def local(green, factors, pattern, coulomb):
    times, orb, _ = green.shape
    own = factors.shape[0]
    barrier = lax.optimization_barrier
    mask = jnp.repeat(jnp.repeat(pattern, BLOCK, axis=0), BLOCK, axis=1)
    masked = factors * mask.astype(factors.dtype)
    high = lax.reduce_precision(coulomb, 8, 7)
    middle = lax.reduce_precision(coulomb - high, 8, 7)
    low = coulomb - high - middle
    packed = jnp.concatenate([high, middle, low]).astype(BF16)
    packed = jnp.pad(packed[None, :], ((0, 7), (0, orb - 3 * own)))
    payload = jnp.concatenate([masked, packed], axis=0)

    half = own // 2
    below = hop(payload, dz=1)
    above = hop(payload, dz=-1)
    far_a = hop(payload[:half], dz=2)
    far_b = hop(payload[half:], dz=-2)

    left = jnp.einsum("qo,tok->tqk", masked, green, preferred_element_type=F32).astype(BF16)
    right = jnp.einsum("qo,tko->tqk", masked, green, preferred_element_type=F32).astype(BF16)
    right_other = hop(right, flip=1)

    weights = [payload[own : own + 1], below[own : own + 1], above[own : own + 1], far_b[half : half + 1]]
    weights = jnp.concatenate(weights + [jnp.zeros((4, orb), BF16)], axis=0)
    here = jnp.concatenate([masked, below[:own], above[:own], far_a, far_b[:half], weights], axis=0)
    here, left = barrier((here, left))

    west = hop(here, dx=1)
    east = hop(here, dx=-1)
    left = hop(left, dz=4)
    left_other = hop(left, flip=1)

    sides = (right, right_other, left, left_other)
    n = 4 * own
    full = [(0, 2 * own, 0, n, 0), (2 * own, 2 * own, 0, n, 2)]

    def whole(at):
        return [(at, 0, 2 * own, at, n, 0), (at, 2 * own, 2 * own, at, n, 2)]

    acc = chunk(sides, (here,), whole(0))
    west, east = barrier((west, east))
    over_a = hop(west[: 2 * own], dx=1)
    over_b = hop(east[2 * own :], dx=-1)
    acc = chunk(sides, (west, east), whole(0) + whole(1), acc)
    spans = [(0, 0, 2 * own, 1, 2 * own, 0), (1, 0, 2 * own, 1, 2 * own, 2)]
    keep, send = chunk(sides, (over_a, over_b), spans, acc)

    got = hop(send, flip=1)
    chips, i_rows = 16, orb // 16
    part = pl.pallas_call(
        finish_kernel,
        out_shape=jax.ShapeDtypeStruct((chips, times, i_rows, own), BF16),
        compiler_params=params(24),
    )(keep, got, coulomb[None, :])
    groups = [[2 * chip + core for chip in range(chips)] for core in range(2)]
    part = lax.all_to_all(part, "aux", 0, 0, axis_index_groups=groups, tiled=True)

    me = lax.axis_index("aux")
    core, x, z = me % 2, me // 2 % 4, me // 8
    where = [(z + dz) % 4 * 4 + (x + dx) % 4 for dx in (0, -1, 1, 2) for dz in (0, -1, 1, 2)]
    where = jnp.stack(where + [core]).astype(jnp.int32)
    spans = [(0, 0, n), (1, 0, n), (2, 0, n), (3, 0, n // 2), (4, 0, n // 2)]
    shape = jax.ShapeDtypeStruct((times, i_rows // 2, orb), F32)
    vmem = pl.BlockSpec(memory_space=pltpu.VMEM)
    keep, send = pl.pallas_call(
        functools.partial(sigma_kernel, tuple(spans)),
        out_shape=(shape, shape),
        in_specs=[pl.BlockSpec(memory_space=pltpu.SMEM)] + [vmem] * 6,
        out_specs=(vmem, vmem),
        scratch_shapes=[
            pltpu.VMEM((times * i_rows, chips * own), BF16),
            pltpu.VMEM((times * i_rows, orb), F32),
        ],
        compiler_params=params(32),
    )(where, part, here, west, east, over_a, over_b)
    got = hop(send, flip=1)
    return pl.pallas_call(
        add_kernel,
        out_shape=jax.ShapeDtypeStruct((i_rows // 2, times, orb), F32),
        compiler_params=params(16),
    )(keep, got)


def solution(mesh):
    in_specs = (P("tm", None, None), P("aux", None), P("aux", None), P("aux"))
    out_specs = P("aux", "tm", None)
    return jax.shard_map(local, mesh=mesh, in_specs=in_specs, out_specs=out_specs, check_vma=False)
```

time: 155 us -> 103 us (0.66)
  blocking collectives: 86.9 us -> 0 us
  starting transfers between devices: 7.83 us -> 41.2 us
  waiting for transfers between devices: 12.6 us -> 36.4 us
  matrix products: 30.2 us -> 7.4 us
  between operations: 13.4 us -> 0.39 us
  Pallas kernels: 0 us -> 10.9 us
  local copies, waits for them, and re-layouts: 1.32 us -> 3.55 us
    all_gather x1 -> x0, blocking collectives: 65 us -> none  [local(): weights = lax.all_gather(coulomb, 'aux', axis=0, tiled=True)]
    ppermute x1 -> x13, starting transfers between devices: 7.83 us -> 31.1 us  [hop(): return lax.ppermute(value, BOTH, sorted(pairs))]
    dot_general x4 -> x2, matrix products: 30.2 us -> 7.4 us  [the longest x1 3.71 us: local(): jnp.einsum('qo,tok->tqk', masked, green, preferred_element_type=F32)]
    ppermute x1 -> x13, waiting for transfers between devices: 0.01 us -> 22.6 us  [hop(): return lax.ppermute(value, BOTH, sorted(pairs))]
    all_to_all x1 -> x0, blocking collectives: 21.9 us -> none  [local(): part = lax.all_to_all(part, 'aux', split_axis=0, concat_axis=0, tiled=True)]
    all_to_all x0 -> x1, waiting for transfers between devices: none -> 13.9 us  [local(): lax.all_to_all(part, 'aux', 0, 0, axis_index_groups=groups, tiled=True)]
    all_gather x1 -> x0, waiting for transfers between devices: 12.6 us -> none  [local(): rows = lax.all_gather(masked, 'aux', axis=0, tiled=True)]
    pallas_call x0 -> x6, Pallas kernels: none -> 10.9 us  [the longest x3 8.02 us: chunk(): pl.pallas_call(functools.partial(chunk_kernel, tuple(spans), acc is None)...]
  transfers between devices with their start and end apart: 2 -> 14, of which waited for: 1 -> 7; matrix products, arithmetic and copies ran while one was open for 9% -> 7% of each run, Pallas kernels for 0% -> 6%
where the time goes in v2:
time: 103 us; the launch traced here: 102 us
  starting transfers between devices  41.2 us (40%)
  waiting for transfers between devices  36.4 us (35%)
  Pallas kernels  10.9 us (11%)
  matrix products  7.4 us (7%)
  local copies, waits for them, and re-layouts  3.55 us (3%)
  other arithmetic  2.33 us (2%)
    ppermute x13, starting transfers between devices, hop(): return lax.ppermute(value, BOTH, sorted(pairs))  31.1 us
    ppermute x13, waiting for transfers between devices, hop(): return lax.ppermute(value, BOTH, sorted(pairs))  22.6 us
    all_to_all x1, waiting for transfers between devices, local(): lax.all_to_all(part, 'aux', 0, 0, axis_index_groups=groups, tiled=True)  13.9 us
    all_to_all x1, starting transfers between devices, local(): lax.all_to_all(part, 'aux', 0, 0, axis_index_groups=groups, tiled=True)  10.1 us
    pallas_call x3, Pallas kernels, chunk(): pl.pallas_call(functools.partial(chunk_kernel, tuple(spans), acc is None)...  8.02 us
    dot_general x1, matrix products, local(): jnp.einsum('qo,tok->tqk', masked, green, preferred_element_type=F32)  3.71 us
    dot_general x1, matrix products, local(): jnp.einsum('qo,tko->tqk', masked, green, preferred_element_type=F32)  3.69 us
    unnamed x12, local copies, waits for them, and re-layouts  2.89 us
  transfers between devices with their start and end apart: 14, of which 7 were waited for; matrix products, arithmetic and copies ran while one was open for 7% of the time, Pallas kernels for 6%

profile of v2, /device:TPU:1, one launch (start us, length us, event | category | flops | bytes accessed | tf_op | source)
XLA Modules:
  0.0 102.3 jit_solution(12953820123462258914)
XLA Ops:
  0.0 0.7 fusion.14
  0.7 0.7 convert_bitcast_fusion
  1.3 0.1 broadcast_bitcast_fusion
  1.4 1.0 broadcast_multiply_fusion
  2.4 2.5 %collective-permute-start.1 = (bf16[136,1024]{1,0:T(8,128)(2,1)S(1)}, bf16[136,1024]{1,0:T(8,128)(2,1)S(1)}, u32[]{:S(2)}, u32[]{:S(2)}) collective-permute-start(bf16[136,1024]{1,0:T(8,128)(2,1)S(1)} %pad_maximum_fusion), channel_id=1, source_target_pairs={{0,8},{1,9},{2,10},{3,11},{4,12},{5,13},{6,14},{7,15},{8,16},{9,17... | collective-permute-start | bytes 835592 | tf_op jit(solution)/shard_map/ppermute | solution.py:30
  5.0 4.0 %collective-permute-start.2 = (bf16[136,1024]{1,0:T(8,128)(2,1)S(1)}, bf16[136,1024]{1,0:T(8,128)(2,1)S(1)}, u32[]{:S(2)}, u32[]{:S(2)}) collective-permute-start(bf16[136,1024]{1,0:T(8,128)(2,1)S(1)} %pad_maximum_fusion), channel_id=1, source_target_pairs={{0,152},{1,153},{2,154},{3,155},{4,156},{5,157},{6,158},{7,159},{8... | collective-permute-start | bytes 835592 | tf_op jit(solution)/shard_map/ppermute | solution.py:30
  9.0 1.9 %collective-permute-start.4 = (bf16[72,1024]{1,0:T(8,128)(2,1)S(1)}, bf16[72,1024]{1,0:T(8,128)(2,1)S(1)}, u32[]{:S(2)}, u32[]{:S(2)}) collective-permute-start(bf16[72,1024]{1,0:T(8,128)(2,1)S(1)} %fusion.4), channel_id=1, source_target_pairs={{0,144},{1,145},{2,146},{3,147},{4,148},{5,149},{6,150},{7,151},{8... | collective-permute-start | bytes 442376 | tf_op jit(solution)/shard_map/ppermute | solution.py:30
  10.9 0.6 collective-permute-start.3
  11.5 3.7 %fusion.1 = bf16[2,128,1024]{2,1,0:T(8,128)(2,1)} fusion(bf16[2,1024,1024]{2,1,0:T(8,128)(2,1)} %param.4, bf16[128,1024]{1,0:T(8,128)(2,1)S(1)} %broadcast_multiply_fusion), kind=kOutput, calls=%fused_computation.3 | convolution fusion | flops 537133056 | bytes 4980736 | tf_op jit(solution)/shard_map/qo,tok->tqk/dot_general | solution.py:153
  15.3 5.4 %collective-permute-done.4 = bf16[72,1024]{1,0:T(8,128)(2,1)S(1)} collective-permute-done((bf16[72,1024]{1,0:T(8,128)(2,1)S(1)}, bf16[72,1024]{1,0:T(8,128)(2,1)S(1)}, u32[]{:S(2)}, u32[]{:S(2)}) %collective-permute-start.4) | collective-permute-done | bytes 147488 | tf_op jit(solution)/shard_map/ppermute | solution.py:30
  20.7 0.0 collective-permute-done.1
  20.7 0.0 collective-permute-done.2
  20.8 0.0 collective-permute-done.3
  20.8 0.3 concatenate.28.refs_4_.refs_0_
  21.1 1.3 %collective-permute-start.7 = (bf16[520,1024]{1,0:T(8,128)(2,1)S(1)}, bf16[520,1024]{1,0:T(8,128)(2,1)S(1)}, u32[]{:S(2)}, u32[]{:S(2)}) collective-permute-start(bf16[520,1024]{1,0:T(8,128)(2,1)S(1)} %concatenate.28.refs_4_.refs_0_), channel_id=1, source_target_pairs={{0,2},{1,3},{2,4},{3,5},{4,6},{5,7},{6,0},{7,1},{8,10},{9,11},{10,... | collective-permute-start | bytes 3194888 | tf_op jit(solution)/shard_map/ppermute | solution.py:30
  22.4 1.5 %collective-permute-start.8 = (bf16[520,1024]{1,0:T(8,128)(2,1)S(1)}, bf16[520,1024]{1,0:T(8,128)(2,1)S(1)}, u32[]{:S(2)}, u32[]{:S(2)}) collective-permute-start(bf16[520,1024]{1,0:T(8,128)(2,1)S(1)} %concatenate.28.refs_4_.refs_0_), channel_id=1, source_target_pairs={{0,6},{1,7},{2,0},{3,1},{4,2},{5,3},{6,4},{7,5},{8,14},{9,15},{10,... | collective-permute-start | bytes 3194888 | tf_op jit(solution)/shard_map/ppermute | solution.py:30
  23.9 4.3 %collective-permute-start.5 = (bf16[2,128,1024]{2,1,0:T(8,128)(2,1)}, bf16[2,128,1024]{2,1,0:T(8,128)(2,1)S(1)}, u32[]{:S(2)}, u32[]{:S(2)}) collective-permute-start(bf16[2,128,1024]{2,1,0:T(8,128)(2,1)} %fusion.1), channel_id=1, source_target_pairs={{0,128},{1,129},{2,130},{3,131},{4,132},{5,133},{6,134},{7,135},{8... | collective-permute-start | bytes 1572872 | tf_op jit(solution)/shard_map/ppermute | solution.py:30
  28.2 3.7 %fusion.refs_0_ = bf16[2,128,1024]{2,1,0:T(8,128)(2,1)S(1)} fusion(bf16[2,1024,1024]{2,1,0:T(8,128)(2,1)} %param.4, bf16[128,1024]{1,0:T(8,128)(2,1)S(1)} %broadcast_multiply_fusion), kind=kOutput, calls=%fused_computation.2 | convolution fusion | flops 537133056 | bytes 4980736 | tf_op jit(solution)/shard_map/qo,tko->tqk/dot_general | solution.py:154
  31.9 2.8 %collective-permute-start = (bf16[2,128,1024]{2,1,0:T(8,128)(2,1)S(1)}, bf16[2,128,1024]{2,1,0:T(8,128)(2,1)S(1)}, u32[]{:S(2)}, u32[]{:S(2)}) collective-permute-start(bf16[2,128,1024]{2,1,0:T(8,128)(2,1)S(1)} %fusion.refs_0_), channel_id=1, source_target_pairs={{0,1},{1,0},{2,3},{3,2},{4,5},{5,4},{6,7},{7,6},{8,9},{9,8},{10,11... | collective-permute-start | bytes 1572872 | tf_op jit(solution)/shard_map/ppermute | solution.py:30
  34.7 4.8 %collective-permute-done.5.refs_2_ = bf16[2,128,1024]{2,1,0:T(8,128)(2,1)S(1)} collective-permute-done((bf16[2,128,1024]{2,1,0:T(8,128)(2,1)}, bf16[2,128,1024]{2,1,0:T(8,128)(2,1)S(1)}, u32[]{:S(2)}, u32[]{:S(2)}) %collective-permute-start.5) | collective-permute-done | bytes 524320 | tf_op jit(solution)/shard_map/ppermute | solution.py:30
  39.5 3.0 %collective-permute-start.6 = (bf16[2,128,1024]{2,1,0:T(8,128)(2,1)S(1)}, bf16[2,128,1024]{2,1,0:T(8,128)(2,1)S(1)}, u32[]{:S(2)}, u32[]{:S(2)}) collective-permute-start(bf16[2,128,1024]{2,1,0:T(8,128)(2,1)S(1)} %collective-permute-done.5.refs_2_), channel_id=1, source_target_pairs={{0,1},{1,0},{2,3},{3,2},{4,5},{5,4},{6,7},{7,6},{8,9},{9,8},{10,11... | collective-permute-start | bytes 1572872 | tf_op jit(solution)/shard_map/ppermute | solution.py:30
  42.5 3.4 %collective-permute-done.7.refs_4_.refs_1_ = bf16[520,1024]{1,0:T(8,128)(2,1)S(1)} collective-permute-done((bf16[520,1024]{1,0:T(8,128)(2,1)S(1)}, bf16[520,1024]{1,0:T(8,128)(2,1)S(1)}, u32[]{:S(2)}, u32[]{:S(2)}) %collective-permute-start.7) | collective-permute-done | bytes 1064992 | tf_op jit(solution)/shard_map/ppermute | solution.py:30
  45.9 0.0 collective-permute-done.8.refs_5_.refs_2_
  45.9 2.5 %collective-permute-start.10 = (bf16[264,1024]{1,0:T(8,128)(2,1)S(1)}, bf16[264,1024]{1,0:T(8,128)(2,1)S(1)}, u32[]{:S(2)}, u32[]{:S(2)}) collective-permute-start(bf16[264,1024]{1,0:T(8,128)(2,1)S(1)} %slice.43), channel_id=1, source_target_pairs={{0,6},{1,7},{2,0},{3,1},{4,2},{5,3},{6,4},{7,5},{8,14},{9,15},{10,... | collective-permute-start | bytes 1622024 | tf_op jit(solution)/shard_map/ppermute | solution.py:30
  48.4 0.3 collective-permute-start.9
  48.7 0.0 collective-permute-done.refs_1_
  48.7 0.0 collective-permute-done.6.refs_3_
  48.7 2.0 %shard_map.46 = (f32[2,128,1024]{2,1,0:T(8,128)S(1)}, f32[2,128,1024]{2,1,0:T(8,128)S(1)}) custom-call(bf16[2,128,1024]{2,1,0:T(8,128)(2,1)S(1)} %fusion.refs_0_, bf16[2,128,1024]{2,1,0:T(8,128)(2,1)S(1)} %collective-permute-done.refs_1_, bf16[2,128,1024]{2,1,0:T(8,128)(2,1)S(1)} %collective-permute-done.5.refs_2_, ...), custom_call_target="tpu_custom_call" | custom-call | flops 1610612736 | bytes 2097152 | tf_op jit(solution)/shard_map/pallas_call | solution.py:81
  50.7 4.0 %shard_map.47 = (f32[2,128,1024]{2,1,0:T(8,128)S(1)}, f32[2,128,1024]{2,1,0:T(8,128)S(1)}) custom-call(bf16[2,128,1024]{2,1,0:T(8,128)(2,1)S(1)} %fusion.refs_0_, bf16[2,128,1024]{2,1,0:T(8,128)(2,1)S(1)} %collective-permute-done.refs_1_, bf16[2,128,1024]{2,1,0:T(8,128)(2,1)S(1)} %collective-permute-done.5.refs_2_, ...), custom_call_target="tpu_custom_call", output_to_operand_aliasing={{0}: (6, {}), {1}: (7, {})} | custom-call | flops 3221225472 | bytes 2097152 | tf_op jit(solution)/shard_map/pallas_call | solution.py:81
  54.7 0.0 copy-start.5
  54.7 5.6 %collective-permute-done.9.refs_4_.refs_3_ = bf16[256,1024]{1,0:T(8,128)(2,1)S(1)} collective-permute-done((bf16[256,1024]{1,0:T(8,128)(2,1)S(1)}, bf16[256,1024]{1,0:T(8,128)(2,1)S(1)}, u32[]{:S(2)}, u32[]{:S(2)}) %collective-permute-start.9) | collective-permute-done | bytes 524320 | tf_op jit(solution)/shard_map/ppermute | solution.py:30
  60.3 0.0 collective-permute-done.10.refs_5_.refs_4_
  60.3 2.0 %shard_map.48 = (f32[2,128,1024]{2,1,0:T(8,128)S(1)}, f32[2,128,1024]{2,1,0:T(8,128)S(1)}) custom-call(bf16[2,128,1024]{2,1,0:T(8,128)(2,1)S(1)} %fusion.refs_0_, bf16[2,128,1024]{2,1,0:T(8,128)(2,1)S(1)} %collective-permute-done.refs_1_, bf16[2,128,1024]{2,1,0:T(8,128)(2,1)S(1)} %collective-permute-done.5.refs_2_, ...), custom_call_target="tpu_custom_call", output_to_operand_aliasing={{0}: (6, {}), {1}: (7, {})} | custom-call | flops 1610612736 | bytes 2097152 | tf_op jit(solution)/shard_map/pallas_call | solution.py:81
  62.3 4.0 %collective-permute-start.11 = (f32[2,128,1024]{2,1,0:T(8,128)S(1)}, f32[2,128,1024]{2,1,0:T(8,128)S(1)}, u32[]{:S(2)}, u32[]{:S(2)}) collective-permute-start(f32[2,128,1024]{2,1,0:T(8,128)S(1)} %get-tuple-element.26), channel_id=1, source_target_pairs={{0,1},{1,0},{2,3},{3,2},{4,5},{5,4},{6,7},{7,6},{8,9},{9,8},{10,11... | collective-permute-start | bytes 3145736 | tf_op jit(solution)/shard_map/ppermute | solution.py:30
  66.4 2.3 %collective-permute-done.11.got_ref = f32[2,128,1024]{2,1,0:T(8,128)S(1)} collective-permute-done((f32[2,128,1024]{2,1,0:T(8,128)S(1)}, f32[2,128,1024]{2,1,0:T(8,128)S(1)}, u32[]{:S(2)}, u32[]{:S(2)}) %collective-permute-start.11) | collective-permute-done | bytes 1048608 | tf_op jit(solution)/shard_map/ppermute | solution.py:30
  68.7 0.0 copy-done.1
  68.7 0.3 shard_map.49
  69.0 0.0 copy-start
  69.0 0.8 copy-done
  69.8 10.1 %all-to-all-start = ((bf16[16,2,64,128]{3,2,1,0:T(8,128)(2,1)}), bf16[16,2,64,128]{3,2,1,0:T(8,128)(2,1)}, u32[]{:S(2)}, u32[]{:S(2)}) async-start(bf16[16,2,64,128]{3,2,1,0:T(8,128)(2,1)} %copy-done), calls=%async_computation | async-start | bytes 1048576 | tf_op jit(solution)/shard_map/all_to_all | solution.py:190
  80.1 0.1 stack.71.where_ref
  80.2 13.9 %all-to-all-done.part_ref = bf16[16,2,64,128]{3,2,1,0:T(8,128)(2,1)} async-done(((bf16[16,2,64,128]{3,2,1,0:T(8,128)(2,1)}), bf16[16,2,64,128]{3,2,1,0:T(8,128)(2,1)}, u32[]{:S(2)}, u32[]{:S(2)}) %all-to-all-start) | async-done | bytes 524320 | tf_op jit(solution)/shard_map/all_to_all | solution.py:190
  94.1 1.0 %copy-done.2 = bf16[264,1024]{1,0:T(8,128)(2,1)S(1)} copy-done((bf16[264,1024]{1,0:T(8,128)(2,1)S(1)}, bf16[264,1024]{1,0:T(8,128)(2,1)}, u32[]{:S(2)}) %copy-start.2) | copy-done | bytes 540696
  95.1 1.0 %copy-done.4 = bf16[256,1024]{1,0:T(8,128)(2,1)S(1)} copy-done((bf16[256,1024]{1,0:T(8,128)(2,1)S(1)}, bf16[256,1024]{1,0:T(8,128)(2,1)}, u32[]{:S(2)}) %copy-start.4) | copy-done | bytes 524312
  96.2 1.8 %shard_map.50 = (f32[2,32,1024]{2,1,0:T(8,128)S(1)}, f32[2,32,1024]{2,1,0:T(8,128)S(1)}) custom-call(s32[17]{0:T(128)S(1)} %stack.71.where_ref, bf16[16,2,64,128]{3,2,1,0:T(8,128)(2,1)} %all-to-all-done.part_ref, bf16[520,1024]{1,0:T(8,128)(2,1)S(1)} %concatenate.28.refs_4_.refs_0_, bf16[520,1024]{1,0:T(8,128)(2,1)S(1)} %collective-permute-done.7.refs_4_.refs_1_, ...), custom_call_target="tpu_custom_call" | custom-call | tf_op jit(solution)/shard_map/pallas_call | solution.py:199
  98.0 2.3 %collective-permute-start.12 = (f32[2,32,1024]{2,1,0:T(8,128)S(1)}, f32[2,32,1024]{2,1,0:T(8,128)S(1)}, u32[]{:S(2)}, u32[]{:S(2)}) collective-permute-start(f32[2,32,1024]{2,1,0:T(8,128)S(1)} %get-tuple-element.28), channel_id=1, source_target_pairs={{0,1},{1,0},{2,3},{3,2},{4,5},{5,4},{6,7},{7,6},{8,9},{9,8},{10,11... | collective-permute-start | bytes 786440 | tf_op jit(solution)/shard_map/ppermute | solution.py:30
  100.3 1.2 %collective-permute-done.12.got_ref = f32[2,32,1024]{2,1,0:T(8,128)S(1)} collective-permute-done((f32[2,32,1024]{2,1,0:T(8,128)S(1)}, f32[2,32,1024]{2,1,0:T(8,128)S(1)}, u32[]{:S(2)}, u32[]{:S(2)}) %collective-permute-start.12) | collective-permute-done | bytes 262176 | tf_op jit(solution)/shard_map/ppermute | solution.py:30
  101.5 0.8 shard_map.51
  (20 shorter events, 0.2 us)
Async XLA Ops:
  2.4 18.2 %collective-permute-start.1 = (bf16[136,1024]{1,0:T(8,128)(2,1)S(1)}, bf16[136,1024]{1,0:T(8,128)(2,1)S(1)}, u32[]{:S(2)}, u32[]{:S(2)}) collective-permute-start(bf16[136,1024]{1,0:T(8,128)(2,1)S(1)} %pad_maximum_fusion), channel_id=1, source_target_pairs={{0,8},{1,9},{2,10},{3,11},{4,12},{5,13},{6,14},{7,15},{8,16},{9,17... | collective-permute-start | bytes 835592 | tf_op jit(solution)/shard_map/ppermute | solution.py:30
  5.0 15.8 %collective-permute-start.2 = (bf16[136,1024]{1,0:T(8,128)(2,1)S(1)}, bf16[136,1024]{1,0:T(8,128)(2,1)S(1)}, u32[]{:S(2)}, u32[]{:S(2)}) collective-permute-start(bf16[136,1024]{1,0:T(8,128)(2,1)S(1)} %pad_maximum_fusion), channel_id=1, source_target_pairs={{0,152},{1,153},{2,154},{3,155},{4,156},{5,157},{6,158},{7,159},{8... | collective-permute-start | bytes 835592 | tf_op jit(solution)/shard_map/ppermute | solution.py:30
  9.0 11.6 %collective-permute-start.4 = (bf16[72,1024]{1,0:T(8,128)(2,1)S(1)}, bf16[72,1024]{1,0:T(8,128)(2,1)S(1)}, u32[]{:S(2)}, u32[]{:S(2)}) collective-permute-start(bf16[72,1024]{1,0:T(8,128)(2,1)S(1)} %fusion.4), channel_id=1, source_target_pairs={{0,144},{1,145},{2,146},{3,147},{4,148},{5,149},{6,150},{7,151},{8... | collective-permute-start | bytes 442376 | tf_op jit(solution)/shard_map/ppermute | solution.py:30
  10.9 9.9 %collective-permute-start.3 = (bf16[64,1024]{1,0:T(8,128)(2,1)S(1)}, bf16[64,1024]{1,0:T(8,128)(2,1)S(1)}, u32[]{:S(2)}, u32[]{:S(2)}) collective-permute-start(bf16[64,1024]{1,0:T(8,128)(2,1)S(1)} %slice.46), channel_id=1, source_target_pairs={{0,16},{1,17},{2,18},{3,19},{4,20},{5,21},{6,22},{7,23},{8,24},{9,... | collective-permute-start | bytes 393224 | tf_op jit(solution)/shard_map/ppermute | solution.py:30
  21.1 24.7 %collective-permute-start.7 = (bf16[520,1024]{1,0:T(8,128)(2,1)S(1)}, bf16[520,1024]{1,0:T(8,128)(2,1)S(1)}, u32[]{:S(2)}, u32[]{:S(2)}) collective-permute-start(bf16[520,1024]{1,0:T(8,128)(2,1)S(1)} %concatenate.28.refs_4_.refs_0_), channel_id=1, source_target_pairs={{0,2},{1,3},{2,4},{3,5},{4,6},{5,7},{6,0},{7,1},{8,10},{9,11},{10,... | collective-permute-start | bytes 3194888 | tf_op jit(solution)/shard_map/ppermute | solution.py:30
  22.4 23.5 %collective-permute-start.8 = (bf16[520,1024]{1,0:T(8,128)(2,1)S(1)}, bf16[520,1024]{1,0:T(8,128)(2,1)S(1)}, u32[]{:S(2)}, u32[]{:S(2)}) collective-permute-start(bf16[520,1024]{1,0:T(8,128)(2,1)S(1)} %concatenate.28.refs_4_.refs_0_), channel_id=1, source_target_pairs={{0,6},{1,7},{2,0},{3,1},{4,2},{5,3},{6,4},{7,5},{8,14},{9,15},{10,... | collective-permute-start | bytes 3194888 | tf_op jit(solution)/shard_map/ppermute | solution.py:30
  23.9 15.6 %collective-permute-start.5 = (bf16[2,128,1024]{2,1,0:T(8,128)(2,1)}, bf16[2,128,1024]{2,1,0:T(8,128)(2,1)S(1)}, u32[]{:S(2)}, u32[]{:S(2)}) collective-permute-start(bf16[2,128,1024]{2,1,0:T(8,128)(2,1)} %fusion.1), channel_id=1, source_target_pairs={{0,128},{1,129},{2,130},{3,131},{4,132},{5,133},{6,134},{7,135},{8... | collective-permute-start | bytes 1572872 | tf_op jit(solution)/shard_map/ppermute | solution.py:30
  31.9 16.8 %collective-permute-start = (bf16[2,128,1024]{2,1,0:T(8,128)(2,1)S(1)}, bf16[2,128,1024]{2,1,0:T(8,128)(2,1)S(1)}, u32[]{:S(2)}, u32[]{:S(2)}) collective-permute-start(bf16[2,128,1024]{2,1,0:T(8,128)(2,1)S(1)} %fusion.refs_0_), channel_id=1, source_target_pairs={{0,1},{1,0},{2,3},{3,2},{4,5},{5,4},{6,7},{7,6},{8,9},{9,8},{10,11... | collective-permute-start | bytes 1572872 | tf_op jit(solution)/shard_map/ppermute | solution.py:30
  39.5 9.2 %collective-permute-start.6 = (bf16[2,128,1024]{2,1,0:T(8,128)(2,1)S(1)}, bf16[2,128,1024]{2,1,0:T(8,128)(2,1)S(1)}, u32[]{:S(2)}, u32[]{:S(2)}) collective-permute-start(bf16[2,128,1024]{2,1,0:T(8,128)(2,1)S(1)} %collective-permute-done.5.refs_2_), channel_id=1, source_target_pairs={{0,1},{1,0},{2,3},{3,2},{4,5},{5,4},{6,7},{7,6},{8,9},{9,8},{10,11... | collective-permute-start | bytes 1572872 | tf_op jit(solution)/shard_map/ppermute | solution.py:30
  45.9 14.4 %collective-permute-start.10 = (bf16[264,1024]{1,0:T(8,128)(2,1)S(1)}, bf16[264,1024]{1,0:T(8,128)(2,1)S(1)}, u32[]{:S(2)}, u32[]{:S(2)}) collective-permute-start(bf16[264,1024]{1,0:T(8,128)(2,1)S(1)} %slice.43), channel_id=1, source_target_pairs={{0,6},{1,7},{2,0},{3,1},{4,2},{5,3},{6,4},{7,5},{8,14},{9,15},{10,... | collective-permute-start | bytes 1622024 | tf_op jit(solution)/shard_map/ppermute | solution.py:30
  48.4 11.9 %collective-permute-start.9 = (bf16[256,1024]{1,0:T(8,128)(2,1)S(1)}, bf16[256,1024]{1,0:T(8,128)(2,1)S(1)}, u32[]{:S(2)}, u32[]{:S(2)}) collective-permute-start(bf16[256,1024]{1,0:T(8,128)(2,1)S(1)} %slice.42), channel_id=1, source_target_pairs={{0,2},{1,3},{2,4},{3,5},{4,6},{5,7},{6,0},{7,1},{8,10},{9,11},{10,... | collective-permute-start | bytes 1572872 | tf_op jit(solution)/shard_map/ppermute | solution.py:30
  54.7 14.0 %copy-start.5 = (f32[128]{0:T(128)S(1)}, f32[128]{0:T(128)}, u32[]{:S(2)}) copy-start(f32[128]{0:T(128)} %param.7) | copy-start | bytes 1540
  60.3 8.4 %copy-start.3 = (bf16[256,1024]{1,0:T(8,128)(2,1)}, bf16[256,1024]{1,0:T(8,128)(2,1)S(1)}, u32[]{:S(2)}) copy-start(bf16[256,1024]{1,0:T(8,128)(2,1)S(1)} %collective-permute-done.9.refs_4_.refs_3_) | copy-start | bytes 1572868
  60.3 8.4 %copy-start.1 = (bf16[264,1024]{1,0:T(8,128)(2,1)}, bf16[264,1024]{1,0:T(8,128)(2,1)S(1)}, u32[]{:S(2)}) copy-start(bf16[264,1024]{1,0:T(8,128)(2,1)S(1)} %collective-permute-done.10.refs_5_.refs_4_) | copy-start | bytes 1622020
  62.3 6.3 %collective-permute-start.11 = (f32[2,128,1024]{2,1,0:T(8,128)S(1)}, f32[2,128,1024]{2,1,0:T(8,128)S(1)}, u32[]{:S(2)}, u32[]{:S(2)}) collective-permute-start(f32[2,128,1024]{2,1,0:T(8,128)S(1)} %get-tuple-element.26), channel_id=1, source_target_pairs={{0,1},{1,0},{2,3},{3,2},{4,5},{5,4},{6,7},{7,6},{8,9},{9,8},{10,11... | collective-permute-start | bytes 3145736 | tf_op jit(solution)/shard_map/ppermute | solution.py:30
  69.0 0.8 copy-start
  69.8 24.3 %all-to-all-start = ((bf16[16,2,64,128]{3,2,1,0:T(8,128)(2,1)}), bf16[16,2,64,128]{3,2,1,0:T(8,128)(2,1)}, u32[]{:S(2)}, u32[]{:S(2)}) async-start(bf16[16,2,64,128]{3,2,1,0:T(8,128)(2,1)} %copy-done), calls=%async_computation | async-start | bytes 1048576 | tf_op jit(solution)/shard_map/all_to_all | solution.py:190
  94.1 1.0 %copy-start.2 = (bf16[264,1024]{1,0:T(8,128)(2,1)S(1)}, bf16[264,1024]{1,0:T(8,128)(2,1)}, u32[]{:S(2)}) copy-start(bf16[264,1024]{1,0:T(8,128)(2,1)} %copy-done.1) | copy-start | bytes 1622020
  95.1 1.0 %copy-start.4 = (bf16[256,1024]{1,0:T(8,128)(2,1)S(1)}, bf16[256,1024]{1,0:T(8,128)(2,1)}, u32[]{:S(2)}) copy-start(bf16[256,1024]{1,0:T(8,128)(2,1)} %copy-done.3) | copy-start | bytes 1572868
  98.0 3.5 %collective-permute-start.12 = (f32[2,32,1024]{2,1,0:T(8,128)S(1)}, f32[2,32,1024]{2,1,0:T(8,128)S(1)}, u32[]{:S(2)}, u32[]{:S(2)}) collective-permute-start(f32[2,32,1024]{2,1,0:T(8,128)S(1)} %get-tuple-element.28), channel_id=1, source_target_pairs={{0,1},{1,0},{2,3},{3,2},{4,5},{5,4},{6,7},{7,6},{8,9},{9,8},{10,11... | collective-permute-start | bytes 786440 | tf_op jit(solution)/shard_map/ppermute | solution.py:30

commit v3 on v2

v3 whole, which is shorter than its diff:
```python
import functools

import jax
import jax.numpy as jnp
from jax import lax
from jax.experimental import pallas as pl
from jax.experimental.pallas import tpu as pltpu
from jax.sharding import PartitionSpec as P

BLOCK = 128
HALF = 64
F32, BF16 = jnp.float32, jnp.bfloat16
BOTH = ("tm", "aux")
NT = (((1,), (1,)), ((), ()))
NN = (((1,), (0,)), ((), ()))
VMEM = pl.BlockSpec(memory_space=pltpu.VMEM)


def device_at(x, y, z, core):
    return (z // 4 * 4 + y) * 32 + (z % 4 * 4 + x) * 2 + core


def hop(value, dx=0, dy=0, dz=0, flip=0):
    pairs = []
    for x in range(4):
        for y in range(4):
            for z in range(8):
                for core in range(2):
                    to = device_at((x + dx) % 4, (y + dy) % 4, (z + dz) % 8, core ^ flip)
                    pairs.append((device_at(x, y, z, core), to))
    return lax.ppermute(value, BOTH, sorted(pairs))


def params(mib):
    return pltpu.CompilerParams(vmem_limit_bytes=mib << 20)


def prologue_kernel(factors, pattern, coulomb, masked_ref, whole_ref, first_ref, second_ref, own_ref):
    parity = lax.axis_index("tm") & 1
    orb = factors.shape[1]
    for block in range(orb // BLOCK):
        lanes = pl.ds(block * BLOCK, BLOCK)
        keep = pattern[:, block : block + 1].astype(F32)
        for half in range(2):
            at = parity if half == 0 else 1 - parity
            part = factors[pl.ds(pl.multiple_of(at * HALF, HALF), HALF), lanes]
            part = (part.astype(F32) * keep).astype(BF16)
            masked_ref[pl.ds(half * HALF, HALF), lanes] = part
            if half == 0:
                whole_ref[pl.ds(0, HALF), lanes] = part
                first_ref[:, lanes] = part[: HALF // 2]
                second_ref[pl.ds(0, HALF // 2), lanes] = part[HALF // 2 :]
    c = coulomb[...]
    turned = pltpu.roll(c, HALF, 1)
    own = jnp.where(parity == 0, c, turned)
    own_ref[...] = own
    lane = lax.broadcasted_iota(jnp.int32, own.shape, 1)
    twice = jnp.where(lane < HALF, own, pltpu.roll(own, HALF, 1))
    high = twice.astype(BF16)
    rest = twice - high.astype(F32)
    middle = rest.astype(BF16)
    low = (rest - middle.astype(F32)).astype(BF16)
    zero = jnp.zeros((1, orb - 3 * BLOCK), BF16)
    row = jnp.concatenate([high, middle, low, zero], axis=1)
    rows = jnp.broadcast_to(row.astype(F32), (8, orb)).astype(BF16)
    whole_ref[pl.ds(HALF, 8), :] = rows
    second_ref[pl.ds(HALF // 2, 8), :] = rows


def prologue(factors, pattern, coulomb):
    own, orb = factors.shape
    shapes = [(own, orb), (HALF + 8, orb), (HALF // 2, orb), (HALF // 2 + 8, orb)]
    return pl.pallas_call(
        prologue_kernel,
        out_shape=[jax.ShapeDtypeStruct(s, BF16) for s in shapes]
        + [jax.ShapeDtypeStruct((1, own), F32)],
        in_specs=[VMEM] * 3,
        out_specs=[VMEM] * 5,
        compiler_params=params(8),
    )(factors, pattern, coulomb[None, :])


def weight_of(ref, row):
    parts = [ref[pl.ds(row, 1), pl.ds(k * BLOCK, BLOCK)].astype(F32) for k in range(3)]
    return parts[0] + (parts[1] + parts[2])


def weights_of(ref, row, blocks):
    lane = lax.broadcasted_iota(jnp.int32, (1, BLOCK), 1)
    pairs = []
    for k in range(0, blocks, 2):
        pairs.append(jnp.where(lane < HALF, weight_of(ref, row + k), weight_of(ref, row + k + 1)))
    return jnp.concatenate(pairs, axis=1) if len(pairs) > 1 else pairs[0]


def chunk_kernel(pieces, count, first, *refs):
    right_own, right_other, left_own, left_other = refs[:4]
    rows = refs[4 : 4 + count]
    rest = refs[4 + count :]
    if not first:
        acc_own, acc_other = rest[:2]
        rest = rest[2:]
    out_own, out_other = rest
    own = out_own.shape[1]
    for t in range(out_own.shape[0]):
        right = jnp.concatenate([right_own[t], right_other[t]], axis=0)
        left = jnp.concatenate([left_own[t], left_other[t]], axis=0)
        total = None
        for piece in pieces:
            part = jnp.concatenate([rows[at][pl.ds(0, n), :] for at, n in piece[0]], axis=0)
            weight = weights_of(rows[piece[1]], piece[2], part.shape[0] // HALF)
            a = lax.dot_general(right, part, NT, preferred_element_type=F32)
            m = lax.dot_general(left, part, NT, preferred_element_type=F32)
            k = (a * weight * (a * m)).astype(BF16)
            d = lax.dot_general(k, part, NN, preferred_element_type=F32)
            total = d if total is None else total + d
        if first:
            out_own[t] = total[:own]
            out_other[t] = total[own:]
        else:
            out_own[t] = acc_own[t] + total[:own]
            out_other[t] = acc_other[t] + total[own:]


def chunk(sides, rows, pieces, acc=None):
    times, own, orb = sides[0].shape
    shape = jax.ShapeDtypeStruct((times, own, orb), F32)
    extra = () if acc is None else tuple(acc)
    aliases = {} if acc is None else {4 + len(rows): 0, 5 + len(rows): 1}
    flops = len(pieces) * 4 * HALF * times * 3 * 2 * (2 * own) * orb
    return pl.pallas_call(
        functools.partial(chunk_kernel, tuple(pieces), len(rows), acc is None),
        out_shape=(shape, shape),
        in_specs=[VMEM] * (4 + len(rows) + len(extra)),
        out_specs=(VMEM, VMEM),
        input_output_aliases=aliases,
        compiler_params=params(16),
        cost_estimate=pl.CostEstimate(flops=flops, bytes_accessed=2 << 20, transcendentals=0),
    )(*sides, *rows, *extra)


def finish_kernel(own_ref, got_ref, coulomb_ref, out_ref):
    chips, times, rows, _ = out_ref.shape
    for t in range(times):
        d = jnp.transpose(own_ref[t] + got_ref[t]) * coulomb_ref[...]
        d = d.astype(BF16)
        for chip in range(chips):
            out_ref[chip, t] = d[chip * rows : (chip + 1) * rows]


def sigma_kernel(part_ref, *refs):
    here, west, east = refs[0:2], refs[2:4], refs[4:6]
    far = (refs[6:8], refs[8:10])
    keep_ref, send_ref, lhs, total_ref = refs[10:]
    chips, times, i_rows, width = part_ref.shape
    me = lax.axis_index("aux")
    core, x, z = me & 1, (me >> 1) & 3, me >> 3
    total = None
    for column, dx in enumerate((0, 3, 1, 2)):
        parts = []
        for k, dz in enumerate((0, 3, 1, 2)):
            source = ((z + dz) & 3) * 4 + ((x + dx) & 3)
            for t in range(times):
                at = pl.ds((column * 4 + k) * width, width)
                lhs[pl.ds(t * i_rows, i_rows), at] = part_ref[source, t]
            for parity in range(2):
                if column < 3:
                    ref, row = (here, west, east)[column][parity], k * HALF
                else:
                    ref, row = far[parity][k // 2], k % 2 * HALF
                parts.append(ref[pl.ds(row, HALF), :])
        d = lax.dot_general(
            lhs[:, pl.ds(column * 4 * width, 4 * width)],
            jnp.concatenate(parts, axis=0),
            NN,
            preferred_element_type=F32,
        )
        total = d if total is None else total + d
    total_ref[...] = total
    half = i_rows // 2
    for t in range(times):
        keep = pl.multiple_of(t * i_rows + core * half, half)
        send = pl.multiple_of(t * i_rows + (1 - core) * half, half)
        keep_ref[t] = total_ref[pl.ds(keep, half), :]
        send_ref[t] = total_ref[pl.ds(send, half), :]


def add_kernel(keep_ref, got_ref, out_ref):
    for t in range(keep_ref.shape[0]):
        out_ref[:, t, :] = keep_ref[t] + got_ref[t]


def local(green, factors, pattern, coulomb):
    times, orb, _ = green.shape
    own = factors.shape[0]
    barrier = lax.optimization_barrier
    masked, whole, first, second, coulomb = prologue(factors, pattern, coulomb)

    below = hop(whole, dz=1)
    above = hop(whole, dz=-1)
    far_a = hop(first, dz=2)
    far_b = hop(second, dz=-2)
    left = jnp.einsum("qo,tok->tqk", masked, green, preferred_element_type=F32).astype(BF16)
    right = jnp.einsum("qo,tko->tqk", masked, green, preferred_element_type=F32).astype(BF16)
    right_other = hop(right, flip=1)

    quarter = HALF // 2
    weights = [whole[HALF : HALF + 1], below[HALF : HALF + 1], above[HALF : HALF + 1]]
    weights += [far_b[quarter : quarter + 1], jnp.zeros((4, orb), BF16)]
    here = [masked[:HALF], below[:HALF], above[:HALF], far_a, far_b[:quarter]] + weights
    here, left = barrier((jnp.concatenate(here, axis=0), left))

    n = 4 * HALF
    west = hop(here, dx=1)
    east = hop(here, dx=-1)
    left = hop(left, dz=4)
    cut = HALF + 3 * quarter
    rest_a = hop(here[HALF:cut], dy=-1)
    rest_b = hop(here[cut:], dy=1)
    left_other = hop(left, flip=1)
    here_q = jnp.concatenate([masked[HALF:], rest_a, rest_b], axis=0)

    west, east = barrier((west, east))
    over_a = hop(west[: n // 2], dx=1)
    over_b = hop(east[n // 2 :], dx=-1)
    west_q = hop(west, dy=-1)
    east_q = hop(east, dy=1)
    over_a, over_b = barrier((over_a, over_b))
    over_aq = hop(over_a, dy=-1)
    over_bq = hop(over_b, dy=1)

    sides = (right, right_other, left, left_other)
    acc = chunk(sides, (here, here_q), [(((0, n),), 0, n), (((1, n),), 1, n)])
    acc = chunk(sides, (west, east), [(((0, n),), 0, n), (((1, n),), 1, n)], acc)
    acc = chunk(sides, (west_q, east_q), [(((0, n),), 0, n), (((1, n),), 1, n)], acc)
    pieces = [(((0, n // 2), (1, n // 2)), 1, n // 2), (((2, n // 2), (3, n // 2)), 3, n // 2)]
    keep, send = chunk(sides, (over_a, over_b, over_aq, over_bq), pieces, acc)

    got = hop(send, flip=1)
    chips, i_rows = 16, orb // 16
    part = pl.pallas_call(
        finish_kernel,
        out_shape=jax.ShapeDtypeStruct((chips, times, i_rows, own), BF16),
        in_specs=[VMEM] * 3,
        out_specs=VMEM,
        compiler_params=params(12),
    )(keep, got, coulomb)
    groups = [[2 * chip + core for chip in range(chips)] for core in range(2)]
    part = lax.all_to_all(part, "aux", 0, 0, axis_index_groups=groups, tiled=True)

    shape = jax.ShapeDtypeStruct((times, i_rows // 2, orb), F32)
    keep, send = pl.pallas_call(
        sigma_kernel,
        out_shape=(shape, shape),
        in_specs=[VMEM] * 11,
        out_specs=(VMEM, VMEM),
        scratch_shapes=[
            pltpu.VMEM((times * i_rows, chips * own), BF16),
            pltpu.VMEM((times * i_rows, orb), F32),
        ],
        compiler_params=params(12),
    )(part, here, here_q, west, west_q, east, east_q, over_a, over_b, over_aq, over_bq)
    got = hop(send, flip=1)
    return pl.pallas_call(
        add_kernel,
        out_shape=jax.ShapeDtypeStruct((i_rows // 2, times, orb), F32),
        in_specs=[VMEM] * 2,
        out_specs=VMEM,
        compiler_params=params(8),
    )(keep, got)


def solution(mesh):
    in_specs = (P("tm", None, None), P("aux", None), P("aux", None), P("aux"))
    out_specs = P("aux", "tm", None)
    return jax.shard_map(local, mesh=mesh, in_specs=in_specs, out_specs=out_specs, check_vma=False)
```

time: 103 us -> 109 us (1.058)
  blocking collectives: 0 us -> 31.8 us
  waiting for transfers between devices: 36.4 us -> 17.5 us
  other arithmetic: 2.33 us -> 0.04 us
    all_to_all x0 -> x1, blocking collectives: none -> 31.8 us  [local(): lax.all_to_all(part, 'aux', 0, 0, axis_index_groups=groups, tiled=True)]
    all_to_all x1 -> x0, waiting for transfers between devices: 13.9 us -> none  [local(): lax.all_to_all(part, 'aux', 0, 0, axis_index_groups=groups, tiled=True)]
    all_to_all x1 -> x0, starting transfers between devices: 10.1 us -> none  [local(): lax.all_to_all(part, 'aux', 0, 0, axis_index_groups=groups, tiled=True)]
    ppermute x13 -> x19, starting transfers between devices: 31.1 us -> 40.2 us  [hop(): return lax.ppermute(value, BOTH, sorted(pairs))]
    ppermute x13 -> x19, waiting for transfers between devices: 22.6 us -> 17.5 us  [hop(): return lax.ppermute(value, BOTH, sorted(pairs))]
    unnamed x12 -> x6, local copies, waits for them, and re-layouts: 2.89 us -> 2.26 us
    pallas_call x4 -> x6, Pallas kernels: 9.83 us -> 9.23 us  [the longest x4 8.27 us: chunk(): pl.pallas_call(functools.partial(chunk_kernel, tuple(pieces), len(rows),...]
  transfers between devices with their start and end apart: 14 -> 19, of which waited for: 7 -> 8; matrix products, arithmetic and copies ran while one was open for 7% -> 6% of each run, Pallas kernels for 6% -> 6%
where the time goes in v3:
time: 109 us
  starting transfers between devices  40.2 us (37%)
  blocking collectives  31.8 us (29%)
  waiting for transfers between devices  17.5 us (16%)
  Pallas kernels  10.3 us (9%)
  matrix products  6.61 us (6%)
  local copies, waits for them, and re-layouts  2.48 us (2%)
    ppermute x19, starting transfers between devices, hop(): return lax.ppermute(value, BOTH, sorted(pairs))  40.2 us
    all_to_all x1, blocking collectives, local(): lax.all_to_all(part, 'aux', 0, 0, axis_index_groups=groups, tiled=True)  31.8 us
    ppermute x19, waiting for transfers between devices, hop(): return lax.ppermute(value, BOTH, sorted(pairs))  17.5 us
    pallas_call x4, Pallas kernels, chunk(): pl.pallas_call(functools.partial(chunk_kernel, tuple(pieces), len(rows),...  8.27 us
    dot_general x1, matrix products, local(): jnp.einsum('qo,tko->tqk', masked, green, preferred_element_type=F32)  3.69 us
    dot_general x1, matrix products, local(): jnp.einsum('qo,tok->tqk', masked, green, preferred_element_type=F32)  2.92 us
    unnamed x6, local copies, waits for them, and re-layouts  2.26 us
  transfers between devices with their start and end apart: 19, of which 8 were waited for; matrix products, arithmetic and copies ran while one was open for 6% of the time, Pallas kernels for 6%

profile of v3, /device:TPU:1, one launch (start us, length us, event | category | flops | bytes accessed | tf_op | source)
XLA Modules:
  0.0 109.2 jit_solution(3299042688934239064)
XLA Ops:
  0.0 0.9 copy-done
  1.0 0.7 copy-done.1
  1.6 0.7 copy-done.2
  2.3 0.2 shard_map.46
  2.5 6.5 %collective-permute-start.2 = (bf16[72,1024]{1,0:T(8,128)(2,1)S(1)}, bf16[72,1024]{1,0:T(8,128)(2,1)S(1)}, u32[]{:S(2)}, u32[]{:S(2)}) collective-permute-start(bf16[72,1024]{1,0:T(8,128)(2,1)S(1)} %get-tuple-element.27), channel_id=1, source_target_pairs={{0,152},{1,153},{2,154},{3,155},{4,156},{5,157},{6,158},{7,159},{8... | collective-permute-start | bytes 442376 | tf_op jit(solution)/shard_map/ppermute | solution.py:31
  8.9 0.0 collective-permute-start.1
  8.9 0.0 collective-permute-start.3
  8.9 3.6 %collective-permute-start.4 = (bf16[40,1024]{1,0:T(8,128)(2,1)S(1)}, bf16[40,1024]{1,0:T(8,128)(2,1)S(1)}, u32[]{:S(2)}, u32[]{:S(2)}) collective-permute-start(bf16[40,1024]{1,0:T(8,128)(2,1)S(1)} %get-tuple-element.29), channel_id=1, source_target_pairs={{0,144},{1,145},{2,146},{3,147},{4,148},{5,149},{6,150},{7,151},{8... | collective-permute-start | bytes 245768 | tf_op jit(solution)/shard_map/ppermute | solution.py:31
  12.5 2.9 %fusion.1 = bf16[2,128,1024]{2,1,0:T(8,128)(2,1)S(1)} fusion(bf16[2,1024,1024]{2,1,0:T(8,128)(2,1)} %param.4, bf16[128,1024]{1,0:T(8,128)(2,1)S(1)} %get-tuple-element.26), kind=kOutput, calls=%fused_computation.3 | convolution fusion | flops 537133056 | bytes 4980736 | tf_op jit(solution)/shard_map/qo,tok->tqk/dot_general | solution.py:203
  15.5 0.0 collective-permute-done.4
  15.5 0.0 collective-permute-done.2
  15.6 0.0 collective-permute-done.1
  15.6 0.0 collective-permute-done.3
  15.6 0.1 concatenate.6.refs_4_.refs_0_
  15.7 2.9 %collective-permute-start.5 = (bf16[2,128,1024]{2,1,0:T(8,128)(2,1)S(1)}, bf16[2,128,1024]{2,1,0:T(8,128)(2,1)S(1)}, u32[]{:S(2)}, u32[]{:S(2)}) collective-permute-start(bf16[2,128,1024]{2,1,0:T(8,128)(2,1)S(1)} %fusion.1), channel_id=1, source_target_pairs={{0,128},{1,129},{2,130},{3,131},{4,132},{5,133},{6,134},{7,135},{8... | collective-permute-start | bytes 1572872 | tf_op jit(solution)/shard_map/ppermute | solution.py:31
  18.6 2.5 %collective-permute-start.8 = (bf16[264,1024]{1,0:T(8,128)(2,1)S(1)}, bf16[264,1024]{1,0:T(8,128)(2,1)S(1)}, u32[]{:S(2)}, u32[]{:S(2)}) collective-permute-start(bf16[264,1024]{1,0:T(8,128)(2,1)S(1)} %concatenate.6.refs_4_.refs_0_), channel_id=1, source_target_pairs={{0,6},{1,7},{2,0},{3,1},{4,2},{5,3},{6,4},{7,5},{8,14},{9,15},{10,... | collective-permute-start | bytes 1622024 | tf_op jit(solution)/shard_map/ppermute | solution.py:31
  21.1 0.0 collective-permute-start.7
  21.1 3.7 %fusion.refs_0_ = bf16[2,128,1024]{2,1,0:T(8,128)(2,1)S(1)} fusion(bf16[2,1024,1024]{2,1,0:T(8,128)(2,1)} %param.4, bf16[128,1024]{1,0:T(8,128)(2,1)S(1)} %get-tuple-element.26), kind=kOutput, calls=%fused_computation.2 | convolution fusion | flops 537133056 | bytes 4980736 | tf_op jit(solution)/shard_map/qo,tko->tqk/dot_general | solution.py:204
  24.8 2.8 %collective-permute-start = (bf16[2,128,1024]{2,1,0:T(8,128)(2,1)S(1)}, bf16[2,128,1024]{2,1,0:T(8,128)(2,1)S(1)}, u32[]{:S(2)}, u32[]{:S(2)}) collective-permute-start(bf16[2,128,1024]{2,1,0:T(8,128)(2,1)S(1)} %fusion.refs_0_), channel_id=1, source_target_pairs={{0,1},{1,0},{2,3},{3,2},{4,5},{5,4},{6,7},{7,6},{8,9},{9,8},{10,11... | collective-permute-start | bytes 1572872 | tf_op jit(solution)/shard_map/ppermute | solution.py:31
  27.5 2.8 %collective-permute-done.5.refs_2_ = bf16[2,128,1024]{2,1,0:T(8,128)(2,1)S(1)} collective-permute-done((bf16[2,128,1024]{2,1,0:T(8,128)(2,1)S(1)}, bf16[2,128,1024]{2,1,0:T(8,128)(2,1)S(1)}, u32[]{:S(2)}, u32[]{:S(2)}) %collective-permute-start.5) | collective-permute-done | bytes 524320 | tf_op jit(solution)/shard_map/ppermute | solution.py:31
  30.4 4.0 %collective-permute-start.6 = (bf16[2,128,1024]{2,1,0:T(8,128)(2,1)S(1)}, bf16[2,128,1024]{2,1,0:T(8,128)(2,1)S(1)}, u32[]{:S(2)}, u32[]{:S(2)}) collective-permute-start(bf16[2,128,1024]{2,1,0:T(8,128)(2,1)S(1)} %collective-permute-done.5.refs_2_), channel_id=1, source_target_pairs={{0,1},{1,0},{2,3},{3,2},{4,5},{5,4},{6,7},{7,6},{8,9},{9,8},{10,11... | collective-permute-start | bytes 1572872 | tf_op jit(solution)/shard_map/ppermute | solution.py:31
  34.4 1.3 %collective-permute-start.9 = (bf16[128,1024]{1,0:T(8,128)(2,1)S(1)}, bf16[128,1024]{1,0:T(8,128)(2,1)S(1)}, u32[]{:S(2)}, u32[]{:S(2)}) collective-permute-start(bf16[128,1024]{1,0:T(8,128)(2,1)S(1)} %slice.47), channel_id=1, source_target_pairs={{0,2},{1,3},{2,4},{3,5},{4,6},{5,7},{6,0},{7,1},{8,10},{9,11},{10,... | collective-permute-start | bytes 786440 | tf_op jit(solution)/shard_map/ppermute | solution.py:31
  35.7 2.8 %collective-permute-start.15 = (bf16[96,1024]{1,0:T(8,128)(2,1)S(1)}, bf16[96,1024]{1,0:T(8,128)(2,1)S(1)}, u32[]{:S(2)}, u32[]{:S(2)}) collective-permute-start(bf16[96,1024]{1,0:T(8,128)(2,1)S(1)} %slice.50), channel_id=1, source_target_pairs={{0,96},{1,97},{2,98},{3,99},{4,100},{5,101},{6,102},{7,103},{8,104... | collective-permute-start | bytes 589832 | tf_op jit(solution)/shard_map/ppermute | solution.py:31
  38.5 0.1 collective-permute-start.16
  38.6 2.5 %collective-permute-done.15 = bf16[96,1024]{1,0:T(8,128)(2,1)S(1)} collective-permute-done((bf16[96,1024]{1,0:T(8,128)(2,1)S(1)}, bf16[96,1024]{1,0:T(8,128)(2,1)S(1)}, u32[]{:S(2)}, u32[]{:S(2)}) %collective-permute-start.15) | collective-permute-done | bytes 196640 | tf_op jit(solution)/shard_map/ppermute | solution.py:31
  41.1 1.5 %collective-permute-start.10 = (bf16[136,1024]{1,0:T(8,128)(2,1)S(1)}, bf16[136,1024]{1,0:T(8,128)(2,1)S(1)}, u32[]{:S(2)}, u32[]{:S(2)}) collective-permute-start(bf16[136,1024]{1,0:T(8,128)(2,1)S(1)} %slice.48), channel_id=1, source_target_pairs={{0,6},{1,7},{2,0},{3,1},{4,2},{5,3},{6,4},{7,5},{8,14},{9,15},{10,... | collective-permute-start | bytes 835592 | tf_op jit(solution)/shard_map/ppermute | solution.py:31
  42.6 2.2 %collective-permute-done.16 = bf16[104,1024]{1,0:T(8,128)(2,1)S(1)} collective-permute-done((bf16[104,1024]{1,0:T(8,128)(2,1)S(1)}, bf16[104,1024]{1,0:T(8,128)(2,1)S(1)}, u32[]{:S(2)}, u32[]{:S(2)}) %collective-permute-start.16) | collective-permute-done | bytes 213024 | tf_op jit(solution)/shard_map/ppermute | solution.py:31
  44.8 0.9 collective-permute-start.13
  45.7 0.0 collective-permute-done.9.refs_4_.refs_6_
  45.7 0.6 collective-permute-start.14
  46.3 2.7 %collective-permute-done.10.refs_5_.refs_7_ = bf16[136,1024]{1,0:T(8,128)(2,1)S(1)} collective-permute-done((bf16[136,1024]{1,0:T(8,128)(2,1)S(1)}, bf16[136,1024]{1,0:T(8,128)(2,1)S(1)}, u32[]{:S(2)}, u32[]{:S(2)}) %collective-permute-start.10) | collective-permute-done | bytes 278560 | tf_op jit(solution)/shard_map/ppermute | solution.py:31
  49.0 3.4 %collective-permute-start.11 = (bf16[128,1024]{1,0:T(8,128)(2,1)S(1)}, bf16[128,1024]{1,0:T(8,128)(2,1)S(1)}, u32[]{:S(2)}, u32[]{:S(2)}) collective-permute-start(bf16[128,1024]{1,0:T(8,128)(2,1)S(1)} %collective-permute-done.9.refs_4_.refs_6_), channel_id=1, source_target_pairs={{0,96},{1,97},{2,98},{3,99},{4,100},{5,101},{6,102},{7,103},{8,104... | collective-permute-start | bytes 786440 | tf_op jit(solution)/shard_map/ppermute | solution.py:31
  52.4 0.0 collective-permute-done.refs_1_
  52.4 2.0 %shard_map.47 = (f32[2,128,1024]{2,1,0:T(8,128)S(1)}, f32[2,128,1024]{2,1,0:T(8,128)S(1)}) custom-call(bf16[2,128,1024]{2,1,0:T(8,128)(2,1)S(1)} %fusion.refs_0_, bf16[2,128,1024]{2,1,0:T(8,128)(2,1)S(1)} %collective-permute-done.refs_1_, bf16[2,128,1024]{2,1,0:T(8,128)(2,1)S(1)} %collective-permute-done.5.refs_2_, ...), custom_call_target="tpu_custom_call" | custom-call | flops 1610612736 | bytes 2097152 | tf_op jit(solution)/shard_map/pallas_call | solution.py:131
  54.5 2.1 %shard_map.48 = (f32[2,128,1024]{2,1,0:T(8,128)S(1)}, f32[2,128,1024]{2,1,0:T(8,128)S(1)}) custom-call(bf16[2,128,1024]{2,1,0:T(8,128)(2,1)S(1)} %fusion.refs_0_, bf16[2,128,1024]{2,1,0:T(8,128)(2,1)S(1)} %collective-permute-done.refs_1_, bf16[2,128,1024]{2,1,0:T(8,128)(2,1)S(1)} %collective-permute-done.5.refs_2_, ...), custom_call_target="tpu_custom_call", output_to_operand_aliasing={{0}: (6, {}), {1}: (7, {})} | custom-call | flops 1610612736 | bytes 2097152 | tf_op jit(solution)/shard_map/pallas_call | solution.py:131
  56.6 0.0 collective-permute-done.14.refs_5_
  56.6 2.1 %shard_map.49 = (f32[2,128,1024]{2,1,0:T(8,128)S(1)}, f32[2,128,1024]{2,1,0:T(8,128)S(1)}) custom-call(bf16[2,128,1024]{2,1,0:T(8,128)(2,1)S(1)} %fusion.refs_0_, bf16[2,128,1024]{2,1,0:T(8,128)(2,1)S(1)} %collective-permute-done.refs_1_, bf16[2,128,1024]{2,1,0:T(8,128)(2,1)S(1)} %collective-permute-done.5.refs_2_, ...), custom_call_target="tpu_custom_call", output_to_operand_aliasing={{0}: (6, {}), {1}: (7, {})} | custom-call | flops 1610612736 | bytes 2097152 | tf_op jit(solution)/shard_map/pallas_call | solution.py:131
  58.7 2.8 %collective-permute-done.11.refs_6_.refs_8_ = bf16[128,1024]{1,0:T(8,128)(2,1)S(1)} collective-permute-done((bf16[128,1024]{1,0:T(8,128)(2,1)S(1)}, bf16[128,1024]{1,0:T(8,128)(2,1)S(1)}, u32[]{:S(2)}, u32[]{:S(2)}) %collective-permute-start.11) | collective-permute-done | bytes 262176 | tf_op jit(solution)/shard_map/ppermute | solution.py:31
  61.5 0.9 collective-permute-done.12.refs_7_.refs_9_
  62.4 2.1 %shard_map.50 = (f32[2,128,1024]{2,1,0:T(8,128)S(1)}, f32[2,128,1024]{2,1,0:T(8,128)S(1)}) custom-call(bf16[2,128,1024]{2,1,0:T(8,128)(2,1)S(1)} %fusion.refs_0_, bf16[2,128,1024]{2,1,0:T(8,128)(2,1)S(1)} %collective-permute-done.refs_1_, bf16[2,128,1024]{2,1,0:T(8,128)(2,1)S(1)} %collective-permute-done.5.refs_2_, ...), custom_call_target="tpu_custom_call", output_to_operand_aliasing={{0}: (8, {}), {1}: (9, {})} | custom-call | flops 1610612736 | bytes 2097152 | tf_op jit(solution)/shard_map/pallas_call | solution.py:131
  64.5 5.2 %collective-permute-start.17 = (f32[2,128,1024]{2,1,0:T(8,128)S(1)}, f32[2,128,1024]{2,1,0:T(8,128)S(1)}, u32[]{:S(2)}, u32[]{:S(2)}) collective-permute-start(f32[2,128,1024]{2,1,0:T(8,128)S(1)} %get-tuple-element.43), channel_id=1, source_target_pairs={{0,1},{1,0},{2,3},{3,2},{4,5},{5,4},{6,7},{7,6},{8,9},{9,8},{10,11... | collective-permute-start | bytes 3145736 | tf_op jit(solution)/shard_map/ppermute | solution.py:31
  69.7 2.3 %collective-permute-done.17.got_ref = f32[2,128,1024]{2,1,0:T(8,128)S(1)} collective-permute-done((f32[2,128,1024]{2,1,0:T(8,128)S(1)}, f32[2,128,1024]{2,1,0:T(8,128)S(1)}, u32[]{:S(2)}, u32[]{:S(2)}) %collective-permute-start.17) | collective-permute-done | bytes 1048608 | tf_op jit(solution)/shard_map/ppermute | solution.py:31
  72.0 0.3 shard_map.51
  72.3 31.8 %all_to_all.5.part_ref = bf16[16,2,64,128]{3,2,1,0:T(8,128)(2,1)S(1)} all-to-all(bf16[16,2,64,128]{3,2,1,0:T(8,128)(2,1)S(1)} %shard_map.51), channel_id=1, replica_groups={{0,2,4,6,8,10,12,14,16,18,20,22,24,26,28,30},{1,3,5,7,9,11,13,15,17,19,..., dimensions={0} | all-to-all | bytes 1048576 | tf_op jit(solution)/shard_map/all_to_all | solution.py:249
  104.2 0.8 shard_map.52
  105.0 2.3 %collective-permute-start.18 = (f32[2,32,1024]{2,1,0:T(8,128)S(1)}, f32[2,32,1024]{2,1,0:T(8,128)S(1)}, u32[]{:S(2)}, u32[]{:S(2)}) collective-permute-start(f32[2,32,1024]{2,1,0:T(8,128)S(1)} %get-tuple-element.46), channel_id=1, source_target_pairs={{0,1},{1,0},{2,3},{3,2},{4,5},{5,4},{6,7},{7,6},{8,9},{9,8},{10,11... | collective-permute-start | bytes 786440 | tf_op jit(solution)/shard_map/ppermute | solution.py:31
  107.3 1.2 %collective-permute-done.18.got_ref = f32[2,32,1024]{2,1,0:T(8,128)S(1)} collective-permute-done((f32[2,32,1024]{2,1,0:T(8,128)S(1)}, f32[2,32,1024]{2,1,0:T(8,128)S(1)}, u32[]{:S(2)}, u32[]{:S(2)}) %collective-permute-start.18) | collective-permute-done | bytes 262176 | tf_op jit(solution)/shard_map/ppermute | solution.py:31
  108.5 0.8 shard_map.53
  (22 shorter events, 0.2 us)
Async XLA Ops:
  0.0 0.9 copy-start
  1.0 0.7 copy-start.1
  1.6 0.7 copy-start.2
  2.5 13.1 %collective-permute-start.2 = (bf16[72,1024]{1,0:T(8,128)(2,1)S(1)}, bf16[72,1024]{1,0:T(8,128)(2,1)S(1)}, u32[]{:S(2)}, u32[]{:S(2)}) collective-permute-start(bf16[72,1024]{1,0:T(8,128)(2,1)S(1)} %get-tuple-element.27), channel_id=1, source_target_pairs={{0,152},{1,153},{2,154},{3,155},{4,156},{5,157},{6,158},{7,159},{8... | collective-permute-start | bytes 442376 | tf_op jit(solution)/shard_map/ppermute | solution.py:31
  8.9 6.6 %collective-permute-start.1 = (bf16[72,1024]{1,0:T(8,128)(2,1)S(1)}, bf16[72,1024]{1,0:T(8,128)(2,1)S(1)}, u32[]{:S(2)}, u32[]{:S(2)}) collective-permute-start(bf16[72,1024]{1,0:T(8,128)(2,1)S(1)} %get-tuple-element.27), channel_id=1, source_target_pairs={{0,8},{1,9},{2,10},{3,11},{4,12},{5,13},{6,14},{7,15},{8,16},{9,17... | collective-permute-start | bytes 442376 | tf_op jit(solution)/shard_map/ppermute | solution.py:31
  8.9 6.7 %collective-permute-start.3 = (bf16[32,1024]{1,0:T(8,128)(2,1)S(1)}, bf16[32,1024]{1,0:T(8,128)(2,1)S(1)}, u32[]{:S(2)}, u32[]{:S(2)}) collective-permute-start(bf16[32,1024]{1,0:T(8,128)(2,1)S(1)} %get-tuple-element.28), channel_id=1, source_target_pairs={{0,16},{1,17},{2,18},{3,19},{4,20},{5,21},{6,22},{7,23},{8,24},{9,... | collective-permute-start | bytes 196616 | tf_op jit(solution)/shard_map/ppermute | solution.py:31
  8.9 6.5 %collective-permute-start.4 = (bf16[40,1024]{1,0:T(8,128)(2,1)S(1)}, bf16[40,1024]{1,0:T(8,128)(2,1)S(1)}, u32[]{:S(2)}, u32[]{:S(2)}) collective-permute-start(bf16[40,1024]{1,0:T(8,128)(2,1)S(1)} %get-tuple-element.29), channel_id=1, source_target_pairs={{0,144},{1,145},{2,146},{3,147},{4,148},{5,149},{6,150},{7,151},{8... | collective-permute-start | bytes 245768 | tf_op jit(solution)/shard_map/ppermute | solution.py:31
  15.7 14.7 %collective-permute-start.5 = (bf16[2,128,1024]{2,1,0:T(8,128)(2,1)S(1)}, bf16[2,128,1024]{2,1,0:T(8,128)(2,1)S(1)}, u32[]{:S(2)}, u32[]{:S(2)}) collective-permute-start(bf16[2,128,1024]{2,1,0:T(8,128)(2,1)S(1)} %fusion.1), channel_id=1, source_target_pairs={{0,128},{1,129},{2,130},{3,131},{4,132},{5,133},{6,134},{7,135},{8... | collective-permute-start | bytes 1572872 | tf_op jit(solution)/shard_map/ppermute | solution.py:31
  18.6 15.7 %collective-permute-start.8 = (bf16[264,1024]{1,0:T(8,128)(2,1)S(1)}, bf16[264,1024]{1,0:T(8,128)(2,1)S(1)}, u32[]{:S(2)}, u32[]{:S(2)}) collective-permute-start(bf16[264,1024]{1,0:T(8,128)(2,1)S(1)} %concatenate.6.refs_4_.refs_0_), channel_id=1, source_target_pairs={{0,6},{1,7},{2,0},{3,1},{4,2},{5,3},{6,4},{7,5},{8,14},{9,15},{10,... | collective-permute-start | bytes 1622024 | tf_op jit(solution)/shard_map/ppermute | solution.py:31
  21.1 13.3 %collective-permute-start.7 = (bf16[264,1024]{1,0:T(8,128)(2,1)S(1)}, bf16[264,1024]{1,0:T(8,128)(2,1)S(1)}, u32[]{:S(2)}, u32[]{:S(2)}) collective-permute-start(bf16[264,1024]{1,0:T(8,128)(2,1)S(1)} %concatenate.6.refs_4_.refs_0_), channel_id=1, source_target_pairs={{0,2},{1,3},{2,4},{3,5},{4,6},{5,7},{6,0},{7,1},{8,10},{9,11},{10,... | collective-permute-start | bytes 1622024 | tf_op jit(solution)/shard_map/ppermute | solution.py:31
  24.8 27.7 %collective-permute-start = (bf16[2,128,1024]{2,1,0:T(8,128)(2,1)S(1)}, bf16[2,128,1024]{2,1,0:T(8,128)(2,1)S(1)}, u32[]{:S(2)}, u32[]{:S(2)}) collective-permute-start(bf16[2,128,1024]{2,1,0:T(8,128)(2,1)S(1)} %fusion.refs_0_), channel_id=1, source_target_pairs={{0,1},{1,0},{2,3},{3,2},{4,5},{5,4},{6,7},{7,6},{8,9},{9,8},{10,11... | collective-permute-start | bytes 1572872 | tf_op jit(solution)/shard_map/ppermute | solution.py:31
  30.4 22.1 %collective-permute-start.6 = (bf16[2,128,1024]{2,1,0:T(8,128)(2,1)S(1)}, bf16[2,128,1024]{2,1,0:T(8,128)(2,1)S(1)}, u32[]{:S(2)}, u32[]{:S(2)}) collective-permute-start(bf16[2,128,1024]{2,1,0:T(8,128)(2,1)S(1)} %collective-permute-done.5.refs_2_), channel_id=1, source_target_pairs={{0,1},{1,0},{2,3},{3,2},{4,5},{5,4},{6,7},{7,6},{8,9},{9,8},{10,11... | collective-permute-start | bytes 1572872 | tf_op jit(solution)/shard_map/ppermute | solution.py:31
  34.4 11.3 %collective-permute-start.9 = (bf16[128,1024]{1,0:T(8,128)(2,1)S(1)}, bf16[128,1024]{1,0:T(8,128)(2,1)S(1)}, u32[]{:S(2)}, u32[]{:S(2)}) collective-permute-start(bf16[128,1024]{1,0:T(8,128)(2,1)S(1)} %slice.47), channel_id=1, source_target_pairs={{0,2},{1,3},{2,4},{3,5},{4,6},{5,7},{6,0},{7,1},{8,10},{9,11},{10,... | collective-permute-start | bytes 786440 | tf_op jit(solution)/shard_map/ppermute | solution.py:31
  35.7 5.4 %collective-permute-start.15 = (bf16[96,1024]{1,0:T(8,128)(2,1)S(1)}, bf16[96,1024]{1,0:T(8,128)(2,1)S(1)}, u32[]{:S(2)}, u32[]{:S(2)}) collective-permute-start(bf16[96,1024]{1,0:T(8,128)(2,1)S(1)} %slice.50), channel_id=1, source_target_pairs={{0,96},{1,97},{2,98},{3,99},{4,100},{5,101},{6,102},{7,103},{8,104... | collective-permute-start | bytes 589832 | tf_op jit(solution)/shard_map/ppermute | solution.py:31
  38.5 6.3 %collective-permute-start.16 = (bf16[104,1024]{1,0:T(8,128)(2,1)S(1)}, bf16[104,1024]{1,0:T(8,128)(2,1)S(1)}, u32[]{:S(2)}, u32[]{:S(2)}) collective-permute-start(bf16[104,1024]{1,0:T(8,128)(2,1)S(1)} %slice.51), channel_id=1, source_target_pairs={{0,32},{1,33},{2,34},{3,35},{4,36},{5,37},{6,38},{7,39},{8,40},{9,... | collective-permute-start | bytes 638984 | tf_op jit(solution)/shard_map/ppermute | solution.py:31
  41.1 7.9 %collective-permute-start.10 = (bf16[136,1024]{1,0:T(8,128)(2,1)S(1)}, bf16[136,1024]{1,0:T(8,128)(2,1)S(1)}, u32[]{:S(2)}, u32[]{:S(2)}) collective-permute-start(bf16[136,1024]{1,0:T(8,128)(2,1)S(1)} %slice.48), channel_id=1, source_target_pairs={{0,6},{1,7},{2,0},{3,1},{4,2},{5,3},{6,4},{7,5},{8,14},{9,15},{10,... | collective-permute-start | bytes 835592 | tf_op jit(solution)/shard_map/ppermute | solution.py:31
  44.8 11.8 %collective-permute-start.13 = (bf16[264,1024]{1,0:T(8,128)(2,1)S(1)}, bf16[264,1024]{1,0:T(8,128)(2,1)S(1)}, u32[]{:S(2)}, u32[]{:S(2)}) collective-permute-start(bf16[264,1024]{1,0:T(8,128)(2,1)S(1)} %collective-permute-done.7.refs_4_.refs_2_), channel_id=1, source_target_pairs={{0,96},{1,97},{2,98},{3,99},{4,100},{5,101},{6,102},{7,103},{8,104... | collective-permute-start | bytes 1622024 | tf_op jit(solution)/shard_map/ppermute | solution.py:31
  45.7 10.9 %collective-permute-start.14 = (bf16[264,1024]{1,0:T(8,128)(2,1)S(1)}, bf16[264,1024]{1,0:T(8,128)(2,1)S(1)}, u32[]{:S(2)}, u32[]{:S(2)}) collective-permute-start(bf16[264,1024]{1,0:T(8,128)(2,1)S(1)} %collective-permute-done.8.refs_5_.refs_4_), channel_id=1, source_target_pairs={{0,32},{1,33},{2,34},{3,35},{4,36},{5,37},{6,38},{7,39},{8,40},{9,... | collective-permute-start | bytes 1622024 | tf_op jit(solution)/shard_map/ppermute | solution.py:31
  49.0 12.5 %collective-permute-start.11 = (bf16[128,1024]{1,0:T(8,128)(2,1)S(1)}, bf16[128,1024]{1,0:T(8,128)(2,1)S(1)}, u32[]{:S(2)}, u32[]{:S(2)}) collective-permute-start(bf16[128,1024]{1,0:T(8,128)(2,1)S(1)} %collective-permute-done.9.refs_4_.refs_6_), channel_id=1, source_target_pairs={{0,96},{1,97},{2,98},{3,99},{4,100},{5,101},{6,102},{7,103},{8,104... | collective-permute-start | bytes 786440 | tf_op jit(solution)/shard_map/ppermute | solution.py:31
  52.4 10.0 %collective-permute-start.12 = (bf16[136,1024]{1,0:T(8,128)(2,1)S(1)}, bf16[136,1024]{1,0:T(8,128)(2,1)S(1)}, u32[]{:S(2)}, u32[]{:S(2)}) collective-permute-start(bf16[136,1024]{1,0:T(8,128)(2,1)S(1)} %collective-permute-done.10.refs_5_.refs_7_), channel_id=1, source_target_pairs={{0,32},{1,33},{2,34},{3,35},{4,36},{5,37},{6,38},{7,39},{8,40},{9,... | collective-permute-start | bytes 835592 | tf_op jit(solution)/shard_map/ppermute | solution.py:31
  64.5 7.5 %collective-permute-start.17 = (f32[2,128,1024]{2,1,0:T(8,128)S(1)}, f32[2,128,1024]{2,1,0:T(8,128)S(1)}, u32[]{:S(2)}, u32[]{:S(2)}) collective-permute-start(f32[2,128,1024]{2,1,0:T(8,128)S(1)} %get-tuple-element.43), channel_id=1, source_target_pairs={{0,1},{1,0},{2,3},{3,2},{4,5},{5,4},{6,7},{7,6},{8,9},{9,8},{10,11... | collective-permute-start | bytes 3145736 | tf_op jit(solution)/shard_map/ppermute | solution.py:31
  105.0 3.5 %collective-permute-start.18 = (f32[2,32,1024]{2,1,0:T(8,128)S(1)}, f32[2,32,1024]{2,1,0:T(8,128)S(1)}, u32[]{:S(2)}, u32[]{:S(2)}) collective-permute-start(f32[2,32,1024]{2,1,0:T(8,128)S(1)} %get-tuple-element.46), channel_id=1, source_target_pairs={{0,1},{1,0},{2,3},{3,2},{4,5},{5,4},{6,7},{7,6},{8,9},{9,8},{10,11... | collective-permute-start | bytes 786440 | tf_op jit(solution)/shard_map/ppermute | solution.py:31

commit v4 on v3

v4 whole, which is shorter than its diff:
```python
import functools

import jax
import jax.numpy as jnp
from jax import lax
from jax.experimental import pallas as pl
from jax.experimental.pallas import tpu as pltpu
from jax.sharding import PartitionSpec as P

BLOCK = 128
HALF = 64
F32, BF16 = jnp.float32, jnp.bfloat16
BOTH = ("tm", "aux")
NT = (((1,), (1,)), ((), ()))
NN = (((1,), (0,)), ((), ()))
VMEM = pl.BlockSpec(memory_space=pltpu.VMEM)


def device_at(x, y, z, core):
    return (z // 4 * 4 + y) * 32 + (z % 4 * 4 + x) * 2 + core


def send(value, to):
    pairs = []
    for x in range(4):
        for y in range(4):
            for z in range(8):
                for core in range(2):
                    tx, ty, tz, tcore = to(x, y, z, core)
                    pairs.append((device_at(x, y, z, core), device_at(tx % 4, ty % 4, tz % 8, tcore)))
    return lax.ppermute(value, BOTH, sorted(pairs))


def along_x(value, step):
    return send(value, lambda x, y, z, core: (x + step, y, z, core))


def along_z(value, step):
    return send(value, lambda x, y, z, core: (x, y, z + step, core))


def other_core(value):
    return send(value, lambda x, y, z, core: (x, y, z, 1 - core))


def two_along_z(value):
    return send(value, lambda x, y, z, core: (x, y, z + (2 if core == 0 else -2), core))


def split_x(value):
    return send(value, lambda x, y, z, core: (x + (1 if core == 0 else -1), y, z, core))


def other_parity(value):
    return send(value, lambda x, y, z, core: (x, y + (1 if y % 2 == core else -1), z, core))


def params(mib):
    return pltpu.CompilerParams(vmem_limit_bytes=mib << 20)


def prologue_kernel(factors_in, pattern_in, coulomb_in, masked_ref, whole_ref, own_ref, factors, pattern, coulomb, sems):
    copies = [
        pltpu.make_async_copy(factors_in, factors, sems.at[0]),
        pltpu.make_async_copy(pattern_in, pattern, sems.at[1]),
        pltpu.make_async_copy(coulomb_in, coulomb, sems.at[2]),
    ]
    for copy in copies:
        copy.start()
    for copy in copies:
        copy.wait()
    parity = lax.axis_index("tm") & 1
    orb = factors.shape[1]
    for block in range(orb // BLOCK):
        lanes = pl.ds(block * BLOCK, BLOCK)
        keep = pattern[:, block : block + 1].astype(F32)
        for half in range(2):
            at = parity if half == 0 else 1 - parity
            part = factors[pl.ds(pl.multiple_of(at * HALF, HALF), HALF), lanes]
            part = (part.astype(F32) * keep).astype(BF16)
            masked_ref[pl.ds(half * HALF, HALF), lanes] = part
            if half == 0:
                whole_ref[pl.ds(0, HALF), lanes] = part
    c = coulomb[...]
    turned = pltpu.roll(c, HALF, 1)
    own = jnp.where(parity == 0, c, turned)
    own_ref[...] = own
    lane = lax.broadcasted_iota(jnp.int32, own.shape, 1)
    twice = jnp.where(lane < HALF, own, pltpu.roll(own, HALF, 1))
    high = twice.astype(BF16)
    rest = twice - high.astype(F32)
    middle = rest.astype(BF16)
    low = (rest - middle.astype(F32)).astype(BF16)
    zero = jnp.zeros((1, orb - 3 * BLOCK), BF16)
    row = jnp.concatenate([high, middle, low, zero], axis=1)
    rows = jnp.broadcast_to(row.astype(F32), (8, orb)).astype(BF16)
    whole_ref[pl.ds(HALF, 8), :] = rows


def prologue(factors, pattern, coulomb):
    own, orb = factors.shape
    return pl.pallas_call(
        prologue_kernel,
        out_shape=[
            jax.ShapeDtypeStruct((own, orb), BF16),
            jax.ShapeDtypeStruct((HALF + 8, orb), BF16),
            jax.ShapeDtypeStruct((1, own), F32),
        ],
        in_specs=[pl.BlockSpec(memory_space=pltpu.HBM)] * 3,
        out_specs=[VMEM] * 3,
        scratch_shapes=[
            pltpu.VMEM((own, orb), BF16),
            pltpu.VMEM(pattern.shape, jnp.int32),
            pltpu.VMEM((1, own), F32),
            pltpu.SemaphoreType.DMA((3,)),
        ],
        compiler_params=params(58),
    )(factors, pattern, coulomb[None, :])


def mix_kernel(west_ref, east_ref, onward_ref, both_ref):
    core = lax.axis_index("aux") & 1
    n = west_ref.shape[0]
    west, east = west_ref[...], east_ref[...]
    onward_ref[...] = jnp.where(core == 0, west, east)
    both_ref[pl.ds(0, n), :] = west
    both_ref[pl.ds(n, n), :] = east


def mix(west, east):
    n, orb = west.shape
    return pl.pallas_call(
        mix_kernel,
        out_shape=(jax.ShapeDtypeStruct((n, orb), BF16), jax.ShapeDtypeStruct((2 * n, orb), BF16)),
        in_specs=[VMEM] * 2,
        out_specs=[VMEM] * 2,
        compiler_params=params(8),
    )(west, east)


def weight_of(ref, row):
    parts = [ref[pl.ds(row, 1), pl.ds(k * BLOCK, BLOCK)].astype(F32) for k in range(3)]
    return parts[0] + (parts[1] + parts[2])


def weights_of(ref, row, blocks):
    lane = lax.broadcasted_iota(jnp.int32, (1, BLOCK), 1)
    pairs = []
    for k in range(0, blocks, 2):
        pairs.append(jnp.where(lane < HALF, weight_of(ref, row + k), weight_of(ref, row + k + 1)))
    return jnp.concatenate(pairs, axis=1) if len(pairs) > 1 else pairs[0]


def chunk_kernel(pieces, count, first, *refs):
    right_own, right_other, left_own, left_other = refs[:4]
    rows = refs[4 : 4 + count]
    rest = refs[4 + count :]
    if not first:
        acc_own, acc_other = rest[:2]
        rest = rest[2:]
    out_own, out_other = rest
    own = out_own.shape[1]
    for t in range(out_own.shape[0]):
        right = jnp.concatenate([right_own[t], right_other[t]], axis=0)
        left = jnp.concatenate([left_own[t], left_other[t]], axis=0)
        total = None
        for piece in pieces:
            part = jnp.concatenate([rows[at][pl.ds(start, n), :] for at, start, n in piece[0]], axis=0)
            weight = weights_of(rows[piece[1]], piece[2], part.shape[0] // HALF)
            a = lax.dot_general(right, part, NT, preferred_element_type=F32)
            m = lax.dot_general(left, part, NT, preferred_element_type=F32)
            k = (a * weight * (a * m)).astype(BF16)
            d = lax.dot_general(k, part, NN, preferred_element_type=F32)
            total = d if total is None else total + d
        mine, theirs = total[:own], total[own:]
        if not first:
            mine, theirs = acc_own[t] + mine, acc_other[t] + theirs
        out_own[t] = mine
        out_other[t] = theirs.astype(out_other.dtype)


def chunk(sides, rows, pieces, acc=None, last=False):
    times, own, orb = sides[0].shape
    shape = jax.ShapeDtypeStruct((times, own, orb), F32)
    extra = () if acc is None else tuple(acc)
    theirs = jax.ShapeDtypeStruct((times, own, orb), BF16 if last else F32)
    aliases = {}
    if acc is not None:
        aliases[4 + len(rows)] = 0
        if not last:
            aliases[5 + len(rows)] = 1
    flops = len(pieces) * 4 * HALF * times * 3 * 2 * (2 * own) * orb
    return pl.pallas_call(
        functools.partial(chunk_kernel, tuple(pieces), len(rows), acc is None),
        out_shape=(shape, theirs),
        in_specs=[VMEM] * (4 + len(rows) + len(extra)),
        out_specs=(VMEM, VMEM),
        input_output_aliases=aliases,
        compiler_params=params(16),
        cost_estimate=pl.CostEstimate(flops=flops, bytes_accessed=2 << 20, transcendentals=0),
    )(*sides, *rows, *extra)


def finish_kernel(own_ref, got_ref, coulomb_ref, out_ref):
    chips, times, rows, _ = out_ref.shape
    for t in range(times):
        d = jnp.transpose(own_ref[t] + got_ref[t].astype(F32)) * coulomb_ref[...]
        d = d.astype(BF16)
        for chip in range(chips):
            out_ref[chip, t] = d[chip * rows : (chip + 1) * rows]


def sigma_kernel(part_ref, *refs):
    here, here_q, west, east, sides_q, far, far_q = refs[:7]
    keep_ref, send_ref, lhs, total_ref = refs[7:]
    skip = west.shape[0]
    columns = [((here, 0), (here_q, 0)), ((west, 0), (sides_q, 0)), ((east, 0), (sides_q, skip)), ((far, 0), (far_q, 0))]
    chips, times, i_rows, width = part_ref.shape
    me = lax.axis_index("aux")
    core, x, z = me & 1, (me >> 1) & 3, me >> 3
    total = None
    for column, dx in enumerate((0, 3, 1, 2)):
        parts = []
        for k, dz in enumerate((0, 3, 1, 2)):
            source = ((z + dz) & 3) * 4 + ((x + dx) & 3)
            for t in range(times):
                at = pl.ds((column * 4 + k) * width, width)
                lhs[pl.ds(t * i_rows, i_rows), at] = part_ref[source, t]
            for ref, start in columns[column]:
                parts.append(ref[pl.ds(start + k * HALF, HALF), :])
        d = lax.dot_general(
            lhs[:, pl.ds(column * 4 * width, 4 * width)],
            jnp.concatenate(parts, axis=0),
            NN,
            preferred_element_type=F32,
        )
        total = d if total is None else total + d
    total_ref[...] = total
    half = i_rows // 2
    for t in range(times):
        keep = pl.multiple_of(t * i_rows + core * half, half)
        send = pl.multiple_of(t * i_rows + (1 - core) * half, half)
        keep_ref[t] = total_ref[pl.ds(keep, half), :]
        send_ref[t] = total_ref[pl.ds(send, half), :]


def add_kernel(keep_ref, got_ref, out_ref):
    for t in range(keep_ref.shape[0]):
        out_ref[:, t, :] = keep_ref[t] + got_ref[t]


def local(green, factors, pattern, coulomb):
    times, orb, _ = green.shape
    own = factors.shape[0]
    barrier = lax.optimization_barrier
    masked, whole, coulomb = prologue(factors, pattern, coulomb)

    below = along_z(whole, 1)
    above = along_z(whole, -1)
    beyond = two_along_z(whole)
    left = jnp.einsum("qo,tok->tqk", masked, green, preferred_element_type=F32).astype(BF16)
    right = jnp.einsum("qo,tko->tqk", masked, green, preferred_element_type=F32).astype(BF16)
    right_other = other_core(right)

    blocks = [whole, below, above, beyond]
    weights = [block[HALF : HALF + 1] for block in blocks] + [jnp.zeros((4, orb), BF16)]
    here = jnp.concatenate([block[:HALF] for block in blocks] + weights, axis=0)
    here, left = barrier((here, left))

    n = 4 * HALF
    west = along_x(here, 1)
    east = along_x(here, -1)
    rest = other_parity(here[HALF:])
    left = two_along_z(left)
    here_q = jnp.concatenate([masked[HALF:], rest], axis=0)

    west, east, here_q, left = barrier((west, east, here_q, left))
    onward, both = mix(west, east)
    far = split_x(onward)
    sides_q = other_parity(both)
    left = two_along_z(left)
    left, _ = barrier((left, far[:8, :BLOCK]))
    far_q = other_parity(far)
    left_other = other_core(left)

    def piece(at, start=0):
        return (((at, start, n),), at, start + n)

    sides = (right, right_other, left, left_other)
    acc = chunk(sides, (here, here_q), [piece(0), piece(1)])
    acc = chunk(sides, (west, east), [piece(0), piece(1)], acc)
    acc = chunk(sides, (sides_q,), [piece(0), piece(0, n + 8)], acc)
    keep, theirs = chunk(sides, (far, far_q), [piece(0), piece(1)], acc, last=True)

    got = other_core(theirs)
    chips, i_rows = 16, orb // 16
    part = pl.pallas_call(
        finish_kernel,
        out_shape=jax.ShapeDtypeStruct((chips, times, i_rows, own), BF16),
        in_specs=[VMEM] * 3,
        out_specs=VMEM,
        compiler_params=params(12),
    )(keep, got, coulomb)
    groups = [[2 * chip + core for chip in range(chips)] for core in range(2)]
    part = lax.all_to_all(part, "aux", 0, 0, axis_index_groups=groups, tiled=True)

    shape = jax.ShapeDtypeStruct((times, i_rows // 2, orb), F32)
    keep, theirs = pl.pallas_call(
        sigma_kernel,
        out_shape=(shape, shape),
        in_specs=[VMEM] * 8,
        out_specs=(VMEM, VMEM),
        scratch_shapes=[
            pltpu.VMEM((times * i_rows, chips * own), BF16),
            pltpu.VMEM((times * i_rows, orb), F32),
        ],
        compiler_params=params(12),
    )(part, here, here_q, west, east, sides_q, far, far_q)
    got = other_core(theirs)
    return pl.pallas_call(
        add_kernel,
        out_shape=jax.ShapeDtypeStruct((i_rows // 2, times, orb), F32),
        in_specs=[VMEM] * 2,
        out_specs=VMEM,
        compiler_params=params(8),
    )(keep, got)


def solution(mesh):
    in_specs = (P("tm", None, None), P("aux", None), P("aux", None), P("aux"))
    out_specs = P("aux", "tm", None)
    return jax.shard_map(local, mesh=mesh, in_specs=in_specs, out_specs=out_specs, check_vma=False)
```

time: 109 us -> 91.7 us (0.84)
  starting transfers between devices: 40.2 us -> 27.7 us
  blocking collectives: 31.8 us -> 20.2 us
  waiting for transfers between devices: 17.5 us -> 24.5 us
  local copies, waits for them, and re-layouts: 2.48 us -> 0.2 us
  Pallas kernels: 10.3 us -> 12.1 us
    ppermute x19 -> x15, starting transfers between devices: 40.2 us -> 27.7 us  [send(): return lax.ppermute(value, BOTH, sorted(pairs))]
    all_to_all x1, blocking collectives: 31.8 us -> 20.2 us  [local(): lax.all_to_all(part, 'aux', 0, 0, axis_index_groups=groups, tiled=True)]
    ppermute x19 -> x15, waiting for transfers between devices: 17.5 us -> 24.5 us  [send(): return lax.ppermute(value, BOTH, sorted(pairs))]
    unnamed x6, local copies, waits for them, and re-layouts: 2.26 us -> 0.01 us
    pallas_call x1 -> x2, Pallas kernels: 0.19 us -> 2 us  [the longest x1 1.9 us: prologue(): pl.pallas_call(prologue_kernel, out_shape=[jax.ShapeDtypeStruct((own, orb...]
  transfers between devices with their start and end apart: 19 -> 15, of which waited for: 8 -> 7; matrix products, arithmetic and copies ran while one was open for 6% -> 7% of each run, Pallas kernels for 6% -> 7%
where the time goes in v4:
time: 91.7 us; the launch traced here: 91.5 us
  starting transfers between devices  27.7 us (30%)
  waiting for transfers between devices  24.5 us (27%)
  blocking collectives  20.2 us (22%)
  Pallas kernels  12.1 us (13%)
  matrix products  6.72 us (7%)
    ppermute x15, starting transfers between devices, send(): return lax.ppermute(value, BOTH, sorted(pairs))  27.7 us
    ppermute x15, waiting for transfers between devices, send(): return lax.ppermute(value, BOTH, sorted(pairs))  24.5 us
    all_to_all x1, blocking collectives, local(): lax.all_to_all(part, 'aux', 0, 0, axis_index_groups=groups, tiled=True)  20.2 us
    pallas_call x4, Pallas kernels, chunk(): pl.pallas_call(functools.partial(chunk_kernel, tuple(pieces), len(rows),...  8.16 us
    dot_general x1, matrix products, local(): jnp.einsum('qo,tko->tqk', masked, green, preferred_element_type=F32)  3.69 us
    dot_general x1, matrix products, local(): jnp.einsum('qo,tok->tqk', masked, green, preferred_element_type=F32)  3.03 us
    pallas_call x1, Pallas kernels, prologue(): pl.pallas_call(prologue_kernel, out_shape=[jax.ShapeDtypeStruct((own, orb...  1.9 us
  transfers between devices with their start and end apart: 15, of which 7 were waited for; matrix products, arithmetic and copies ran while one was open for 7% of the time, Pallas kernels for 7%

profile of v4, /device:TPU:1, one launch (start us, length us, event | category | flops | bytes accessed | tf_op | source)
XLA Modules:
  0.0 91.5 jit_solution(6651630573358106808)
XLA Ops:
  0.0 1.9 %shard_map.46 = (bf16[128,1024]{1,0:T(8,128)(2,1)}, bf16[72,1024]{1,0:T(8,128)(2,1)}, f32[1,128]{1,0:T(1,128)}) custom-call(bf16[128,1024]{1,0:T(8,128)(2,1)} %factors_in.1, s32[1,8]{1,0:T(1,128)} %pattern_in.1, f32[1,128]{1,0:T(1,128)} %bitcast.12), custom_call_target="tpu_custom_call" | custom-call | tf_op jit(solution)/shard_map/pallas_call | solution.py:102
  1.9 0.0 copy-start.2
  1.9 2.5 %collective-permute-start.1 = (bf16[72,1024]{1,0:T(8,128)(2,1)}, bf16[72,1024]{1,0:T(8,128)(2,1)S(1)}, u32[]{:S(2)}, u32[]{:S(2)}) collective-permute-start(bf16[72,1024]{1,0:T(8,128)(2,1)} %get-tuple-element.27), channel_id=1, source_target_pairs={{0,8},{1,9},{2,10},{3,11},{4,12},{5,13},{6,14},{7,15},{8,16},{9,17... | collective-permute-start | bytes 442376 | tf_op jit(solution)/shard_map/ppermute | solution.py:31
  4.5 4.0 %collective-permute-start.2 = (bf16[72,1024]{1,0:T(8,128)(2,1)}, bf16[72,1024]{1,0:T(8,128)(2,1)S(1)}, u32[]{:S(2)}, u32[]{:S(2)}) collective-permute-start(bf16[72,1024]{1,0:T(8,128)(2,1)} %get-tuple-element.27), channel_id=1, source_target_pairs={{0,152},{1,153},{2,154},{3,155},{4,156},{5,157},{6,158},{7,159},{8... | collective-permute-start | bytes 442376 | tf_op jit(solution)/shard_map/ppermute | solution.py:31
  8.5 1.8 %collective-permute-start.3 = (bf16[72,1024]{1,0:T(8,128)(2,1)}, bf16[72,1024]{1,0:T(8,128)(2,1)S(1)}, u32[]{:S(2)}, u32[]{:S(2)}) collective-permute-start(bf16[72,1024]{1,0:T(8,128)(2,1)} %get-tuple-element.27), channel_id=1, source_target_pairs={{0,16},{1,145},{2,18},{3,147},{4,20},{5,149},{6,22},{7,151},{8,24}... | collective-permute-start | bytes 442376 | tf_op jit(solution)/shard_map/ppermute | solution.py:31
  10.3 3.0 %fusion.1 = bf16[2,128,1024]{2,1,0:T(8,128)(2,1)S(1)} fusion(bf16[2,1024,1024]{2,1,0:T(8,128)(2,1)} %param.4, bf16[128,1024]{1,0:T(8,128)(2,1)} %get-tuple-element.26), kind=kOutput, calls=%fused_computation.3 | convolution fusion | flops 537133056 | bytes 4980736 | tf_op jit(solution)/shard_map/qo,tok->tqk/dot_general | solution.py:261
  13.3 0.0 copy-done.2
  13.4 0.0 collective-permute-done.1
  13.4 0.0 collective-permute-done.2
  13.5 2.2 %collective-permute-done.3 = bf16[72,1024]{1,0:T(8,128)(2,1)S(1)} collective-permute-done((bf16[72,1024]{1,0:T(8,128)(2,1)}, bf16[72,1024]{1,0:T(8,128)(2,1)S(1)}, u32[]{:S(2)}, u32[]{:S(2)}) %collective-permute-start.3) | collective-permute-done | bytes 147488 | tf_op jit(solution)/shard_map/ppermute | solution.py:31
  15.7 0.1 concatenate.6.refs_4_.refs_0_
  15.8 1.3 %collective-permute-start.4 = (bf16[264,1024]{1,0:T(8,128)(2,1)S(1)}, bf16[264,1024]{1,0:T(8,128)(2,1)S(1)}, u32[]{:S(2)}, u32[]{:S(2)}) collective-permute-start(bf16[264,1024]{1,0:T(8,128)(2,1)S(1)} %concatenate.6.refs_4_.refs_0_), channel_id=1, source_target_pairs={{0,2},{1,3},{2,4},{3,5},{4,6},{5,7},{6,0},{7,1},{8,10},{9,11},{10,... | collective-permute-start | bytes 1622024 | tf_op jit(solution)/shard_map/ppermute | solution.py:31
  17.1 1.5 %collective-permute-start.5 = (bf16[264,1024]{1,0:T(8,128)(2,1)S(1)}, bf16[264,1024]{1,0:T(8,128)(2,1)S(1)}, u32[]{:S(2)}, u32[]{:S(2)}) collective-permute-start(bf16[264,1024]{1,0:T(8,128)(2,1)S(1)} %concatenate.6.refs_4_.refs_0_), channel_id=1, source_target_pairs={{0,6},{1,7},{2,0},{3,1},{4,2},{5,3},{6,4},{7,5},{8,14},{9,15},{10,... | collective-permute-start | bytes 1622024 | tf_op jit(solution)/shard_map/ppermute | solution.py:31
  18.6 2.8 %collective-permute-start.6 = (bf16[200,1024]{1,0:T(8,128)(2,1)S(1)}, bf16[200,1024]{1,0:T(8,128)(2,1)S(1)}, u32[]{:S(2)}, u32[]{:S(2)}) collective-permute-start(bf16[200,1024]{1,0:T(8,128)(2,1)S(1)} %slice.40), channel_id=1, source_target_pairs={{0,32},{1,97},{2,34},{3,99},{4,36},{5,101},{6,38},{7,103},{8,40},{... | collective-permute-start | bytes 1228808 | tf_op jit(solution)/shard_map/ppermute | solution.py:31
  21.4 3.9 %collective-permute-start.7 = (bf16[2,128,1024]{2,1,0:T(8,128)(2,1)S(1)}, bf16[2,128,1024]{2,1,0:T(8,128)(2,1)S(1)}, u32[]{:S(2)}, u32[]{:S(2)}) collective-permute-start(bf16[2,128,1024]{2,1,0:T(8,128)(2,1)S(1)} %fusion.1), channel_id=1, source_target_pairs={{0,16},{1,145},{2,18},{3,147},{4,20},{5,149},{6,22},{7,151},{8,24}... | collective-permute-start | bytes 1572872 | tf_op jit(solution)/shard_map/ppermute | solution.py:31
  25.3 0.0 copy-done.1
  25.3 1.7 %collective-permute-done.6 = bf16[200,1024]{1,0:T(8,128)(2,1)S(1)} collective-permute-done((bf16[200,1024]{1,0:T(8,128)(2,1)S(1)}, bf16[200,1024]{1,0:T(8,128)(2,1)S(1)}, u32[]{:S(2)}, u32[]{:S(2)}) %collective-permute-start.6) | collective-permute-done | bytes 409632 | tf_op jit(solution)/shard_map/ppermute | solution.py:31
  27.1 10.0 %collective-permute-done.7 = bf16[2,128,1024]{2,1,0:T(8,128)(2,1)S(1)} collective-permute-done((bf16[2,128,1024]{2,1,0:T(8,128)(2,1)S(1)}, bf16[2,128,1024]{2,1,0:T(8,128)(2,1)S(1)}, u32[]{:S(2)}, u32[]{:S(2)}) %collective-permute-start.7) | collective-permute-done | bytes 524320 | tf_op jit(solution)/shard_map/ppermute | solution.py:31
  37.1 0.0 collective-permute-done.4.west_ref.refs_4_.refs_2_
  37.1 0.0 collective-permute-done.5.east_ref.refs_5_.refs_3_
  37.1 3.1 %collective-permute-start.8 = (bf16[2,128,1024]{2,1,0:T(8,128)(2,1)S(1)}, bf16[2,128,1024]{2,1,0:T(8,128)(2,1)S(1)}, u32[]{:S(2)}, u32[]{:S(2)}) collective-permute-start(bf16[2,128,1024]{2,1,0:T(8,128)(2,1)S(1)} %collective-permute-done.7), channel_id=1, source_target_pairs={{0,16},{1,145},{2,18},{3,147},{4,20},{5,149},{6,22},{7,151},{8,24}... | collective-permute-start | bytes 1572872 | tf_op jit(solution)/shard_map/ppermute | solution.py:31
  40.2 0.1 shard_map.47
  40.3 0.2 collective-permute-start.12
  40.4 1.3 %collective-permute-start.10 = (bf16[264,1024]{1,0:T(8,128)(2,1)S(1)}, bf16[264,1024]{1,0:T(8,128)(2,1)S(1)}, u32[]{:S(2)}, u32[]{:S(2)}) collective-permute-start(bf16[264,1024]{1,0:T(8,128)(2,1)S(1)} %get-tuple-element.33), channel_id=1, source_target_pairs={{0,2},{1,7},{2,4},{3,1},{4,6},{5,3},{6,0},{7,5},{8,10},{9,15},{10,... | collective-permute-start | bytes 1622024 | tf_op jit(solution)/shard_map/ppermute | solution.py:31
  41.7 3.7 %fusion.refs_0_ = bf16[2,128,1024]{2,1,0:T(8,128)(2,1)S(1)} fusion(bf16[2,1024,1024]{2,1,0:T(8,128)(2,1)} %param.4, bf16[128,1024]{1,0:T(8,128)(2,1)S(1)} %copy-done.1), kind=kOutput, calls=%fused_computation.2 | convolution fusion | flops 537133056 | bytes 4980736 | tf_op jit(solution)/shard_map/qo,tko->tqk/dot_general | solution.py:262
  45.4 0.1 collective-permute-start
  45.5 6.1 %collective-permute-done.8.refs_2_ = bf16[2,128,1024]{2,1,0:T(8,128)(2,1)S(1)} collective-permute-done((bf16[2,128,1024]{2,1,0:T(8,128)(2,1)S(1)}, bf16[2,128,1024]{2,1,0:T(8,128)(2,1)S(1)}, u32[]{:S(2)}, u32[]{:S(2)}) %collective-permute-start.8) | collective-permute-done | bytes 524320 | tf_op jit(solution)/shard_map/ppermute | solution.py:31
  51.6 1.2 %collective-permute-start.9 = (bf16[2,128,1024]{2,1,0:T(8,128)(2,1)S(1)}, bf16[2,128,1024]{2,1,0:T(8,128)(2,1)S(1)}, u32[]{:S(2)}, u32[]{:S(2)}) collective-permute-start(bf16[2,128,1024]{2,1,0:T(8,128)(2,1)S(1)} %collective-permute-done.8.refs_2_), channel_id=1, source_target_pairs={{0,1},{1,0},{2,3},{3,2},{4,5},{5,4},{6,7},{7,6},{8,9},{9,8},{10,11... | collective-permute-start | bytes 1572872 | tf_op jit(solution)/shard_map/ppermute | solution.py:31
  52.8 0.0 collective-permute-done.10.refs_4_.refs_5_
  52.8 1.9 %collective-permute-start.11 = (bf16[264,1024]{1,0:T(8,128)(2,1)S(1)}, bf16[264,1024]{1,0:T(8,128)(2,1)S(1)}, u32[]{:S(2)}, u32[]{:S(2)}) collective-permute-start(bf16[264,1024]{1,0:T(8,128)(2,1)S(1)} %collective-permute-done.10.refs_4_.refs_5_), channel_id=1, source_target_pairs={{0,32},{1,97},{2,34},{3,99},{4,36},{5,101},{6,38},{7,103},{8,40},{... | collective-permute-start | bytes 1622024 | tf_op jit(solution)/shard_map/ppermute | solution.py:31
  54.7 0.0 collective-permute-done.refs_1_
  54.7 0.0 collective-permute-done.9.refs_3_
  54.7 2.0 %shard_map.48 = (f32[2,128,1024]{2,1,0:T(8,128)S(1)}, f32[2,128,1024]{2,1,0:T(8,128)S(1)}) custom-call(bf16[2,128,1024]{2,1,0:T(8,128)(2,1)S(1)} %fusion.refs_0_, bf16[2,128,1024]{2,1,0:T(8,128)(2,1)S(1)} %collective-permute-done.refs_1_, bf16[2,128,1024]{2,1,0:T(8,128)(2,1)S(1)} %collective-permute-done.8.refs_2_, ...), custom_call_target="tpu_custom_call" | custom-call | flops 1610612736 | bytes 2097152 | tf_op jit(solution)/shard_map/pallas_call | solution.py:193
  56.7 2.1 %shard_map.49 = (f32[2,128,1024]{2,1,0:T(8,128)S(1)}, f32[2,128,1024]{2,1,0:T(8,128)S(1)}) custom-call(bf16[2,128,1024]{2,1,0:T(8,128)(2,1)S(1)} %fusion.refs_0_, bf16[2,128,1024]{2,1,0:T(8,128)(2,1)S(1)} %collective-permute-done.refs_1_, bf16[2,128,1024]{2,1,0:T(8,128)(2,1)S(1)} %collective-permute-done.8.refs_2_, ...), custom_call_target="tpu_custom_call", output_to_operand_aliasing={{0}: (6, {}), {1}: (7, {})} | custom-call | flops 1610612736 | bytes 2097152 | tf_op jit(solution)/shard_map/pallas_call | solution.py:193
  58.8 0.0 collective-permute-done.12.refs_4_
  58.8 2.0 %shard_map.50 = (f32[2,128,1024]{2,1,0:T(8,128)S(1)}, f32[2,128,1024]{2,1,0:T(8,128)S(1)}) custom-call(bf16[2,128,1024]{2,1,0:T(8,128)(2,1)S(1)} %fusion.refs_0_, bf16[2,128,1024]{2,1,0:T(8,128)(2,1)S(1)} %collective-permute-done.refs_1_, bf16[2,128,1024]{2,1,0:T(8,128)(2,1)S(1)} %collective-permute-done.8.refs_2_, ...), custom_call_target="tpu_custom_call", output_to_operand_aliasing={{0}: (5, {}), {1}: (6, {})} | custom-call | flops 1610612736 | bytes 2097152 | tf_op jit(solution)/shard_map/pallas_call | solution.py:193
  60.9 0.0 copy-start
  60.9 1.3 %collective-permute-done.11.refs_5_.refs_6_ = bf16[264,1024]{1,0:T(8,128)(2,1)S(1)} collective-permute-done((bf16[264,1024]{1,0:T(8,128)(2,1)S(1)}, bf16[264,1024]{1,0:T(8,128)(2,1)S(1)}, u32[]{:S(2)}, u32[]{:S(2)}) %collective-permute-start.11) | collective-permute-done | bytes 540704 | tf_op jit(solution)/shard_map/ppermute | solution.py:31
  62.2 2.0 %shard_map.51 = (f32[2,128,1024]{2,1,0:T(8,128)S(1)}, bf16[2,128,1024]{2,1,0:T(8,128)(2,1)S(1)}) custom-call(bf16[2,128,1024]{2,1,0:T(8,128)(2,1)S(1)} %fusion.refs_0_, bf16[2,128,1024]{2,1,0:T(8,128)(2,1)S(1)} %collective-permute-done.refs_1_, bf16[2,128,1024]{2,1,0:T(8,128)(2,1)S(1)} %collective-permute-done.8.refs_2_, ...), custom_call_target="tpu_custom_call", output_to_operand_aliasing={{0}: (6, {})} | custom-call | flops 1610612736 | bytes 2097152 | tf_op jit(solution)/shard_map/pallas_call | solution.py:193
  64.2 0.1 collective-permute-start.13
  64.3 1.9 %collective-permute-done.13.got_ref = bf16[2,128,1024]{2,1,0:T(8,128)(2,1)S(1)} collective-permute-done((bf16[2,128,1024]{2,1,0:T(8,128)(2,1)S(1)}, bf16[2,128,1024]{2,1,0:T(8,128)(2,1)S(1)}, u32[]{:S(2)}, u32[]{:S(2)}) %collective-permute-start.13) | collective-permute-done | bytes 524320 | tf_op jit(solution)/shard_map/ppermute | solution.py:31
  66.2 0.0 copy-done
  66.2 0.3 shard_map.52
  66.6 20.2 %all_to_all.5.part_ref = bf16[16,2,64,128]{3,2,1,0:T(8,128)(2,1)S(1)} all-to-all(bf16[16,2,64,128]{3,2,1,0:T(8,128)(2,1)S(1)} %shard_map.52), channel_id=1, replica_groups={{0,2,4,6,8,10,12,14,16,18,20,22,24,26,28,30},{1,3,5,7,9,11,13,15,17,19,..., dimensions={0} | all-to-all | bytes 1048576 | tf_op jit(solution)/shard_map/all_to_all | solution.py:305
  86.7 0.8 shard_map.53
  87.5 2.0 %collective-permute-start.14 = (f32[2,32,1024]{2,1,0:T(8,128)S(1)}, f32[2,32,1024]{2,1,0:T(8,128)S(1)}, u32[]{:S(2)}, u32[]{:S(2)}) collective-permute-start(f32[2,32,1024]{2,1,0:T(8,128)S(1)} %get-tuple-element.46), channel_id=1, source_target_pairs={{0,1},{1,0},{2,3},{3,2},{4,5},{5,4},{6,7},{7,6},{8,9},{9,8},{10,11... | collective-permute-start | bytes 786440 | tf_op jit(solution)/shard_map/ppermute | solution.py:31
  89.6 1.2 %collective-permute-done.14.got_ref = f32[2,32,1024]{2,1,0:T(8,128)S(1)} collective-permute-done((f32[2,32,1024]{2,1,0:T(8,128)S(1)}, f32[2,32,1024]{2,1,0:T(8,128)S(1)}, u32[]{:S(2)}, u32[]{:S(2)}) %collective-permute-start.14) | collective-permute-done | bytes 262176 | tf_op jit(solution)/shard_map/ppermute | solution.py:31
  90.7 0.8 shard_map.54
  (13 shorter events, 0.1 us)
Async XLA Ops:
  1.9 11.4 %copy-start.2 = (bf16[72,1024]{1,0:T(8,128)(2,1)S(1)}, bf16[72,1024]{1,0:T(8,128)(2,1)}, u32[]{:S(2)}) copy-start(bf16[72,1024]{1,0:T(8,128)(2,1)} %get-tuple-element.27) | copy-start | bytes 442372
  1.9 11.5 %collective-permute-start.1 = (bf16[72,1024]{1,0:T(8,128)(2,1)}, bf16[72,1024]{1,0:T(8,128)(2,1)S(1)}, u32[]{:S(2)}, u32[]{:S(2)}) collective-permute-start(bf16[72,1024]{1,0:T(8,128)(2,1)} %get-tuple-element.27), channel_id=1, source_target_pairs={{0,8},{1,9},{2,10},{3,11},{4,12},{5,13},{6,14},{7,15},{8,16},{9,17... | collective-permute-start | bytes 442376 | tf_op jit(solution)/shard_map/ppermute | solution.py:31
  4.5 9.0 %collective-permute-start.2 = (bf16[72,1024]{1,0:T(8,128)(2,1)}, bf16[72,1024]{1,0:T(8,128)(2,1)S(1)}, u32[]{:S(2)}, u32[]{:S(2)}) collective-permute-start(bf16[72,1024]{1,0:T(8,128)(2,1)} %get-tuple-element.27), channel_id=1, source_target_pairs={{0,152},{1,153},{2,154},{3,155},{4,156},{5,157},{6,158},{7,159},{8... | collective-permute-start | bytes 442376 | tf_op jit(solution)/shard_map/ppermute | solution.py:31
  8.5 7.2 %collective-permute-start.3 = (bf16[72,1024]{1,0:T(8,128)(2,1)}, bf16[72,1024]{1,0:T(8,128)(2,1)S(1)}, u32[]{:S(2)}, u32[]{:S(2)}) collective-permute-start(bf16[72,1024]{1,0:T(8,128)(2,1)} %get-tuple-element.27), channel_id=1, source_target_pairs={{0,16},{1,145},{2,18},{3,147},{4,20},{5,149},{6,22},{7,151},{8,24}... | collective-permute-start | bytes 442376 | tf_op jit(solution)/shard_map/ppermute | solution.py:31
  10.3 15.0 %copy-start.1 = (bf16[128,1024]{1,0:T(8,128)(2,1)S(1)}, bf16[128,1024]{1,0:T(8,128)(2,1)}, u32[]{:S(2)}) copy-start(bf16[128,1024]{1,0:T(8,128)(2,1)} %get-tuple-element.26) | copy-start | bytes 786436
  15.8 21.3 %collective-permute-start.4 = (bf16[264,1024]{1,0:T(8,128)(2,1)S(1)}, bf16[264,1024]{1,0:T(8,128)(2,1)S(1)}, u32[]{:S(2)}, u32[]{:S(2)}) collective-permute-start(bf16[264,1024]{1,0:T(8,128)(2,1)S(1)} %concatenate.6.refs_4_.refs_0_), channel_id=1, source_target_pairs={{0,2},{1,3},{2,4},{3,5},{4,6},{5,7},{6,0},{7,1},{8,10},{9,11},{10,... | collective-permute-start | bytes 1622024 | tf_op jit(solution)/shard_map/ppermute | solution.py:31
  17.1 20.0 %collective-permute-start.5 = (bf16[264,1024]{1,0:T(8,128)(2,1)S(1)}, bf16[264,1024]{1,0:T(8,128)(2,1)S(1)}, u32[]{:S(2)}, u32[]{:S(2)}) collective-permute-start(bf16[264,1024]{1,0:T(8,128)(2,1)S(1)} %concatenate.6.refs_4_.refs_0_), channel_id=1, source_target_pairs={{0,6},{1,7},{2,0},{3,1},{4,2},{5,3},{6,4},{7,5},{8,14},{9,15},{10,... | collective-permute-start | bytes 1622024 | tf_op jit(solution)/shard_map/ppermute | solution.py:31
  18.6 8.5 %collective-permute-start.6 = (bf16[200,1024]{1,0:T(8,128)(2,1)S(1)}, bf16[200,1024]{1,0:T(8,128)(2,1)S(1)}, u32[]{:S(2)}, u32[]{:S(2)}) collective-permute-start(bf16[200,1024]{1,0:T(8,128)(2,1)S(1)} %slice.40), channel_id=1, source_target_pairs={{0,32},{1,97},{2,34},{3,99},{4,36},{5,101},{6,38},{7,103},{8,40},{... | collective-permute-start | bytes 1228808 | tf_op jit(solution)/shard_map/ppermute | solution.py:31
  21.4 15.7 %collective-permute-start.7 = (bf16[2,128,1024]{2,1,0:T(8,128)(2,1)S(1)}, bf16[2,128,1024]{2,1,0:T(8,128)(2,1)S(1)}, u32[]{:S(2)}, u32[]{:S(2)}) collective-permute-start(bf16[2,128,1024]{2,1,0:T(8,128)(2,1)S(1)} %fusion.1), channel_id=1, source_target_pairs={{0,16},{1,145},{2,18},{3,147},{4,20},{5,149},{6,22},{7,151},{8,24}... | collective-permute-start | bytes 1572872 | tf_op jit(solution)/shard_map/ppermute | solution.py:31
  37.1 14.5 %collective-permute-start.8 = (bf16[2,128,1024]{2,1,0:T(8,128)(2,1)S(1)}, bf16[2,128,1024]{2,1,0:T(8,128)(2,1)S(1)}, u32[]{:S(2)}, u32[]{:S(2)}) collective-permute-start(bf16[2,128,1024]{2,1,0:T(8,128)(2,1)S(1)} %collective-permute-done.7), channel_id=1, source_target_pairs={{0,16},{1,145},{2,18},{3,147},{4,20},{5,149},{6,22},{7,151},{8,24}... | collective-permute-start | bytes 1572872 | tf_op jit(solution)/shard_map/ppermute | solution.py:31
  40.3 18.5 %collective-permute-start.12 = (bf16[528,1024]{1,0:T(8,128)(2,1)S(1)}, bf16[528,1024]{1,0:T(8,128)(2,1)S(1)}, u32[]{:S(2)}, u32[]{:S(2)}) collective-permute-start(bf16[528,1024]{1,0:T(8,128)(2,1)S(1)} %get-tuple-element.34), channel_id=1, source_target_pairs={{0,32},{1,97},{2,34},{3,99},{4,36},{5,101},{6,38},{7,103},{8,40},{... | collective-permute-start | bytes 3244040 | tf_op jit(solution)/shard_map/ppermute | solution.py:31
  40.4 12.4 %collective-permute-start.10 = (bf16[264,1024]{1,0:T(8,128)(2,1)S(1)}, bf16[264,1024]{1,0:T(8,128)(2,1)S(1)}, u32[]{:S(2)}, u32[]{:S(2)}) collective-permute-start(bf16[264,1024]{1,0:T(8,128)(2,1)S(1)} %get-tuple-element.33), channel_id=1, source_target_pairs={{0,2},{1,7},{2,4},{3,1},{4,6},{5,3},{6,0},{7,5},{8,10},{9,15},{10,... | collective-permute-start | bytes 1622024 | tf_op jit(solution)/shard_map/ppermute | solution.py:31
  45.4 9.3 %collective-permute-start = (bf16[2,128,1024]{2,1,0:T(8,128)(2,1)S(1)}, bf16[2,128,1024]{2,1,0:T(8,128)(2,1)S(1)}, u32[]{:S(2)}, u32[]{:S(2)}) collective-permute-start(bf16[2,128,1024]{2,1,0:T(8,128)(2,1)S(1)} %fusion.refs_0_), channel_id=1, source_target_pairs={{0,1},{1,0},{2,3},{3,2},{4,5},{5,4},{6,7},{7,6},{8,9},{9,8},{10,11... | collective-permute-start | bytes 1572872 | tf_op jit(solution)/shard_map/ppermute | solution.py:31
  51.6 3.1 %collective-permute-start.9 = (bf16[2,128,1024]{2,1,0:T(8,128)(2,1)S(1)}, bf16[2,128,1024]{2,1,0:T(8,128)(2,1)S(1)}, u32[]{:S(2)}, u32[]{:S(2)}) collective-permute-start(bf16[2,128,1024]{2,1,0:T(8,128)(2,1)S(1)} %collective-permute-done.8.refs_2_), channel_id=1, source_target_pairs={{0,1},{1,0},{2,3},{3,2},{4,5},{5,4},{6,7},{7,6},{8,9},{9,8},{10,11... | collective-permute-start | bytes 1572872 | tf_op jit(solution)/shard_map/ppermute | solution.py:31
  52.8 9.4 %collective-permute-start.11 = (bf16[264,1024]{1,0:T(8,128)(2,1)S(1)}, bf16[264,1024]{1,0:T(8,128)(2,1)S(1)}, u32[]{:S(2)}, u32[]{:S(2)}) collective-permute-start(bf16[264,1024]{1,0:T(8,128)(2,1)S(1)} %collective-permute-done.10.refs_4_.refs_5_), channel_id=1, source_target_pairs={{0,32},{1,97},{2,34},{3,99},{4,36},{5,101},{6,38},{7,103},{8,40},{... | collective-permute-start | bytes 1622024 | tf_op jit(solution)/shard_map/ppermute | solution.py:31
  60.9 5.4 %copy-start = (f32[1,128]{1,0:T(1,128)S(1)}, f32[1,128]{1,0:T(1,128)}, u32[]{:S(2)}) copy-start(f32[1,128]{1,0:T(1,128)} %get-tuple-element.44.coulomb_ref) | copy-start | bytes 1540
  64.2 2.0 %collective-permute-start.13 = (bf16[2,128,1024]{2,1,0:T(8,128)(2,1)S(1)}, bf16[2,128,1024]{2,1,0:T(8,128)(2,1)S(1)}, u32[]{:S(2)}, u32[]{:S(2)}) collective-permute-start(bf16[2,128,1024]{2,1,0:T(8,128)(2,1)S(1)} %get-tuple-element.43), channel_id=1, source_target_pairs={{0,1},{1,0},{2,3},{3,2},{4,5},{5,4},{6,7},{7,6},{8,9},{9,8},{10,11... | collective-permute-start | bytes 1572872 | tf_op jit(solution)/shard_map/ppermute | solution.py:31
  87.5 3.2 %collective-permute-start.14 = (f32[2,32,1024]{2,1,0:T(8,128)S(1)}, f32[2,32,1024]{2,1,0:T(8,128)S(1)}, u32[]{:S(2)}, u32[]{:S(2)}) collective-permute-start(f32[2,32,1024]{2,1,0:T(8,128)S(1)} %get-tuple-element.46), channel_id=1, source_target_pairs={{0,1},{1,0},{2,3},{3,2},{4,5},{5,4},{6,7},{7,6},{8,9},{9,8},{10,11... | collective-permute-start | bytes 786440 | tf_op jit(solution)/shard_map/ppermute | solution.py:31

commit v5 on v4

--- a/solution.py
+++ b/solution.py
@@ -255,9 +255,9 @@
     barrier = lax.optimization_barrier
     masked, whole, coulomb = prologue(factors, pattern, coulomb)
 
+    beyond = two_along_z(whole)
     below = along_z(whole, 1)
     above = along_z(whole, -1)
-    beyond = two_along_z(whole)
     left = jnp.einsum("qo,tok->tqk", masked, green, preferred_element_type=F32).astype(BF16)
     right = jnp.einsum("qo,tko->tqk", masked, green, preferred_element_type=F32).astype(BF16)
     right_other = other_core(right)
@@ -268,13 +268,13 @@
     here, left = barrier((here, left))
 
     n = 4 * HALF
+    left = two_along_z(left)
     west = along_x(here, 1)
     east = along_x(here, -1)
     rest = other_parity(here[HALF:])
-    left = two_along_z(left)
     here_q = jnp.concatenate([masked[HALF:], rest], axis=0)
 
-    west, east, here_q, left = barrier((west, east, here_q, left))
+    west, east, here_q = barrier((west, east, here_q))
     onward, both = mix(west, east)
     far = split_x(onward)
     sides_q = other_parity(both)
@@ -289,8 +289,8 @@
     sides = (right, right_other, left, left_other)
     acc = chunk(sides, (here, here_q), [piece(0), piece(1)])
     acc = chunk(sides, (west, east), [piece(0), piece(1)], acc)
-    acc = chunk(sides, (sides_q,), [piece(0), piece(0, n + 8)], acc)
-    keep, theirs = chunk(sides, (far, far_q), [piece(0), piece(1)], acc, last=True)
+    acc = chunk(sides, (sides_q, far), [piece(0), piece(0, n + 8), piece(1)], acc)
+    keep, theirs = chunk(sides, (far_q,), [piece(0)], acc, last=True)
 
     got = other_core(theirs)
     chips, i_rows = 16, orb // 16

time: 91.7 us -> 87.6 us (0.955)
  waiting for transfers between devices: 24.5 us -> 13.7 us
  starting transfers between devices: 27.7 us -> 32.9 us
  blocking collectives: 20.2 us -> 21.4 us
    ppermute x15, waiting for transfers between devices: 24.5 us -> 13.7 us  [send(): return lax.ppermute(value, BOTH, sorted(pairs))]
    ppermute x15, starting transfers between devices: 27.7 us -> 32.9 us  [send(): return lax.ppermute(value, BOTH, sorted(pairs))]
    all_to_all x1, blocking collectives: 20.2 us -> 21.4 us  [local(): lax.all_to_all(part, 'aux', 0, 0, axis_index_groups=groups, tiled=True)]
  transfers between devices with their start and end apart: 15 -> 15, of which waited for: 7 -> 5; matrix products, arithmetic and copies ran while one was open for 7% -> 8% of each run, Pallas kernels for 7% -> 8%
where the time goes in v5:
time: 87.6 us; the launch traced here: 87.5 us
  starting transfers between devices  32.9 us (38%)
  blocking collectives  21.4 us (24%)
  waiting for transfers between devices  13.7 us (16%)
  Pallas kernels  12.2 us (14%)
  matrix products  6.71 us (8%)
    ppermute x15, starting transfers between devices, send(): return lax.ppermute(value, BOTH, sorted(pairs))  32.9 us
    all_to_all x1, blocking collectives, local(): lax.all_to_all(part, 'aux', 0, 0, axis_index_groups=groups, tiled=True)  21.4 us
    ppermute x15, waiting for transfers between devices, send(): return lax.ppermute(value, BOTH, sorted(pairs))  13.7 us
    pallas_call x4, Pallas kernels, chunk(): pl.pallas_call(functools.partial(chunk_kernel, tuple(pieces), len(rows),...  8.33 us
    dot_general x1, matrix products, local(): jnp.einsum('qo,tko->tqk', masked, green, preferred_element_type=F32)  3.69 us
    dot_general x1, matrix products, local(): jnp.einsum('qo,tok->tqk', masked, green, preferred_element_type=F32)  3.03 us
    pallas_call x1, Pallas kernels, prologue(): pl.pallas_call(prologue_kernel, out_shape=[jax.ShapeDtypeStruct((own, orb...  1.9 us
  transfers between devices with their start and end apart: 15, of which 5 were waited for; matrix products, arithmetic and copies ran while one was open for 8% of the time, Pallas kernels for 8%

profile of v5, /device:TPU:1, one launch (start us, length us, event | category | flops | bytes accessed | tf_op | source)
XLA Modules:
  0.0 87.5 jit_solution(2765000231184431798)
XLA Ops:
  0.0 1.9 %shard_map.46 = (bf16[128,1024]{1,0:T(8,128)(2,1)}, bf16[72,1024]{1,0:T(8,128)(2,1)}, f32[1,128]{1,0:T(1,128)}) custom-call(bf16[128,1024]{1,0:T(8,128)(2,1)} %factors_in.1, s32[1,8]{1,0:T(1,128)} %pattern_in.1, f32[1,128]{1,0:T(1,128)} %bitcast.12), custom_call_target="tpu_custom_call" | custom-call | tf_op jit(solution)/shard_map/pallas_call | solution.py:102
  1.9 0.0 copy-start.2
  1.9 2.5 %collective-permute-start.1 = (bf16[72,1024]{1,0:T(8,128)(2,1)}, bf16[72,1024]{1,0:T(8,128)(2,1)S(1)}, u32[]{:S(2)}, u32[]{:S(2)}) collective-permute-start(bf16[72,1024]{1,0:T(8,128)(2,1)} %get-tuple-element.26), channel_id=1, source_target_pairs={{0,8},{1,9},{2,10},{3,11},{4,12},{5,13},{6,14},{7,15},{8,16},{9,17... | collective-permute-start | bytes 442376 | tf_op jit(solution)/shard_map/ppermute | solution.py:31
  4.5 4.0 %collective-permute-start.2 = (bf16[72,1024]{1,0:T(8,128)(2,1)}, bf16[72,1024]{1,0:T(8,128)(2,1)S(1)}, u32[]{:S(2)}, u32[]{:S(2)}) collective-permute-start(bf16[72,1024]{1,0:T(8,128)(2,1)} %get-tuple-element.26), channel_id=1, source_target_pairs={{0,152},{1,153},{2,154},{3,155},{4,156},{5,157},{6,158},{7,159},{8... | collective-permute-start | bytes 442376 | tf_op jit(solution)/shard_map/ppermute | solution.py:31
  8.5 1.8 %collective-permute-start.3 = (bf16[72,1024]{1,0:T(8,128)(2,1)}, bf16[72,1024]{1,0:T(8,128)(2,1)S(1)}, u32[]{:S(2)}, u32[]{:S(2)}) collective-permute-start(bf16[72,1024]{1,0:T(8,128)(2,1)} %get-tuple-element.26), channel_id=1, source_target_pairs={{0,16},{1,145},{2,18},{3,147},{4,20},{5,149},{6,22},{7,151},{8,24}... | collective-permute-start | bytes 442376 | tf_op jit(solution)/shard_map/ppermute | solution.py:31
  10.3 3.0 %fusion.1 = bf16[2,128,1024]{2,1,0:T(8,128)(2,1)S(1)} fusion(bf16[2,1024,1024]{2,1,0:T(8,128)(2,1)} %param.4, bf16[128,1024]{1,0:T(8,128)(2,1)} %get-tuple-element.25), kind=kOutput, calls=%fused_computation.3 | convolution fusion | flops 537133056 | bytes 4980736 | tf_op jit(solution)/shard_map/qo,tok->tqk/dot_general | solution.py:261
  13.3 0.0 copy-done.2
  13.4 0.0 collective-permute-done.1
  13.4 0.0 collective-permute-done.2
  13.5 2.2 %collective-permute-done.3 = bf16[72,1024]{1,0:T(8,128)(2,1)S(1)} collective-permute-done((bf16[72,1024]{1,0:T(8,128)(2,1)}, bf16[72,1024]{1,0:T(8,128)(2,1)S(1)}, u32[]{:S(2)}, u32[]{:S(2)}) %collective-permute-start.3) | collective-permute-done | bytes 147488 | tf_op jit(solution)/shard_map/ppermute | solution.py:31
  15.7 0.1 concatenate.6.refs_4_.refs_0_
  15.8 4.0 %collective-permute-start.4 = (bf16[2,128,1024]{2,1,0:T(8,128)(2,1)S(1)}, bf16[2,128,1024]{2,1,0:T(8,128)(2,1)S(1)}, u32[]{:S(2)}, u32[]{:S(2)}) collective-permute-start(bf16[2,128,1024]{2,1,0:T(8,128)(2,1)S(1)} %fusion.1), channel_id=1, source_target_pairs={{0,16},{1,145},{2,18},{3,147},{4,20},{5,149},{6,22},{7,151},{8,24}... | collective-permute-start | bytes 1572872 | tf_op jit(solution)/shard_map/ppermute | solution.py:31
  19.7 1.2 %collective-permute-start.7 = (bf16[264,1024]{1,0:T(8,128)(2,1)S(1)}, bf16[264,1024]{1,0:T(8,128)(2,1)S(1)}, u32[]{:S(2)}, u32[]{:S(2)}) collective-permute-start(bf16[264,1024]{1,0:T(8,128)(2,1)S(1)} %concatenate.6.refs_4_.refs_0_), channel_id=1, source_target_pairs={{0,2},{1,3},{2,4},{3,5},{4,6},{5,7},{6,0},{7,1},{8,10},{9,11},{10,... | collective-permute-start | bytes 1622024 | tf_op jit(solution)/shard_map/ppermute | solution.py:31
  20.9 1.5 %collective-permute-start.8 = (bf16[264,1024]{1,0:T(8,128)(2,1)S(1)}, bf16[264,1024]{1,0:T(8,128)(2,1)S(1)}, u32[]{:S(2)}, u32[]{:S(2)}) collective-permute-start(bf16[264,1024]{1,0:T(8,128)(2,1)S(1)} %concatenate.6.refs_4_.refs_0_), channel_id=1, source_target_pairs={{0,6},{1,7},{2,0},{3,1},{4,2},{5,3},{6,4},{7,5},{8,14},{9,15},{10,... | collective-permute-start | bytes 1622024 | tf_op jit(solution)/shard_map/ppermute | solution.py:31
  22.4 2.8 %collective-permute-start.9 = (bf16[200,1024]{1,0:T(8,128)(2,1)S(1)}, bf16[200,1024]{1,0:T(8,128)(2,1)S(1)}, u32[]{:S(2)}, u32[]{:S(2)}) collective-permute-start(bf16[200,1024]{1,0:T(8,128)(2,1)S(1)} %slice.40), channel_id=1, source_target_pairs={{0,32},{1,97},{2,34},{3,99},{4,36},{5,101},{6,38},{7,103},{8,40},{... | collective-permute-start | bytes 1228808 | tf_op jit(solution)/shard_map/ppermute | solution.py:31
  25.3 6.3 %collective-permute-done.4 = bf16[2,128,1024]{2,1,0:T(8,128)(2,1)S(1)} collective-permute-done((bf16[2,128,1024]{2,1,0:T(8,128)(2,1)S(1)}, bf16[2,128,1024]{2,1,0:T(8,128)(2,1)S(1)}, u32[]{:S(2)}, u32[]{:S(2)}) %collective-permute-start.4) | collective-permute-done | bytes 524320 | tf_op jit(solution)/shard_map/ppermute | solution.py:31
  31.6 3.1 %collective-permute-start.5 = (bf16[2,128,1024]{2,1,0:T(8,128)(2,1)S(1)}, bf16[2,128,1024]{2,1,0:T(8,128)(2,1)S(1)}, u32[]{:S(2)}, u32[]{:S(2)}) collective-permute-start(bf16[2,128,1024]{2,1,0:T(8,128)(2,1)S(1)} %collective-permute-done.4), channel_id=1, source_target_pairs={{0,16},{1,145},{2,18},{3,147},{4,20},{5,149},{6,22},{7,151},{8,24}... | collective-permute-start | bytes 1572872 | tf_op jit(solution)/shard_map/ppermute | solution.py:31
  34.6 0.0 copy-done.1
  34.6 0.0 collective-permute-done.9
  34.7 0.0 collective-permute-done.7.west_ref.refs_4_.refs_2_
  34.7 0.0 collective-permute-done.8.east_ref.refs_5_.refs_3_
  34.7 0.1 shard_map.47
  34.8 2.8 %collective-permute-start.12 = (bf16[528,1024]{1,0:T(8,128)(2,1)S(1)}, bf16[528,1024]{1,0:T(8,128)(2,1)S(1)}, u32[]{:S(2)}, u32[]{:S(2)}) collective-permute-start(bf16[528,1024]{1,0:T(8,128)(2,1)S(1)} %get-tuple-element.32), channel_id=1, source_target_pairs={{0,32},{1,97},{2,34},{3,99},{4,36},{5,101},{6,38},{7,103},{8,40},{... | collective-permute-start | bytes 3244040 | tf_op jit(solution)/shard_map/ppermute | solution.py:31
  37.6 2.5 %collective-permute-start.10 = (bf16[264,1024]{1,0:T(8,128)(2,1)S(1)}, bf16[264,1024]{1,0:T(8,128)(2,1)S(1)}, u32[]{:S(2)}, u32[]{:S(2)}) collective-permute-start(bf16[264,1024]{1,0:T(8,128)(2,1)S(1)} %get-tuple-element.31), channel_id=1, source_target_pairs={{0,2},{1,7},{2,4},{3,1},{4,6},{5,3},{6,0},{7,5},{8,10},{9,15},{10,... | collective-permute-start | bytes 1622024 | tf_op jit(solution)/shard_map/ppermute | solution.py:31
  40.1 3.7 %fusion.refs_0_ = bf16[2,128,1024]{2,1,0:T(8,128)(2,1)S(1)} fusion(bf16[2,1024,1024]{2,1,0:T(8,128)(2,1)} %param.4, bf16[128,1024]{1,0:T(8,128)(2,1)S(1)} %copy-done.1), kind=kOutput, calls=%fused_computation.2 | convolution fusion | flops 537133056 | bytes 4980736 | tf_op jit(solution)/shard_map/qo,tko->tqk/dot_general | solution.py:262
  43.8 0.1 collective-permute-start
  43.9 2.2 %collective-permute-done.5.refs_2_ = bf16[2,128,1024]{2,1,0:T(8,128)(2,1)S(1)} collective-permute-done((bf16[2,128,1024]{2,1,0:T(8,128)(2,1)S(1)}, bf16[2,128,1024]{2,1,0:T(8,128)(2,1)S(1)}, u32[]{:S(2)}, u32[]{:S(2)}) %collective-permute-start.5) | collective-permute-done | bytes 524320 | tf_op jit(solution)/shard_map/ppermute | solution.py:31
  46.1 1.8 %collective-permute-start.6 = (bf16[2,128,1024]{2,1,0:T(8,128)(2,1)S(1)}, bf16[2,128,1024]{2,1,0:T(8,128)(2,1)S(1)}, u32[]{:S(2)}, u32[]{:S(2)}) collective-permute-start(bf16[2,128,1024]{2,1,0:T(8,128)(2,1)S(1)} %collective-permute-done.5.refs_2_), channel_id=1, source_target_pairs={{0,1},{1,0},{2,3},{3,2},{4,5},{5,4},{6,7},{7,6},{8,9},{9,8},{10,11... | collective-permute-start | bytes 1572872 | tf_op jit(solution)/shard_map/ppermute | solution.py:31
  47.8 0.0 collective-permute-done.10.refs_5_
  47.9 2.7 %collective-permute-start.11 = (bf16[264,1024]{1,0:T(8,128)(2,1)S(1)}, bf16[264,1024]{1,0:T(8,128)(2,1)S(1)}, u32[]{:S(2)}, u32[]{:S(2)}) collective-permute-start(bf16[264,1024]{1,0:T(8,128)(2,1)S(1)} %collective-permute-done.10.refs_5_), channel_id=1, source_target_pairs={{0,32},{1,97},{2,34},{3,99},{4,36},{5,101},{6,38},{7,103},{8,40},{... | collective-permute-start | bytes 1622024 | tf_op jit(solution)/shard_map/ppermute | solution.py:31
  50.6 0.0 collective-permute-done.refs_1_
  50.6 0.0 collective-permute-done.6.refs_3_
  50.6 2.0 %shard_map.48 = (f32[2,128,1024]{2,1,0:T(8,128)S(1)}, f32[2,128,1024]{2,1,0:T(8,128)S(1)}) custom-call(bf16[2,128,1024]{2,1,0:T(8,128)(2,1)S(1)} %fusion.refs_0_, bf16[2,128,1024]{2,1,0:T(8,128)(2,1)S(1)} %collective-permute-done.refs_1_, bf16[2,128,1024]{2,1,0:T(8,128)(2,1)S(1)} %collective-permute-done.5.refs_2_, ...), custom_call_target="tpu_custom_call" | custom-call | flops 1610612736 | bytes 2097152 | tf_op jit(solution)/shard_map/pallas_call | solution.py:193
  52.6 2.1 %shard_map.49 = (f32[2,128,1024]{2,1,0:T(8,128)S(1)}, f32[2,128,1024]{2,1,0:T(8,128)S(1)}) custom-call(bf16[2,128,1024]{2,1,0:T(8,128)(2,1)S(1)} %fusion.refs_0_, bf16[2,128,1024]{2,1,0:T(8,128)(2,1)S(1)} %collective-permute-done.refs_1_, bf16[2,128,1024]{2,1,0:T(8,128)(2,1)S(1)} %collective-permute-done.5.refs_2_, ...), custom_call_target="tpu_custom_call", output_to_operand_aliasing={{0}: (6, {}), {1}: (7, {})} | custom-call | flops 1610612736 | bytes 2097152 | tf_op jit(solution)/shard_map/pallas_call | solution.py:193
  54.7 0.0 collective-permute-done.12.refs_4_
  54.7 3.0 %shard_map.50 = (f32[2,128,1024]{2,1,0:T(8,128)S(1)}, f32[2,128,1024]{2,1,0:T(8,128)S(1)}) custom-call(bf16[2,128,1024]{2,1,0:T(8,128)(2,1)S(1)} %fusion.refs_0_, bf16[2,128,1024]{2,1,0:T(8,128)(2,1)S(1)} %collective-permute-done.refs_1_, bf16[2,128,1024]{2,1,0:T(8,128)(2,1)S(1)} %collective-permute-done.5.refs_2_, ...), custom_call_target="tpu_custom_call", output_to_operand_aliasing={{0}: (6, {}), {1}: (7, {})} | custom-call | flops 2415919104 | bytes 2097152 | tf_op jit(solution)/shard_map/pallas_call | solution.py:193
  57.7 0.0 copy-start
  57.8 0.0 collective-permute-done.11.refs_4_.refs_6_
  57.8 1.2 %shard_map.51 = (f32[2,128,1024]{2,1,0:T(8,128)S(1)}, bf16[2,128,1024]{2,1,0:T(8,128)(2,1)S(1)}) custom-call(bf16[2,128,1024]{2,1,0:T(8,128)(2,1)S(1)} %fusion.refs_0_, bf16[2,128,1024]{2,1,0:T(8,128)(2,1)S(1)} %collective-permute-done.refs_1_, bf16[2,128,1024]{2,1,0:T(8,128)(2,1)S(1)} %collective-permute-done.5.refs_2_, ...), custom_call_target="tpu_custom_call", output_to_operand_aliasing={{0}: (5, {})} | custom-call | flops 805306368 | bytes 2097152 | tf_op jit(solution)/shard_map/pallas_call | solution.py:193
  59.0 0.1 collective-permute-start.13
  59.1 1.9 %collective-permute-done.13.got_ref = bf16[2,128,1024]{2,1,0:T(8,128)(2,1)S(1)} collective-permute-done((bf16[2,128,1024]{2,1,0:T(8,128)(2,1)S(1)}, bf16[2,128,1024]{2,1,0:T(8,128)(2,1)S(1)}, u32[]{:S(2)}, u32[]{:S(2)}) %collective-permute-start.13) | collective-permute-done | bytes 524320 | tf_op jit(solution)/shard_map/ppermute | solution.py:31
  61.0 0.0 copy-done
  61.0 0.3 shard_map.52
  61.3 21.4 %all_to_all.5.part_ref = bf16[16,2,64,128]{3,2,1,0:T(8,128)(2,1)S(1)} all-to-all(bf16[16,2,64,128]{3,2,1,0:T(8,128)(2,1)S(1)} %shard_map.52), channel_id=1, replica_groups={{0,2,4,6,8,10,12,14,16,18,20,22,24,26,28,30},{1,3,5,7,9,11,13,15,17,19,..., dimensions={0} | all-to-all | bytes 1048576 | tf_op jit(solution)/shard_map/all_to_all | solution.py:305
  82.7 0.8 shard_map.53
  83.5 2.0 %collective-permute-start.14 = (f32[2,32,1024]{2,1,0:T(8,128)S(1)}, f32[2,32,1024]{2,1,0:T(8,128)S(1)}, u32[]{:S(2)}, u32[]{:S(2)}) collective-permute-start(f32[2,32,1024]{2,1,0:T(8,128)S(1)} %get-tuple-element.44), channel_id=1, source_target_pairs={{0,1},{1,0},{2,3},{3,2},{4,5},{5,4},{6,7},{7,6},{8,9},{9,8},{10,11... | collective-permute-start | bytes 786440 | tf_op jit(solution)/shard_map/ppermute | solution.py:31
  85.5 1.2 %collective-permute-done.14.got_ref = f32[2,32,1024]{2,1,0:T(8,128)S(1)} collective-permute-done((f32[2,32,1024]{2,1,0:T(8,128)S(1)}, f32[2,32,1024]{2,1,0:T(8,128)S(1)}, u32[]{:S(2)}, u32[]{:S(2)}) %collective-permute-start.14) | collective-permute-done | bytes 262176 | tf_op jit(solution)/shard_map/ppermute | solution.py:31
  86.7 0.8 shard_map.54
  (13 shorter events, 0.1 us)
Async XLA Ops:
  1.9 11.4 %copy-start.2 = (bf16[72,1024]{1,0:T(8,128)(2,1)S(1)}, bf16[72,1024]{1,0:T(8,128)(2,1)}, u32[]{:S(2)}) copy-start(bf16[72,1024]{1,0:T(8,128)(2,1)} %get-tuple-element.26) | copy-start | bytes 442372
  1.9 11.5 %collective-permute-start.1 = (bf16[72,1024]{1,0:T(8,128)(2,1)}, bf16[72,1024]{1,0:T(8,128)(2,1)S(1)}, u32[]{:S(2)}, u32[]{:S(2)}) collective-permute-start(bf16[72,1024]{1,0:T(8,128)(2,1)} %get-tuple-element.26), channel_id=1, source_target_pairs={{0,8},{1,9},{2,10},{3,11},{4,12},{5,13},{6,14},{7,15},{8,16},{9,17... | collective-permute-start | bytes 442376 | tf_op jit(solution)/shard_map/ppermute | solution.py:31
  4.5 9.0 %collective-permute-start.2 = (bf16[72,1024]{1,0:T(8,128)(2,1)}, bf16[72,1024]{1,0:T(8,128)(2,1)S(1)}, u32[]{:S(2)}, u32[]{:S(2)}) collective-permute-start(bf16[72,1024]{1,0:T(8,128)(2,1)} %get-tuple-element.26), channel_id=1, source_target_pairs={{0,152},{1,153},{2,154},{3,155},{4,156},{5,157},{6,158},{7,159},{8... | collective-permute-start | bytes 442376 | tf_op jit(solution)/shard_map/ppermute | solution.py:31
  8.5 7.2 %collective-permute-start.3 = (bf16[72,1024]{1,0:T(8,128)(2,1)}, bf16[72,1024]{1,0:T(8,128)(2,1)S(1)}, u32[]{:S(2)}, u32[]{:S(2)}) collective-permute-start(bf16[72,1024]{1,0:T(8,128)(2,1)} %get-tuple-element.26), channel_id=1, source_target_pairs={{0,16},{1,145},{2,18},{3,147},{4,20},{5,149},{6,22},{7,151},{8,24}... | collective-permute-start | bytes 442376 | tf_op jit(solution)/shard_map/ppermute | solution.py:31
  10.3 24.3 %copy-start.1 = (bf16[128,1024]{1,0:T(8,128)(2,1)S(1)}, bf16[128,1024]{1,0:T(8,128)(2,1)}, u32[]{:S(2)}) copy-start(bf16[128,1024]{1,0:T(8,128)(2,1)} %get-tuple-element.25) | copy-start | bytes 786436
  15.8 15.8 %collective-permute-start.4 = (bf16[2,128,1024]{2,1,0:T(8,128)(2,1)S(1)}, bf16[2,128,1024]{2,1,0:T(8,128)(2,1)S(1)}, u32[]{:S(2)}, u32[]{:S(2)}) collective-permute-start(bf16[2,128,1024]{2,1,0:T(8,128)(2,1)S(1)} %fusion.1), channel_id=1, source_target_pairs={{0,16},{1,145},{2,18},{3,147},{4,20},{5,149},{6,22},{7,151},{8,24}... | collective-permute-start | bytes 1572872 | tf_op jit(solution)/shard_map/ppermute | solution.py:31
  19.7 15.0 %collective-permute-start.7 = (bf16[264,1024]{1,0:T(8,128)(2,1)S(1)}, bf16[264,1024]{1,0:T(8,128)(2,1)S(1)}, u32[]{:S(2)}, u32[]{:S(2)}) collective-permute-start(bf16[264,1024]{1,0:T(8,128)(2,1)S(1)} %concatenate.6.refs_4_.refs_0_), channel_id=1, source_target_pairs={{0,2},{1,3},{2,4},{3,5},{4,6},{5,7},{6,0},{7,1},{8,10},{9,11},{10,... | collective-permute-start | bytes 1622024 | tf_op jit(solution)/shard_map/ppermute | solution.py:31
  20.9 13.8 %collective-permute-start.8 = (bf16[264,1024]{1,0:T(8,128)(2,1)S(1)}, bf16[264,1024]{1,0:T(8,128)(2,1)S(1)}, u32[]{:S(2)}, u32[]{:S(2)}) collective-permute-start(bf16[264,1024]{1,0:T(8,128)(2,1)S(1)} %concatenate.6.refs_4_.refs_0_), channel_id=1, source_target_pairs={{0,6},{1,7},{2,0},{3,1},{4,2},{5,3},{6,4},{7,5},{8,14},{9,15},{10,... | collective-permute-start | bytes 1622024 | tf_op jit(solution)/shard_map/ppermute | solution.py:31
  22.4 12.2 %collective-permute-start.9 = (bf16[200,1024]{1,0:T(8,128)(2,1)S(1)}, bf16[200,1024]{1,0:T(8,128)(2,1)S(1)}, u32[]{:S(2)}, u32[]{:S(2)}) collective-permute-start(bf16[200,1024]{1,0:T(8,128)(2,1)S(1)} %slice.40), channel_id=1, source_target_pairs={{0,32},{1,97},{2,34},{3,99},{4,36},{5,101},{6,38},{7,103},{8,40},{... | collective-permute-start | bytes 1228808 | tf_op jit(solution)/shard_map/ppermute | solution.py:31
  31.6 14.5 %collective-permute-start.5 = (bf16[2,128,1024]{2,1,0:T(8,128)(2,1)S(1)}, bf16[2,128,1024]{2,1,0:T(8,128)(2,1)S(1)}, u32[]{:S(2)}, u32[]{:S(2)}) collective-permute-start(bf16[2,128,1024]{2,1,0:T(8,128)(2,1)S(1)} %collective-permute-done.4), channel_id=1, source_target_pairs={{0,16},{1,145},{2,18},{3,147},{4,20},{5,149},{6,22},{7,151},{8,24}... | collective-permute-start | bytes 1572872 | tf_op jit(solution)/shard_map/ppermute | solution.py:31
  34.8 19.9 %collective-permute-start.12 = (bf16[528,1024]{1,0:T(8,128)(2,1)S(1)}, bf16[528,1024]{1,0:T(8,128)(2,1)S(1)}, u32[]{:S(2)}, u32[]{:S(2)}) collective-permute-start(bf16[528,1024]{1,0:T(8,128)(2,1)S(1)} %get-tuple-element.32), channel_id=1, source_target_pairs={{0,32},{1,97},{2,34},{3,99},{4,36},{5,101},{6,38},{7,103},{8,40},{... | collective-permute-start | bytes 3244040 | tf_op jit(solution)/shard_map/ppermute | solution.py:31
  37.6 10.2 %collective-permute-start.10 = (bf16[264,1024]{1,0:T(8,128)(2,1)S(1)}, bf16[264,1024]{1,0:T(8,128)(2,1)S(1)}, u32[]{:S(2)}, u32[]{:S(2)}) collective-permute-start(bf16[264,1024]{1,0:T(8,128)(2,1)S(1)} %get-tuple-element.31), channel_id=1, source_target_pairs={{0,2},{1,7},{2,4},{3,1},{4,6},{5,3},{6,0},{7,5},{8,10},{9,15},{10,... | collective-permute-start | bytes 1622024 | tf_op jit(solution)/shard_map/ppermute | solution.py:31
  43.8 6.8 %collective-permute-start = (bf16[2,128,1024]{2,1,0:T(8,128)(2,1)S(1)}, bf16[2,128,1024]{2,1,0:T(8,128)(2,1)S(1)}, u32[]{:S(2)}, u32[]{:S(2)}) collective-permute-start(bf16[2,128,1024]{2,1,0:T(8,128)(2,1)S(1)} %fusion.refs_0_), channel_id=1, source_target_pairs={{0,1},{1,0},{2,3},{3,2},{4,5},{5,4},{6,7},{7,6},{8,9},{9,8},{10,11... | collective-permute-start | bytes 1572872 | tf_op jit(solution)/shard_map/ppermute | solution.py:31
  46.1 4.5 %collective-permute-start.6 = (bf16[2,128,1024]{2,1,0:T(8,128)(2,1)S(1)}, bf16[2,128,1024]{2,1,0:T(8,128)(2,1)S(1)}, u32[]{:S(2)}, u32[]{:S(2)}) collective-permute-start(bf16[2,128,1024]{2,1,0:T(8,128)(2,1)S(1)} %collective-permute-done.5.refs_2_), channel_id=1, source_target_pairs={{0,1},{1,0},{2,3},{3,2},{4,5},{5,4},{6,7},{7,6},{8,9},{9,8},{10,11... | collective-permute-start | bytes 1572872 | tf_op jit(solution)/shard_map/ppermute | solution.py:31
  47.9 9.9 %collective-permute-start.11 = (bf16[264,1024]{1,0:T(8,128)(2,1)S(1)}, bf16[264,1024]{1,0:T(8,128)(2,1)S(1)}, u32[]{:S(2)}, u32[]{:S(2)}) collective-permute-start(bf16[264,1024]{1,0:T(8,128)(2,1)S(1)} %collective-permute-done.10.refs_5_), channel_id=1, source_target_pairs={{0,32},{1,97},{2,34},{3,99},{4,36},{5,101},{6,38},{7,103},{8,40},{... | collective-permute-start | bytes 1622024 | tf_op jit(solution)/shard_map/ppermute | solution.py:31
  57.7 3.2 %copy-start = (f32[1,128]{1,0:T(1,128)S(1)}, f32[1,128]{1,0:T(1,128)}, u32[]{:S(2)}) copy-start(f32[1,128]{1,0:T(1,128)} %get-tuple-element.42.coulomb_ref) | copy-start | bytes 1540
  59.0 2.0 %collective-permute-start.13 = (bf16[2,128,1024]{2,1,0:T(8,128)(2,1)S(1)}, bf16[2,128,1024]{2,1,0:T(8,128)(2,1)S(1)}, u32[]{:S(2)}, u32[]{:S(2)}) collective-permute-start(bf16[2,128,1024]{2,1,0:T(8,128)(2,1)S(1)} %get-tuple-element.41), channel_id=1, source_target_pairs={{0,1},{1,0},{2,3},{3,2},{4,5},{5,4},{6,7},{7,6},{8,9},{9,8},{10,11... | collective-permute-start | bytes 1572872 | tf_op jit(solution)/shard_map/ppermute | solution.py:31
  83.5 3.2 %collective-permute-start.14 = (f32[2,32,1024]{2,1,0:T(8,128)S(1)}, f32[2,32,1024]{2,1,0:T(8,128)S(1)}, u32[]{:S(2)}, u32[]{:S(2)}) collective-permute-start(f32[2,32,1024]{2,1,0:T(8,128)S(1)} %get-tuple-element.44), channel_id=1, source_target_pairs={{0,1},{1,0},{2,3},{3,2},{4,5},{5,4},{6,7},{7,6},{8,9},{9,8},{10,11... | collective-permute-start | bytes 786440 | tf_op jit(solution)/shard_map/ppermute | solution.py:31

commit v6 on v5

--- a/solution.py
+++ b/solution.py
@@ -9,6 +9,7 @@
 
 BLOCK = 128
 HALF = 64
+COLUMN = 512
 F32, BF16 = jnp.float32, jnp.bfloat16
 BOTH = ("tm", "aux")
 NT = (((1,), (1,)), ((), ()))
@@ -59,7 +60,7 @@
     return pltpu.CompilerParams(vmem_limit_bytes=mib << 20)
 
 
-def prologue_kernel(factors_in, pattern_in, coulomb_in, masked_ref, whole_ref, own_ref, factors, pattern, coulomb, sems):
+def prologue_kernel(factors_in, pattern_in, coulomb_in, block_ref, whole_ref, own_ref, factors, pattern, coulomb, sems):
     copies = [
         pltpu.make_async_copy(factors_in, factors, sems.at[0]),
         pltpu.make_async_copy(pattern_in, pattern, sems.at[1]),
@@ -70,7 +71,7 @@
     for copy in copies:
         copy.wait()
     parity = lax.axis_index("tm") & 1
-    orb = factors.shape[1]
+    rows, orb = factors.shape
     for block in range(orb // BLOCK):
         lanes = pl.ds(block * BLOCK, BLOCK)
         keep = pattern[:, block : block + 1].astype(F32)
@@ -78,23 +79,22 @@
             at = parity if half == 0 else 1 - parity
             part = factors[pl.ds(pl.multiple_of(at * HALF, HALF), HALF), lanes]
             part = (part.astype(F32) * keep).astype(BF16)
-            masked_ref[pl.ds(half * HALF, HALF), lanes] = part
+            block_ref[pl.ds(half * HALF, HALF), lanes] = part
             if half == 0:
                 whole_ref[pl.ds(0, HALF), lanes] = part
     c = coulomb[...]
-    turned = pltpu.roll(c, HALF, 1)
-    own = jnp.where(parity == 0, c, turned)
+    own = jnp.where(parity == 0, c, pltpu.roll(c, HALF, 1))
     own_ref[...] = own
     lane = lax.broadcasted_iota(jnp.int32, own.shape, 1)
     twice = jnp.where(lane < HALF, own, pltpu.roll(own, HALF, 1))
-    high = twice.astype(BF16)
-    rest = twice - high.astype(F32)
-    middle = rest.astype(BF16)
-    low = (rest - middle.astype(F32)).astype(BF16)
-    zero = jnp.zeros((1, orb - 3 * BLOCK), BF16)
-    row = jnp.concatenate([high, middle, low, zero], axis=1)
-    rows = jnp.broadcast_to(row.astype(F32), (8, orb)).astype(BF16)
-    whole_ref[pl.ds(HALF, 8), :] = rows
+    for ref, row, value in ((block_ref, rows, own), (whole_ref, HALF, twice)):
+        high = value.astype(BF16)
+        rest = value - high.astype(F32)
+        middle = rest.astype(BF16)
+        low = (rest - middle.astype(F32)).astype(BF16)
+        zero = jnp.zeros((1, orb - 3 * BLOCK), BF16)
+        line = jnp.concatenate([high, middle, low, zero], axis=1)
+        ref[pl.ds(row, 8), :] = jnp.broadcast_to(line.astype(F32), (8, orb)).astype(BF16)
 
 
 def prologue(factors, pattern, coulomb):
@@ -102,7 +102,7 @@
     return pl.pallas_call(
         prologue_kernel,
         out_shape=[
-            jax.ShapeDtypeStruct((own, orb), BF16),
+            jax.ShapeDtypeStruct((own + 8, orb), BF16),
             jax.ShapeDtypeStruct((HALF + 8, orb), BF16),
             jax.ShapeDtypeStruct((1, own), F32),
         ],
@@ -118,6 +118,21 @@
     )(factors, pattern, coulomb[None, :])
 
 
+def pick_kernel(west_ref, east_ref, onward_ref):
+    core = lax.axis_index("aux") & 1
+    onward_ref[...] = jnp.where(core == 0, west_ref[...], east_ref[...])
+
+
+def pick(west, east):
+    return pl.pallas_call(
+        pick_kernel,
+        out_shape=jax.ShapeDtypeStruct(west.shape, BF16),
+        in_specs=[VMEM] * 2,
+        out_specs=VMEM,
+        compiler_params=params(8),
+    )(west, east)
+
+
 def mix_kernel(west_ref, east_ref, onward_ref, both_ref):
     core = lax.axis_index("aux") & 1
     n = west_ref.shape[0]
@@ -143,33 +158,68 @@
     return parts[0] + (parts[1] + parts[2])
 
 
-def weights_of(ref, row, blocks):
+def column_of(refs, column):
+    o, p, p_start, q, q_start = column
+    third = 3 * HALF
     lane = lax.broadcasted_iota(jnp.int32, (1, BLOCK), 1)
-    pairs = []
-    for k in range(0, blocks, 2):
-        pairs.append(jnp.where(lane < HALF, weight_of(ref, row + k), weight_of(ref, row + k + 1)))
-    return jnp.concatenate(pairs, axis=1) if len(pairs) > 1 else pairs[0]
-
-
-def chunk_kernel(pieces, count, first, *refs):
-    right_own, right_other, left_own, left_other = refs[:4]
-    rows = refs[4 : 4 + count]
-    rest = refs[4 + count :]
+    rows = [refs[o][pl.ds(0, BLOCK), :], refs[p][pl.ds(p_start, third), :], refs[q][pl.ds(q_start, third), :]]
+    p_lines = [weight_of(refs[p], p_start + third + k) for k in range(3)]
+    q_lines = [weight_of(refs[q], q_start + third + k) for k in range(3)]
+    lines = p_lines + q_lines
+    pairs = [jnp.where(lane < HALF, lines[k], lines[k + 1]) for k in range(0, 6, 2)]
+    return jnp.concatenate(rows, axis=0), jnp.concatenate([weight_of(refs[o], BLOCK)] + pairs, axis=1)
+
+
+def square_kernel(columns, *refs):
+    right_own, right_other = refs[:2]
+    rows = refs[2 : len(refs) - len(columns)]
+    outs = refs[len(refs) - len(columns) :]
+    for column, out in zip(columns, outs):
+        for t in range(right_own.shape[0]):
+            right = jnp.concatenate([right_own[t], right_other[t]], axis=0)
+            part, weight = column_of(rows, column)
+            a = lax.dot_general(right, part, NT, preferred_element_type=F32)
+            out[t] = a * a * weight
+
+
+def squares(right, right_other, rows, columns):
+    times, own, orb = right.shape
+    shape = jax.ShapeDtypeStruct((times, 2 * own, COLUMN), F32)
+    flops = len(columns) * times * 2 * (2 * own) * COLUMN * orb
+    return pl.pallas_call(
+        functools.partial(square_kernel, tuple(columns)),
+        out_shape=[shape] * len(columns),
+        in_specs=[VMEM] * (2 + len(rows)),
+        out_specs=[VMEM] * len(columns),
+        compiler_params=params(12),
+        cost_estimate=pl.CostEstimate(flops=flops, bytes_accessed=2 << 20, transcendentals=0),
+    )(right, right_other, *rows)
+
+
+def chunk_kernel(columns, sides, count, first, *refs):
+    left_own, left_other = refs[sides - 2 : sides]
+    rows = refs[sides : sides + count]
+    rest = refs[sides + count :]
+    given = () if sides == 4 else rest[: len(columns)]
+    rest = rest[len(given) :]
     if not first:
         acc_own, acc_other = rest[:2]
         rest = rest[2:]
     out_own, out_other = rest
     own = out_own.shape[1]
     for t in range(out_own.shape[0]):
-        right = jnp.concatenate([right_own[t], right_other[t]], axis=0)
         left = jnp.concatenate([left_own[t], left_other[t]], axis=0)
         total = None
-        for piece in pieces:
-            part = jnp.concatenate([rows[at][pl.ds(start, n), :] for at, start, n in piece[0]], axis=0)
-            weight = weights_of(rows[piece[1]], piece[2], part.shape[0] // HALF)
-            a = lax.dot_general(right, part, NT, preferred_element_type=F32)
+        for at, column in enumerate(columns):
+            part, weight = column_of(rows, column)
+            if given:
+                square = given[at][t]
+            else:
+                right = jnp.concatenate([refs[0][t], refs[1][t]], axis=0)
+                a = lax.dot_general(right, part, NT, preferred_element_type=F32)
+                square = a * a * weight
             m = lax.dot_general(left, part, NT, preferred_element_type=F32)
-            k = (a * weight * (a * m)).astype(BF16)
+            k = (square * m).astype(BF16)
             d = lax.dot_general(k, part, NN, preferred_element_type=F32)
             total = d if total is None else total + d
         mine, theirs = total[:own], total[own:]
@@ -179,26 +229,26 @@
         out_other[t] = theirs.astype(out_other.dtype)
 
 
-def chunk(sides, rows, pieces, acc=None, last=False):
+def chunk(sides, rows, columns, given=(), acc=(), last=False):
     times, own, orb = sides[0].shape
     shape = jax.ShapeDtypeStruct((times, own, orb), F32)
-    extra = () if acc is None else tuple(acc)
     theirs = jax.ShapeDtypeStruct((times, own, orb), BF16 if last else F32)
+    at = len(sides) + len(rows) + len(given)
     aliases = {}
-    if acc is not None:
-        aliases[4 + len(rows)] = 0
+    if acc:
+        aliases[at] = 0
         if not last:
-            aliases[5 + len(rows)] = 1
-    flops = len(pieces) * 4 * HALF * times * 3 * 2 * (2 * own) * orb
-    return pl.pallas_call(
-        functools.partial(chunk_kernel, tuple(pieces), len(rows), acc is None),
+            aliases[at + 1] = 1
+    flops = len(columns) * times * 2 * 2 * (2 * own) * COLUMN * orb
+    return pl.pallas_call(
+        functools.partial(chunk_kernel, tuple(columns), len(sides), len(rows), not acc),
         out_shape=(shape, theirs),
-        in_specs=[VMEM] * (4 + len(rows) + len(extra)),
+        in_specs=[VMEM] * (at + len(acc)),
         out_specs=(VMEM, VMEM),
         input_output_aliases=aliases,
         compiler_params=params(16),
         cost_estimate=pl.CostEstimate(flops=flops, bytes_accessed=2 << 20, transcendentals=0),
-    )(*sides, *rows, *extra)
+    )(*sides, *rows, *given, *acc)
 
 
 def finish_kernel(own_ref, got_ref, coulomb_ref, out_ref):
@@ -211,23 +261,23 @@
 
 
 def sigma_kernel(part_ref, *refs):
-    here, here_q, west, east, sides_q, far, far_q = refs[:7]
-    keep_ref, send_ref, lhs, total_ref = refs[7:]
-    skip = west.shape[0]
-    columns = [((here, 0), (here_q, 0)), ((west, 0), (sides_q, 0)), ((east, 0), (sides_q, skip)), ((far, 0), (far_q, 0))]
+    blocks, p_parts, q_parts = refs[:4], refs[4:8], (refs[8], refs[9], refs[9], refs[10])
+    keep_ref, send_ref, lhs, total_ref = refs[11:]
     chips, times, i_rows, width = part_ref.shape
     me = lax.axis_index("aux")
     core, x, z = me & 1, (me >> 1) & 3, me >> 3
     total = None
     for column, dx in enumerate((0, 3, 1, 2)):
-        parts = []
+        q_start = p_parts[2].shape[0] if column == 2 else 0
+        parts = [blocks[column][pl.ds(0, BLOCK), :]]
         for k, dz in enumerate((0, 3, 1, 2)):
             source = ((z + dz) & 3) * 4 + ((x + dx) & 3)
             for t in range(times):
                 at = pl.ds((column * 4 + k) * width, width)
                 lhs[pl.ds(t * i_rows, i_rows), at] = part_ref[source, t]
-            for ref, start in columns[column]:
-                parts.append(ref[pl.ds(start + k * HALF, HALF), :])
+            if k > 0:
+                parts.append(p_parts[column][pl.ds((k - 1) * HALF, HALF), :])
+                parts.append(q_parts[column][pl.ds(q_start + (k - 1) * HALF, HALF), :])
         d = lax.dot_general(
             lhs[:, pl.ds(column * 4 * width, 4 * width)],
             jnp.concatenate(parts, axis=0),
@@ -253,44 +303,46 @@
     times, orb, _ = green.shape
     own = factors.shape[0]
     barrier = lax.optimization_barrier
-    masked, whole, coulomb = prologue(factors, pattern, coulomb)
+    block, whole, coulomb = prologue(factors, pattern, coulomb)
+    masked = block[:own]
 
     beyond = two_along_z(whole)
     below = along_z(whole, 1)
     above = along_z(whole, -1)
     left = jnp.einsum("qo,tok->tqk", masked, green, preferred_element_type=F32).astype(BF16)
+    left = two_along_z(left)
+    west_o = along_x(block, 1)
+    east_o = along_x(block, -1)
+
+    near = [below, above, beyond]
+    lines = [part[HALF : HALF + 1] for part in near] + [jnp.zeros((5, orb), BF16)]
+    here_p = jnp.concatenate([part[:HALF] for part in near] + lines, axis=0)
+    here_p, west_o, east_o = barrier((here_p, west_o, east_o))
+    west_p = along_x(here_p, 1)
+    east_p = along_x(here_p, -1)
+    here_q = other_parity(here_p)
+    far_o = split_x(pick(west_o, east_o))
+    left = two_along_z(left)
     right = jnp.einsum("qo,tko->tqk", masked, green, preferred_element_type=F32).astype(BF16)
     right_other = other_core(right)
 
-    blocks = [whole, below, above, beyond]
-    weights = [block[HALF : HALF + 1] for block in blocks] + [jnp.zeros((4, orb), BF16)]
-    here = jnp.concatenate([block[:HALF] for block in blocks] + weights, axis=0)
-    here, left = barrier((here, left))
-
-    n = 4 * HALF
-    left = two_along_z(left)
-    west = along_x(here, 1)
-    east = along_x(here, -1)
-    rest = other_parity(here[HALF:])
-    here_q = jnp.concatenate([masked[HALF:], rest], axis=0)
-
-    west, east, here_q = barrier((west, east, here_q))
-    onward, both = mix(west, east)
-    far = split_x(onward)
+    west_p, east_p, here_q, far_o, right_other = barrier((west_p, east_p, here_q, far_o, right_other))
+    onward, both = mix(west_p, east_p)
+    far_p = split_x(onward)
     sides_q = other_parity(both)
-    left = two_along_z(left)
-    left, _ = barrier((left, far[:8, :BLOCK]))
-    far_q = other_parity(far)
+    (here_z,) = squares(right, right_other, (block, here_p, here_q), [(0, 1, 0, 2, 0)])
+    far_q = other_parity(far_p)
     left_other = other_core(left)
 
-    def piece(at, start=0):
-        return (((at, start, n),), at, start + n)
-
+    skip = west_p.shape[0]
+    pair = (west_o, west_p, east_o, east_p, sides_q)
+    columns = [(0, 1, 0, 4, 0), (2, 3, 0, 4, skip)]
+    pair_z = squares(right, right_other, pair, columns)
+    lefts = (left, left_other)
+    acc = chunk(lefts, pair, columns, given=pair_z)
+    acc = chunk(lefts, (block, here_p, here_q), [(0, 1, 0, 2, 0)], given=(here_z,), acc=acc)
     sides = (right, right_other, left, left_other)
-    acc = chunk(sides, (here, here_q), [piece(0), piece(1)])
-    acc = chunk(sides, (west, east), [piece(0), piece(1)], acc)
-    acc = chunk(sides, (sides_q, far), [piece(0), piece(0, n + 8), piece(1)], acc)
-    keep, theirs = chunk(sides, (far_q,), [piece(0)], acc, last=True)
+    keep, theirs = chunk(sides, (far_o, far_p, far_q), [(0, 1, 0, 2, 0)], acc=acc, last=True)
 
     got = other_core(theirs)
     chips, i_rows = 16, orb // 16
@@ -308,14 +360,14 @@
     keep, theirs = pl.pallas_call(
         sigma_kernel,
         out_shape=(shape, shape),
-        in_specs=[VMEM] * 8,
+        in_specs=[VMEM] * 12,
         out_specs=(VMEM, VMEM),
         scratch_shapes=[
             pltpu.VMEM((times * i_rows, chips * own), BF16),
             pltpu.VMEM((times * i_rows, orb), F32),
         ],
         compiler_params=params(12),
-    )(part, here, here_q, west, east, sides_q, far, far_q)
+    )(part, block, west_o, east_o, far_o, here_p, west_p, east_p, far_p, here_q, sides_q, far_q)
     got = other_core(theirs)
     return pl.pallas_call(
         add_kernel,

time: 87.6 us -> 100 us (1.14)
  waiting for transfers between devices: 13.7 us -> 27.2 us
  starting transfers between devices: 32.9 us -> 34.7 us
  matrix products: 6.71 us -> 5.33 us
  blocking collectives: 21.4 us -> 20.3 us
    ppermute x15 -> x18, waiting for transfers between devices: 13.7 us -> 27.2 us  [send(): return lax.ppermute(value, BOTH, sorted(pairs))]
    ppermute x15 -> x18, starting transfers between devices: 32.9 us -> 34.7 us  [send(): return lax.ppermute(value, BOTH, sorted(pairs))]
    dot_general x1, matrix products: 3.03 us -> 1.55 us  [local(): jnp.einsum('qo,tok->tqk', masked, green, preferred_element_type=F32)]
    all_to_all x1, blocking collectives: 21.4 us -> 20.3 us  [local(): lax.all_to_all(part, 'aux', 0, 0, axis_index_groups=groups, tiled=True)]
    pallas_call x5 -> x7, Pallas kernels: 10.2 us -> 10.1 us  [the longest x3 6.15 us: chunk(): pl.pallas_call(functools.partial(chunk_kernel, tuple(columns), len(sides)...]
  transfers between devices with their start and end apart: 15 -> 18, of which waited for: 5 -> 7; matrix products, arithmetic and copies ran while one was open for 8% -> 5% of each run, Pallas kernels for 8% -> 6%
where the time goes in v6:
time: 100 us; the launch traced here: 99.8 us
  starting transfers between devices  34.7 us (35%)
  waiting for transfers between devices  27.2 us (27%)
  blocking collectives  20.3 us (20%)
  Pallas kernels  12 us (12%)
  matrix products  5.33 us (5%)
    ppermute x18, starting transfers between devices, send(): return lax.ppermute(value, BOTH, sorted(pairs))  34.7 us
    ppermute x18, waiting for transfers between devices, send(): return lax.ppermute(value, BOTH, sorted(pairs))  27.2 us
    all_to_all x1, blocking collectives, local(): lax.all_to_all(part, 'aux', 0, 0, axis_index_groups=groups, tiled=True)  20.3 us
    pallas_call x3, Pallas kernels, chunk(): pl.pallas_call(functools.partial(chunk_kernel, tuple(columns), len(sides)...  6.15 us
    dot_general x1, matrix products, local(): jnp.einsum('qo,tko->tqk', masked, green, preferred_element_type=F32)  3.78 us
    pallas_call x2, Pallas kernels, squares(): pl.pallas_call(functools.partial(square_kernel, tuple(columns)), out_shap...  2.02 us
  transfers between devices with their start and end apart: 18, of which 7 were waited for; matrix products, arithmetic and copies ran while one was open for 5% of the time, Pallas kernels for 6%

profile of v6, /device:TPU:1, one launch (start us, length us, event | category | flops | bytes accessed | tf_op | source)
XLA Modules:
  0.0 99.8 jit_solution(15763850298646623642)
XLA Ops:
  0.0 1.9 %shard_map.46 = (bf16[136,1024]{1,0:T(8,128)(2,1)}, bf16[72,1024]{1,0:T(8,128)(2,1)}, f32[1,128]{1,0:T(1,128)}) custom-call(bf16[128,1024]{1,0:T(8,128)(2,1)} %factors_in.1, s32[1,8]{1,0:T(1,128)} %pattern_in.1, f32[1,128]{1,0:T(1,128)} %bitcast.12), custom_call_target="tpu_custom_call" | custom-call | tf_op jit(solution)/shard_map/pallas_call | solution.py:102
  1.9 0.0 copy-start.2
  1.9 2.5 %collective-permute-start = (bf16[72,1024]{1,0:T(8,128)(2,1)}, bf16[72,1024]{1,0:T(8,128)(2,1)S(1)}, u32[]{:S(2)}, u32[]{:S(2)}) collective-permute-start(bf16[72,1024]{1,0:T(8,128)(2,1)} %get-tuple-element.29), channel_id=1, source_target_pairs={{0,8},{1,9},{2,10},{3,11},{4,12},{5,13},{6,14},{7,15},{8,16},{9,17... | collective-permute-start | bytes 442376 | tf_op jit(solution)/shard_map/ppermute | solution.py:32
  4.5 4.0 %collective-permute-start.1 = (bf16[72,1024]{1,0:T(8,128)(2,1)}, bf16[72,1024]{1,0:T(8,128)(2,1)S(1)}, u32[]{:S(2)}, u32[]{:S(2)}) collective-permute-start(bf16[72,1024]{1,0:T(8,128)(2,1)} %get-tuple-element.29), channel_id=1, source_target_pairs={{0,152},{1,153},{2,154},{3,155},{4,156},{5,157},{6,158},{7,159},{8... | collective-permute-start | bytes 442376 | tf_op jit(solution)/shard_map/ppermute | solution.py:32
  8.5 1.2 %collective-permute-start.3 = (bf16[136,1024]{1,0:T(8,128)(2,1)}, bf16[136,1024]{1,0:T(8,128)(2,1)S(1)}, u32[]{:S(2)}, u32[]{:S(2)}) collective-permute-start(bf16[136,1024]{1,0:T(8,128)(2,1)} %get-tuple-element.28.refs_2_.refs_0_), channel_id=1, source_target_pairs={{0,2},{1,3},{2,4},{3,5},{4,6},{5,7},{6,0},{7,1},{8,10},{9,11},{10,... | collective-permute-start | bytes 835592 | tf_op jit(solution)/shard_map/ppermute | solution.py:32
  9.7 1.5 %collective-permute-start.4 = (bf16[136,1024]{1,0:T(8,128)(2,1)}, bf16[136,1024]{1,0:T(8,128)(2,1)S(1)}, u32[]{:S(2)}, u32[]{:S(2)}) collective-permute-start(bf16[136,1024]{1,0:T(8,128)(2,1)} %get-tuple-element.28.refs_2_.refs_0_), channel_id=1, source_target_pairs={{0,6},{1,7},{2,0},{3,1},{4,2},{5,3},{6,4},{7,5},{8,14},{9,15},{10,... | collective-permute-start | bytes 835592 | tf_op jit(solution)/shard_map/ppermute | solution.py:32
  11.2 3.8 %fusion.refs_0_ = bf16[2,128,1024]{2,1,0:T(8,128)(2,1)S(1)} fusion(bf16[2,1024,1024]{2,1,0:T(8,128)(2,1)} %param.4, bf16[136,1024]{1,0:T(8,128)(2,1)} %get-tuple-element.28.refs_2_.refs_0_), kind=kOutput, calls=%fused_computation.2 | convolution fusion | flops 537133056 | bytes 4980736 | tf_op jit(solution)/shard_map/qo,tko->tqk/dot_general | solution.py:326
  15.0 1.6 %collective-permute-start.9 = (bf16[2,128,1024]{2,1,0:T(8,128)(2,1)S(1)}, bf16[2,128,1024]{2,1,0:T(8,128)(2,1)S(1)}, u32[]{:S(2)}, u32[]{:S(2)}) collective-permute-start(bf16[2,128,1024]{2,1,0:T(8,128)(2,1)S(1)} %fusion.refs_0_), channel_id=1, source_target_pairs={{0,1},{1,0},{2,3},{3,2},{4,5},{5,4},{6,7},{7,6},{8,9},{9,8},{10,11... | collective-permute-start | bytes 1572872 | tf_op jit(solution)/shard_map/ppermute | solution.py:32
  16.6 1.6 %fusion.1 = bf16[2,128,1024]{2,1,0:T(8,128)(2,1)} fusion(bf16[2,1024,1024]{2,1,0:T(8,128)(2,1)S(1)} %copy-done.2, bf16[136,1024]{1,0:T(8,128)(2,1)S(1)} %copy-done), kind=kOutput, calls=%fused_computation.3 | convolution fusion | flops 537133056 | bytes 4980736 | tf_op jit(solution)/shard_map/qo,tok->tqk/dot_general | solution.py:312
  18.1 0.0 collective-permute-done
  18.1 2.1 %collective-permute-start.10 = (bf16[2,128,1024]{2,1,0:T(8,128)(2,1)}, bf16[2,128,1024]{2,1,0:T(8,128)(2,1)}, u32[]{:S(2)}, u32[]{:S(2)}) collective-permute-start(bf16[2,128,1024]{2,1,0:T(8,128)(2,1)} %fusion.1), channel_id=1, source_target_pairs={{0,16},{1,145},{2,18},{3,147},{4,20},{5,149},{6,22},{7,151},{8,24}... | collective-permute-start | bytes 1572872 | tf_op jit(solution)/shard_map/ppermute | solution.py:32
  20.2 2.4 %collective-permute-start.2 = (bf16[72,1024]{1,0:T(8,128)(2,1)S(1)}, bf16[72,1024]{1,0:T(8,128)(2,1)S(1)}, u32[]{:S(2)}, u32[]{:S(2)}) collective-permute-start(bf16[72,1024]{1,0:T(8,128)(2,1)S(1)} %copy-done.3), channel_id=1, source_target_pairs={{0,16},{1,145},{2,18},{3,147},{4,20},{5,149},{6,22},{7,151},{8,24}... | collective-permute-start | bytes 442376 | tf_op jit(solution)/shard_map/ppermute | solution.py:32
  22.7 13.0 %collective-permute-done.2 = bf16[72,1024]{1,0:T(8,128)(2,1)S(1)} collective-permute-done((bf16[72,1024]{1,0:T(8,128)(2,1)S(1)}, bf16[72,1024]{1,0:T(8,128)(2,1)S(1)}, u32[]{:S(2)}, u32[]{:S(2)}) %collective-permute-start.2) | collective-permute-done | bytes 147488 | tf_op jit(solution)/shard_map/ppermute | solution.py:32
  35.7 0.1 concatenate.3.refs_3_.refs_4_
  35.8 0.0 collective-permute-done.3.west_ref.refs_2_.refs_1_
  35.8 0.0 collective-permute-done.4.east_ref.refs_4_.refs_2_
  35.8 0.1 collective-permute-start.5
  35.9 2.7 %collective-permute-start.6 = (bf16[200,1024]{1,0:T(8,128)(2,1)S(1)}, bf16[200,1024]{1,0:T(8,128)(2,1)S(1)}, u32[]{:S(2)}, u32[]{:S(2)}) collective-permute-start(bf16[200,1024]{1,0:T(8,128)(2,1)S(1)} %concatenate.3.refs_3_.refs_4_), channel_id=1, source_target_pairs={{0,6},{1,7},{2,0},{3,1},{4,2},{5,3},{6,4},{7,5},{8,14},{9,15},{10,... | collective-permute-start | bytes 1228808 | tf_op jit(solution)/shard_map/ppermute | solution.py:32
  38.5 2.7 %collective-permute-start.7 = (bf16[200,1024]{1,0:T(8,128)(2,1)S(1)}, bf16[200,1024]{1,0:T(8,128)(2,1)S(1)}, u32[]{:S(2)}, u32[]{:S(2)}) collective-permute-start(bf16[200,1024]{1,0:T(8,128)(2,1)S(1)} %concatenate.3.refs_3_.refs_4_), channel_id=1, source_target_pairs={{0,32},{1,97},{2,34},{3,99},{4,36},{5,101},{6,38},{7,103},{8,40},{... | collective-permute-start | bytes 1228808 | tf_op jit(solution)/shard_map/ppermute | solution.py:32
  41.3 0.0 collective-permute-done.9.refs_1_
  41.3 0.1 collective-permute-start.8
  41.5 2.6 %collective-permute-start.11 = (bf16[2,128,1024]{2,1,0:T(8,128)(2,1)}, bf16[2,128,1024]{2,1,0:T(8,128)(2,1)S(1)}, u32[]{:S(2)}, u32[]{:S(2)}) collective-permute-start(bf16[2,128,1024]{2,1,0:T(8,128)(2,1)} %collective-permute-done.10), channel_id=1, source_target_pairs={{0,16},{1,145},{2,18},{3,147},{4,20},{5,149},{6,22},{7,151},{8,24}... | collective-permute-start | bytes 1572872 | tf_op jit(solution)/shard_map/ppermute | solution.py:32
  44.0 6.2 %collective-permute-done.8.refs_4_.refs_3_ = bf16[136,1024]{1,0:T(8,128)(2,1)S(1)} collective-permute-done((bf16[136,1024]{1,0:T(8,128)(2,1)S(1)}, bf16[136,1024]{1,0:T(8,128)(2,1)S(1)}, u32[]{:S(2)}, u32[]{:S(2)}) %collective-permute-start.8) | collective-permute-done | bytes 278560 | tf_op jit(solution)/shard_map/ppermute | solution.py:32
  50.2 0.0 collective-permute-done.5.west_ref.refs_3_.refs_5_
  50.2 0.0 collective-permute-done.6.east_ref.refs_5_.refs_6_
  50.2 0.0 collective-permute-done.7.refs_4_.refs_8_
  50.2 0.1 shard_map.48
  50.3 2.8 %collective-permute-start.15 = (bf16[400,1024]{1,0:T(8,128)(2,1)S(1)}, bf16[400,1024]{1,0:T(8,128)(2,1)S(1)}, u32[]{:S(2)}, u32[]{:S(2)}) collective-permute-start(bf16[400,1024]{1,0:T(8,128)(2,1)S(1)} %get-tuple-element.39), channel_id=1, source_target_pairs={{0,32},{1,97},{2,34},{3,99},{4,36},{5,101},{6,38},{7,103},{8,40},{... | collective-permute-start | bytes 2457608 | tf_op jit(solution)/shard_map/ppermute | solution.py:32
  53.1 3.4 %collective-permute-start.13 = (bf16[200,1024]{1,0:T(8,128)(2,1)S(1)}, bf16[200,1024]{1,0:T(8,128)(2,1)S(1)}, u32[]{:S(2)}, u32[]{:S(2)}) collective-permute-start(bf16[200,1024]{1,0:T(8,128)(2,1)S(1)} %get-tuple-element.37), channel_id=1, source_target_pairs={{0,2},{1,7},{2,4},{3,1},{4,6},{5,3},{6,0},{7,5},{8,10},{9,15},{10,... | collective-permute-start | bytes 1228808 | tf_op jit(solution)/shard_map/ppermute | solution.py:32
  56.6 0.0 collective-permute-done.11.refs_0_.refs_2_
  56.6 1.3 %collective-permute-start.12 = (bf16[2,128,1024]{2,1,0:T(8,128)(2,1)S(1)}, bf16[2,128,1024]{2,1,0:T(8,128)(2,1)S(1)}, u32[]{:S(2)}, u32[]{:S(2)}) collective-permute-start(bf16[2,128,1024]{2,1,0:T(8,128)(2,1)S(1)} %collective-permute-done.11.refs_0_.refs_2_), channel_id=1, source_target_pairs={{0,1},{1,0},{2,3},{3,2},{4,5},{5,4},{6,7},{7,6},{8,9},{9,8},{10,11... | collective-permute-start | bytes 1572872 | tf_op jit(solution)/shard_map/ppermute | solution.py:32
  57.9 3.6 %collective-permute-done.13.refs_5_.refs_7_ = bf16[200,1024]{1,0:T(8,128)(2,1)S(1)} collective-permute-done((bf16[200,1024]{1,0:T(8,128)(2,1)S(1)}, bf16[200,1024]{1,0:T(8,128)(2,1)S(1)}, u32[]{:S(2)}, u32[]{:S(2)}) %collective-permute-start.13) | collective-permute-done | bytes 409632 | tf_op jit(solution)/shard_map/ppermute | solution.py:32
  61.5 0.1 collective-permute-start.14
  61.5 0.7 shard_map.49.refs_5_
  62.3 0.6 collective-permute-done.15.refs_6_.refs_9_
  62.9 1.3 %shard_map.50 = (f32[2,256,512]{2,1,0:T(8,128)S(1)}, f32[2,256,512]{2,1,0:T(8,128)S(1)}) custom-call(bf16[2,128,1024]{2,1,0:T(8,128)(2,1)S(1)} %fusion.refs_0_, bf16[2,128,1024]{2,1,0:T(8,128)(2,1)S(1)} %collective-permute-done.9.refs_1_, bf16[136,1024]{1,0:T(8,128)(2,1)S(1)} %collective-permute-done.3.west_ref.refs_2_.refs_1_, ...), custom_call_target="tpu_custom_call" | custom-call | flops 1073741824 | bytes 2097152 | tf_op jit(solution)/shard_map/pallas_call | solution.py:189
  64.2 2.6 %shard_map.51 = (f32[2,128,1024]{2,1,0:T(8,128)S(1)}, f32[2,128,1024]{2,1,0:T(8,128)S(1)}) custom-call(bf16[2,128,1024]{2,1,0:T(8,128)(2,1)S(1)} %collective-permute-done.11.refs_0_.refs_2_, bf16[2,128,1024]{2,1,0:T(8,128)(2,1)S(1)} %collective-permute-done.12.refs_1_.refs_3_, bf16[136,1024]{1,0:T(8,128)(2,1)S(1)} %collective-permute-done.3.west_ref.refs_2_.refs_1_, ...), custom_call_target="tpu_custom_call" | custom-call | flops 2147483648 | bytes 2097152 | tf_op jit(solution)/shard_map/pallas_call | solution.py:243
  66.8 1.5 %shard_map.52 = (f32[2,128,1024]{2,1,0:T(8,128)S(1)}, f32[2,128,1024]{2,1,0:T(8,128)S(1)}) custom-call(bf16[2,128,1024]{2,1,0:T(8,128)(2,1)S(1)} %collective-permute-done.11.refs_0_.refs_2_, bf16[2,128,1024]{2,1,0:T(8,128)(2,1)S(1)} %collective-permute-done.12.refs_1_.refs_3_, ...), custom_call_target="tpu_custom_call", output_to_operand_aliasing={{0}: (6, {}), {1}: (7, {})} | custom-call | flops 1073741824 | bytes 2097152 | tf_op jit(solution)/shard_map/pallas_call | solution.py:243
  68.3 1.2 %collective-permute-done.14.refs_6_.refs_10_ = bf16[200,1024]{1,0:T(8,128)(2,1)S(1)} collective-permute-done((bf16[200,1024]{1,0:T(8,128)(2,1)S(1)}, bf16[200,1024]{1,0:T(8,128)(2,1)S(1)}, u32[]{:S(2)}, u32[]{:S(2)}) %collective-permute-start.14) | collective-permute-done | bytes 409632 | tf_op jit(solution)/shard_map/ppermute | solution.py:32
  69.5 2.0 %shard_map.53 = (f32[2,128,1024]{2,1,0:T(8,128)S(1)}, bf16[2,128,1024]{2,1,0:T(8,128)(2,1)S(1)}) custom-call(bf16[2,128,1024]{2,1,0:T(8,128)(2,1)S(1)} %fusion.refs_0_, bf16[2,128,1024]{2,1,0:T(8,128)(2,1)S(1)} %collective-permute-done.9.refs_1_, bf16[2,128,1024]{2,1,0:T(8,128)(2,1)S(1)} %collective-permute-done.11.refs_0_.refs_2_, ...), custom_call_target="tpu_custom_call", output_to_operand_aliasing={{0}: (7, {})} | custom-call | flops 1073741824 | bytes 2097152 | tf_op jit(solution)/shard_map/pallas_call | solution.py:243
  71.5 1.5 %collective-permute-start.16 = (bf16[2,128,1024]{2,1,0:T(8,128)(2,1)S(1)}, bf16[2,128,1024]{2,1,0:T(8,128)(2,1)S(1)}, u32[]{:S(2)}, u32[]{:S(2)}) collective-permute-start(bf16[2,128,1024]{2,1,0:T(8,128)(2,1)S(1)} %get-tuple-element.47), channel_id=1, source_target_pairs={{0,1},{1,0},{2,3},{3,2},{4,5},{5,4},{6,7},{7,6},{8,9},{9,8},{10,11... | collective-permute-start | bytes 1572872 | tf_op jit(solution)/shard_map/ppermute | solution.py:32
  73.0 1.5 %collective-permute-done.16.got_ref = bf16[2,128,1024]{2,1,0:T(8,128)(2,1)S(1)} collective-permute-done((bf16[2,128,1024]{2,1,0:T(8,128)(2,1)S(1)}, bf16[2,128,1024]{2,1,0:T(8,128)(2,1)S(1)}, u32[]{:S(2)}, u32[]{:S(2)}) %collective-permute-start.16) | collective-permute-done | bytes 524320 | tf_op jit(solution)/shard_map/ppermute | solution.py:32
  74.5 0.3 shard_map.54
  74.9 20.3 %all_to_all.5.part_ref = bf16[16,2,64,128]{3,2,1,0:T(8,128)(2,1)S(1)} all-to-all(bf16[16,2,64,128]{3,2,1,0:T(8,128)(2,1)S(1)} %shard_map.54), channel_id=1, replica_groups={{0,2,4,6,8,10,12,14,16,18,20,22,24,26,28,30},{1,3,5,7,9,11,13,15,17,19,..., dimensions={0} | all-to-all | bytes 1048576 | tf_op jit(solution)/shard_map/all_to_all | solution.py:357
  95.1 0.8 shard_map.55
  95.9 2.0 %collective-permute-start.17 = (f32[2,32,1024]{2,1,0:T(8,128)S(1)}, f32[2,32,1024]{2,1,0:T(8,128)S(1)}, u32[]{:S(2)}, u32[]{:S(2)}) collective-permute-start(f32[2,32,1024]{2,1,0:T(8,128)S(1)} %get-tuple-element.50), channel_id=1, source_target_pairs={{0,1},{1,0},{2,3},{3,2},{4,5},{5,4},{6,7},{7,6},{8,9},{9,8},{10,11... | collective-permute-start | bytes 786440 | tf_op jit(solution)/shard_map/ppermute | solution.py:32
  97.9 1.2 %collective-permute-done.17.got_ref = f32[2,32,1024]{2,1,0:T(8,128)S(1)} collective-permute-done((f32[2,32,1024]{2,1,0:T(8,128)S(1)}, f32[2,32,1024]{2,1,0:T(8,128)S(1)}, u32[]{:S(2)}, u32[]{:S(2)}) %collective-permute-start.17) | collective-permute-done | bytes 262176 | tf_op jit(solution)/shard_map/ppermute | solution.py:32
  99.1 0.8 shard_map.56
  (18 shorter events, 0.1 us)
Async XLA Ops:
  1.9 14.7 %copy-start = (bf16[136,1024]{1,0:T(8,128)(2,1)S(1)}, bf16[136,1024]{1,0:T(8,128)(2,1)}, u32[]{:S(2)}) copy-start(bf16[136,1024]{1,0:T(8,128)(2,1)} %get-tuple-element.28.refs_2_.refs_0_) | copy-start | bytes 835588
  1.9 14.7 %copy-start.2 = (bf16[2,1024,1024]{2,1,0:T(8,128)(2,1)S(1)}, bf16[2,1024,1024]{2,1,0:T(8,128)(2,1)}, u32[]{:S(2)}) copy-start(bf16[2,1024,1024]{2,1,0:T(8,128)(2,1)} %param.4) | copy-start | bytes 12582916
  1.9 16.2 %collective-permute-start = (bf16[72,1024]{1,0:T(8,128)(2,1)}, bf16[72,1024]{1,0:T(8,128)(2,1)S(1)}, u32[]{:S(2)}, u32[]{:S(2)}) collective-permute-start(bf16[72,1024]{1,0:T(8,128)(2,1)} %get-tuple-element.29), channel_id=1, source_target_pairs={{0,8},{1,9},{2,10},{3,11},{4,12},{5,13},{6,14},{7,15},{8,16},{9,17... | collective-permute-start | bytes 442376 | tf_op jit(solution)/shard_map/ppermute | solution.py:32
  4.5 15.8 %collective-permute-start.1 = (bf16[72,1024]{1,0:T(8,128)(2,1)}, bf16[72,1024]{1,0:T(8,128)(2,1)S(1)}, u32[]{:S(2)}, u32[]{:S(2)}) collective-permute-start(bf16[72,1024]{1,0:T(8,128)(2,1)} %get-tuple-element.29), channel_id=1, source_target_pairs={{0,152},{1,153},{2,154},{3,155},{4,156},{5,157},{6,158},{7,159},{8... | collective-permute-start | bytes 442376 | tf_op jit(solution)/shard_map/ppermute | solution.py:32
  8.5 11.7 %copy-start.3 = (bf16[72,1024]{1,0:T(8,128)(2,1)S(1)}, bf16[72,1024]{1,0:T(8,128)(2,1)}, u32[]{:S(2)}) copy-start(bf16[72,1024]{1,0:T(8,128)(2,1)} %get-tuple-element.29) | copy-start | bytes 442372
  8.5 27.3 %collective-permute-start.3 = (bf16[136,1024]{1,0:T(8,128)(2,1)}, bf16[136,1024]{1,0:T(8,128)(2,1)S(1)}, u32[]{:S(2)}, u32[]{:S(2)}) collective-permute-start(bf16[136,1024]{1,0:T(8,128)(2,1)} %get-tuple-element.28.refs_2_.refs_0_), channel_id=1, source_target_pairs={{0,2},{1,3},{2,4},{3,5},{4,6},{5,7},{6,0},{7,1},{8,10},{9,11},{10,... | collective-permute-start | bytes 835592 | tf_op jit(solution)/shard_map/ppermute | solution.py:32
  9.7 26.1 %collective-permute-start.4 = (bf16[136,1024]{1,0:T(8,128)(2,1)}, bf16[136,1024]{1,0:T(8,128)(2,1)S(1)}, u32[]{:S(2)}, u32[]{:S(2)}) collective-permute-start(bf16[136,1024]{1,0:T(8,128)(2,1)} %get-tuple-element.28.refs_2_.refs_0_), channel_id=1, source_target_pairs={{0,6},{1,7},{2,0},{3,1},{4,2},{5,3},{6,4},{7,5},{8,14},{9,15},{10,... | collective-permute-start | bytes 835592 | tf_op jit(solution)/shard_map/ppermute | solution.py:32
  15.0 26.4 %collective-permute-start.9 = (bf16[2,128,1024]{2,1,0:T(8,128)(2,1)S(1)}, bf16[2,128,1024]{2,1,0:T(8,128)(2,1)S(1)}, u32[]{:S(2)}, u32[]{:S(2)}) collective-permute-start(bf16[2,128,1024]{2,1,0:T(8,128)(2,1)S(1)} %fusion.refs_0_), channel_id=1, source_target_pairs={{0,1},{1,0},{2,3},{3,2},{4,5},{5,4},{6,7},{7,6},{8,9},{9,8},{10,11... | collective-permute-start | bytes 1572872 | tf_op jit(solution)/shard_map/ppermute | solution.py:32
  18.1 23.3 %collective-permute-start.10 = (bf16[2,128,1024]{2,1,0:T(8,128)(2,1)}, bf16[2,128,1024]{2,1,0:T(8,128)(2,1)}, u32[]{:S(2)}, u32[]{:S(2)}) collective-permute-start(bf16[2,128,1024]{2,1,0:T(8,128)(2,1)} %fusion.1), channel_id=1, source_target_pairs={{0,16},{1,145},{2,18},{3,147},{4,20},{5,149},{6,22},{7,151},{8,24}... | collective-permute-start | bytes 1572872 | tf_op jit(solution)/shard_map/ppermute | solution.py:32
  20.2 15.4 %collective-permute-start.2 = (bf16[72,1024]{1,0:T(8,128)(2,1)S(1)}, bf16[72,1024]{1,0:T(8,128)(2,1)S(1)}, u32[]{:S(2)}, u32[]{:S(2)}) collective-permute-start(bf16[72,1024]{1,0:T(8,128)(2,1)S(1)} %copy-done.3), channel_id=1, source_target_pairs={{0,16},{1,145},{2,18},{3,147},{4,20},{5,149},{6,22},{7,151},{8,24}... | collective-permute-start | bytes 442376 | tf_op jit(solution)/shard_map/ppermute | solution.py:32
  35.8 14.4 %collective-permute-start.5 = (bf16[200,1024]{1,0:T(8,128)(2,1)S(1)}, bf16[200,1024]{1,0:T(8,128)(2,1)S(1)}, u32[]{:S(2)}, u32[]{:S(2)}) collective-permute-start(bf16[200,1024]{1,0:T(8,128)(2,1)S(1)} %concatenate.3.refs_3_.refs_4_), channel_id=1, source_target_pairs={{0,2},{1,3},{2,4},{3,5},{4,6},{5,7},{6,0},{7,1},{8,10},{9,11},{10,... | collective-permute-start | bytes 1228808 | tf_op jit(solution)/shard_map/ppermute | solution.py:32
  35.9 14.3 %collective-permute-start.6 = (bf16[200,1024]{1,0:T(8,128)(2,1)S(1)}, bf16[200,1024]{1,0:T(8,128)(2,1)S(1)}, u32[]{:S(2)}, u32[]{:S(2)}) collective-permute-start(bf16[200,1024]{1,0:T(8,128)(2,1)S(1)} %concatenate.3.refs_3_.refs_4_), channel_id=1, source_target_pairs={{0,6},{1,7},{2,0},{3,1},{4,2},{5,3},{6,4},{7,5},{8,14},{9,15},{10,... | collective-permute-start | bytes 1228808 | tf_op jit(solution)/shard_map/ppermute | solution.py:32
  38.5 11.7 %collective-permute-start.7 = (bf16[200,1024]{1,0:T(8,128)(2,1)S(1)}, bf16[200,1024]{1,0:T(8,128)(2,1)S(1)}, u32[]{:S(2)}, u32[]{:S(2)}) collective-permute-start(bf16[200,1024]{1,0:T(8,128)(2,1)S(1)} %concatenate.3.refs_3_.refs_4_), channel_id=1, source_target_pairs={{0,32},{1,97},{2,34},{3,99},{4,36},{5,101},{6,38},{7,103},{8,40},{... | collective-permute-start | bytes 1228808 | tf_op jit(solution)/shard_map/ppermute | solution.py:32
  41.3 8.9 %collective-permute-start.8 = (bf16[136,1024]{1,0:T(8,128)(2,1)S(1)}, bf16[136,1024]{1,0:T(8,128)(2,1)S(1)}, u32[]{:S(2)}, u32[]{:S(2)}) collective-permute-start(bf16[136,1024]{1,0:T(8,128)(2,1)S(1)} %shard_map.47), channel_id=1, source_target_pairs={{0,2},{1,7},{2,4},{3,1},{4,6},{5,3},{6,0},{7,5},{8,10},{9,15},{10,... | collective-permute-start | bytes 835592 | tf_op jit(solution)/shard_map/ppermute | solution.py:32
  41.5 15.1 %collective-permute-start.11 = (bf16[2,128,1024]{2,1,0:T(8,128)(2,1)}, bf16[2,128,1024]{2,1,0:T(8,128)(2,1)S(1)}, u32[]{:S(2)}, u32[]{:S(2)}) collective-permute-start(bf16[2,128,1024]{2,1,0:T(8,128)(2,1)} %collective-permute-done.10), channel_id=1, source_target_pairs={{0,16},{1,145},{2,18},{3,147},{4,20},{5,149},{6,22},{7,151},{8,24}... | collective-permute-start | bytes 1572872 | tf_op jit(solution)/shard_map/ppermute | solution.py:32
  50.3 12.6 %collective-permute-start.15 = (bf16[400,1024]{1,0:T(8,128)(2,1)S(1)}, bf16[400,1024]{1,0:T(8,128)(2,1)S(1)}, u32[]{:S(2)}, u32[]{:S(2)}) collective-permute-start(bf16[400,1024]{1,0:T(8,128)(2,1)S(1)} %get-tuple-element.39), channel_id=1, source_target_pairs={{0,32},{1,97},{2,34},{3,99},{4,36},{5,101},{6,38},{7,103},{8,40},{... | collective-permute-start | bytes 2457608 | tf_op jit(solution)/shard_map/ppermute | solution.py:32
  53.1 8.3 %collective-permute-start.13 = (bf16[200,1024]{1,0:T(8,128)(2,1)S(1)}, bf16[200,1024]{1,0:T(8,128)(2,1)S(1)}, u32[]{:S(2)}, u32[]{:S(2)}) collective-permute-start(bf16[200,1024]{1,0:T(8,128)(2,1)S(1)} %get-tuple-element.37), channel_id=1, source_target_pairs={{0,2},{1,7},{2,4},{3,1},{4,6},{5,3},{6,0},{7,5},{8,10},{9,15},{10,... | collective-permute-start | bytes 1228808 | tf_op jit(solution)/shard_map/ppermute | solution.py:32
  56.6 7.6 %collective-permute-start.12 = (bf16[2,128,1024]{2,1,0:T(8,128)(2,1)S(1)}, bf16[2,128,1024]{2,1,0:T(8,128)(2,1)S(1)}, u32[]{:S(2)}, u32[]{:S(2)}) collective-permute-start(bf16[2,128,1024]{2,1,0:T(8,128)(2,1)S(1)} %collective-permute-done.11.refs_0_.refs_2_), channel_id=1, source_target_pairs={{0,1},{1,0},{2,3},{3,2},{4,5},{5,4},{6,7},{7,6},{8,9},{9,8},{10,11... | collective-permute-start | bytes 1572872 | tf_op jit(solution)/shard_map/ppermute | solution.py:32
  61.5 8.0 %collective-permute-start.14 = (bf16[200,1024]{1,0:T(8,128)(2,1)S(1)}, bf16[200,1024]{1,0:T(8,128)(2,1)S(1)}, u32[]{:S(2)}, u32[]{:S(2)}) collective-permute-start(bf16[200,1024]{1,0:T(8,128)(2,1)S(1)} %collective-permute-done.13.refs_5_.refs_7_), channel_id=1, source_target_pairs={{0,32},{1,97},{2,34},{3,99},{4,36},{5,101},{6,38},{7,103},{8,40},{... | collective-permute-start | bytes 1228808 | tf_op jit(solution)/shard_map/ppermute | solution.py:32
  66.7 7.8 %copy-start.1 = (f32[1,128]{1,0:T(1,128)S(1)}, f32[1,128]{1,0:T(1,128)}, u32[]{:S(2)}) copy-start(f32[1,128]{1,0:T(1,128)} %get-tuple-element.48.coulomb_ref) | copy-start | bytes 1540
  71.5 3.0 %collective-permute-start.16 = (bf16[2,128,1024]{2,1,0:T(8,128)(2,1)S(1)}, bf16[2,128,1024]{2,1,0:T(8,128)(2,1)S(1)}, u32[]{:S(2)}, u32[]{:S(2)}) collective-permute-start(bf16[2,128,1024]{2,1,0:T(8,128)(2,1)S(1)} %get-tuple-element.47), channel_id=1, source_target_pairs={{0,1},{1,0},{2,3},{3,2},{4,5},{5,4},{6,7},{7,6},{8,9},{9,8},{10,11... | collective-permute-start | bytes 1572872 | tf_op jit(solution)/shard_map/ppermute | solution.py:32
  95.9 3.2 %collective-permute-start.17 = (f32[2,32,1024]{2,1,0:T(8,128)S(1)}, f32[2,32,1024]{2,1,0:T(8,128)S(1)}, u32[]{:S(2)}, u32[]{:S(2)}) collective-permute-start(f32[2,32,1024]{2,1,0:T(8,128)S(1)} %get-tuple-element.50), channel_id=1, source_target_pairs={{0,1},{1,0},{2,3},{3,2},{4,5},{5,4},{6,7},{7,6},{8,9},{9,8},{10,11... | collective-permute-start | bytes 786440 | tf_op jit(solution)/shard_map/ppermute | solution.py:32

commit v7 on v6

--- a/solution.py
+++ b/solution.py
@@ -118,39 +118,26 @@
     )(factors, pattern, coulomb[None, :])
 
 
-def pick_kernel(west_ref, east_ref, onward_ref):
+def mix_kernel(west_o, east_o, west_p, east_p, onward_ref, both_ref):
     core = lax.axis_index("aux") & 1
-    onward_ref[...] = jnp.where(core == 0, west_ref[...], east_ref[...])
-
-
-def pick(west, east):
-    return pl.pallas_call(
-        pick_kernel,
-        out_shape=jax.ShapeDtypeStruct(west.shape, BF16),
-        in_specs=[VMEM] * 2,
-        out_specs=VMEM,
-        compiler_params=params(8),
-    )(west, east)
-
-
-def mix_kernel(west_ref, east_ref, onward_ref, both_ref):
-    core = lax.axis_index("aux") & 1
-    n = west_ref.shape[0]
-    west, east = west_ref[...], east_ref[...]
-    onward_ref[...] = jnp.where(core == 0, west, east)
-    both_ref[pl.ds(0, n), :] = west
-    both_ref[pl.ds(n, n), :] = east
-
-
-def mix(west, east):
-    n, orb = west.shape
+    n, m = west_o.shape[0], west_p.shape[0]
+    west, east = west_p[...], east_p[...]
+    onward_ref[pl.ds(0, n), :] = jnp.where(core == 0, west_o[...], east_o[...])
+    onward_ref[pl.ds(n, m), :] = jnp.where(core == 0, west, east)
+    both_ref[pl.ds(0, m), :] = west
+    both_ref[pl.ds(m, m), :] = east
+
+
+def mix(west_o, east_o, west_p, east_p):
+    n, orb = west_p.shape
+    sizes = (west_o.shape[0] + n, 2 * n)
     return pl.pallas_call(
         mix_kernel,
-        out_shape=(jax.ShapeDtypeStruct((n, orb), BF16), jax.ShapeDtypeStruct((2 * n, orb), BF16)),
-        in_specs=[VMEM] * 2,
+        out_shape=[jax.ShapeDtypeStruct((size, orb), BF16) for size in sizes],
+        in_specs=[VMEM] * 4,
         out_specs=[VMEM] * 2,
         compiler_params=params(8),
-    )(west, east)
+    )(west_o, east_o, west_p, east_p)
 
 
 def weight_of(ref, row):
@@ -261,14 +248,16 @@
 
 
 def sigma_kernel(part_ref, *refs):
-    blocks, p_parts, q_parts = refs[:4], refs[4:8], (refs[8], refs[9], refs[9], refs[10])
-    keep_ref, send_ref, lhs, total_ref = refs[11:]
+    blocks, q_parts = refs[:4], (refs[7], refs[8], refs[8], refs[9])
+    p_parts = refs[4:7] + (refs[3],)
+    keep_ref, send_ref, lhs, total_ref = refs[10:]
     chips, times, i_rows, width = part_ref.shape
     me = lax.axis_index("aux")
     core, x, z = me & 1, (me >> 1) & 3, me >> 3
     total = None
     for column, dx in enumerate((0, 3, 1, 2)):
         q_start = p_parts[2].shape[0] if column == 2 else 0
+        p_start = BLOCK + 8 if column == 3 else 0
         parts = [blocks[column][pl.ds(0, BLOCK), :]]
         for k, dz in enumerate((0, 3, 1, 2)):
             source = ((z + dz) & 3) * 4 + ((x + dx) & 3)
@@ -276,7 +265,7 @@
                 at = pl.ds((column * 4 + k) * width, width)
                 lhs[pl.ds(t * i_rows, i_rows), at] = part_ref[source, t]
             if k > 0:
-                parts.append(p_parts[column][pl.ds((k - 1) * HALF, HALF), :])
+                parts.append(p_parts[column][pl.ds(p_start + (k - 1) * HALF, HALF), :])
                 parts.append(q_parts[column][pl.ds(q_start + (k - 1) * HALF, HALF), :])
         d = lax.dot_general(
             lhs[:, pl.ds(column * 4 * width, 4 * width)],
@@ -310,6 +299,7 @@
     below = along_z(whole, 1)
     above = along_z(whole, -1)
     left = jnp.einsum("qo,tok->tqk", masked, green, preferred_element_type=F32).astype(BF16)
+    below, left = barrier((below, left))
     left = two_along_z(left)
     west_o = along_x(block, 1)
     east_o = along_x(block, -1)
@@ -321,17 +311,17 @@
     west_p = along_x(here_p, 1)
     east_p = along_x(here_p, -1)
     here_q = other_parity(here_p)
-    far_o = split_x(pick(west_o, east_o))
     left = two_along_z(left)
+    here_q, masked = barrier((here_q, masked))
     right = jnp.einsum("qo,tko->tqk", masked, green, preferred_element_type=F32).astype(BF16)
     right_other = other_core(right)
 
-    west_p, east_p, here_q, far_o, right_other = barrier((west_p, east_p, here_q, far_o, right_other))
-    onward, both = mix(west_p, east_p)
-    far_p = split_x(onward)
+    west_p, east_p, here_q = barrier((west_p, east_p, here_q))
+    onward, both = mix(west_o, east_o, west_p, east_p)
+    far = split_x(onward)
     sides_q = other_parity(both)
     (here_z,) = squares(right, right_other, (block, here_p, here_q), [(0, 1, 0, 2, 0)])
-    far_q = other_parity(far_p)
+    far_q = other_parity(far[own + 8 :])
     left_other = other_core(left)
 
     skip = west_p.shape[0]
@@ -342,7 +332,7 @@
     acc = chunk(lefts, pair, columns, given=pair_z)
     acc = chunk(lefts, (block, here_p, here_q), [(0, 1, 0, 2, 0)], given=(here_z,), acc=acc)
     sides = (right, right_other, left, left_other)
-    keep, theirs = chunk(sides, (far_o, far_p, far_q), [(0, 1, 0, 2, 0)], acc=acc, last=True)
+    keep, theirs = chunk(sides, (far, far_q), [(0, 0, own + 8, 1, 0)], acc=acc, last=True)
 
     got = other_core(theirs)
     chips, i_rows = 16, orb // 16
@@ -360,14 +350,14 @@
     keep, theirs = pl.pallas_call(
         sigma_kernel,
         out_shape=(shape, shape),
-        in_specs=[VMEM] * 12,
+        in_specs=[VMEM] * 11,
         out_specs=(VMEM, VMEM),
         scratch_shapes=[
             pltpu.VMEM((times * i_rows, chips * own), BF16),
             pltpu.VMEM((times * i_rows, orb), F32),
         ],
         compiler_params=params(12),
-    )(part, block, west_o, east_o, far_o, here_p, west_p, east_p, far_p, here_q, sides_q, far_q)
+    )(part, block, west_o, east_o, far, here_p, west_p, east_p, here_q, sides_q, far_q)
     got = other_core(theirs)
     return pl.pallas_call(
         add_kernel,

time: 100 us -> 86.9 us (0.87)
  waiting for transfers between devices: 27.2 us -> 12.5 us
  matrix products: 5.33 us -> 6.69 us
    ppermute x18 -> x17, waiting for transfers between devices: 27.2 us -> 12.5 us  [send(): return lax.ppermute(value, BOTH, sorted(pairs))]
    dot_general x1, matrix products: 1.55 us -> 2.99 us  [local(): jnp.einsum('qo,tok->tqk', masked, green, preferred_element_type=F32)]
    ppermute x18 -> x17, starting transfers between devices: 34.7 us -> 35.3 us  [send(): return lax.ppermute(value, BOTH, sorted(pairs))]
  transfers between devices with their start and end apart: 18 -> 17, of which waited for: 7 -> 7; matrix products, arithmetic and copies ran while one was open for 5% -> 8% of each run, Pallas kernels for 6% -> 7%
where the time goes in v7:
time: 86.9 us; the launch traced here: 86.7 us
  starting transfers between devices  35.3 us (41%)
  blocking collectives  19.7 us (23%)
  waiting for transfers between devices  12.5 us (14%)
  Pallas kernels  12.2 us (14%)
  matrix products  6.69 us (8%)
    ppermute x17, starting transfers between devices, send(): return lax.ppermute(value, BOTH, sorted(pairs))  35.3 us
    all_to_all x1, blocking collectives, local(): lax.all_to_all(part, 'aux', 0, 0, axis_index_groups=groups, tiled=True)  19.7 us
    ppermute x17, waiting for transfers between devices, send(): return lax.ppermute(value, BOTH, sorted(pairs))  12.5 us
    pallas_call x3, Pallas kernels, chunk(): pl.pallas_call(functools.partial(chunk_kernel, tuple(columns), len(sides)...  6.2 us
    dot_general x1, matrix products, local(): jnp.einsum('qo,tko->tqk', masked, green, preferred_element_type=F32)  3.71 us
    dot_general x1, matrix products, local(): jnp.einsum('qo,tok->tqk', masked, green, preferred_element_type=F32)  2.99 us
    pallas_call x2, Pallas kernels, squares(): pl.pallas_call(functools.partial(square_kernel, tuple(columns)), out_shap...  2.06 us
    pallas_call x1, Pallas kernels, prologue(): pl.pallas_call(prologue_kernel, out_shape=[jax.ShapeDtypeStruct((own + 8,...  1.9 us
  transfers between devices with their start and end apart: 17, of which 7 were waited for; matrix products, arithmetic and copies ran while one was open for 8% of the time, Pallas kernels for 7%

profile of v7, /device:TPU:1, one launch (start us, length us, event | category | flops | bytes accessed | tf_op | source)
XLA Modules:
  0.0 86.7 jit_solution(15048288952214718266)
XLA Ops:
  0.0 1.9 %shard_map.46 = (bf16[136,1024]{1,0:T(8,128)(2,1)}, bf16[72,1024]{1,0:T(8,128)(2,1)}, f32[1,128]{1,0:T(1,128)}) custom-call(bf16[128,1024]{1,0:T(8,128)(2,1)} %factors_in.1, s32[1,8]{1,0:T(1,128)} %pattern_in.1, f32[1,128]{1,0:T(1,128)} %bitcast.13), custom_call_target="tpu_custom_call" | custom-call | tf_op jit(solution)/shard_map/pallas_call | solution.py:102
  1.9 2.5 %collective-permute-start = (bf16[72,1024]{1,0:T(8,128)(2,1)}, bf16[72,1024]{1,0:T(8,128)(2,1)S(1)}, u32[]{:S(2)}, u32[]{:S(2)}) collective-permute-start(bf16[72,1024]{1,0:T(8,128)(2,1)} %get-tuple-element.30), channel_id=1, source_target_pairs={{0,8},{1,9},{2,10},{3,11},{4,12},{5,13},{6,14},{7,15},{8,16},{9,17... | collective-permute-start | bytes 442376 | tf_op jit(solution)/shard_map/ppermute | solution.py:32
  4.5 4.0 %collective-permute-start.1 = (bf16[72,1024]{1,0:T(8,128)(2,1)}, bf16[72,1024]{1,0:T(8,128)(2,1)S(1)}, u32[]{:S(2)}, u32[]{:S(2)}) collective-permute-start(bf16[72,1024]{1,0:T(8,128)(2,1)} %get-tuple-element.30), channel_id=1, source_target_pairs={{0,152},{1,153},{2,154},{3,155},{4,156},{5,157},{6,158},{7,159},{8... | collective-permute-start | bytes 442376 | tf_op jit(solution)/shard_map/ppermute | solution.py:32
  8.5 1.8 %collective-permute-start.2 = (bf16[72,1024]{1,0:T(8,128)(2,1)}, bf16[72,1024]{1,0:T(8,128)(2,1)S(1)}, u32[]{:S(2)}, u32[]{:S(2)}) collective-permute-start(bf16[72,1024]{1,0:T(8,128)(2,1)} %get-tuple-element.30), channel_id=1, source_target_pairs={{0,16},{1,145},{2,18},{3,147},{4,20},{5,149},{6,22},{7,151},{8,24}... | collective-permute-start | bytes 442376 | tf_op jit(solution)/shard_map/ppermute | solution.py:32
  10.3 1.2 %collective-permute-start.3 = (bf16[136,1024]{1,0:T(8,128)(2,1)}, bf16[136,1024]{1,0:T(8,128)(2,1)S(1)}, u32[]{:S(2)}, u32[]{:S(2)}) collective-permute-start(bf16[136,1024]{1,0:T(8,128)(2,1)} %get-tuple-element.31.refs_2_.refs_0_), channel_id=1, source_target_pairs={{0,2},{1,3},{2,4},{3,5},{4,6},{5,7},{6,0},{7,1},{8,10},{9,11},{10,... | collective-permute-start | bytes 835592 | tf_op jit(solution)/shard_map/ppermute | solution.py:32
  11.5 1.5 %collective-permute-start.4 = (bf16[136,1024]{1,0:T(8,128)(2,1)}, bf16[136,1024]{1,0:T(8,128)(2,1)S(1)}, u32[]{:S(2)}, u32[]{:S(2)}) collective-permute-start(bf16[136,1024]{1,0:T(8,128)(2,1)} %get-tuple-element.31.refs_2_.refs_0_), channel_id=1, source_target_pairs={{0,6},{1,7},{2,0},{3,1},{4,2},{5,3},{6,4},{7,5},{8,14},{9,15},{10,... | collective-permute-start | bytes 835592 | tf_op jit(solution)/shard_map/ppermute | solution.py:32
  13.0 3.0 %fusion = bf16[2,128,1024]{2,1,0:T(8,128)(2,1)S(1)} fusion(bf16[2,1024,1024]{2,1,0:T(8,128)(2,1)} %param.4, bf16[136,1024]{1,0:T(8,128)(2,1)} %get-tuple-element.31.refs_2_.refs_0_), kind=kOutput, calls=%fused_computation.2 | convolution fusion | flops 537133056 | bytes 4980736 | tf_op jit(solution)/shard_map/qo,tok->tqk/dot_general | solution.py:301
  16.0 0.0 collective-permute-done
  16.0 2.5 %collective-permute-start.7 = (bf16[2,128,1024]{2,1,0:T(8,128)(2,1)S(1)}, bf16[2,128,1024]{2,1,0:T(8,128)(2,1)S(1)}, u32[]{:S(2)}, u32[]{:S(2)}) collective-permute-start(bf16[2,128,1024]{2,1,0:T(8,128)(2,1)S(1)} %fusion), channel_id=1, source_target_pairs={{0,16},{1,145},{2,18},{3,147},{4,20},{5,149},{6,22},{7,151},{8,24}... | collective-permute-start | bytes 1572872 | tf_op jit(solution)/shard_map/ppermute | solution.py:32
  18.5 0.0 collective-permute-done.1
  18.5 0.0 collective-permute-done.2
  18.6 0.1 concatenate.3.refs_3_.refs_4_
  18.6 1.1 %collective-permute-done.3.west_o.refs_2_.refs_1_ = bf16[136,1024]{1,0:T(8,128)(2,1)S(1)} collective-permute-done((bf16[136,1024]{1,0:T(8,128)(2,1)}, bf16[136,1024]{1,0:T(8,128)(2,1)S(1)}, u32[]{:S(2)}, u32[]{:S(2)}) %collective-permute-start.3) | collective-permute-done | bytes 278560 | tf_op jit(solution)/shard_map/ppermute | solution.py:32
  19.7 0.4 collective-permute-done.4.east_o.refs_4_.refs_2_
  20.2 2.7 %collective-permute-start.5 = (bf16[200,1024]{1,0:T(8,128)(2,1)S(1)}, bf16[200,1024]{1,0:T(8,128)(2,1)S(1)}, u32[]{:S(2)}, u32[]{:S(2)}) collective-permute-start(bf16[200,1024]{1,0:T(8,128)(2,1)S(1)} %concatenate.3.refs_3_.refs_4_), channel_id=1, source_target_pairs={{0,32},{1,97},{2,34},{3,99},{4,36},{5,101},{6,38},{7,103},{8,40},{... | collective-permute-start | bytes 1228808 | tf_op jit(solution)/shard_map/ppermute | solution.py:32
  22.9 1.3 %collective-permute-start.10 = (bf16[200,1024]{1,0:T(8,128)(2,1)S(1)}, bf16[200,1024]{1,0:T(8,128)(2,1)S(1)}, u32[]{:S(2)}, u32[]{:S(2)}) collective-permute-start(bf16[200,1024]{1,0:T(8,128)(2,1)S(1)} %concatenate.3.refs_3_.refs_4_), channel_id=1, source_target_pairs={{0,2},{1,3},{2,4},{3,5},{4,6},{5,7},{6,0},{7,1},{8,10},{9,11},{10,... | collective-permute-start | bytes 1228808 | tf_op jit(solution)/shard_map/ppermute | solution.py:32
  24.2 1.5 %collective-permute-start.11 = (bf16[200,1024]{1,0:T(8,128)(2,1)S(1)}, bf16[200,1024]{1,0:T(8,128)(2,1)S(1)}, u32[]{:S(2)}, u32[]{:S(2)}) collective-permute-start(bf16[200,1024]{1,0:T(8,128)(2,1)S(1)} %concatenate.3.refs_3_.refs_4_), channel_id=1, source_target_pairs={{0,6},{1,7},{2,0},{3,1},{4,2},{5,3},{6,4},{7,5},{8,14},{9,15},{10,... | collective-permute-start | bytes 1228808 | tf_op jit(solution)/shard_map/ppermute | solution.py:32
  25.7 5.2 %collective-permute-done.7 = bf16[2,128,1024]{2,1,0:T(8,128)(2,1)S(1)} collective-permute-done((bf16[2,128,1024]{2,1,0:T(8,128)(2,1)S(1)}, bf16[2,128,1024]{2,1,0:T(8,128)(2,1)S(1)}, u32[]{:S(2)}, u32[]{:S(2)}) %collective-permute-start.7) | collective-permute-done | bytes 524320 | tf_op jit(solution)/shard_map/ppermute | solution.py:32
  30.9 2.8 %collective-permute-start.8 = (bf16[2,128,1024]{2,1,0:T(8,128)(2,1)S(1)}, bf16[2,128,1024]{2,1,0:T(8,128)(2,1)S(1)}, u32[]{:S(2)}, u32[]{:S(2)}) collective-permute-start(bf16[2,128,1024]{2,1,0:T(8,128)(2,1)S(1)} %collective-permute-done.7), channel_id=1, source_target_pairs={{0,16},{1,145},{2,18},{3,147},{4,20},{5,149},{6,22},{7,151},{8,24}... | collective-permute-start | bytes 1572872 | tf_op jit(solution)/shard_map/ppermute | solution.py:32
  33.8 0.0 collective-permute-done.5.refs_4_.refs_7_
  33.8 1.8 %collective-permute-done.10.west_p.refs_3_.refs_5_ = bf16[200,1024]{1,0:T(8,128)(2,1)S(1)} collective-permute-done((bf16[200,1024]{1,0:T(8,128)(2,1)S(1)}, bf16[200,1024]{1,0:T(8,128)(2,1)S(1)}, u32[]{:S(2)}, u32[]{:S(2)}) %collective-permute-start.10) | collective-permute-done | bytes 409632 | tf_op jit(solution)/shard_map/ppermute | solution.py:32
  35.6 0.0 collective-permute-done.11.east_p.refs_5_.refs_6_
  35.6 0.1 shard_map.47
  35.7 1.0 %collective-permute-start.14 = (bf16[400,1024]{1,0:T(8,128)(2,1)S(1)}, bf16[400,1024]{1,0:T(8,128)(2,1)S(1)}, u32[]{:S(2)}, u32[]{:S(2)}) collective-permute-start(bf16[400,1024]{1,0:T(8,128)(2,1)S(1)} %get-tuple-element.43), channel_id=1, source_target_pairs={{0,32},{1,97},{2,34},{3,99},{4,36},{5,101},{6,38},{7,103},{8,40},{... | collective-permute-start | bytes 2457608 | tf_op jit(solution)/shard_map/ppermute | solution.py:32
  36.8 1.6 %collective-permute-start.12 = (bf16[336,1024]{1,0:T(8,128)(2,1)S(1)}, bf16[336,1024]{1,0:T(8,128)(2,1)S(1)}, u32[]{:S(2)}, u32[]{:S(2)}) collective-permute-start(bf16[336,1024]{1,0:T(8,128)(2,1)S(1)} %get-tuple-element.41), channel_id=1, source_target_pairs={{0,2},{1,7},{2,4},{3,1},{4,6},{5,3},{6,0},{7,5},{8,10},{9,15},{10,... | collective-permute-start | bytes 2064392 | tf_op jit(solution)/shard_map/ppermute | solution.py:32
  38.4 3.7 %fusion.1.refs_0_ = bf16[2,128,1024]{2,1,0:T(8,128)(2,1)S(1)} fusion(bf16[2,1024,1024]{2,1,0:T(8,128)(2,1)} %param.4, bf16[128,1024]{1,0:T(8,128)(2,1)S(1)} %slice.24), kind=kOutput, calls=%fused_computation.3 | convolution fusion | flops 537133056 | bytes 4980736 | tf_op jit(solution)/shard_map/qo,tko->tqk/dot_general | solution.py:316
  42.1 0.1 collective-permute-start.6
  42.2 1.2 %collective-permute-done.8.refs_0_.refs_2_ = bf16[2,128,1024]{2,1,0:T(8,128)(2,1)S(1)} collective-permute-done((bf16[2,128,1024]{2,1,0:T(8,128)(2,1)S(1)}, bf16[2,128,1024]{2,1,0:T(8,128)(2,1)S(1)}, u32[]{:S(2)}, u32[]{:S(2)}) %collective-permute-start.8) | collective-permute-done | bytes 524320 | tf_op jit(solution)/shard_map/ppermute | solution.py:32
  43.4 4.8 %collective-permute-start.9 = (bf16[2,128,1024]{2,1,0:T(8,128)(2,1)S(1)}, bf16[2,128,1024]{2,1,0:T(8,128)(2,1)S(1)}, u32[]{:S(2)}, u32[]{:S(2)}) collective-permute-start(bf16[2,128,1024]{2,1,0:T(8,128)(2,1)S(1)} %collective-permute-done.8.refs_0_.refs_2_), channel_id=1, source_target_pairs={{0,1},{1,0},{2,3},{3,2},{4,5},{5,4},{6,7},{7,6},{8,9},{9,8},{10,11... | collective-permute-start | bytes 1572872 | tf_op jit(solution)/shard_map/ppermute | solution.py:32
  48.1 0.0 collective-permute-done.12.refs_4_.refs_3_
  48.2 3.0 %collective-permute-start.13 = (bf16[200,1024]{1,0:T(8,128)(2,1)S(1)}, bf16[200,1024]{1,0:T(8,128)(2,1)S(1)}, u32[]{:S(2)}, u32[]{:S(2)}) collective-permute-start(bf16[200,1024]{1,0:T(8,128)(2,1)S(1)} %slice.36), channel_id=1, source_target_pairs={{0,32},{1,97},{2,34},{3,99},{4,36},{5,101},{6,38},{7,103},{8,40},{... | collective-permute-start | bytes 1228808 | tf_op jit(solution)/shard_map/ppermute | solution.py:32
  51.2 0.0 collective-permute-done.6.refs_1_
  51.2 0.8 shard_map.48.refs_5_
  51.9 0.0 collective-permute-done.14.refs_6_.refs_8_
  52.0 1.3 %shard_map.49 = (f32[2,256,512]{2,1,0:T(8,128)S(1)}, f32[2,256,512]{2,1,0:T(8,128)S(1)}) custom-call(bf16[2,128,1024]{2,1,0:T(8,128)(2,1)S(1)} %fusion.1.refs_0_, bf16[2,128,1024]{2,1,0:T(8,128)(2,1)S(1)} %collective-permute-done.6.refs_1_, bf16[136,1024]{1,0:T(8,128)(2,1)S(1)} %collective-permute-done.3.west_o.refs_2_.refs_1_, ...), custom_call_target="tpu_custom_call" | custom-call | flops 1073741824 | bytes 2097152 | tf_op jit(solution)/shard_map/pallas_call | solution.py:176
  53.3 0.0 collective-permute-done.9.refs_1_.refs_3_
  53.3 2.6 %shard_map.50 = (f32[2,128,1024]{2,1,0:T(8,128)S(1)}, f32[2,128,1024]{2,1,0:T(8,128)S(1)}) custom-call(bf16[2,128,1024]{2,1,0:T(8,128)(2,1)S(1)} %collective-permute-done.8.refs_0_.refs_2_, bf16[2,128,1024]{2,1,0:T(8,128)(2,1)S(1)} %collective-permute-done.9.refs_1_.refs_3_, bf16[136,1024]{1,0:T(8,128)(2,1)S(1)} %collective-permute-done.3.west_o.refs_2_.refs_1_, ...), custom_call_target="tpu_custom_call" | custom-call | flops 2147483648 | bytes 2097152 | tf_op jit(solution)/shard_map/pallas_call | solution.py:230
  55.9 1.5 %shard_map.51 = (f32[2,128,1024]{2,1,0:T(8,128)S(1)}, f32[2,128,1024]{2,1,0:T(8,128)S(1)}) custom-call(bf16[2,128,1024]{2,1,0:T(8,128)(2,1)S(1)} %collective-permute-done.8.refs_0_.refs_2_, bf16[2,128,1024]{2,1,0:T(8,128)(2,1)S(1)} %collective-permute-done.9.refs_1_.refs_3_, ...), custom_call_target="tpu_custom_call", output_to_operand_aliasing={{0}: (6, {}), {1}: (7, {})} | custom-call | flops 1073741824 | bytes 2097152 | tf_op jit(solution)/shard_map/pallas_call | solution.py:230
  57.4 0.0 collective-permute-done.13.refs_5_.refs_9_
  57.4 2.1 %shard_map.52 = (f32[2,128,1024]{2,1,0:T(8,128)S(1)}, bf16[2,128,1024]{2,1,0:T(8,128)(2,1)S(1)}) custom-call(bf16[2,128,1024]{2,1,0:T(8,128)(2,1)S(1)} %fusion.1.refs_0_, bf16[2,128,1024]{2,1,0:T(8,128)(2,1)S(1)} %collective-permute-done.6.refs_1_, bf16[2,128,1024]{2,1,0:T(8,128)(2,1)S(1)} %collective-permute-done.8.refs_0_.refs_2_, ...), custom_call_target="tpu_custom_call", output_to_operand_aliasing={{0}: (6, {})} | custom-call | flops 1073741824 | bytes 2097152 | tf_op jit(solution)/shard_map/pallas_call | solution.py:230
  59.5 0.9 collective-permute-start.15
  60.4 1.5 %collective-permute-done.15.got_ref = bf16[2,128,1024]{2,1,0:T(8,128)(2,1)S(1)} collective-permute-done((bf16[2,128,1024]{2,1,0:T(8,128)(2,1)S(1)}, bf16[2,128,1024]{2,1,0:T(8,128)(2,1)S(1)}, u32[]{:S(2)}, u32[]{:S(2)}) %collective-permute-start.15) | collective-permute-done | bytes 524320 | tf_op jit(solution)/shard_map/ppermute | solution.py:32
  61.9 0.3 shard_map.53
  62.3 19.7 %all_to_all.5.part_ref = bf16[16,2,64,128]{3,2,1,0:T(8,128)(2,1)S(1)} all-to-all(bf16[16,2,64,128]{3,2,1,0:T(8,128)(2,1)S(1)} %shard_map.53), channel_id=1, replica_groups={{0,2,4,6,8,10,12,14,16,18,20,22,24,26,28,30},{1,3,5,7,9,11,13,15,17,19,..., dimensions={0} | all-to-all | bytes 1048576 | tf_op jit(solution)/shard_map/all_to_all | solution.py:347
  81.9 0.8 shard_map.54
  82.7 2.0 %collective-permute-start.16 = (f32[2,32,1024]{2,1,0:T(8,128)S(1)}, f32[2,32,1024]{2,1,0:T(8,128)S(1)}, u32[]{:S(2)}, u32[]{:S(2)}) collective-permute-start(f32[2,32,1024]{2,1,0:T(8,128)S(1)} %get-tuple-element.54), channel_id=1, source_target_pairs={{0,1},{1,0},{2,3},{3,2},{4,5},{5,4},{6,7},{7,6},{8,9},{9,8},{10,11... | collective-permute-start | bytes 786440 | tf_op jit(solution)/shard_map/ppermute | solution.py:32
  84.8 1.2 %collective-permute-done.16.got_ref = f32[2,32,1024]{2,1,0:T(8,128)S(1)} collective-permute-done((f32[2,32,1024]{2,1,0:T(8,128)S(1)}, f32[2,32,1024]{2,1,0:T(8,128)S(1)}, u32[]{:S(2)}, u32[]{:S(2)}) %collective-permute-start.16) | collective-permute-done | bytes 262176 | tf_op jit(solution)/shard_map/ppermute | solution.py:32
  85.9 0.8 shard_map.55
  (13 shorter events, 0.1 us)
Async XLA Ops:
  1.9 31.8 %copy-start = (bf16[136,1024]{1,0:T(8,128)(2,1)S(1)}, bf16[136,1024]{1,0:T(8,128)(2,1)}, u32[]{:S(2)}) copy-start(bf16[136,1024]{1,0:T(8,128)(2,1)} %get-tuple-element.31.refs_2_.refs_0_) | copy-start | bytes 835588
  1.9 14.1 %collective-permute-start = (bf16[72,1024]{1,0:T(8,128)(2,1)}, bf16[72,1024]{1,0:T(8,128)(2,1)S(1)}, u32[]{:S(2)}, u32[]{:S(2)}) collective-permute-start(bf16[72,1024]{1,0:T(8,128)(2,1)} %get-tuple-element.30), channel_id=1, source_target_pairs={{0,8},{1,9},{2,10},{3,11},{4,12},{5,13},{6,14},{7,15},{8,16},{9,17... | collective-permute-start | bytes 442376 | tf_op jit(solution)/shard_map/ppermute | solution.py:32
  4.5 14.0 %collective-permute-start.1 = (bf16[72,1024]{1,0:T(8,128)(2,1)}, bf16[72,1024]{1,0:T(8,128)(2,1)S(1)}, u32[]{:S(2)}, u32[]{:S(2)}) collective-permute-start(bf16[72,1024]{1,0:T(8,128)(2,1)} %get-tuple-element.30), channel_id=1, source_target_pairs={{0,152},{1,153},{2,154},{3,155},{4,156},{5,157},{6,158},{7,159},{8... | collective-permute-start | bytes 442376 | tf_op jit(solution)/shard_map/ppermute | solution.py:32
  8.5 10.0 %collective-permute-start.2 = (bf16[72,1024]{1,0:T(8,128)(2,1)}, bf16[72,1024]{1,0:T(8,128)(2,1)S(1)}, u32[]{:S(2)}, u32[]{:S(2)}) collective-permute-start(bf16[72,1024]{1,0:T(8,128)(2,1)} %get-tuple-element.30), channel_id=1, source_target_pairs={{0,16},{1,145},{2,18},{3,147},{4,20},{5,149},{6,22},{7,151},{8,24}... | collective-permute-start | bytes 442376 | tf_op jit(solution)/shard_map/ppermute | solution.py:32
  10.3 9.4 %collective-permute-start.3 = (bf16[136,1024]{1,0:T(8,128)(2,1)}, bf16[136,1024]{1,0:T(8,128)(2,1)S(1)}, u32[]{:S(2)}, u32[]{:S(2)}) collective-permute-start(bf16[136,1024]{1,0:T(8,128)(2,1)} %get-tuple-element.31.refs_2_.refs_0_), channel_id=1, source_target_pairs={{0,2},{1,3},{2,4},{3,5},{4,6},{5,7},{6,0},{7,1},{8,10},{9,11},{10,... | collective-permute-start | bytes 835592 | tf_op jit(solution)/shard_map/ppermute | solution.py:32
  11.5 8.6 %collective-permute-start.4 = (bf16[136,1024]{1,0:T(8,128)(2,1)}, bf16[136,1024]{1,0:T(8,128)(2,1)S(1)}, u32[]{:S(2)}, u32[]{:S(2)}) collective-permute-start(bf16[136,1024]{1,0:T(8,128)(2,1)} %get-tuple-element.31.refs_2_.refs_0_), channel_id=1, source_target_pairs={{0,6},{1,7},{2,0},{3,1},{4,2},{5,3},{6,4},{7,5},{8,14},{9,15},{10,... | collective-permute-start | bytes 835592 | tf_op jit(solution)/shard_map/ppermute | solution.py:32
  16.0 14.9 %collective-permute-start.7 = (bf16[2,128,1024]{2,1,0:T(8,128)(2,1)S(1)}, bf16[2,128,1024]{2,1,0:T(8,128)(2,1)S(1)}, u32[]{:S(2)}, u32[]{:S(2)}) collective-permute-start(bf16[2,128,1024]{2,1,0:T(8,128)(2,1)S(1)} %fusion), channel_id=1, source_target_pairs={{0,16},{1,145},{2,18},{3,147},{4,20},{5,149},{6,22},{7,151},{8,24}... | collective-permute-start | bytes 1572872 | tf_op jit(solution)/shard_map/ppermute | solution.py:32
  20.2 13.6 %collective-permute-start.5 = (bf16[200,1024]{1,0:T(8,128)(2,1)S(1)}, bf16[200,1024]{1,0:T(8,128)(2,1)S(1)}, u32[]{:S(2)}, u32[]{:S(2)}) collective-permute-start(bf16[200,1024]{1,0:T(8,128)(2,1)S(1)} %concatenate.3.refs_3_.refs_4_), channel_id=1, source_target_pairs={{0,32},{1,97},{2,34},{3,99},{4,36},{5,101},{6,38},{7,103},{8,40},{... | collective-permute-start | bytes 1228808 | tf_op jit(solution)/shard_map/ppermute | solution.py:32
  22.9 12.7 %collective-permute-start.10 = (bf16[200,1024]{1,0:T(8,128)(2,1)S(1)}, bf16[200,1024]{1,0:T(8,128)(2,1)S(1)}, u32[]{:S(2)}, u32[]{:S(2)}) collective-permute-start(bf16[200,1024]{1,0:T(8,128)(2,1)S(1)} %concatenate.3.refs_3_.refs_4_), channel_id=1, source_target_pairs={{0,2},{1,3},{2,4},{3,5},{4,6},{5,7},{6,0},{7,1},{8,10},{9,11},{10,... | collective-permute-start | bytes 1228808 | tf_op jit(solution)/shard_map/ppermute | solution.py:32
  24.2 11.4 %collective-permute-start.11 = (bf16[200,1024]{1,0:T(8,128)(2,1)S(1)}, bf16[200,1024]{1,0:T(8,128)(2,1)S(1)}, u32[]{:S(2)}, u32[]{:S(2)}) collective-permute-start(bf16[200,1024]{1,0:T(8,128)(2,1)S(1)} %concatenate.3.refs_3_.refs_4_), channel_id=1, source_target_pairs={{0,6},{1,7},{2,0},{3,1},{4,2},{5,3},{6,4},{7,5},{8,14},{9,15},{10,... | collective-permute-start | bytes 1228808 | tf_op jit(solution)/shard_map/ppermute | solution.py:32
  30.9 12.4 %collective-permute-start.8 = (bf16[2,128,1024]{2,1,0:T(8,128)(2,1)S(1)}, bf16[2,128,1024]{2,1,0:T(8,128)(2,1)S(1)}, u32[]{:S(2)}, u32[]{:S(2)}) collective-permute-start(bf16[2,128,1024]{2,1,0:T(8,128)(2,1)S(1)} %collective-permute-done.7), channel_id=1, source_target_pairs={{0,16},{1,145},{2,18},{3,147},{4,20},{5,149},{6,22},{7,151},{8,24}... | collective-permute-start | bytes 1572872 | tf_op jit(solution)/shard_map/ppermute | solution.py:32
  35.7 16.2 %collective-permute-start.14 = (bf16[400,1024]{1,0:T(8,128)(2,1)S(1)}, bf16[400,1024]{1,0:T(8,128)(2,1)S(1)}, u32[]{:S(2)}, u32[]{:S(2)}) collective-permute-start(bf16[400,1024]{1,0:T(8,128)(2,1)S(1)} %get-tuple-element.43), channel_id=1, source_target_pairs={{0,32},{1,97},{2,34},{3,99},{4,36},{5,101},{6,38},{7,103},{8,40},{... | collective-permute-start | bytes 2457608 | tf_op jit(solution)/shard_map/ppermute | solution.py:32
  36.8 11.4 %collective-permute-start.12 = (bf16[336,1024]{1,0:T(8,128)(2,1)S(1)}, bf16[336,1024]{1,0:T(8,128)(2,1)S(1)}, u32[]{:S(2)}, u32[]{:S(2)}) collective-permute-start(bf16[336,1024]{1,0:T(8,128)(2,1)S(1)} %get-tuple-element.41), channel_id=1, source_target_pairs={{0,2},{1,7},{2,4},{3,1},{4,6},{5,3},{6,0},{7,5},{8,10},{9,15},{10,... | collective-permute-start | bytes 2064392 | tf_op jit(solution)/shard_map/ppermute | solution.py:32
  42.1 9.1 %collective-permute-start.6 = (bf16[2,128,1024]{2,1,0:T(8,128)(2,1)S(1)}, bf16[2,128,1024]{2,1,0:T(8,128)(2,1)S(1)}, u32[]{:S(2)}, u32[]{:S(2)}) collective-permute-start(bf16[2,128,1024]{2,1,0:T(8,128)(2,1)S(1)} %fusion.1.refs_0_), channel_id=1, source_target_pairs={{0,1},{1,0},{2,3},{3,2},{4,5},{5,4},{6,7},{7,6},{8,9},{9,8},{10,11... | collective-permute-start | bytes 1572872 | tf_op jit(solution)/shard_map/ppermute | solution.py:32
  43.4 9.9 %collective-permute-start.9 = (bf16[2,128,1024]{2,1,0:T(8,128)(2,1)S(1)}, bf16[2,128,1024]{2,1,0:T(8,128)(2,1)S(1)}, u32[]{:S(2)}, u32[]{:S(2)}) collective-permute-start(bf16[2,128,1024]{2,1,0:T(8,128)(2,1)S(1)} %collective-permute-done.8.refs_0_.refs_2_), channel_id=1, source_target_pairs={{0,1},{1,0},{2,3},{3,2},{4,5},{5,4},{6,7},{7,6},{8,9},{9,8},{10,11... | collective-permute-start | bytes 1572872 | tf_op jit(solution)/shard_map/ppermute | solution.py:32
  48.2 9.3 %collective-permute-start.13 = (bf16[200,1024]{1,0:T(8,128)(2,1)S(1)}, bf16[200,1024]{1,0:T(8,128)(2,1)S(1)}, u32[]{:S(2)}, u32[]{:S(2)}) collective-permute-start(bf16[200,1024]{1,0:T(8,128)(2,1)S(1)} %slice.36), channel_id=1, source_target_pairs={{0,32},{1,97},{2,34},{3,99},{4,36},{5,101},{6,38},{7,103},{8,40},{... | collective-permute-start | bytes 1228808 | tf_op jit(solution)/shard_map/ppermute | solution.py:32
  55.9 6.0 %copy-start.1 = (f32[1,128]{1,0:T(1,128)S(1)}, f32[1,128]{1,0:T(1,128)}, u32[]{:S(2)}) copy-start(f32[1,128]{1,0:T(1,128)} %get-tuple-element.52.coulomb_ref) | copy-start | bytes 1540
  59.5 2.4 %collective-permute-start.15 = (bf16[2,128,1024]{2,1,0:T(8,128)(2,1)S(1)}, bf16[2,128,1024]{2,1,0:T(8,128)(2,1)S(1)}, u32[]{:S(2)}, u32[]{:S(2)}) collective-permute-start(bf16[2,128,1024]{2,1,0:T(8,128)(2,1)S(1)} %get-tuple-element.51), channel_id=1, source_target_pairs={{0,1},{1,0},{2,3},{3,2},{4,5},{5,4},{6,7},{7,6},{8,9},{9,8},{10,11... | collective-permute-start | bytes 1572872 | tf_op jit(solution)/shard_map/ppermute | solution.py:32
  82.7 3.2 %collective-permute-start.16 = (f32[2,32,1024]{2,1,0:T(8,128)S(1)}, f32[2,32,1024]{2,1,0:T(8,128)S(1)}, u32[]{:S(2)}, u32[]{:S(2)}) collective-permute-start(f32[2,32,1024]{2,1,0:T(8,128)S(1)} %get-tuple-element.54), channel_id=1, source_target_pairs={{0,1},{1,0},{2,3},{3,2},{4,5},{5,4},{6,7},{7,6},{8,9},{9,8},{10,11... | collective-permute-start | bytes 786440 | tf_op jit(solution)/shard_map/ppermute | solution.py:32

commit v8 on v5

--- a/solution.py
+++ b/solution.py
@@ -138,6 +138,23 @@
     )(west, east)
 
 
+def after_kernel(value_ref, first_ref, out_ref):
+    del first_ref
+    pltpu.touch(value_ref)
+    pltpu.touch(out_ref)
+
+
+def after(value, first):
+    return pl.pallas_call(
+        after_kernel,
+        out_shape=jax.ShapeDtypeStruct(value.shape, value.dtype),
+        in_specs=[VMEM] * 2,
+        out_specs=VMEM,
+        input_output_aliases={0: 0},
+        compiler_params=params(8),
+    )(value, first)
+
+
 def weight_of(ref, row):
     parts = [ref[pl.ds(row, 1), pl.ds(k * BLOCK, BLOCK)].astype(F32) for k in range(3)]
     return parts[0] + (parts[1] + parts[2])
@@ -151,25 +168,65 @@
     return jnp.concatenate(pairs, axis=1) if len(pairs) > 1 else pairs[0]
 
 
-def chunk_kernel(pieces, count, first, *refs):
-    right_own, right_other, left_own, left_other = refs[:4]
-    rows = refs[4 : 4 + count]
-    rest = refs[4 + count :]
+def rows_of(refs, piece):
+    at, start, size = piece
+    return refs[at][pl.ds(start, size), :], weights_of(refs[at], start + size, size // HALF)
+
+
+def square_kernel(pieces, right_own, right_other, *refs):
+    rows, out = refs[:-1], refs[-1]
+    for t in range(right_own.shape[0]):
+        right = jnp.concatenate([right_own[t], right_other[t]], axis=0)
+        offset = 0
+        for piece in pieces:
+            part, weight = rows_of(rows, piece)
+            a = lax.dot_general(right, part, NT, preferred_element_type=F32)
+            out[t, :, pl.ds(offset, piece[2])] = a * a * weight
+            offset += piece[2]
+
+
+def squares(right, right_other, rows, pieces):
+    times, own, orb = right.shape
+    n = sum(piece[2] for piece in pieces)
+    return pl.pallas_call(
+        functools.partial(square_kernel, tuple(pieces)),
+        out_shape=jax.ShapeDtypeStruct((times, 2 * own, n), F32),
+        in_specs=[VMEM] * (2 + len(rows)),
+        out_specs=VMEM,
+        compiler_params=params(12),
+        cost_estimate=pl.CostEstimate(
+            flops=times * 2 * (2 * own) * n * orb, bytes_accessed=2 << 20, transcendentals=0
+        ),
+    )(right, right_other, *rows)
+
+
+def chunk_kernel(pieces, sides, count, given, first, *refs):
+    left_own, left_other = refs[sides - 2 : sides]
+    rows = refs[sides : sides + count]
+    rest = refs[sides + count :]
+    if given:
+        squared = rest[0]
+        rest = rest[1:]
     if not first:
         acc_own, acc_other = rest[:2]
         rest = rest[2:]
     out_own, out_other = rest
     own = out_own.shape[1]
     for t in range(out_own.shape[0]):
-        right = jnp.concatenate([right_own[t], right_other[t]], axis=0)
         left = jnp.concatenate([left_own[t], left_other[t]], axis=0)
         total = None
+        offset = 0
         for piece in pieces:
-            part = jnp.concatenate([rows[at][pl.ds(start, n), :] for at, start, n in piece[0]], axis=0)
-            weight = weights_of(rows[piece[1]], piece[2], part.shape[0] // HALF)
-            a = lax.dot_general(right, part, NT, preferred_element_type=F32)
+            part, weight = rows_of(rows, piece)
+            if given:
+                square = squared[t, :, pl.ds(offset, piece[2])]
+            else:
+                right = jnp.concatenate([refs[0][t], refs[1][t]], axis=0)
+                a = lax.dot_general(right, part, NT, preferred_element_type=F32)
+                square = a * a * weight
+            offset += piece[2]
             m = lax.dot_general(left, part, NT, preferred_element_type=F32)
-            k = (a * weight * (a * m)).astype(BF16)
+            k = (square * m).astype(BF16)
             d = lax.dot_general(k, part, NN, preferred_element_type=F32)
             total = d if total is None else total + d
         mine, theirs = total[:own], total[own:]
@@ -179,26 +236,29 @@
         out_other[t] = theirs.astype(out_other.dtype)
 
 
-def chunk(sides, rows, pieces, acc=None, last=False):
+def chunk(sides, rows, pieces, given=(), acc=(), last=False):
     times, own, orb = sides[0].shape
     shape = jax.ShapeDtypeStruct((times, own, orb), F32)
-    extra = () if acc is None else tuple(acc)
     theirs = jax.ShapeDtypeStruct((times, own, orb), BF16 if last else F32)
+    at = len(sides) + len(rows) + len(given)
     aliases = {}
-    if acc is not None:
-        aliases[4 + len(rows)] = 0
+    if acc:
+        aliases[at] = 0
         if not last:
-            aliases[5 + len(rows)] = 1
-    flops = len(pieces) * 4 * HALF * times * 3 * 2 * (2 * own) * orb
-    return pl.pallas_call(
-        functools.partial(chunk_kernel, tuple(pieces), len(rows), acc is None),
+            aliases[at + 1] = 1
+    n = sum(piece[2] for piece in pieces)
+    flops = times * 2 * 2 * (2 * own) * n * orb
+    return pl.pallas_call(
+        functools.partial(
+            chunk_kernel, tuple(pieces), len(sides), len(rows), bool(given), not acc
+        ),
         out_shape=(shape, theirs),
-        in_specs=[VMEM] * (4 + len(rows) + len(extra)),
+        in_specs=[VMEM] * (at + len(acc)),
         out_specs=(VMEM, VMEM),
         input_output_aliases=aliases,
         compiler_params=params(16),
         cost_estimate=pl.CostEstimate(flops=flops, bytes_accessed=2 << 20, transcendentals=0),
-    )(*sides, *rows, *extra)
+    )(*sides, *rows, *given, *acc)
 
 
 def finish_kernel(own_ref, got_ref, coulomb_ref, out_ref):
@@ -259,38 +319,37 @@
     below = along_z(whole, 1)
     above = along_z(whole, -1)
     left = jnp.einsum("qo,tok->tqk", masked, green, preferred_element_type=F32).astype(BF16)
-    right = jnp.einsum("qo,tko->tqk", masked, green, preferred_element_type=F32).astype(BF16)
-    right_other = other_core(right)
+    below, left = barrier((below, left))
+    left = along_z(left, 4)
 
     blocks = [whole, below, above, beyond]
     weights = [block[HALF : HALF + 1] for block in blocks] + [jnp.zeros((4, orb), BF16)]
-    here = jnp.concatenate([block[:HALF] for block in blocks] + weights, axis=0)
-    here, left = barrier((here, left))
+    here = barrier(jnp.concatenate([block[:HALF] for block in blocks] + weights, axis=0))
 
     n = 4 * HALF
-    left = two_along_z(left)
     west = along_x(here, 1)
     east = along_x(here, -1)
     rest = other_parity(here[HALF:])
     here_q = jnp.concatenate([masked[HALF:], rest], axis=0)
-
-    west, east, here_q = barrier((west, east, here_q))
+    right = jnp.einsum("qo,tko->tqk", masked, green, preferred_element_type=F32).astype(BF16)
+    west, east, right, here_q = barrier((west, east, right, here_q))
+    right_other = other_core(right)
     onward, both = mix(west, east)
     far = split_x(onward)
     sides_q = other_parity(both)
-    left = two_along_z(left)
-    left, _ = barrier((left, far[:8, :BLOCK]))
     far_q = other_parity(far)
+    left = after(left, onward)
     left_other = other_core(left)
 
-    def piece(at, start=0):
-        return (((at, start, n),), at, start + n)
-
-    sides = (right, right_other, left, left_other)
-    acc = chunk(sides, (here, here_q), [piece(0), piece(1)])
-    acc = chunk(sides, (west, east), [piece(0), piece(1)], acc)
-    acc = chunk(sides, (sides_q, far), [piece(0), piece(0, n + 8), piece(1)], acc)
-    keep, theirs = chunk(sides, (far_q,), [piece(0)], acc, last=True)
+    rights, lefts = (right, right_other), (left, left_other)
+    two = [(0, 0, n), (1, 0, n)]
+    here_z = squares(*rights, (here, here_q), two)
+    sides_z = squares(*rights, (west, east), two)
+    acc = chunk(lefts, (here, here_q), two, given=(here_z,))
+    acc = chunk(lefts, (west, east), two, given=(sides_z,), acc=acc)
+    sides = rights + lefts
+    acc = chunk(sides, (sides_q, far), [(0, 0, n), (0, n + 8, n), (1, 0, n)], acc=acc)
+    keep, theirs = chunk(sides, (far_q,), [(0, 0, n)], acc=acc, last=True)
 
     got = other_core(theirs)
     chips, i_rows = 16, orb // 16

time: 87.6 us -> 88.8 us (1.014)
  starting transfers between devices: 32.9 us -> 30.5 us
  waiting for transfers between devices: 13.7 us -> 15.8 us
  blocking collectives: 21.4 us -> 22.5 us
    ppermute x15 -> x14, starting transfers between devices: 32.9 us -> 30.5 us  [send(): return lax.ppermute(value, BOTH, sorted(pairs))]
    ppermute x15 -> x14, waiting for transfers between devices: 13.7 us -> 15.8 us  [send(): return lax.ppermute(value, BOTH, sorted(pairs))]
    all_to_all x1, blocking collectives: 21.4 us -> 22.5 us  [local(): lax.all_to_all(part, 'aux', 0, 0, axis_index_groups=groups, tiled=True)]
    pallas_call x4 -> x7, Pallas kernels: 8.33 us -> 8.74 us  [the longest x4 7.23 us: chunk(): pl.pallas_call(functools.partial(chunk_kernel, tuple(pieces), len(sides),...]
  transfers between devices with their start and end apart: 15 -> 14, of which waited for: 5 -> 5; matrix products, arithmetic and copies ran while one was open for 8% -> 8% of each run, Pallas kernels for 8% -> 9%
where the time goes in v8:
time: 88.8 us; the launch traced here: 88.6 us
  starting transfers between devices  30.5 us (34%)
  blocking collectives  22.5 us (25%)
  waiting for transfers between devices  15.8 us (18%)
  Pallas kernels  12.6 us (14%)
  matrix products  6.72 us (8%)
    ppermute x14, starting transfers between devices, send(): return lax.ppermute(value, BOTH, sorted(pairs))  30.5 us
    all_to_all x1, blocking collectives, local(): lax.all_to_all(part, 'aux', 0, 0, axis_index_groups=groups, tiled=True)  22.5 us
    ppermute x14, waiting for transfers between devices, send(): return lax.ppermute(value, BOTH, sorted(pairs))  15.8 us
    pallas_call x4, Pallas kernels, chunk(): pl.pallas_call(functools.partial(chunk_kernel, tuple(pieces), len(sides),...  7.23 us
    dot_general x1, matrix products, local(): jnp.einsum('qo,tko->tqk', masked, green, preferred_element_type=F32)  3.69 us
    dot_general x1, matrix products, local(): jnp.einsum('qo,tok->tqk', masked, green, preferred_element_type=F32)  3.03 us
    pallas_call x1, Pallas kernels, prologue(): pl.pallas_call(prologue_kernel, out_shape=[jax.ShapeDtypeStruct((own, orb...  1.9 us
  transfers between devices with their start and end apart: 14, of which 5 were waited for; matrix products, arithmetic and copies ran while one was open for 8% of the time, Pallas kernels for 9%

profile of v8, /device:TPU:1, one launch (start us, length us, event | category | flops | bytes accessed | tf_op | source)
XLA Modules:
  0.0 88.6 jit_solution(3740820616133661950)
XLA Ops:
  0.0 1.9 %shard_map.46 = (bf16[128,1024]{1,0:T(8,128)(2,1)}, bf16[72,1024]{1,0:T(8,128)(2,1)}, f32[1,128]{1,0:T(1,128)}) custom-call(bf16[128,1024]{1,0:T(8,128)(2,1)} %factors_in.1, s32[1,8]{1,0:T(1,128)} %pattern_in.1, f32[1,128]{1,0:T(1,128)} %bitcast.12), custom_call_target="tpu_custom_call" | custom-call | tf_op jit(solution)/shard_map/pallas_call | solution.py:102
  1.9 0.0 copy-start.2
  1.9 2.5 %collective-permute-start = (bf16[72,1024]{1,0:T(8,128)(2,1)}, bf16[72,1024]{1,0:T(8,128)(2,1)S(1)}, u32[]{:S(2)}, u32[]{:S(2)}) collective-permute-start(bf16[72,1024]{1,0:T(8,128)(2,1)} %get-tuple-element.26), channel_id=1, source_target_pairs={{0,8},{1,9},{2,10},{3,11},{4,12},{5,13},{6,14},{7,15},{8,16},{9,17... | collective-permute-start | bytes 442376 | tf_op jit(solution)/shard_map/ppermute | solution.py:31
  4.5 4.0 %collective-permute-start.1 = (bf16[72,1024]{1,0:T(8,128)(2,1)}, bf16[72,1024]{1,0:T(8,128)(2,1)S(1)}, u32[]{:S(2)}, u32[]{:S(2)}) collective-permute-start(bf16[72,1024]{1,0:T(8,128)(2,1)} %get-tuple-element.26), channel_id=1, source_target_pairs={{0,152},{1,153},{2,154},{3,155},{4,156},{5,157},{6,158},{7,159},{8... | collective-permute-start | bytes 442376 | tf_op jit(solution)/shard_map/ppermute | solution.py:31
  8.5 1.8 %collective-permute-start.2 = (bf16[72,1024]{1,0:T(8,128)(2,1)}, bf16[72,1024]{1,0:T(8,128)(2,1)S(1)}, u32[]{:S(2)}, u32[]{:S(2)}) collective-permute-start(bf16[72,1024]{1,0:T(8,128)(2,1)} %get-tuple-element.26), channel_id=1, source_target_pairs={{0,16},{1,145},{2,18},{3,147},{4,20},{5,149},{6,22},{7,151},{8,24}... | collective-permute-start | bytes 442376 | tf_op jit(solution)/shard_map/ppermute | solution.py:31
  10.3 3.0 %fusion = bf16[2,128,1024]{2,1,0:T(8,128)(2,1)S(1)} fusion(bf16[2,1024,1024]{2,1,0:T(8,128)(2,1)} %param.4, bf16[128,1024]{1,0:T(8,128)(2,1)} %get-tuple-element.27), kind=kOutput, calls=%fused_computation.2 | convolution fusion | flops 537133056 | bytes 4980736 | tf_op jit(solution)/shard_map/qo,tok->tqk/dot_general | solution.py:321
  13.3 0.0 copy-done.2
  13.4 0.0 collective-permute-done
  13.4 0.0 collective-permute-done.1
  13.5 2.2 %collective-permute-done.2 = bf16[72,1024]{1,0:T(8,128)(2,1)S(1)} collective-permute-done((bf16[72,1024]{1,0:T(8,128)(2,1)}, bf16[72,1024]{1,0:T(8,128)(2,1)S(1)}, u32[]{:S(2)}, u32[]{:S(2)}) %collective-permute-start.2) | collective-permute-done | bytes 147488 | tf_op jit(solution)/shard_map/ppermute | solution.py:31
  15.7 0.1 concatenate.6.refs_0_.refs_2_
  15.8 1.3 %collective-permute-start.3 = (bf16[264,1024]{1,0:T(8,128)(2,1)S(1)}, bf16[264,1024]{1,0:T(8,128)(2,1)S(1)}, u32[]{:S(2)}, u32[]{:S(2)}) collective-permute-start(bf16[264,1024]{1,0:T(8,128)(2,1)S(1)} %concatenate.6.refs_0_.refs_2_), channel_id=1, source_target_pairs={{0,2},{1,3},{2,4},{3,5},{4,6},{5,7},{6,0},{7,1},{8,10},{9,11},{10,... | collective-permute-start | bytes 1622024 | tf_op jit(solution)/shard_map/ppermute | solution.py:31
  17.1 1.5 %collective-permute-start.4 = (bf16[264,1024]{1,0:T(8,128)(2,1)S(1)}, bf16[264,1024]{1,0:T(8,128)(2,1)S(1)}, u32[]{:S(2)}, u32[]{:S(2)}) collective-permute-start(bf16[264,1024]{1,0:T(8,128)(2,1)S(1)} %concatenate.6.refs_0_.refs_2_), channel_id=1, source_target_pairs={{0,6},{1,7},{2,0},{3,1},{4,2},{5,3},{6,4},{7,5},{8,14},{9,15},{10,... | collective-permute-start | bytes 1622024 | tf_op jit(solution)/shard_map/ppermute | solution.py:31
  18.6 2.8 %collective-permute-start.5 = (bf16[200,1024]{1,0:T(8,128)(2,1)S(1)}, bf16[200,1024]{1,0:T(8,128)(2,1)S(1)}, u32[]{:S(2)}, u32[]{:S(2)}) collective-permute-start(bf16[200,1024]{1,0:T(8,128)(2,1)S(1)} %slice.44), channel_id=1, source_target_pairs={{0,32},{1,97},{2,34},{3,99},{4,36},{5,101},{6,38},{7,103},{8,40},{... | collective-permute-start | bytes 1228808 | tf_op jit(solution)/shard_map/ppermute | solution.py:31
  21.4 4.5 %collective-permute-start.7 = (bf16[2,128,1024]{2,1,0:T(8,128)(2,1)S(1)}, bf16[2,128,1024]{2,1,0:T(8,128)(2,1)S(1)}, u32[]{:S(2)}, u32[]{:S(2)}) collective-permute-start(bf16[2,128,1024]{2,1,0:T(8,128)(2,1)S(1)} %fusion), channel_id=1, source_target_pairs={{0,128},{1,129},{2,130},{3,131},{4,132},{5,133},{6,134},{7,135},{8... | collective-permute-start | bytes 1572872 | tf_op jit(solution)/shard_map/ppermute | solution.py:31
  25.9 0.0 copy-done.1
  25.9 3.7 %fusion.1.right_own.refs_0_ = bf16[2,128,1024]{2,1,0:T(8,128)(2,1)S(1)} fusion(bf16[2,1024,1024]{2,1,0:T(8,128)(2,1)} %param.4, bf16[128,1024]{1,0:T(8,128)(2,1)S(1)} %copy-done.1), kind=kOutput, calls=%fused_computation.3 | convolution fusion | flops 537133056 | bytes 4980736 | tf_op jit(solution)/shard_map/qo,tko->tqk/dot_general | solution.py:334
  29.6 0.0 collective-permute-done.5
  29.7 0.0 collective-permute-done.3.west_ref.refs_0_.refs_2_
  29.7 0.0 collective-permute-done.4.east_ref.refs_1_.refs_3_
  29.7 0.1 shard_map.47
  29.8 2.2 %collective-permute-start.11 = (bf16[528,1024]{1,0:T(8,128)(2,1)S(1)}, bf16[528,1024]{1,0:T(8,128)(2,1)S(1)}, u32[]{:S(2)}, u32[]{:S(2)}) collective-permute-start(bf16[528,1024]{1,0:T(8,128)(2,1)S(1)} %get-tuple-element.34), channel_id=1, source_target_pairs={{0,32},{1,97},{2,34},{3,99},{4,36},{5,101},{6,38},{7,103},{8,40},{... | collective-permute-start | bytes 3244040 | tf_op jit(solution)/shard_map/ppermute | solution.py:31
  32.0 2.4 %collective-permute-start.9 = (bf16[264,1024]{1,0:T(8,128)(2,1)S(1)}, bf16[264,1024]{1,0:T(8,128)(2,1)S(1)}, u32[]{:S(2)}, u32[]{:S(2)}) collective-permute-start(bf16[264,1024]{1,0:T(8,128)(2,1)S(1)} %get-tuple-element.33.first_ref), channel_id=1, source_target_pairs={{0,2},{1,7},{2,4},{3,1},{4,6},{5,3},{6,0},{7,5},{8,10},{9,15},{10,... | collective-permute-start | bytes 1622024 | tf_op jit(solution)/shard_map/ppermute | solution.py:31
  34.4 0.7 collective-permute-start.6
  35.0 8.8 %collective-permute-done.7.value_ref = bf16[2,128,1024]{2,1,0:T(8,128)(2,1)S(1)} collective-permute-done((bf16[2,128,1024]{2,1,0:T(8,128)(2,1)S(1)}, bf16[2,128,1024]{2,1,0:T(8,128)(2,1)S(1)}, u32[]{:S(2)}, u32[]{:S(2)}) %collective-permute-start.7) | collective-permute-done | bytes 524320 | tf_op jit(solution)/shard_map/ppermute | solution.py:31
  43.9 4.4 %collective-permute-start.8 = (bf16[2,128,1024]{2,1,0:T(8,128)(2,1)S(1)}, bf16[2,128,1024]{2,1,0:T(8,128)(2,1)S(1)}, u32[]{:S(2)}, u32[]{:S(2)}) collective-permute-start(bf16[2,128,1024]{2,1,0:T(8,128)(2,1)S(1)} %shard_map.48.refs_0_.refs_2_), channel_id=1, source_target_pairs={{0,1},{1,0},{2,3},{3,2},{4,5},{5,4},{6,7},{7,6},{8,9},{9,8},{10,11... | collective-permute-start | bytes 1572872 | tf_op jit(solution)/shard_map/ppermute | solution.py:31
  48.3 0.0 collective-permute-done.9.refs_5_
  48.3 0.0 collective-permute-start.10
  48.3 0.0 collective-permute-done.6.right_other.refs_1_
  48.3 0.7 shard_map.49.refs_4_
  49.0 0.8 shard_map.50.refs_4_
  49.8 0.0 collective-permute-done.8.refs_1_.refs_3_
  49.8 1.5 %shard_map.51 = (f32[2,128,1024]{2,1,0:T(8,128)S(1)}, f32[2,128,1024]{2,1,0:T(8,128)S(1)}) custom-call(bf16[2,128,1024]{2,1,0:T(8,128)(2,1)S(1)} %shard_map.48.refs_0_.refs_2_, bf16[2,128,1024]{2,1,0:T(8,128)(2,1)S(1)} %collective-permute-done.8.refs_1_.refs_3_, bf16[264,1024]{1,0:T(8,128)(2,1)S(1)} %concatenate.6.refs_0_.refs_2_, ...), custom_call_target="tpu_custom_call" | custom-call | flops 1073741824 | bytes 2097152 | tf_op jit(solution)/shard_map/pallas_call | solution.py:251
  51.3 1.5 %shard_map.52 = (f32[2,128,1024]{2,1,0:T(8,128)S(1)}, f32[2,128,1024]{2,1,0:T(8,128)S(1)}) custom-call(bf16[2,128,1024]{2,1,0:T(8,128)(2,1)S(1)} %shard_map.48.refs_0_.refs_2_, bf16[2,128,1024]{2,1,0:T(8,128)(2,1)S(1)} %collective-permute-done.8.refs_1_.refs_3_, ...), custom_call_target="tpu_custom_call", output_to_operand_aliasing={{0}: (5, {}), {1}: (6, {})} | custom-call | flops 1073741824 | bytes 2097152 | tf_op jit(solution)/shard_map/pallas_call | solution.py:251
  52.8 0.0 collective-permute-done.11.refs_4_
  52.8 0.0 copy-start
  52.8 3.1 %shard_map.53 = (f32[2,128,1024]{2,1,0:T(8,128)S(1)}, f32[2,128,1024]{2,1,0:T(8,128)S(1)}) custom-call(bf16[2,128,1024]{2,1,0:T(8,128)(2,1)S(1)} %fusion.1.right_own.refs_0_, bf16[2,128,1024]{2,1,0:T(8,128)(2,1)S(1)} %collective-permute-done.6.right_other.refs_1_, ...), custom_call_target="tpu_custom_call", output_to_operand_aliasing={{0}: (6, {}), {1}: (7, {})} | custom-call | flops 1610612736 | bytes 2097152 | tf_op jit(solution)/shard_map/pallas_call | solution.py:251
  55.9 1.8 %collective-permute-done.10.refs_4_.refs_6_ = bf16[264,1024]{1,0:T(8,128)(2,1)S(1)} collective-permute-done((bf16[264,1024]{1,0:T(8,128)(2,1)S(1)}, bf16[264,1024]{1,0:T(8,128)(2,1)S(1)}, u32[]{:S(2)}, u32[]{:S(2)}) %collective-permute-start.10) | collective-permute-done | bytes 540704 | tf_op jit(solution)/shard_map/ppermute | solution.py:31
  57.7 1.2 %shard_map.54 = (f32[2,128,1024]{2,1,0:T(8,128)S(1)}, bf16[2,128,1024]{2,1,0:T(8,128)(2,1)S(1)}) custom-call(bf16[2,128,1024]{2,1,0:T(8,128)(2,1)S(1)} %fusion.1.right_own.refs_0_, bf16[2,128,1024]{2,1,0:T(8,128)(2,1)S(1)} %collective-permute-done.6.right_other.refs_1_, ...), custom_call_target="tpu_custom_call", output_to_operand_aliasing={{0}: (5, {})} | custom-call | flops 536870912 | bytes 2097152 | tf_op jit(solution)/shard_map/pallas_call | solution.py:251
  58.9 0.3 collective-permute-start.12
  59.2 1.7 %collective-permute-done.12.got_ref = bf16[2,128,1024]{2,1,0:T(8,128)(2,1)S(1)} collective-permute-done((bf16[2,128,1024]{2,1,0:T(8,128)(2,1)S(1)}, bf16[2,128,1024]{2,1,0:T(8,128)(2,1)S(1)}, u32[]{:S(2)}, u32[]{:S(2)}) %collective-permute-start.12) | collective-permute-done | bytes 524320 | tf_op jit(solution)/shard_map/ppermute | solution.py:31
  60.9 0.0 copy-done
  60.9 0.3 shard_map.55
  61.3 22.5 %all_to_all.5.part_ref = bf16[16,2,64,128]{3,2,1,0:T(8,128)(2,1)S(1)} all-to-all(bf16[16,2,64,128]{3,2,1,0:T(8,128)(2,1)S(1)} %shard_map.55), channel_id=1, replica_groups={{0,2,4,6,8,10,12,14,16,18,20,22,24,26,28,30},{1,3,5,7,9,11,13,15,17,19,..., dimensions={0} | all-to-all | bytes 1048576 | tf_op jit(solution)/shard_map/all_to_all | solution.py:364
  83.8 0.8 shard_map.56
  84.6 2.1 %collective-permute-start.13 = (f32[2,32,1024]{2,1,0:T(8,128)S(1)}, f32[2,32,1024]{2,1,0:T(8,128)S(1)}, u32[]{:S(2)}, u32[]{:S(2)}) collective-permute-start(f32[2,32,1024]{2,1,0:T(8,128)S(1)} %get-tuple-element.46), channel_id=1, source_target_pairs={{0,1},{1,0},{2,3},{3,2},{4,5},{5,4},{6,7},{7,6},{8,9},{9,8},{10,11... | collective-permute-start | bytes 786440 | tf_op jit(solution)/shard_map/ppermute | solution.py:31
  86.7 1.2 %collective-permute-done.13.got_ref = f32[2,32,1024]{2,1,0:T(8,128)S(1)} collective-permute-done((f32[2,32,1024]{2,1,0:T(8,128)S(1)}, f32[2,32,1024]{2,1,0:T(8,128)S(1)}, u32[]{:S(2)}, u32[]{:S(2)}) %collective-permute-start.13) | collective-permute-done | bytes 262176 | tf_op jit(solution)/shard_map/ppermute | solution.py:31
  87.8 0.8 shard_map.57
  (14 shorter events, 0.1 us)
Async XLA Ops:
  1.9 11.4 %copy-start.2 = (bf16[72,1024]{1,0:T(8,128)(2,1)S(1)}, bf16[72,1024]{1,0:T(8,128)(2,1)}, u32[]{:S(2)}) copy-start(bf16[72,1024]{1,0:T(8,128)(2,1)} %get-tuple-element.26) | copy-start | bytes 442372
  1.9 11.5 %collective-permute-start = (bf16[72,1024]{1,0:T(8,128)(2,1)}, bf16[72,1024]{1,0:T(8,128)(2,1)S(1)}, u32[]{:S(2)}, u32[]{:S(2)}) collective-permute-start(bf16[72,1024]{1,0:T(8,128)(2,1)} %get-tuple-element.26), channel_id=1, source_target_pairs={{0,8},{1,9},{2,10},{3,11},{4,12},{5,13},{6,14},{7,15},{8,16},{9,17... | collective-permute-start | bytes 442376 | tf_op jit(solution)/shard_map/ppermute | solution.py:31
  4.5 9.0 %collective-permute-start.1 = (bf16[72,1024]{1,0:T(8,128)(2,1)}, bf16[72,1024]{1,0:T(8,128)(2,1)S(1)}, u32[]{:S(2)}, u32[]{:S(2)}) collective-permute-start(bf16[72,1024]{1,0:T(8,128)(2,1)} %get-tuple-element.26), channel_id=1, source_target_pairs={{0,152},{1,153},{2,154},{3,155},{4,156},{5,157},{6,158},{7,159},{8... | collective-permute-start | bytes 442376 | tf_op jit(solution)/shard_map/ppermute | solution.py:31
  8.5 7.2 %collective-permute-start.2 = (bf16[72,1024]{1,0:T(8,128)(2,1)}, bf16[72,1024]{1,0:T(8,128)(2,1)S(1)}, u32[]{:S(2)}, u32[]{:S(2)}) collective-permute-start(bf16[72,1024]{1,0:T(8,128)(2,1)} %get-tuple-element.26), channel_id=1, source_target_pairs={{0,16},{1,145},{2,18},{3,147},{4,20},{5,149},{6,22},{7,151},{8,24}... | collective-permute-start | bytes 442376 | tf_op jit(solution)/shard_map/ppermute | solution.py:31
  10.3 15.6 %copy-start.1 = (bf16[128,1024]{1,0:T(8,128)(2,1)S(1)}, bf16[128,1024]{1,0:T(8,128)(2,1)}, u32[]{:S(2)}) copy-start(bf16[128,1024]{1,0:T(8,128)(2,1)} %get-tuple-element.27) | copy-start | bytes 786436
  15.8 13.9 %collective-permute-start.3 = (bf16[264,1024]{1,0:T(8,128)(2,1)S(1)}, bf16[264,1024]{1,0:T(8,128)(2,1)S(1)}, u32[]{:S(2)}, u32[]{:S(2)}) collective-permute-start(bf16[264,1024]{1,0:T(8,128)(2,1)S(1)} %concatenate.6.refs_0_.refs_2_), channel_id=1, source_target_pairs={{0,2},{1,3},{2,4},{3,5},{4,6},{5,7},{6,0},{7,1},{8,10},{9,11},{10,... | collective-permute-start | bytes 1622024 | tf_op jit(solution)/shard_map/ppermute | solution.py:31
  17.1 12.6 %collective-permute-start.4 = (bf16[264,1024]{1,0:T(8,128)(2,1)S(1)}, bf16[264,1024]{1,0:T(8,128)(2,1)S(1)}, u32[]{:S(2)}, u32[]{:S(2)}) collective-permute-start(bf16[264,1024]{1,0:T(8,128)(2,1)S(1)} %concatenate.6.refs_0_.refs_2_), channel_id=1, source_target_pairs={{0,6},{1,7},{2,0},{3,1},{4,2},{5,3},{6,4},{7,5},{8,14},{9,15},{10,... | collective-permute-start | bytes 1622024 | tf_op jit(solution)/shard_map/ppermute | solution.py:31
  18.6 11.0 %collective-permute-start.5 = (bf16[200,1024]{1,0:T(8,128)(2,1)S(1)}, bf16[200,1024]{1,0:T(8,128)(2,1)S(1)}, u32[]{:S(2)}, u32[]{:S(2)}) collective-permute-start(bf16[200,1024]{1,0:T(8,128)(2,1)S(1)} %slice.44), channel_id=1, source_target_pairs={{0,32},{1,97},{2,34},{3,99},{4,36},{5,101},{6,38},{7,103},{8,40},{... | collective-permute-start | bytes 1228808 | tf_op jit(solution)/shard_map/ppermute | solution.py:31
  21.4 22.5 %collective-permute-start.7 = (bf16[2,128,1024]{2,1,0:T(8,128)(2,1)S(1)}, bf16[2,128,1024]{2,1,0:T(8,128)(2,1)S(1)}, u32[]{:S(2)}, u32[]{:S(2)}) collective-permute-start(bf16[2,128,1024]{2,1,0:T(8,128)(2,1)S(1)} %fusion), channel_id=1, source_target_pairs={{0,128},{1,129},{2,130},{3,131},{4,132},{5,133},{6,134},{7,135},{8... | collective-permute-start | bytes 1572872 | tf_op jit(solution)/shard_map/ppermute | solution.py:31
  29.8 23.0 %collective-permute-start.11 = (bf16[528,1024]{1,0:T(8,128)(2,1)S(1)}, bf16[528,1024]{1,0:T(8,128)(2,1)S(1)}, u32[]{:S(2)}, u32[]{:S(2)}) collective-permute-start(bf16[528,1024]{1,0:T(8,128)(2,1)S(1)} %get-tuple-element.34), channel_id=1, source_target_pairs={{0,32},{1,97},{2,34},{3,99},{4,36},{5,101},{6,38},{7,103},{8,40},{... | collective-permute-start | bytes 3244040 | tf_op jit(solution)/shard_map/ppermute | solution.py:31
  32.0 16.3 %collective-permute-start.9 = (bf16[264,1024]{1,0:T(8,128)(2,1)S(1)}, bf16[264,1024]{1,0:T(8,128)(2,1)S(1)}, u32[]{:S(2)}, u32[]{:S(2)}) collective-permute-start(bf16[264,1024]{1,0:T(8,128)(2,1)S(1)} %get-tuple-element.33.first_ref), channel_id=1, source_target_pairs={{0,2},{1,7},{2,4},{3,1},{4,6},{5,3},{6,0},{7,5},{8,10},{9,15},{10,... | collective-permute-start | bytes 1622024 | tf_op jit(solution)/shard_map/ppermute | solution.py:31
  34.4 13.9 %collective-permute-start.6 = (bf16[2,128,1024]{2,1,0:T(8,128)(2,1)S(1)}, bf16[2,128,1024]{2,1,0:T(8,128)(2,1)S(1)}, u32[]{:S(2)}, u32[]{:S(2)}) collective-permute-start(bf16[2,128,1024]{2,1,0:T(8,128)(2,1)S(1)} %fusion.1.right_own.refs_0_), channel_id=1, source_target_pairs={{0,1},{1,0},{2,3},{3,2},{4,5},{5,4},{6,7},{7,6},{8,9},{9,8},{10,11... | collective-permute-start | bytes 1572872 | tf_op jit(solution)/shard_map/ppermute | solution.py:31
  43.9 5.9 %collective-permute-start.8 = (bf16[2,128,1024]{2,1,0:T(8,128)(2,1)S(1)}, bf16[2,128,1024]{2,1,0:T(8,128)(2,1)S(1)}, u32[]{:S(2)}, u32[]{:S(2)}) collective-permute-start(bf16[2,128,1024]{2,1,0:T(8,128)(2,1)S(1)} %shard_map.48.refs_0_.refs_2_), channel_id=1, source_target_pairs={{0,1},{1,0},{2,3},{3,2},{4,5},{5,4},{6,7},{7,6},{8,9},{9,8},{10,11... | collective-permute-start | bytes 1572872 | tf_op jit(solution)/shard_map/ppermute | solution.py:31
  48.3 9.4 %collective-permute-start.10 = (bf16[264,1024]{1,0:T(8,128)(2,1)S(1)}, bf16[264,1024]{1,0:T(8,128)(2,1)S(1)}, u32[]{:S(2)}, u32[]{:S(2)}) collective-permute-start(bf16[264,1024]{1,0:T(8,128)(2,1)S(1)} %collective-permute-done.9.refs_5_), channel_id=1, source_target_pairs={{0,32},{1,97},{2,34},{3,99},{4,36},{5,101},{6,38},{7,103},{8,40},{... | collective-permute-start | bytes 1622024 | tf_op jit(solution)/shard_map/ppermute | solution.py:31
  52.8 8.1 %copy-start = (f32[1,128]{1,0:T(1,128)S(1)}, f32[1,128]{1,0:T(1,128)}, u32[]{:S(2)}) copy-start(f32[1,128]{1,0:T(1,128)} %get-tuple-element.44.coulomb_ref) | copy-start | bytes 1540
  58.9 2.0 %collective-permute-start.12 = (bf16[2,128,1024]{2,1,0:T(8,128)(2,1)S(1)}, bf16[2,128,1024]{2,1,0:T(8,128)(2,1)S(1)}, u32[]{:S(2)}, u32[]{:S(2)}) collective-permute-start(bf16[2,128,1024]{2,1,0:T(8,128)(2,1)S(1)} %get-tuple-element.43), channel_id=1, source_target_pairs={{0,1},{1,0},{2,3},{3,2},{4,5},{5,4},{6,7},{7,6},{8,9},{9,8},{10,11... | collective-permute-start | bytes 1572872 | tf_op jit(solution)/shard_map/ppermute | solution.py:31
  84.6 3.3 %collective-permute-start.13 = (f32[2,32,1024]{2,1,0:T(8,128)S(1)}, f32[2,32,1024]{2,1,0:T(8,128)S(1)}, u32[]{:S(2)}, u32[]{:S(2)}) collective-permute-start(f32[2,32,1024]{2,1,0:T(8,128)S(1)} %get-tuple-element.46), channel_id=1, source_target_pairs={{0,1},{1,0},{2,3},{3,2},{4,5},{5,4},{6,7},{7,6},{8,9},{9,8},{10,11... | collective-permute-start | bytes 786440 | tf_op jit(solution)/shard_map/ppermute | solution.py:31

commit v9 on v8

--- a/solution.py
+++ b/solution.py
@@ -59,13 +59,20 @@
     return pltpu.CompilerParams(vmem_limit_bytes=mib << 20)
 
 
-def prologue_kernel(factors_in, pattern_in, coulomb_in, masked_ref, whole_ref, own_ref, factors, pattern, coulomb, sems):
+def prologue_kernel(
+    factors_in, pattern_in, coulomb_in, green_in, masked_ref, whole_ref, own_ref, left_ref,
+    factors, pattern, coulomb, green, sems,
+):
     copies = [
         pltpu.make_async_copy(factors_in, factors, sems.at[0]),
         pltpu.make_async_copy(pattern_in, pattern, sems.at[1]),
         pltpu.make_async_copy(coulomb_in, coulomb, sems.at[2]),
     ]
-    for copy in copies:
+    greens = [
+        pltpu.make_async_copy(green_in.at[t], green.at[t], sems.at[3 + t])
+        for t in range(green_in.shape[0])
+    ]
+    for copy in copies + greens:
         copy.start()
     for copy in copies:
         copy.wait()
@@ -95,9 +102,14 @@
     row = jnp.concatenate([high, middle, low, zero], axis=1)
     rows = jnp.broadcast_to(row.astype(F32), (8, orb)).astype(BF16)
     whole_ref[pl.ds(HALF, 8), :] = rows
-
-
-def prologue(factors, pattern, coulomb):
+    for t, copy in enumerate(greens):
+        copy.wait()
+        left_ref[t] = lax.dot_general(
+            masked_ref[...], green[t], NN, preferred_element_type=F32
+        ).astype(BF16)
+
+
+def prologue(factors, pattern, coulomb, green):
     own, orb = factors.shape
     return pl.pallas_call(
         prologue_kernel,
@@ -105,17 +117,19 @@
             jax.ShapeDtypeStruct((own, orb), BF16),
             jax.ShapeDtypeStruct((HALF + 8, orb), BF16),
             jax.ShapeDtypeStruct((1, own), F32),
+            jax.ShapeDtypeStruct((green.shape[0], own, orb), BF16),
         ],
-        in_specs=[pl.BlockSpec(memory_space=pltpu.HBM)] * 3,
-        out_specs=[VMEM] * 3,
+        in_specs=[pl.BlockSpec(memory_space=pltpu.HBM)] * 4,
+        out_specs=[VMEM] * 4,
         scratch_shapes=[
             pltpu.VMEM((own, orb), BF16),
             pltpu.VMEM(pattern.shape, jnp.int32),
             pltpu.VMEM((1, own), F32),
-            pltpu.SemaphoreType.DMA((3,)),
+            pltpu.VMEM(green.shape, BF16),
+            pltpu.SemaphoreType.DMA((3 + green.shape[0],)),
         ],
-        compiler_params=params(58),
-    )(factors, pattern, coulomb[None, :])
+        compiler_params=params(16),
+    )(*[pltpu.with_memory_space_constraint(v, pltpu.HBM) for v in (factors, pattern, coulomb[None, :], green)])
 
 
 def mix_kernel(west_ref, east_ref, onward_ref, both_ref):
@@ -313,14 +327,12 @@
     times, orb, _ = green.shape
     own = factors.shape[0]
     barrier = lax.optimization_barrier
-    masked, whole, coulomb = prologue(factors, pattern, coulomb)
+    masked, whole, coulomb, left = prologue(factors, pattern, coulomb, green)
 
     beyond = two_along_z(whole)
     below = along_z(whole, 1)
     above = along_z(whole, -1)
-    left = jnp.einsum("qo,tok->tqk", masked, green, preferred_element_type=F32).astype(BF16)
-    below, left = barrier((below, left))
-    left = along_z(left, 4)
+    left = two_along_z(left)
 
     blocks = [whole, below, above, beyond]
     weights = [block[HALF : HALF + 1] for block in blocks] + [jnp.zeros((4, orb), BF16)]
@@ -338,7 +350,7 @@
     far = split_x(onward)
     sides_q = other_parity(both)
     far_q = other_parity(far)
-    left = after(left, onward)
+    left = two_along_z(left)
     left_other = other_core(left)
 
     rights, lefts = (right, right_other), (left, left_other)

time: 88.8 us -> 93.1 us (1.048)
  waiting for transfers between devices: 15.8 us -> 27 us
  blocking collectives: 22.5 us -> 19.4 us
  matrix products: 6.72 us -> 3.69 us
  starting transfers between devices: 30.5 us -> 28.9 us
    ppermute x14 -> x15, waiting for transfers between devices: 15.8 us -> 27 us  [send(): return lax.ppermute(value, BOTH, sorted(pairs))]
    all_to_all x1, blocking collectives: 22.5 us -> 19.4 us  [local(): lax.all_to_all(part, 'aux', 0, 0, axis_index_groups=groups, tiled=True)]
    dot_general x1 -> x0, matrix products: 3.03 us -> none  [local(): jnp.einsum('qo,tok->tqk', masked, green, preferred_element_type=F32)]
    ppermute x14 -> x15, starting transfers between devices: 30.5 us -> 28.9 us  [send(): return lax.ppermute(value, BOTH, sorted(pairs))]
    pallas_call x1, Pallas kernels: 1.9 us -> 2.85 us  [prologue(): pl.pallas_call(prologue_kernel, out_shape=[jax.ShapeDtypeStruct((own, orb...]
  transfers between devices with their start and end apart: 14 -> 15, of which waited for: 5 -> 8; matrix products, arithmetic and copies ran while one was open for 8% -> 4% of each run, Pallas kernels for 9% -> 8%
where the time goes in v9:
time: 93.1 us; the launch traced here: 92.9 us
  starting transfers between devices  28.9 us (31%)
  waiting for transfers between devices  27 us (29%)
  blocking collectives  19.4 us (21%)
  Pallas kernels  13.5 us (15%)
  matrix products  3.69 us (4%)
    ppermute x15, starting transfers between devices, send(): return lax.ppermute(value, BOTH, sorted(pairs))  28.9 us
    ppermute x15, waiting for transfers between devices, send(): return lax.ppermute(value, BOTH, sorted(pairs))  27 us
    all_to_all x1, blocking collectives, local(): lax.all_to_all(part, 'aux', 0, 0, axis_index_groups=groups, tiled=True)  19.4 us
    pallas_call x4, Pallas kernels, chunk(): pl.pallas_call(functools.partial(chunk_kernel, tuple(pieces), len(sides),...  7.19 us
    dot_general x1, matrix products, local(): jnp.einsum('qo,tko->tqk', masked, green, preferred_element_type=F32)  3.69 us
    pallas_call x1, Pallas kernels, prologue(): pl.pallas_call(prologue_kernel, out_shape=[jax.ShapeDtypeStruct((own, orb...  2.85 us
  transfers between devices with their start and end apart: 15, of which 8 were waited for; matrix products, arithmetic and copies ran while one was open for 4% of the time, Pallas kernels for 8%

profile of v9, /device:TPU:1, one launch (start us, length us, event | category | flops | bytes accessed | tf_op | source)
XLA Modules:
  0.0 92.9 jit_solution(15002326486237961309)
XLA Ops:
  0.0 2.9 %shard_map.46 = (bf16[128,1024]{1,0:T(8,128)(2,1)S(1)}, bf16[72,1024]{1,0:T(8,128)(2,1)S(1)}, f32[1,128]{1,0:T(1,128)S(1)}, bf16[2,128,1024]{2,1,0:T(8,128)(2,1)S(1)}) custom-call(bf16[128,1024]{1,0:T(8,128)(2,1)} %factors_in.1, s32[1,8]{1,0:T(1,128)} %pattern_in.1, f32[1,128]{1,0:T(1,128)} %bitcast.7, bf16[2,1024,1024]{2,1,0:T(8,128)(2,1)} %green_in.1), custom_call_target="tpu_custom_call" | custom-call | tf_op jit(solution)/shard_map/pallas_call | solution.py:114
  2.9 6.9 %collective-permute-start.7 = (bf16[2,128,1024]{2,1,0:T(8,128)(2,1)S(1)}, bf16[2,128,1024]{2,1,0:T(8,128)(2,1)S(1)}, u32[]{:S(2)}, u32[]{:S(2)}) collective-permute-start(bf16[2,128,1024]{2,1,0:T(8,128)(2,1)S(1)} %get-tuple-element.28), channel_id=1, source_target_pairs={{0,16},{1,145},{2,18},{3,147},{4,20},{5,149},{6,22},{7,151},{8,24}... | collective-permute-start | bytes 1572872 | tf_op jit(solution)/shard_map/ppermute | solution.py:31
  9.8 0.7 collective-permute-start
  10.5 1.9 %collective-permute-start.1 = (bf16[72,1024]{1,0:T(8,128)(2,1)S(1)}, bf16[72,1024]{1,0:T(8,128)(2,1)S(1)}, u32[]{:S(2)}, u32[]{:S(2)}) collective-permute-start(bf16[72,1024]{1,0:T(8,128)(2,1)S(1)} %get-tuple-element.25), channel_id=1, source_target_pairs={{0,152},{1,153},{2,154},{3,155},{4,156},{5,157},{6,158},{7,159},{8... | collective-permute-start | bytes 442376 | tf_op jit(solution)/shard_map/ppermute | solution.py:31
  12.5 0.0 collective-permute-start.2
  12.5 8.4 %collective-permute-done = bf16[72,1024]{1,0:T(8,128)(2,1)S(1)} collective-permute-done((bf16[72,1024]{1,0:T(8,128)(2,1)S(1)}, bf16[72,1024]{1,0:T(8,128)(2,1)S(1)}, u32[]{:S(2)}, u32[]{:S(2)}) %collective-permute-start) | collective-permute-done | bytes 147488 | tf_op jit(solution)/shard_map/ppermute | solution.py:31
  20.9 5.4 %collective-permute-done.1 = bf16[72,1024]{1,0:T(8,128)(2,1)S(1)} collective-permute-done((bf16[72,1024]{1,0:T(8,128)(2,1)S(1)}, bf16[72,1024]{1,0:T(8,128)(2,1)S(1)}, u32[]{:S(2)}, u32[]{:S(2)}) %collective-permute-start.1) | collective-permute-done | bytes 147488 | tf_op jit(solution)/shard_map/ppermute | solution.py:31
  26.4 1.5 %collective-permute-done.2 = bf16[72,1024]{1,0:T(8,128)(2,1)S(1)} collective-permute-done((bf16[72,1024]{1,0:T(8,128)(2,1)S(1)}, bf16[72,1024]{1,0:T(8,128)(2,1)S(1)}, u32[]{:S(2)}, u32[]{:S(2)}) %collective-permute-start.2) | collective-permute-done | bytes 147488 | tf_op jit(solution)/shard_map/ppermute | solution.py:31
  27.9 0.1 concatenate.6.refs_0_.refs_2_
  28.0 1.3 %collective-permute-start.3 = (bf16[264,1024]{1,0:T(8,128)(2,1)S(1)}, bf16[264,1024]{1,0:T(8,128)(2,1)S(1)}, u32[]{:S(2)}, u32[]{:S(2)}) collective-permute-start(bf16[264,1024]{1,0:T(8,128)(2,1)S(1)} %concatenate.6.refs_0_.refs_2_), channel_id=1, source_target_pairs={{0,2},{1,3},{2,4},{3,5},{4,6},{5,7},{6,0},{7,1},{8,10},{9,11},{10,... | collective-permute-start | bytes 1622024 | tf_op jit(solution)/shard_map/ppermute | solution.py:31
  29.3 1.5 %collective-permute-start.4 = (bf16[264,1024]{1,0:T(8,128)(2,1)S(1)}, bf16[264,1024]{1,0:T(8,128)(2,1)S(1)}, u32[]{:S(2)}, u32[]{:S(2)}) collective-permute-start(bf16[264,1024]{1,0:T(8,128)(2,1)S(1)} %concatenate.6.refs_0_.refs_2_), channel_id=1, source_target_pairs={{0,6},{1,7},{2,0},{3,1},{4,2},{5,3},{6,4},{7,5},{8,14},{9,15},{10,... | collective-permute-start | bytes 1622024 | tf_op jit(solution)/shard_map/ppermute | solution.py:31
  30.8 2.8 %collective-permute-start.5 = (bf16[200,1024]{1,0:T(8,128)(2,1)S(1)}, bf16[200,1024]{1,0:T(8,128)(2,1)S(1)}, u32[]{:S(2)}, u32[]{:S(2)}) collective-permute-start(bf16[200,1024]{1,0:T(8,128)(2,1)S(1)} %slice.46), channel_id=1, source_target_pairs={{0,32},{1,97},{2,34},{3,99},{4,36},{5,101},{6,38},{7,103},{8,40},{... | collective-permute-start | bytes 1228808 | tf_op jit(solution)/shard_map/ppermute | solution.py:31
  33.6 0.0 collective-permute-done.7
  33.6 4.0 %collective-permute-start.8 = (bf16[2,128,1024]{2,1,0:T(8,128)(2,1)S(1)}, bf16[2,128,1024]{2,1,0:T(8,128)(2,1)S(1)}, u32[]{:S(2)}, u32[]{:S(2)}) collective-permute-start(bf16[2,128,1024]{2,1,0:T(8,128)(2,1)S(1)} %collective-permute-done.7), channel_id=1, source_target_pairs={{0,16},{1,145},{2,18},{3,147},{4,20},{5,149},{6,22},{7,151},{8,24}... | collective-permute-start | bytes 1572872 | tf_op jit(solution)/shard_map/ppermute | solution.py:31
  37.6 3.7 %fusion.right_own.refs_0_ = bf16[2,128,1024]{2,1,0:T(8,128)(2,1)S(1)} fusion(bf16[2,1024,1024]{2,1,0:T(8,128)(2,1)} %green_in.1, bf16[128,1024]{1,0:T(8,128)(2,1)S(1)} %get-tuple-element.26), kind=kOutput, calls=%fused_computation.1 | convolution fusion | flops 537133056 | bytes 4980736 | tf_op jit(solution)/shard_map/qo,tko->tqk/dot_general | solution.py:346
  41.3 0.0 collective-permute-done.5
  41.4 1.2 %collective-permute-done.3.west_ref.refs_0_.refs_2_ = bf16[264,1024]{1,0:T(8,128)(2,1)S(1)} collective-permute-done((bf16[264,1024]{1,0:T(8,128)(2,1)S(1)}, bf16[264,1024]{1,0:T(8,128)(2,1)S(1)}, u32[]{:S(2)}, u32[]{:S(2)}) %collective-permute-start.3) | collective-permute-done | bytes 540704 | tf_op jit(solution)/shard_map/ppermute | solution.py:31
  42.5 0.0 collective-permute-done.4.east_ref.refs_1_.refs_3_
  42.5 0.1 shard_map.47
  42.7 2.8 %collective-permute-start.12 = (bf16[528,1024]{1,0:T(8,128)(2,1)S(1)}, bf16[528,1024]{1,0:T(8,128)(2,1)S(1)}, u32[]{:S(2)}, u32[]{:S(2)}) collective-permute-start(bf16[528,1024]{1,0:T(8,128)(2,1)S(1)} %get-tuple-element.32), channel_id=1, source_target_pairs={{0,32},{1,97},{2,34},{3,99},{4,36},{5,101},{6,38},{7,103},{8,40},{... | collective-permute-start | bytes 3244040 | tf_op jit(solution)/shard_map/ppermute | solution.py:31
  45.5 2.4 %collective-permute-start.10 = (bf16[264,1024]{1,0:T(8,128)(2,1)S(1)}, bf16[264,1024]{1,0:T(8,128)(2,1)S(1)}, u32[]{:S(2)}, u32[]{:S(2)}) collective-permute-start(bf16[264,1024]{1,0:T(8,128)(2,1)S(1)} %get-tuple-element.31), channel_id=1, source_target_pairs={{0,2},{1,7},{2,4},{3,1},{4,6},{5,3},{6,0},{7,5},{8,10},{9,15},{10,... | collective-permute-start | bytes 1622024 | tf_op jit(solution)/shard_map/ppermute | solution.py:31
  47.8 0.0 collective-permute-start.6
  47.8 0.0 collective-permute-done.8.refs_0_.refs_2_
  47.8 0.5 collective-permute-start.9
  48.3 5.8 %collective-permute-done.10.refs_5_ = bf16[264,1024]{1,0:T(8,128)(2,1)S(1)} collective-permute-done((bf16[264,1024]{1,0:T(8,128)(2,1)S(1)}, bf16[264,1024]{1,0:T(8,128)(2,1)S(1)}, u32[]{:S(2)}, u32[]{:S(2)}) %collective-permute-start.10) | collective-permute-done | bytes 540704 | tf_op jit(solution)/shard_map/ppermute | solution.py:31
  54.1 0.1 collective-permute-start.11
  54.2 0.0 collective-permute-done.6.right_other.refs_1_
  54.2 0.7 shard_map.48.refs_4_
  55.0 0.8 shard_map.49.refs_4_
  55.7 0.0 collective-permute-done.9.refs_1_.refs_3_
  55.7 1.5 %shard_map.50 = (f32[2,128,1024]{2,1,0:T(8,128)S(1)}, f32[2,128,1024]{2,1,0:T(8,128)S(1)}) custom-call(bf16[2,128,1024]{2,1,0:T(8,128)(2,1)S(1)} %collective-permute-done.8.refs_0_.refs_2_, bf16[2,128,1024]{2,1,0:T(8,128)(2,1)S(1)} %collective-permute-done.9.refs_1_.refs_3_, bf16[264,1024]{1,0:T(8,128)(2,1)S(1)} %concatenate.6.refs_0_.refs_2_, ...), custom_call_target="tpu_custom_call" | custom-call | flops 1073741824 | bytes 2097152 | tf_op jit(solution)/shard_map/pallas_call | solution.py:265
  57.2 1.5 %shard_map.51 = (f32[2,128,1024]{2,1,0:T(8,128)S(1)}, f32[2,128,1024]{2,1,0:T(8,128)S(1)}) custom-call(bf16[2,128,1024]{2,1,0:T(8,128)(2,1)S(1)} %collective-permute-done.8.refs_0_.refs_2_, bf16[2,128,1024]{2,1,0:T(8,128)(2,1)S(1)} %collective-permute-done.9.refs_1_.refs_3_, ...), custom_call_target="tpu_custom_call", output_to_operand_aliasing={{0}: (5, {}), {1}: (6, {})} | custom-call | flops 1073741824 | bytes 2097152 | tf_op jit(solution)/shard_map/pallas_call | solution.py:265
  58.7 0.0 collective-permute-done.12.refs_4_
  58.7 3.0 %shard_map.52 = (f32[2,128,1024]{2,1,0:T(8,128)S(1)}, f32[2,128,1024]{2,1,0:T(8,128)S(1)}) custom-call(bf16[2,128,1024]{2,1,0:T(8,128)(2,1)S(1)} %fusion.right_own.refs_0_, bf16[2,128,1024]{2,1,0:T(8,128)(2,1)S(1)} %collective-permute-done.6.right_other.refs_1_, ...), custom_call_target="tpu_custom_call", output_to_operand_aliasing={{0}: (6, {}), {1}: (7, {})} | custom-call | flops 1610612736 | bytes 2097152 | tf_op jit(solution)/shard_map/pallas_call | solution.py:265
  61.8 2.0 %collective-permute-done.11.refs_4_.refs_6_ = bf16[264,1024]{1,0:T(8,128)(2,1)S(1)} collective-permute-done((bf16[264,1024]{1,0:T(8,128)(2,1)S(1)}, bf16[264,1024]{1,0:T(8,128)(2,1)S(1)}, u32[]{:S(2)}, u32[]{:S(2)}) %collective-permute-start.11) | collective-permute-done | bytes 540704 | tf_op jit(solution)/shard_map/ppermute | solution.py:31
  63.8 1.2 %shard_map.53 = (f32[2,128,1024]{2,1,0:T(8,128)S(1)}, bf16[2,128,1024]{2,1,0:T(8,128)(2,1)S(1)}) custom-call(bf16[2,128,1024]{2,1,0:T(8,128)(2,1)S(1)} %fusion.right_own.refs_0_, bf16[2,128,1024]{2,1,0:T(8,128)(2,1)S(1)} %collective-permute-done.6.right_other.refs_1_, ...), custom_call_target="tpu_custom_call", output_to_operand_aliasing={{0}: (5, {})} | custom-call | flops 536870912 | bytes 2097152 | tf_op jit(solution)/shard_map/pallas_call | solution.py:265
  65.0 2.0 %collective-permute-start.13 = (bf16[2,128,1024]{2,1,0:T(8,128)(2,1)S(1)}, bf16[2,128,1024]{2,1,0:T(8,128)(2,1)S(1)}, u32[]{:S(2)}, u32[]{:S(2)}) collective-permute-start(bf16[2,128,1024]{2,1,0:T(8,128)(2,1)S(1)} %get-tuple-element.41), channel_id=1, source_target_pairs={{0,1},{1,0},{2,3},{3,2},{4,5},{5,4},{6,7},{7,6},{8,9},{9,8},{10,11... | collective-permute-start | bytes 1572872 | tf_op jit(solution)/shard_map/ppermute | solution.py:31
  66.9 1.5 %collective-permute-done.13.got_ref = bf16[2,128,1024]{2,1,0:T(8,128)(2,1)S(1)} collective-permute-done((bf16[2,128,1024]{2,1,0:T(8,128)(2,1)S(1)}, bf16[2,128,1024]{2,1,0:T(8,128)(2,1)S(1)}, u32[]{:S(2)}, u32[]{:S(2)}) %collective-permute-start.13) | collective-permute-done | bytes 524320 | tf_op jit(solution)/shard_map/ppermute | solution.py:31
  68.5 0.3 shard_map.54
  68.8 19.4 %all_to_all.5.part_ref = bf16[16,2,64,128]{3,2,1,0:T(8,128)(2,1)S(1)} all-to-all(bf16[16,2,64,128]{3,2,1,0:T(8,128)(2,1)S(1)} %shard_map.54), channel_id=1, replica_groups={{0,2,4,6,8,10,12,14,16,18,20,22,24,26,28,30},{1,3,5,7,9,11,13,15,17,19,..., dimensions={0} | all-to-all | bytes 1048576 | tf_op jit(solution)/shard_map/all_to_all | solution.py:376
  88.2 0.8 shard_map.55
  89.0 2.0 %collective-permute-start.14 = (f32[2,32,1024]{2,1,0:T(8,128)S(1)}, f32[2,32,1024]{2,1,0:T(8,128)S(1)}, u32[]{:S(2)}, u32[]{:S(2)}) collective-permute-start(f32[2,32,1024]{2,1,0:T(8,128)S(1)} %get-tuple-element.44), channel_id=1, source_target_pairs={{0,1},{1,0},{2,3},{3,2},{4,5},{5,4},{6,7},{7,6},{8,9},{9,8},{10,11... | collective-permute-start | bytes 786440 | tf_op jit(solution)/shard_map/ppermute | solution.py:31
  91.0 1.2 %collective-permute-done.14.got_ref = f32[2,32,1024]{2,1,0:T(8,128)S(1)} collective-permute-done((f32[2,32,1024]{2,1,0:T(8,128)S(1)}, f32[2,32,1024]{2,1,0:T(8,128)S(1)}, u32[]{:S(2)}, u32[]{:S(2)}) %collective-permute-start.14) | collective-permute-done | bytes 262176 | tf_op jit(solution)/shard_map/ppermute | solution.py:31
  92.2 0.8 shard_map.56
  (12 shorter events, 0.1 us)
Async XLA Ops:
  2.9 30.7 %collective-permute-start.7 = (bf16[2,128,1024]{2,1,0:T(8,128)(2,1)S(1)}, bf16[2,128,1024]{2,1,0:T(8,128)(2,1)S(1)}, u32[]{:S(2)}, u32[]{:S(2)}) collective-permute-start(bf16[2,128,1024]{2,1,0:T(8,128)(2,1)S(1)} %get-tuple-element.28), channel_id=1, source_target_pairs={{0,16},{1,145},{2,18},{3,147},{4,20},{5,149},{6,22},{7,151},{8,24}... | collective-permute-start | bytes 1572872 | tf_op jit(solution)/shard_map/ppermute | solution.py:31
  9.8 11.1 %collective-permute-start = (bf16[72,1024]{1,0:T(8,128)(2,1)S(1)}, bf16[72,1024]{1,0:T(8,128)(2,1)S(1)}, u32[]{:S(2)}, u32[]{:S(2)}) collective-permute-start(bf16[72,1024]{1,0:T(8,128)(2,1)S(1)} %get-tuple-element.25), channel_id=1, source_target_pairs={{0,8},{1,9},{2,10},{3,11},{4,12},{5,13},{6,14},{7,15},{8,16},{9,17... | collective-permute-start | bytes 442376 | tf_op jit(solution)/shard_map/ppermute | solution.py:31
  10.5 15.8 %collective-permute-start.1 = (bf16[72,1024]{1,0:T(8,128)(2,1)S(1)}, bf16[72,1024]{1,0:T(8,128)(2,1)S(1)}, u32[]{:S(2)}, u32[]{:S(2)}) collective-permute-start(bf16[72,1024]{1,0:T(8,128)(2,1)S(1)} %get-tuple-element.25), channel_id=1, source_target_pairs={{0,152},{1,153},{2,154},{3,155},{4,156},{5,157},{6,158},{7,159},{8... | collective-permute-start | bytes 442376 | tf_op jit(solution)/shard_map/ppermute | solution.py:31
  12.5 15.4 %collective-permute-start.2 = (bf16[72,1024]{1,0:T(8,128)(2,1)S(1)}, bf16[72,1024]{1,0:T(8,128)(2,1)S(1)}, u32[]{:S(2)}, u32[]{:S(2)}) collective-permute-start(bf16[72,1024]{1,0:T(8,128)(2,1)S(1)} %get-tuple-element.25), channel_id=1, source_target_pairs={{0,16},{1,145},{2,18},{3,147},{4,20},{5,149},{6,22},{7,151},{8,24}... | collective-permute-start | bytes 442376 | tf_op jit(solution)/shard_map/ppermute | solution.py:31
  28.0 14.6 %collective-permute-start.3 = (bf16[264,1024]{1,0:T(8,128)(2,1)S(1)}, bf16[264,1024]{1,0:T(8,128)(2,1)S(1)}, u32[]{:S(2)}, u32[]{:S(2)}) collective-permute-start(bf16[264,1024]{1,0:T(8,128)(2,1)S(1)} %concatenate.6.refs_0_.refs_2_), channel_id=1, source_target_pairs={{0,2},{1,3},{2,4},{3,5},{4,6},{5,7},{6,0},{7,1},{8,10},{9,11},{10,... | collective-permute-start | bytes 1622024 | tf_op jit(solution)/shard_map/ppermute | solution.py:31
  29.3 13.3 %collective-permute-start.4 = (bf16[264,1024]{1,0:T(8,128)(2,1)S(1)}, bf16[264,1024]{1,0:T(8,128)(2,1)S(1)}, u32[]{:S(2)}, u32[]{:S(2)}) collective-permute-start(bf16[264,1024]{1,0:T(8,128)(2,1)S(1)} %concatenate.6.refs_0_.refs_2_), channel_id=1, source_target_pairs={{0,6},{1,7},{2,0},{3,1},{4,2},{5,3},{6,4},{7,5},{8,14},{9,15},{10,... | collective-permute-start | bytes 1622024 | tf_op jit(solution)/shard_map/ppermute | solution.py:31
  30.8 10.6 %collective-permute-start.5 = (bf16[200,1024]{1,0:T(8,128)(2,1)S(1)}, bf16[200,1024]{1,0:T(8,128)(2,1)S(1)}, u32[]{:S(2)}, u32[]{:S(2)}) collective-permute-start(bf16[200,1024]{1,0:T(8,128)(2,1)S(1)} %slice.46), channel_id=1, source_target_pairs={{0,32},{1,97},{2,34},{3,99},{4,36},{5,101},{6,38},{7,103},{8,40},{... | collective-permute-start | bytes 1228808 | tf_op jit(solution)/shard_map/ppermute | solution.py:31
  33.6 14.2 %collective-permute-start.8 = (bf16[2,128,1024]{2,1,0:T(8,128)(2,1)S(1)}, bf16[2,128,1024]{2,1,0:T(8,128)(2,1)S(1)}, u32[]{:S(2)}, u32[]{:S(2)}) collective-permute-start(bf16[2,128,1024]{2,1,0:T(8,128)(2,1)S(1)} %collective-permute-done.7), channel_id=1, source_target_pairs={{0,16},{1,145},{2,18},{3,147},{4,20},{5,149},{6,22},{7,151},{8,24}... | collective-permute-start | bytes 1572872 | tf_op jit(solution)/shard_map/ppermute | solution.py:31
  42.7 16.1 %collective-permute-start.12 = (bf16[528,1024]{1,0:T(8,128)(2,1)S(1)}, bf16[528,1024]{1,0:T(8,128)(2,1)S(1)}, u32[]{:S(2)}, u32[]{:S(2)}) collective-permute-start(bf16[528,1024]{1,0:T(8,128)(2,1)S(1)} %get-tuple-element.32), channel_id=1, source_target_pairs={{0,32},{1,97},{2,34},{3,99},{4,36},{5,101},{6,38},{7,103},{8,40},{... | collective-permute-start | bytes 3244040 | tf_op jit(solution)/shard_map/ppermute | solution.py:31
  45.5 8.7 %collective-permute-start.10 = (bf16[264,1024]{1,0:T(8,128)(2,1)S(1)}, bf16[264,1024]{1,0:T(8,128)(2,1)S(1)}, u32[]{:S(2)}, u32[]{:S(2)}) collective-permute-start(bf16[264,1024]{1,0:T(8,128)(2,1)S(1)} %get-tuple-element.31), channel_id=1, source_target_pairs={{0,2},{1,7},{2,4},{3,1},{4,6},{5,3},{6,0},{7,5},{8,10},{9,15},{10,... | collective-permute-start | bytes 1622024 | tf_op jit(solution)/shard_map/ppermute | solution.py:31
  47.8 6.4 %collective-permute-start.6 = (bf16[2,128,1024]{2,1,0:T(8,128)(2,1)S(1)}, bf16[2,128,1024]{2,1,0:T(8,128)(2,1)S(1)}, u32[]{:S(2)}, u32[]{:S(2)}) collective-permute-start(bf16[2,128,1024]{2,1,0:T(8,128)(2,1)S(1)} %fusion.right_own.refs_0_), channel_id=1, source_target_pairs={{0,1},{1,0},{2,3},{3,2},{4,5},{5,4},{6,7},{7,6},{8,9},{9,8},{10,11... | collective-permute-start | bytes 1572872 | tf_op jit(solution)/shard_map/ppermute | solution.py:31
  47.8 7.9 %collective-permute-start.9 = (bf16[2,128,1024]{2,1,0:T(8,128)(2,1)S(1)}, bf16[2,128,1024]{2,1,0:T(8,128)(2,1)S(1)}, u32[]{:S(2)}, u32[]{:S(2)}) collective-permute-start(bf16[2,128,1024]{2,1,0:T(8,128)(2,1)S(1)} %collective-permute-done.8.refs_0_.refs_2_), channel_id=1, source_target_pairs={{0,1},{1,0},{2,3},{3,2},{4,5},{5,4},{6,7},{7,6},{8,9},{9,8},{10,11... | collective-permute-start | bytes 1572872 | tf_op jit(solution)/shard_map/ppermute | solution.py:31
  54.1 9.7 %collective-permute-start.11 = (bf16[264,1024]{1,0:T(8,128)(2,1)S(1)}, bf16[264,1024]{1,0:T(8,128)(2,1)S(1)}, u32[]{:S(2)}, u32[]{:S(2)}) collective-permute-start(bf16[264,1024]{1,0:T(8,128)(2,1)S(1)} %collective-permute-done.10.refs_5_), channel_id=1, source_target_pairs={{0,32},{1,97},{2,34},{3,99},{4,36},{5,101},{6,38},{7,103},{8,40},{... | collective-permute-start | bytes 1622024 | tf_op jit(solution)/shard_map/ppermute | solution.py:31
  65.0 3.5 %collective-permute-start.13 = (bf16[2,128,1024]{2,1,0:T(8,128)(2,1)S(1)}, bf16[2,128,1024]{2,1,0:T(8,128)(2,1)S(1)}, u32[]{:S(2)}, u32[]{:S(2)}) collective-permute-start(bf16[2,128,1024]{2,1,0:T(8,128)(2,1)S(1)} %get-tuple-element.41), channel_id=1, source_target_pairs={{0,1},{1,0},{2,3},{3,2},{4,5},{5,4},{6,7},{7,6},{8,9},{9,8},{10,11... | collective-permute-start | bytes 1572872 | tf_op jit(solution)/shard_map/ppermute | solution.py:31
  89.0 3.2 %collective-permute-start.14 = (f32[2,32,1024]{2,1,0:T(8,128)S(1)}, f32[2,32,1024]{2,1,0:T(8,128)S(1)}, u32[]{:S(2)}, u32[]{:S(2)}) collective-permute-start(f32[2,32,1024]{2,1,0:T(8,128)S(1)} %get-tuple-element.44), channel_id=1, source_target_pairs={{0,1},{1,0},{2,3},{3,2},{4,5},{5,4},{6,7},{7,6},{8,9},{9,8},{10,11... | collective-permute-start | bytes 786440 | tf_op jit(solution)/shard_map/ppermute | solution.py:31

commit v10 on v8

--- a/solution.py
+++ b/solution.py
@@ -114,8 +114,8 @@
             pltpu.VMEM((1, own), F32),
             pltpu.SemaphoreType.DMA((3,)),
         ],
-        compiler_params=params(58),
-    )(factors, pattern, coulomb[None, :])
+        compiler_params=params(16),
+    )(*[pltpu.with_memory_space_constraint(v, pltpu.HBM) for v in (factors, pattern, coulomb[None, :])])
 
 
 def mix_kernel(west_ref, east_ref, onward_ref, both_ref):
@@ -247,7 +247,7 @@
         if not last:
             aliases[at + 1] = 1
     n = sum(piece[2] for piece in pieces)
-    flops = times * 2 * 2 * (2 * own) * n * orb
+    flops = times * 2 * 2 * (2 * own) * n * orb // 2
     return pl.pallas_call(
         functools.partial(
             chunk_kernel, tuple(pieces), len(sides), len(rows), bool(given), not acc
@@ -319,8 +319,7 @@
     below = along_z(whole, 1)
     above = along_z(whole, -1)
     left = jnp.einsum("qo,tok->tqk", masked, green, preferred_element_type=F32).astype(BF16)
-    below, left = barrier((below, left))
-    left = along_z(left, 4)
+    left = two_along_z(left)
 
     blocks = [whole, below, above, beyond]
     weights = [block[HALF : HALF + 1] for block in blocks] + [jnp.zeros((4, orb), BF16)]
@@ -338,7 +337,7 @@
     far = split_x(onward)
     sides_q = other_parity(both)
     far_q = other_parity(far)
-    left = after(left, onward)
+    left = two_along_z(left)
     left_other = other_core(left)
 
     rights, lefts = (right, right_other), (left, left_other)

time: 88.8 us -> 84.3 us (0.949)
  waiting for transfers between devices: 15.8 us -> 12 us
  starting transfers between devices: 30.5 us -> 31.9 us
  blocking collectives: 22.5 us -> 21.3 us
    ppermute x14 -> x15, waiting for transfers between devices: 15.8 us -> 12 us  [send(): return lax.ppermute(value, BOTH, sorted(pairs))]
    ppermute x14 -> x15, starting transfers between devices: 30.5 us -> 31.9 us  [send(): return lax.ppermute(value, BOTH, sorted(pairs))]
    all_to_all x1, blocking collectives: 22.5 us -> 21.3 us  [local(): lax.all_to_all(part, 'aux', 0, 0, axis_index_groups=groups, tiled=True)]
  transfers between devices with their start and end apart: 14 -> 15, of which waited for: 5 -> 4; matrix products, arithmetic and copies ran while one was open for 8% -> 8% of each run, Pallas kernels for 9% -> 9%
where the time goes in v10:
time: 84.3 us; the launch traced here: 84.2 us
  starting transfers between devices  31.9 us (38%)
  blocking collectives  21.3 us (25%)
  waiting for transfers between devices  12 us (14%)
  Pallas kernels  11.9 us (14%)
  matrix products  6.61 us (8%)
    ppermute x15, starting transfers between devices, send(): return lax.ppermute(value, BOTH, sorted(pairs))  31.9 us
    all_to_all x1, blocking collectives, local(): lax.all_to_all(part, 'aux', 0, 0, axis_index_groups=groups, tiled=True)  21.3 us
    ppermute x15, waiting for transfers between devices, send(): return lax.ppermute(value, BOTH, sorted(pairs))  12 us
    pallas_call x4, Pallas kernels, chunk(): pl.pallas_call(functools.partial(chunk_kernel, tuple(pieces), len(sides),...  7.24 us
    dot_general x1, matrix products, local(): jnp.einsum('qo,tko->tqk', masked, green, preferred_element_type=F32)  3.69 us
    dot_general x1, matrix products, local(): jnp.einsum('qo,tok->tqk', masked, green, preferred_element_type=F32)  2.92 us
  transfers between devices with their start and end apart: 15, of which 4 were waited for; matrix products, arithmetic and copies ran while one was open for 8% of the time, Pallas kernels for 9%

profile of v10, /device:TPU:1, one launch (start us, length us, event | category | flops | bytes accessed | tf_op | source)
XLA Modules:
  0.0 84.2 jit_solution(4213444465246612299)
XLA Ops:
  0.0 1.1 %shard_map.46 = (bf16[128,1024]{1,0:T(8,128)(2,1)S(1)}, bf16[72,1024]{1,0:T(8,128)(2,1)S(1)}, f32[1,128]{1,0:T(1,128)S(1)}) custom-call(bf16[128,1024]{1,0:T(8,128)(2,1)} %factors_in.1, s32[1,8]{1,0:T(1,128)} %pattern_in.1, f32[1,128]{1,0:T(1,128)} %bitcast.12), custom_call_target="tpu_custom_call" | custom-call | tf_op jit(solution)/shard_map/pallas_call | solution.py:102
  1.2 2.5 %collective-permute-start = (bf16[72,1024]{1,0:T(8,128)(2,1)S(1)}, bf16[72,1024]{1,0:T(8,128)(2,1)S(1)}, u32[]{:S(2)}, u32[]{:S(2)}) collective-permute-start(bf16[72,1024]{1,0:T(8,128)(2,1)S(1)} %get-tuple-element.24), channel_id=1, source_target_pairs={{0,8},{1,9},{2,10},{3,11},{4,12},{5,13},{6,14},{7,15},{8,16},{9,17... | collective-permute-start | bytes 442376 | tf_op jit(solution)/shard_map/ppermute | solution.py:31
  3.7 4.0 %collective-permute-start.1 = (bf16[72,1024]{1,0:T(8,128)(2,1)S(1)}, bf16[72,1024]{1,0:T(8,128)(2,1)S(1)}, u32[]{:S(2)}, u32[]{:S(2)}) collective-permute-start(bf16[72,1024]{1,0:T(8,128)(2,1)S(1)} %get-tuple-element.24), channel_id=1, source_target_pairs={{0,152},{1,153},{2,154},{3,155},{4,156},{5,157},{6,158},{7,159},{8... | collective-permute-start | bytes 442376 | tf_op jit(solution)/shard_map/ppermute | solution.py:31
  7.7 1.8 %collective-permute-start.2 = (bf16[72,1024]{1,0:T(8,128)(2,1)S(1)}, bf16[72,1024]{1,0:T(8,128)(2,1)S(1)}, u32[]{:S(2)}, u32[]{:S(2)}) collective-permute-start(bf16[72,1024]{1,0:T(8,128)(2,1)S(1)} %get-tuple-element.24), channel_id=1, source_target_pairs={{0,16},{1,145},{2,18},{3,147},{4,20},{5,149},{6,22},{7,151},{8,24}... | collective-permute-start | bytes 442376 | tf_op jit(solution)/shard_map/ppermute | solution.py:31
  9.5 2.9 %fusion.1 = bf16[2,128,1024]{2,1,0:T(8,128)(2,1)S(1)} fusion(bf16[2,1024,1024]{2,1,0:T(8,128)(2,1)} %param.4, bf16[128,1024]{1,0:T(8,128)(2,1)S(1)} %get-tuple-element.25), kind=kOutput, calls=%fused_computation.3 | convolution fusion | flops 537133056 | bytes 4980736 | tf_op jit(solution)/shard_map/qo,tok->tqk/dot_general | solution.py:321
  12.5 2.5 %collective-permute-start.7 = (bf16[2,128,1024]{2,1,0:T(8,128)(2,1)S(1)}, bf16[2,128,1024]{2,1,0:T(8,128)(2,1)S(1)}, u32[]{:S(2)}, u32[]{:S(2)}) collective-permute-start(bf16[2,128,1024]{2,1,0:T(8,128)(2,1)S(1)} %fusion.1), channel_id=1, source_target_pairs={{0,16},{1,145},{2,18},{3,147},{4,20},{5,149},{6,22},{7,151},{8,24}... | collective-permute-start | bytes 1572872 | tf_op jit(solution)/shard_map/ppermute | solution.py:31
  15.0 0.0 collective-permute-done
  15.0 0.0 collective-permute-done.1
  15.0 0.0 collective-permute-done.2
  15.1 0.1 concatenate.6.refs_0_.refs_2_
  15.2 1.3 %collective-permute-start.3 = (bf16[264,1024]{1,0:T(8,128)(2,1)S(1)}, bf16[264,1024]{1,0:T(8,128)(2,1)S(1)}, u32[]{:S(2)}, u32[]{:S(2)}) collective-permute-start(bf16[264,1024]{1,0:T(8,128)(2,1)S(1)} %concatenate.6.refs_0_.refs_2_), channel_id=1, source_target_pairs={{0,2},{1,3},{2,4},{3,5},{4,6},{5,7},{6,0},{7,1},{8,10},{9,11},{10,... | collective-permute-start | bytes 1622024 | tf_op jit(solution)/shard_map/ppermute | solution.py:31
  16.5 1.5 %collective-permute-start.4 = (bf16[264,1024]{1,0:T(8,128)(2,1)S(1)}, bf16[264,1024]{1,0:T(8,128)(2,1)S(1)}, u32[]{:S(2)}, u32[]{:S(2)}) collective-permute-start(bf16[264,1024]{1,0:T(8,128)(2,1)S(1)} %concatenate.6.refs_0_.refs_2_), channel_id=1, source_target_pairs={{0,6},{1,7},{2,0},{3,1},{4,2},{5,3},{6,4},{7,5},{8,14},{9,15},{10,... | collective-permute-start | bytes 1622024 | tf_op jit(solution)/shard_map/ppermute | solution.py:31
  18.0 2.8 %collective-permute-start.5 = (bf16[200,1024]{1,0:T(8,128)(2,1)S(1)}, bf16[200,1024]{1,0:T(8,128)(2,1)S(1)}, u32[]{:S(2)}, u32[]{:S(2)}) collective-permute-start(bf16[200,1024]{1,0:T(8,128)(2,1)S(1)} %slice.46), channel_id=1, source_target_pairs={{0,32},{1,97},{2,34},{3,99},{4,36},{5,101},{6,38},{7,103},{8,40},{... | collective-permute-start | bytes 1228808 | tf_op jit(solution)/shard_map/ppermute | solution.py:31
  20.8 3.7 %fusion.right_own.refs_0_ = bf16[2,128,1024]{2,1,0:T(8,128)(2,1)S(1)} fusion(bf16[2,1024,1024]{2,1,0:T(8,128)(2,1)} %param.4, bf16[128,1024]{1,0:T(8,128)(2,1)S(1)} %get-tuple-element.25), kind=kOutput, calls=%fused_computation.2 | convolution fusion | flops 537133056 | bytes 4980736 | tf_op jit(solution)/shard_map/qo,tko->tqk/dot_general | solution.py:333
  24.5 2.9 %collective-permute-done.7 = bf16[2,128,1024]{2,1,0:T(8,128)(2,1)S(1)} collective-permute-done((bf16[2,128,1024]{2,1,0:T(8,128)(2,1)S(1)}, bf16[2,128,1024]{2,1,0:T(8,128)(2,1)S(1)}, u32[]{:S(2)}, u32[]{:S(2)}) %collective-permute-start.7) | collective-permute-done | bytes 524320 | tf_op jit(solution)/shard_map/ppermute | solution.py:31
  27.4 2.7 %collective-permute-start.8 = (bf16[2,128,1024]{2,1,0:T(8,128)(2,1)S(1)}, bf16[2,128,1024]{2,1,0:T(8,128)(2,1)S(1)}, u32[]{:S(2)}, u32[]{:S(2)}) collective-permute-start(bf16[2,128,1024]{2,1,0:T(8,128)(2,1)S(1)} %collective-permute-done.7), channel_id=1, source_target_pairs={{0,16},{1,145},{2,18},{3,147},{4,20},{5,149},{6,22},{7,151},{8,24}... | collective-permute-start | bytes 1572872 | tf_op jit(solution)/shard_map/ppermute | solution.py:31
  30.1 0.0 collective-permute-done.5
  30.2 0.0 collective-permute-done.3.west_ref.refs_0_.refs_2_
  30.2 0.0 collective-permute-done.4.east_ref.refs_1_.refs_3_
  30.2 0.1 shard_map.47
  30.3 2.8 %collective-permute-start.12 = (bf16[528,1024]{1,0:T(8,128)(2,1)S(1)}, bf16[528,1024]{1,0:T(8,128)(2,1)S(1)}, u32[]{:S(2)}, u32[]{:S(2)}) collective-permute-start(bf16[528,1024]{1,0:T(8,128)(2,1)S(1)} %get-tuple-element.30), channel_id=1, source_target_pairs={{0,32},{1,97},{2,34},{3,99},{4,36},{5,101},{6,38},{7,103},{8,40},{... | collective-permute-start | bytes 3244040 | tf_op jit(solution)/shard_map/ppermute | solution.py:31
  33.1 2.5 %collective-permute-start.10 = (bf16[264,1024]{1,0:T(8,128)(2,1)S(1)}, bf16[264,1024]{1,0:T(8,128)(2,1)S(1)}, u32[]{:S(2)}, u32[]{:S(2)}) collective-permute-start(bf16[264,1024]{1,0:T(8,128)(2,1)S(1)} %get-tuple-element.29), channel_id=1, source_target_pairs={{0,2},{1,7},{2,4},{3,1},{4,6},{5,3},{6,0},{7,5},{8,10},{9,15},{10,... | collective-permute-start | bytes 1622024 | tf_op jit(solution)/shard_map/ppermute | solution.py:31
  35.6 0.0 collective-permute-start.6
  35.6 6.1 %collective-permute-done.8.refs_0_.refs_2_ = bf16[2,128,1024]{2,1,0:T(8,128)(2,1)S(1)} collective-permute-done((bf16[2,128,1024]{2,1,0:T(8,128)(2,1)S(1)}, bf16[2,128,1024]{2,1,0:T(8,128)(2,1)S(1)}, u32[]{:S(2)}, u32[]{:S(2)}) %collective-permute-start.8) | collective-permute-done | bytes 524320 | tf_op jit(solution)/shard_map/ppermute | solution.py:31
  41.7 2.5 %collective-permute-start.9 = (bf16[2,128,1024]{2,1,0:T(8,128)(2,1)S(1)}, bf16[2,128,1024]{2,1,0:T(8,128)(2,1)S(1)}, u32[]{:S(2)}, u32[]{:S(2)}) collective-permute-start(bf16[2,128,1024]{2,1,0:T(8,128)(2,1)S(1)} %collective-permute-done.8.refs_0_.refs_2_), channel_id=1, source_target_pairs={{0,1},{1,0},{2,3},{3,2},{4,5},{5,4},{6,7},{7,6},{8,9},{9,8},{10,11... | collective-permute-start | bytes 1572872 | tf_op jit(solution)/shard_map/ppermute | solution.py:31
  44.2 0.0 collective-permute-done.10.refs_5_
  44.2 2.7 %collective-permute-start.11 = (bf16[264,1024]{1,0:T(8,128)(2,1)S(1)}, bf16[264,1024]{1,0:T(8,128)(2,1)S(1)}, u32[]{:S(2)}, u32[]{:S(2)}) collective-permute-start(bf16[264,1024]{1,0:T(8,128)(2,1)S(1)} %collective-permute-done.10.refs_5_), channel_id=1, source_target_pairs={{0,32},{1,97},{2,34},{3,99},{4,36},{5,101},{6,38},{7,103},{8,40},{... | collective-permute-start | bytes 1622024 | tf_op jit(solution)/shard_map/ppermute | solution.py:31
  47.0 0.0 collective-permute-done.6.right_other.refs_1_
  47.0 0.8 shard_map.48.refs_4_
  47.7 0.8 shard_map.49.refs_4_
  48.5 0.0 collective-permute-done.9.refs_1_.refs_3_
  48.5 1.5 %shard_map.50 = (f32[2,128,1024]{2,1,0:T(8,128)S(1)}, f32[2,128,1024]{2,1,0:T(8,128)S(1)}) custom-call(bf16[2,128,1024]{2,1,0:T(8,128)(2,1)S(1)} %collective-permute-done.8.refs_0_.refs_2_, bf16[2,128,1024]{2,1,0:T(8,128)(2,1)S(1)} %collective-permute-done.9.refs_1_.refs_3_, bf16[264,1024]{1,0:T(8,128)(2,1)S(1)} %concatenate.6.refs_0_.refs_2_, ...), custom_call_target="tpu_custom_call" | custom-call | flops 536870912 | bytes 2097152 | tf_op jit(solution)/shard_map/pallas_call | solution.py:251
  50.0 1.5 %shard_map.51 = (f32[2,128,1024]{2,1,0:T(8,128)S(1)}, f32[2,128,1024]{2,1,0:T(8,128)S(1)}) custom-call(bf16[2,128,1024]{2,1,0:T(8,128)(2,1)S(1)} %collective-permute-done.8.refs_0_.refs_2_, bf16[2,128,1024]{2,1,0:T(8,128)(2,1)S(1)} %collective-permute-done.9.refs_1_.refs_3_, ...), custom_call_target="tpu_custom_call", output_to_operand_aliasing={{0}: (5, {}), {1}: (6, {})} | custom-call | flops 536870912 | bytes 2097152 | tf_op jit(solution)/shard_map/pallas_call | solution.py:251
  51.5 0.0 collective-permute-done.12.refs_4_
  51.5 3.1 %shard_map.52 = (f32[2,128,1024]{2,1,0:T(8,128)S(1)}, f32[2,128,1024]{2,1,0:T(8,128)S(1)}) custom-call(bf16[2,128,1024]{2,1,0:T(8,128)(2,1)S(1)} %fusion.right_own.refs_0_, bf16[2,128,1024]{2,1,0:T(8,128)(2,1)S(1)} %collective-permute-done.6.right_other.refs_1_, ...), custom_call_target="tpu_custom_call", output_to_operand_aliasing={{0}: (6, {}), {1}: (7, {})} | custom-call | flops 805306368 | bytes 2097152 | tf_op jit(solution)/shard_map/pallas_call | solution.py:251
  54.6 0.0 collective-permute-done.11.refs_4_.refs_6_
  54.6 1.2 %shard_map.53 = (f32[2,128,1024]{2,1,0:T(8,128)S(1)}, bf16[2,128,1024]{2,1,0:T(8,128)(2,1)S(1)}) custom-call(bf16[2,128,1024]{2,1,0:T(8,128)(2,1)S(1)} %fusion.right_own.refs_0_, bf16[2,128,1024]{2,1,0:T(8,128)(2,1)S(1)} %collective-permute-done.6.right_other.refs_1_, ...), custom_call_target="tpu_custom_call", output_to_operand_aliasing={{0}: (5, {})} | custom-call | flops 268435456 | bytes 2097152 | tf_op jit(solution)/shard_map/pallas_call | solution.py:251
  55.8 0.1 collective-permute-start.13
  55.9 1.9 %collective-permute-done.13.got_ref = bf16[2,128,1024]{2,1,0:T(8,128)(2,1)S(1)} collective-permute-done((bf16[2,128,1024]{2,1,0:T(8,128)(2,1)S(1)}, bf16[2,128,1024]{2,1,0:T(8,128)(2,1)S(1)}, u32[]{:S(2)}, u32[]{:S(2)}) %collective-permute-start.13) | collective-permute-done | bytes 524320 | tf_op jit(solution)/shard_map/ppermute | solution.py:31
  57.8 0.3 shard_map.54
  58.1 21.3 %all_to_all.5.part_ref = bf16[16,2,64,128]{3,2,1,0:T(8,128)(2,1)S(1)} all-to-all(bf16[16,2,64,128]{3,2,1,0:T(8,128)(2,1)S(1)} %shard_map.54), channel_id=1, replica_groups={{0,2,4,6,8,10,12,14,16,18,20,22,24,26,28,30},{1,3,5,7,9,11,13,15,17,19,..., dimensions={0} | all-to-all | bytes 1048576 | tf_op jit(solution)/shard_map/all_to_all | solution.py:363
  79.4 0.8 shard_map.55
  80.2 2.0 %collective-permute-start.14 = (f32[2,32,1024]{2,1,0:T(8,128)S(1)}, f32[2,32,1024]{2,1,0:T(8,128)S(1)}, u32[]{:S(2)}, u32[]{:S(2)}) collective-permute-start(f32[2,32,1024]{2,1,0:T(8,128)S(1)} %get-tuple-element.42), channel_id=1, source_target_pairs={{0,1},{1,0},{2,3},{3,2},{4,5},{5,4},{6,7},{7,6},{8,9},{9,8},{10,11... | collective-permute-start | bytes 786440 | tf_op jit(solution)/shard_map/ppermute | solution.py:31
  82.2 1.2 %collective-permute-done.14.got_ref = f32[2,32,1024]{2,1,0:T(8,128)S(1)} collective-permute-done((f32[2,32,1024]{2,1,0:T(8,128)S(1)}, f32[2,32,1024]{2,1,0:T(8,128)S(1)}, u32[]{:S(2)}, u32[]{:S(2)}) %collective-permute-start.14) | collective-permute-done | bytes 262176 | tf_op jit(solution)/shard_map/ppermute | solution.py:31
  83.4 0.8 shard_map.56
  (12 shorter events, 0.1 us)
Async XLA Ops:
  1.2 13.8 %collective-permute-start = (bf16[72,1024]{1,0:T(8,128)(2,1)S(1)}, bf16[72,1024]{1,0:T(8,128)(2,1)S(1)}, u32[]{:S(2)}, u32[]{:S(2)}) collective-permute-start(bf16[72,1024]{1,0:T(8,128)(2,1)S(1)} %get-tuple-element.24), channel_id=1, source_target_pairs={{0,8},{1,9},{2,10},{3,11},{4,12},{5,13},{6,14},{7,15},{8,16},{9,17... | collective-permute-start | bytes 442376 | tf_op jit(solution)/shard_map/ppermute | solution.py:31
  3.7 11.3 %collective-permute-start.1 = (bf16[72,1024]{1,0:T(8,128)(2,1)S(1)}, bf16[72,1024]{1,0:T(8,128)(2,1)S(1)}, u32[]{:S(2)}, u32[]{:S(2)}) collective-permute-start(bf16[72,1024]{1,0:T(8,128)(2,1)S(1)} %get-tuple-element.24), channel_id=1, source_target_pairs={{0,152},{1,153},{2,154},{3,155},{4,156},{5,157},{6,158},{7,159},{8... | collective-permute-start | bytes 442376 | tf_op jit(solution)/shard_map/ppermute | solution.py:31
  7.7 7.3 %collective-permute-start.2 = (bf16[72,1024]{1,0:T(8,128)(2,1)S(1)}, bf16[72,1024]{1,0:T(8,128)(2,1)S(1)}, u32[]{:S(2)}, u32[]{:S(2)}) collective-permute-start(bf16[72,1024]{1,0:T(8,128)(2,1)S(1)} %get-tuple-element.24), channel_id=1, source_target_pairs={{0,16},{1,145},{2,18},{3,147},{4,20},{5,149},{6,22},{7,151},{8,24}... | collective-permute-start | bytes 442376 | tf_op jit(solution)/shard_map/ppermute | solution.py:31
  12.5 14.9 %collective-permute-start.7 = (bf16[2,128,1024]{2,1,0:T(8,128)(2,1)S(1)}, bf16[2,128,1024]{2,1,0:T(8,128)(2,1)S(1)}, u32[]{:S(2)}, u32[]{:S(2)}) collective-permute-start(bf16[2,128,1024]{2,1,0:T(8,128)(2,1)S(1)} %fusion.1), channel_id=1, source_target_pairs={{0,16},{1,145},{2,18},{3,147},{4,20},{5,149},{6,22},{7,151},{8,24}... | collective-permute-start | bytes 1572872 | tf_op jit(solution)/shard_map/ppermute | solution.py:31
  15.2 15.0 %collective-permute-start.3 = (bf16[264,1024]{1,0:T(8,128)(2,1)S(1)}, bf16[264,1024]{1,0:T(8,128)(2,1)S(1)}, u32[]{:S(2)}, u32[]{:S(2)}) collective-permute-start(bf16[264,1024]{1,0:T(8,128)(2,1)S(1)} %concatenate.6.refs_0_.refs_2_), channel_id=1, source_target_pairs={{0,2},{1,3},{2,4},{3,5},{4,6},{5,7},{6,0},{7,1},{8,10},{9,11},{10,... | collective-permute-start | bytes 1622024 | tf_op jit(solution)/shard_map/ppermute | solution.py:31
  16.5 13.7 %collective-permute-start.4 = (bf16[264,1024]{1,0:T(8,128)(2,1)S(1)}, bf16[264,1024]{1,0:T(8,128)(2,1)S(1)}, u32[]{:S(2)}, u32[]{:S(2)}) collective-permute-start(bf16[264,1024]{1,0:T(8,128)(2,1)S(1)} %concatenate.6.refs_0_.refs_2_), channel_id=1, source_target_pairs={{0,6},{1,7},{2,0},{3,1},{4,2},{5,3},{6,4},{7,5},{8,14},{9,15},{10,... | collective-permute-start | bytes 1622024 | tf_op jit(solution)/shard_map/ppermute | solution.py:31
  18.0 12.2 %collective-permute-start.5 = (bf16[200,1024]{1,0:T(8,128)(2,1)S(1)}, bf16[200,1024]{1,0:T(8,128)(2,1)S(1)}, u32[]{:S(2)}, u32[]{:S(2)}) collective-permute-start(bf16[200,1024]{1,0:T(8,128)(2,1)S(1)} %slice.46), channel_id=1, source_target_pairs={{0,32},{1,97},{2,34},{3,99},{4,36},{5,101},{6,38},{7,103},{8,40},{... | collective-permute-start | bytes 1228808 | tf_op jit(solution)/shard_map/ppermute | solution.py:31
  27.4 14.3 %collective-permute-start.8 = (bf16[2,128,1024]{2,1,0:T(8,128)(2,1)S(1)}, bf16[2,128,1024]{2,1,0:T(8,128)(2,1)S(1)}, u32[]{:S(2)}, u32[]{:S(2)}) collective-permute-start(bf16[2,128,1024]{2,1,0:T(8,128)(2,1)S(1)} %collective-permute-done.7), channel_id=1, source_target_pairs={{0,16},{1,145},{2,18},{3,147},{4,20},{5,149},{6,22},{7,151},{8,24}... | collective-permute-start | bytes 1572872 | tf_op jit(solution)/shard_map/ppermute | solution.py:31
  30.3 21.2 %collective-permute-start.12 = (bf16[528,1024]{1,0:T(8,128)(2,1)S(1)}, bf16[528,1024]{1,0:T(8,128)(2,1)S(1)}, u32[]{:S(2)}, u32[]{:S(2)}) collective-permute-start(bf16[528,1024]{1,0:T(8,128)(2,1)S(1)} %get-tuple-element.30), channel_id=1, source_target_pairs={{0,32},{1,97},{2,34},{3,99},{4,36},{5,101},{6,38},{7,103},{8,40},{... | collective-permute-start | bytes 3244040 | tf_op jit(solution)/shard_map/ppermute | solution.py:31
  33.1 11.1 %collective-permute-start.10 = (bf16[264,1024]{1,0:T(8,128)(2,1)S(1)}, bf16[264,1024]{1,0:T(8,128)(2,1)S(1)}, u32[]{:S(2)}, u32[]{:S(2)}) collective-permute-start(bf16[264,1024]{1,0:T(8,128)(2,1)S(1)} %get-tuple-element.29), channel_id=1, source_target_pairs={{0,2},{1,7},{2,4},{3,1},{4,6},{5,3},{6,0},{7,5},{8,10},{9,15},{10,... | collective-permute-start | bytes 1622024 | tf_op jit(solution)/shard_map/ppermute | solution.py:31
  35.6 11.4 %collective-permute-start.6 = (bf16[2,128,1024]{2,1,0:T(8,128)(2,1)S(1)}, bf16[2,128,1024]{2,1,0:T(8,128)(2,1)S(1)}, u32[]{:S(2)}, u32[]{:S(2)}) collective-permute-start(bf16[2,128,1024]{2,1,0:T(8,128)(2,1)S(1)} %fusion.right_own.refs_0_), channel_id=1, source_target_pairs={{0,1},{1,0},{2,3},{3,2},{4,5},{5,4},{6,7},{7,6},{8,9},{9,8},{10,11... | collective-permute-start | bytes 1572872 | tf_op jit(solution)/shard_map/ppermute | solution.py:31
  41.7 6.8 %collective-permute-start.9 = (bf16[2,128,1024]{2,1,0:T(8,128)(2,1)S(1)}, bf16[2,128,1024]{2,1,0:T(8,128)(2,1)S(1)}, u32[]{:S(2)}, u32[]{:S(2)}) collective-permute-start(bf16[2,128,1024]{2,1,0:T(8,128)(2,1)S(1)} %collective-permute-done.8.refs_0_.refs_2_), channel_id=1, source_target_pairs={{0,1},{1,0},{2,3},{3,2},{4,5},{5,4},{6,7},{7,6},{8,9},{9,8},{10,11... | collective-permute-start | bytes 1572872 | tf_op jit(solution)/shard_map/ppermute | solution.py:31
  44.2 10.3 %collective-permute-start.11 = (bf16[264,1024]{1,0:T(8,128)(2,1)S(1)}, bf16[264,1024]{1,0:T(8,128)(2,1)S(1)}, u32[]{:S(2)}, u32[]{:S(2)}) collective-permute-start(bf16[264,1024]{1,0:T(8,128)(2,1)S(1)} %collective-permute-done.10.refs_5_), channel_id=1, source_target_pairs={{0,32},{1,97},{2,34},{3,99},{4,36},{5,101},{6,38},{7,103},{8,40},{... | collective-permute-start | bytes 1622024 | tf_op jit(solution)/shard_map/ppermute | solution.py:31
  55.8 2.0 %collective-permute-start.13 = (bf16[2,128,1024]{2,1,0:T(8,128)(2,1)S(1)}, bf16[2,128,1024]{2,1,0:T(8,128)(2,1)S(1)}, u32[]{:S(2)}, u32[]{:S(2)}) collective-permute-start(bf16[2,128,1024]{2,1,0:T(8,128)(2,1)S(1)} %get-tuple-element.39), channel_id=1, source_target_pairs={{0,1},{1,0},{2,3},{3,2},{4,5},{5,4},{6,7},{7,6},{8,9},{9,8},{10,11... | collective-permute-start | bytes 1572872 | tf_op jit(solution)/shard_map/ppermute | solution.py:31
  80.2 3.2 %collective-permute-start.14 = (f32[2,32,1024]{2,1,0:T(8,128)S(1)}, f32[2,32,1024]{2,1,0:T(8,128)S(1)}, u32[]{:S(2)}, u32[]{:S(2)}) collective-permute-start(f32[2,32,1024]{2,1,0:T(8,128)S(1)} %get-tuple-element.42), channel_id=1, source_target_pairs={{0,1},{1,0},{2,3},{3,2},{4,5},{5,4},{6,7},{7,6},{8,9},{9,8},{10,11... | collective-permute-start | bytes 786440 | tf_op jit(solution)/shard_map/ppermute | solution.py:31

commit v11 on v10

--- a/solution.py
+++ b/solution.py
@@ -138,21 +138,20 @@
     )(west, east)
 
 
-def after_kernel(value_ref, first_ref, out_ref):
-    del first_ref
+def after_kernel(value_ref, *refs):
     pltpu.touch(value_ref)
-    pltpu.touch(out_ref)
-
-
-def after(value, first):
+    pltpu.touch(refs[-1])
+
+
+def after(value, *first):
     return pl.pallas_call(
         after_kernel,
         out_shape=jax.ShapeDtypeStruct(value.shape, value.dtype),
-        in_specs=[VMEM] * 2,
+        in_specs=[VMEM] * (1 + len(first)),
         out_specs=VMEM,
         input_output_aliases={0: 0},
         compiler_params=params(8),
-    )(value, first)
+    )(value, *first)
 
 
 def weight_of(ref, row):
@@ -301,12 +300,12 @@
         keep = pl.multiple_of(t * i_rows + core * half, half)
         send = pl.multiple_of(t * i_rows + (1 - core) * half, half)
         keep_ref[t] = total_ref[pl.ds(keep, half), :]
-        send_ref[t] = total_ref[pl.ds(send, half), :]
+        send_ref[t] = total_ref[pl.ds(send, half), :].astype(BF16)
 
 
 def add_kernel(keep_ref, got_ref, out_ref):
     for t in range(keep_ref.shape[0]):
-        out_ref[:, t, :] = keep_ref[t] + got_ref[t]
+        out_ref[:, t, :] = keep_ref[t] + got_ref[t].astype(F32)
 
 
 def local(green, factors, pattern, coulomb):
@@ -338,14 +337,13 @@
     sides_q = other_parity(both)
     far_q = other_parity(far)
     left = two_along_z(left)
+    rights = (right, right_other)
+    squared = squares(*rights, (here, here_q, west, east), [(k, 0, n) for k in range(4)])
     left_other = other_core(left)
 
-    rights, lefts = (right, right_other), (left, left_other)
-    two = [(0, 0, n), (1, 0, n)]
-    here_z = squares(*rights, (here, here_q), two)
-    sides_z = squares(*rights, (west, east), two)
-    acc = chunk(lefts, (here, here_q), two, given=(here_z,))
-    acc = chunk(lefts, (west, east), two, given=(sides_z,), acc=acc)
+    lefts = (left, left_other)
+    four = [(k, 0, n) for k in range(4)]
+    acc = chunk(lefts, (here, here_q, west, east), four, given=(squared,))
     sides = rights + lefts
     acc = chunk(sides, (sides_q, far), [(0, 0, n), (0, n + 8, n), (1, 0, n)], acc=acc)
     keep, theirs = chunk(sides, (far_q,), [(0, 0, n)], acc=acc, last=True)
@@ -365,7 +363,7 @@
     shape = jax.ShapeDtypeStruct((times, i_rows // 2, orb), F32)
     keep, theirs = pl.pallas_call(
         sigma_kernel,
-        out_shape=(shape, shape),
+        out_shape=(shape, jax.ShapeDtypeStruct(shape.shape, BF16)),
         in_specs=[VMEM] * 8,
         out_specs=(VMEM, VMEM),
         scratch_shapes=[

time: 84.3 us -> 84.4 us (level)
    pallas_call x4 -> x3, Pallas kernels: 7.24 us -> 7.67 us  [chunk(): pl.pallas_call(functools.partial(chunk_kernel, tuple(pieces), len(sides),...]
where the time goes in v11:
time: 84.4 us; the launch traced here: 84.2 us
  starting transfers between devices  31.9 us (38%)
  blocking collectives  21.3 us (25%)
  Pallas kernels  12.1 us (14%)
  waiting for transfers between devices  11.9 us (14%)
  matrix products  6.61 us (8%)
    ppermute x15, starting transfers between devices, send(): return lax.ppermute(value, BOTH, sorted(pairs))  31.9 us
    all_to_all x1, blocking collectives, local(): lax.all_to_all(part, 'aux', 0, 0, axis_index_groups=groups, tiled=True)  21.3 us
    ppermute x15, waiting for transfers between devices, send(): return lax.ppermute(value, BOTH, sorted(pairs))  11.9 us
    pallas_call x3, Pallas kernels, chunk(): pl.pallas_call(functools.partial(chunk_kernel, tuple(pieces), len(sides),...  7.67 us
    dot_general x1, matrix products, local(): jnp.einsum('qo,tko->tqk', masked, green, preferred_element_type=F32)  3.69 us
    dot_general x1, matrix products, local(): jnp.einsum('qo,tok->tqk', masked, green, preferred_element_type=F32)  2.92 us
  transfers between devices with their start and end apart: 15, of which 4 were waited for; matrix products, arithmetic and copies ran while one was open for 8% of the time, Pallas kernels for 9%

profile of v11, /device:TPU:1, one launch (start us, length us, event | category | flops | bytes accessed | tf_op | source)
XLA Modules:
  0.0 84.2 jit_solution(12703401548810338123)
XLA Ops:
  0.0 1.1 %shard_map.46 = (bf16[128,1024]{1,0:T(8,128)(2,1)S(1)}, bf16[72,1024]{1,0:T(8,128)(2,1)S(1)}, f32[1,128]{1,0:T(1,128)S(1)}) custom-call(bf16[128,1024]{1,0:T(8,128)(2,1)} %factors_in.1, s32[1,8]{1,0:T(1,128)} %pattern_in.1, f32[1,128]{1,0:T(1,128)} %bitcast.12), custom_call_target="tpu_custom_call" | custom-call | tf_op jit(solution)/shard_map/pallas_call | solution.py:102
  1.2 2.5 %collective-permute-start = (bf16[72,1024]{1,0:T(8,128)(2,1)S(1)}, bf16[72,1024]{1,0:T(8,128)(2,1)S(1)}, u32[]{:S(2)}, u32[]{:S(2)}) collective-permute-start(bf16[72,1024]{1,0:T(8,128)(2,1)S(1)} %get-tuple-element.22), channel_id=1, source_target_pairs={{0,8},{1,9},{2,10},{3,11},{4,12},{5,13},{6,14},{7,15},{8,16},{9,17... | collective-permute-start | bytes 442376 | tf_op jit(solution)/shard_map/ppermute | solution.py:31
  3.7 4.0 %collective-permute-start.1 = (bf16[72,1024]{1,0:T(8,128)(2,1)S(1)}, bf16[72,1024]{1,0:T(8,128)(2,1)S(1)}, u32[]{:S(2)}, u32[]{:S(2)}) collective-permute-start(bf16[72,1024]{1,0:T(8,128)(2,1)S(1)} %get-tuple-element.22), channel_id=1, source_target_pairs={{0,152},{1,153},{2,154},{3,155},{4,156},{5,157},{6,158},{7,159},{8... | collective-permute-start | bytes 442376 | tf_op jit(solution)/shard_map/ppermute | solution.py:31
  7.7 1.8 %collective-permute-start.2 = (bf16[72,1024]{1,0:T(8,128)(2,1)S(1)}, bf16[72,1024]{1,0:T(8,128)(2,1)S(1)}, u32[]{:S(2)}, u32[]{:S(2)}) collective-permute-start(bf16[72,1024]{1,0:T(8,128)(2,1)S(1)} %get-tuple-element.22), channel_id=1, source_target_pairs={{0,16},{1,145},{2,18},{3,147},{4,20},{5,149},{6,22},{7,151},{8,24}... | collective-permute-start | bytes 442376 | tf_op jit(solution)/shard_map/ppermute | solution.py:31
  9.5 2.9 %fusion.1 = bf16[2,128,1024]{2,1,0:T(8,128)(2,1)S(1)} fusion(bf16[2,1024,1024]{2,1,0:T(8,128)(2,1)} %param.4, bf16[128,1024]{1,0:T(8,128)(2,1)S(1)} %get-tuple-element.23), kind=kOutput, calls=%fused_computation.3 | convolution fusion | flops 537133056 | bytes 4980736 | tf_op jit(solution)/shard_map/qo,tok->tqk/dot_general | solution.py:320
  12.5 2.5 %collective-permute-start.7 = (bf16[2,128,1024]{2,1,0:T(8,128)(2,1)S(1)}, bf16[2,128,1024]{2,1,0:T(8,128)(2,1)S(1)}, u32[]{:S(2)}, u32[]{:S(2)}) collective-permute-start(bf16[2,128,1024]{2,1,0:T(8,128)(2,1)S(1)} %fusion.1), channel_id=1, source_target_pairs={{0,16},{1,145},{2,18},{3,147},{4,20},{5,149},{6,22},{7,151},{8,24}... | collective-permute-start | bytes 1572872 | tf_op jit(solution)/shard_map/ppermute | solution.py:31
  15.0 0.0 collective-permute-done
  15.0 0.0 collective-permute-done.1
  15.0 0.0 collective-permute-done.2
  15.1 0.1 concatenate.6.refs_0_.refs_2_
  15.2 1.3 %collective-permute-start.3 = (bf16[264,1024]{1,0:T(8,128)(2,1)S(1)}, bf16[264,1024]{1,0:T(8,128)(2,1)S(1)}, u32[]{:S(2)}, u32[]{:S(2)}) collective-permute-start(bf16[264,1024]{1,0:T(8,128)(2,1)S(1)} %concatenate.6.refs_0_.refs_2_), channel_id=1, source_target_pairs={{0,2},{1,3},{2,4},{3,5},{4,6},{5,7},{6,0},{7,1},{8,10},{9,11},{10,... | collective-permute-start | bytes 1622024 | tf_op jit(solution)/shard_map/ppermute | solution.py:31
  16.5 1.5 %collective-permute-start.4 = (bf16[264,1024]{1,0:T(8,128)(2,1)S(1)}, bf16[264,1024]{1,0:T(8,128)(2,1)S(1)}, u32[]{:S(2)}, u32[]{:S(2)}) collective-permute-start(bf16[264,1024]{1,0:T(8,128)(2,1)S(1)} %concatenate.6.refs_0_.refs_2_), channel_id=1, source_target_pairs={{0,6},{1,7},{2,0},{3,1},{4,2},{5,3},{6,4},{7,5},{8,14},{9,15},{10,... | collective-permute-start | bytes 1622024 | tf_op jit(solution)/shard_map/ppermute | solution.py:31
  18.0 2.8 %collective-permute-start.5 = (bf16[200,1024]{1,0:T(8,128)(2,1)S(1)}, bf16[200,1024]{1,0:T(8,128)(2,1)S(1)}, u32[]{:S(2)}, u32[]{:S(2)}) collective-permute-start(bf16[200,1024]{1,0:T(8,128)(2,1)S(1)} %slice.46), channel_id=1, source_target_pairs={{0,32},{1,97},{2,34},{3,99},{4,36},{5,101},{6,38},{7,103},{8,40},{... | collective-permute-start | bytes 1228808 | tf_op jit(solution)/shard_map/ppermute | solution.py:31
  20.8 3.7 %fusion.right_own.refs_0_ = bf16[2,128,1024]{2,1,0:T(8,128)(2,1)S(1)} fusion(bf16[2,1024,1024]{2,1,0:T(8,128)(2,1)} %param.4, bf16[128,1024]{1,0:T(8,128)(2,1)S(1)} %get-tuple-element.23), kind=kOutput, calls=%fused_computation.2 | convolution fusion | flops 537133056 | bytes 4980736 | tf_op jit(solution)/shard_map/qo,tko->tqk/dot_general | solution.py:332
  24.5 2.9 %collective-permute-done.7 = bf16[2,128,1024]{2,1,0:T(8,128)(2,1)S(1)} collective-permute-done((bf16[2,128,1024]{2,1,0:T(8,128)(2,1)S(1)}, bf16[2,128,1024]{2,1,0:T(8,128)(2,1)S(1)}, u32[]{:S(2)}, u32[]{:S(2)}) %collective-permute-start.7) | collective-permute-done | bytes 524320 | tf_op jit(solution)/shard_map/ppermute | solution.py:31
  27.4 2.7 %collective-permute-start.8 = (bf16[2,128,1024]{2,1,0:T(8,128)(2,1)S(1)}, bf16[2,128,1024]{2,1,0:T(8,128)(2,1)S(1)}, u32[]{:S(2)}, u32[]{:S(2)}) collective-permute-start(bf16[2,128,1024]{2,1,0:T(8,128)(2,1)S(1)} %collective-permute-done.7), channel_id=1, source_target_pairs={{0,16},{1,145},{2,18},{3,147},{4,20},{5,149},{6,22},{7,151},{8,24}... | collective-permute-start | bytes 1572872 | tf_op jit(solution)/shard_map/ppermute | solution.py:31
  30.1 0.0 collective-permute-done.5
  30.2 0.0 collective-permute-done.3.west_ref.refs_2_.refs_4_
  30.2 0.0 collective-permute-done.4.east_ref.refs_3_.refs_5_
  30.2 0.1 shard_map.47
  30.3 2.8 %collective-permute-start.12 = (bf16[528,1024]{1,0:T(8,128)(2,1)S(1)}, bf16[528,1024]{1,0:T(8,128)(2,1)S(1)}, u32[]{:S(2)}, u32[]{:S(2)}) collective-permute-start(bf16[528,1024]{1,0:T(8,128)(2,1)S(1)} %get-tuple-element.28), channel_id=1, source_target_pairs={{0,32},{1,97},{2,34},{3,99},{4,36},{5,101},{6,38},{7,103},{8,40},{... | collective-permute-start | bytes 3244040 | tf_op jit(solution)/shard_map/ppermute | solution.py:31
  33.1 2.5 %collective-permute-start.10 = (bf16[264,1024]{1,0:T(8,128)(2,1)S(1)}, bf16[264,1024]{1,0:T(8,128)(2,1)S(1)}, u32[]{:S(2)}, u32[]{:S(2)}) collective-permute-start(bf16[264,1024]{1,0:T(8,128)(2,1)S(1)} %get-tuple-element.27), channel_id=1, source_target_pairs={{0,2},{1,7},{2,4},{3,1},{4,6},{5,3},{6,0},{7,5},{8,10},{9,15},{10,... | collective-permute-start | bytes 1622024 | tf_op jit(solution)/shard_map/ppermute | solution.py:31
  35.6 0.0 collective-permute-start.6
  35.6 6.1 %collective-permute-done.8.refs_0_.refs_2_ = bf16[2,128,1024]{2,1,0:T(8,128)(2,1)S(1)} collective-permute-done((bf16[2,128,1024]{2,1,0:T(8,128)(2,1)S(1)}, bf16[2,128,1024]{2,1,0:T(8,128)(2,1)S(1)}, u32[]{:S(2)}, u32[]{:S(2)}) %collective-permute-start.8) | collective-permute-done | bytes 524320 | tf_op jit(solution)/shard_map/ppermute | solution.py:31
  41.7 2.5 %collective-permute-start.9 = (bf16[2,128,1024]{2,1,0:T(8,128)(2,1)S(1)}, bf16[2,128,1024]{2,1,0:T(8,128)(2,1)S(1)}, u32[]{:S(2)}, u32[]{:S(2)}) collective-permute-start(bf16[2,128,1024]{2,1,0:T(8,128)(2,1)S(1)} %collective-permute-done.8.refs_0_.refs_2_), channel_id=1, source_target_pairs={{0,1},{1,0},{2,3},{3,2},{4,5},{5,4},{6,7},{7,6},{8,9},{9,8},{10,11... | collective-permute-start | bytes 1572872 | tf_op jit(solution)/shard_map/ppermute | solution.py:31
  44.2 0.0 collective-permute-done.10.refs_5_
  44.2 2.7 %collective-permute-start.11 = (bf16[264,1024]{1,0:T(8,128)(2,1)S(1)}, bf16[264,1024]{1,0:T(8,128)(2,1)S(1)}, u32[]{:S(2)}, u32[]{:S(2)}) collective-permute-start(bf16[264,1024]{1,0:T(8,128)(2,1)S(1)} %collective-permute-done.10.refs_5_), channel_id=1, source_target_pairs={{0,32},{1,97},{2,34},{3,99},{4,36},{5,101},{6,38},{7,103},{8,40},{... | collective-permute-start | bytes 1622024 | tf_op jit(solution)/shard_map/ppermute | solution.py:31
  47.0 0.0 collective-permute-done.6.right_other.refs_1_
  47.0 1.3 %shard_map.48.refs_6_ = f32[2,256,1024]{2,1,0:T(8,128)S(1)} custom-call(bf16[2,128,1024]{2,1,0:T(8,128)(2,1)S(1)} %fusion.right_own.refs_0_, bf16[2,128,1024]{2,1,0:T(8,128)(2,1)S(1)} %collective-permute-done.6.right_other.refs_1_, bf16[264,1024]{1,0:T(8,128)(2,1)S(1)} %concatenate.6.refs_0_.refs_2_, bf16[264,1024]{1,0:T(8,128)(2,1)S(1)} %pad_maximum_fusion.refs_1_.refs_3_, ...), custom_call_target="tpu_custom_call" | custom-call | flops 1073741824 | bytes 2097152 | tf_op jit(solution)/shard_map/pallas_call | solution.py:190
  48.3 0.0 collective-permute-done.9.refs_1_.refs_3_
  48.3 3.4 %shard_map.49 = (f32[2,128,1024]{2,1,0:T(8,128)S(1)}, f32[2,128,1024]{2,1,0:T(8,128)S(1)}) custom-call(bf16[2,128,1024]{2,1,0:T(8,128)(2,1)S(1)} %collective-permute-done.8.refs_0_.refs_2_, bf16[2,128,1024]{2,1,0:T(8,128)(2,1)S(1)} %collective-permute-done.9.refs_1_.refs_3_, bf16[264,1024]{1,0:T(8,128)(2,1)S(1)} %concatenate.6.refs_0_.refs_2_, ...), custom_call_target="tpu_custom_call" | custom-call | flops 1073741824 | bytes 2097152 | tf_op jit(solution)/shard_map/pallas_call | solution.py:250
  51.7 0.0 collective-permute-done.12.refs_4_
  51.7 3.0 %shard_map.50 = (f32[2,128,1024]{2,1,0:T(8,128)S(1)}, f32[2,128,1024]{2,1,0:T(8,128)S(1)}) custom-call(bf16[2,128,1024]{2,1,0:T(8,128)(2,1)S(1)} %fusion.right_own.refs_0_, bf16[2,128,1024]{2,1,0:T(8,128)(2,1)S(1)} %collective-permute-done.6.right_other.refs_1_, ...), custom_call_target="tpu_custom_call", output_to_operand_aliasing={{0}: (6, {}), {1}: (7, {})} | custom-call | flops 805306368 | bytes 2097152 | tf_op jit(solution)/shard_map/pallas_call | solution.py:250
  54.8 0.0 collective-permute-done.11.refs_4_.refs_6_
  54.8 1.2 %shard_map.51 = (f32[2,128,1024]{2,1,0:T(8,128)S(1)}, bf16[2,128,1024]{2,1,0:T(8,128)(2,1)S(1)}) custom-call(bf16[2,128,1024]{2,1,0:T(8,128)(2,1)S(1)} %fusion.right_own.refs_0_, bf16[2,128,1024]{2,1,0:T(8,128)(2,1)S(1)} %collective-permute-done.6.right_other.refs_1_, ...), custom_call_target="tpu_custom_call", output_to_operand_aliasing={{0}: (5, {})} | custom-call | flops 268435456 | bytes 2097152 | tf_op jit(solution)/shard_map/pallas_call | solution.py:250
  56.0 0.1 collective-permute-start.13
  56.1 1.9 %collective-permute-done.13.got_ref = bf16[2,128,1024]{2,1,0:T(8,128)(2,1)S(1)} collective-permute-done((bf16[2,128,1024]{2,1,0:T(8,128)(2,1)S(1)}, bf16[2,128,1024]{2,1,0:T(8,128)(2,1)S(1)}, u32[]{:S(2)}, u32[]{:S(2)}) %collective-permute-start.13) | collective-permute-done | bytes 524320 | tf_op jit(solution)/shard_map/ppermute | solution.py:31
  58.0 0.3 shard_map.52
  58.3 21.3 %all_to_all.5.part_ref = bf16[16,2,64,128]{3,2,1,0:T(8,128)(2,1)S(1)} all-to-all(bf16[16,2,64,128]{3,2,1,0:T(8,128)(2,1)S(1)} %shard_map.52), channel_id=1, replica_groups={{0,2,4,6,8,10,12,14,16,18,20,22,24,26,28,30},{1,3,5,7,9,11,13,15,17,19,..., dimensions={0} | all-to-all | bytes 1048576 | tf_op jit(solution)/shard_map/all_to_all | solution.py:361
  79.6 0.8 shard_map.53
  80.4 2.0 %collective-permute-start.14 = (bf16[2,32,1024]{2,1,0:T(8,128)(2,1)S(1)}, bf16[2,32,1024]{2,1,0:T(8,128)(2,1)S(1)}, u32[]{:S(2)}, u32[]{:S(2)}) collective-permute-start(bf16[2,32,1024]{2,1,0:T(8,128)(2,1)S(1)} %get-tuple-element.38), channel_id=1, source_target_pairs={{0,1},{1,0},{2,3},{3,2},{4,5},{5,4},{6,7},{7,6},{8,9},{9,8},{10,11... | collective-permute-start | bytes 393224 | tf_op jit(solution)/shard_map/ppermute | solution.py:31
  82.4 1.0 %collective-permute-done.14.got_ref = bf16[2,32,1024]{2,1,0:T(8,128)(2,1)S(1)} collective-permute-done((bf16[2,32,1024]{2,1,0:T(8,128)(2,1)S(1)}, bf16[2,32,1024]{2,1,0:T(8,128)(2,1)S(1)}, u32[]{:S(2)}, u32[]{:S(2)}) %collective-permute-start.14) | collective-permute-done | bytes 131104 | tf_op jit(solution)/shard_map/ppermute | solution.py:31
  83.4 0.8 shard_map.54
  (12 shorter events, 0.1 us)
Async XLA Ops:
  1.2 13.8 %collective-permute-start = (bf16[72,1024]{1,0:T(8,128)(2,1)S(1)}, bf16[72,1024]{1,0:T(8,128)(2,1)S(1)}, u32[]{:S(2)}, u32[]{:S(2)}) collective-permute-start(bf16[72,1024]{1,0:T(8,128)(2,1)S(1)} %get-tuple-element.22), channel_id=1, source_target_pairs={{0,8},{1,9},{2,10},{3,11},{4,12},{5,13},{6,14},{7,15},{8,16},{9,17... | collective-permute-start | bytes 442376 | tf_op jit(solution)/shard_map/ppermute | solution.py:31
  3.7 11.3 %collective-permute-start.1 = (bf16[72,1024]{1,0:T(8,128)(2,1)S(1)}, bf16[72,1024]{1,0:T(8,128)(2,1)S(1)}, u32[]{:S(2)}, u32[]{:S(2)}) collective-permute-start(bf16[72,1024]{1,0:T(8,128)(2,1)S(1)} %get-tuple-element.22), channel_id=1, source_target_pairs={{0,152},{1,153},{2,154},{3,155},{4,156},{5,157},{6,158},{7,159},{8... | collective-permute-start | bytes 442376 | tf_op jit(solution)/shard_map/ppermute | solution.py:31
  7.7 7.3 %collective-permute-start.2 = (bf16[72,1024]{1,0:T(8,128)(2,1)S(1)}, bf16[72,1024]{1,0:T(8,128)(2,1)S(1)}, u32[]{:S(2)}, u32[]{:S(2)}) collective-permute-start(bf16[72,1024]{1,0:T(8,128)(2,1)S(1)} %get-tuple-element.22), channel_id=1, source_target_pairs={{0,16},{1,145},{2,18},{3,147},{4,20},{5,149},{6,22},{7,151},{8,24}... | collective-permute-start | bytes 442376 | tf_op jit(solution)/shard_map/ppermute | solution.py:31
  12.5 14.9 %collective-permute-start.7 = (bf16[2,128,1024]{2,1,0:T(8,128)(2,1)S(1)}, bf16[2,128,1024]{2,1,0:T(8,128)(2,1)S(1)}, u32[]{:S(2)}, u32[]{:S(2)}) collective-permute-start(bf16[2,128,1024]{2,1,0:T(8,128)(2,1)S(1)} %fusion.1), channel_id=1, source_target_pairs={{0,16},{1,145},{2,18},{3,147},{4,20},{5,149},{6,22},{7,151},{8,24}... | collective-permute-start | bytes 1572872 | tf_op jit(solution)/shard_map/ppermute | solution.py:31
  15.2 15.0 %collective-permute-start.3 = (bf16[264,1024]{1,0:T(8,128)(2,1)S(1)}, bf16[264,1024]{1,0:T(8,128)(2,1)S(1)}, u32[]{:S(2)}, u32[]{:S(2)}) collective-permute-start(bf16[264,1024]{1,0:T(8,128)(2,1)S(1)} %concatenate.6.refs_0_.refs_2_), channel_id=1, source_target_pairs={{0,2},{1,3},{2,4},{3,5},{4,6},{5,7},{6,0},{7,1},{8,10},{9,11},{10,... | collective-permute-start | bytes 1622024 | tf_op jit(solution)/shard_map/ppermute | solution.py:31
  16.5 13.7 %collective-permute-start.4 = (bf16[264,1024]{1,0:T(8,128)(2,1)S(1)}, bf16[264,1024]{1,0:T(8,128)(2,1)S(1)}, u32[]{:S(2)}, u32[]{:S(2)}) collective-permute-start(bf16[264,1024]{1,0:T(8,128)(2,1)S(1)} %concatenate.6.refs_0_.refs_2_), channel_id=1, source_target_pairs={{0,6},{1,7},{2,0},{3,1},{4,2},{5,3},{6,4},{7,5},{8,14},{9,15},{10,... | collective-permute-start | bytes 1622024 | tf_op jit(solution)/shard_map/ppermute | solution.py:31
  18.0 12.2 %collective-permute-start.5 = (bf16[200,1024]{1,0:T(8,128)(2,1)S(1)}, bf16[200,1024]{1,0:T(8,128)(2,1)S(1)}, u32[]{:S(2)}, u32[]{:S(2)}) collective-permute-start(bf16[200,1024]{1,0:T(8,128)(2,1)S(1)} %slice.46), channel_id=1, source_target_pairs={{0,32},{1,97},{2,34},{3,99},{4,36},{5,101},{6,38},{7,103},{8,40},{... | collective-permute-start | bytes 1228808 | tf_op jit(solution)/shard_map/ppermute | solution.py:31
  27.4 14.3 %collective-permute-start.8 = (bf16[2,128,1024]{2,1,0:T(8,128)(2,1)S(1)}, bf16[2,128,1024]{2,1,0:T(8,128)(2,1)S(1)}, u32[]{:S(2)}, u32[]{:S(2)}) collective-permute-start(bf16[2,128,1024]{2,1,0:T(8,128)(2,1)S(1)} %collective-permute-done.7), channel_id=1, source_target_pairs={{0,16},{1,145},{2,18},{3,147},{4,20},{5,149},{6,22},{7,151},{8,24}... | collective-permute-start | bytes 1572872 | tf_op jit(solution)/shard_map/ppermute | solution.py:31
  30.3 21.4 %collective-permute-start.12 = (bf16[528,1024]{1,0:T(8,128)(2,1)S(1)}, bf16[528,1024]{1,0:T(8,128)(2,1)S(1)}, u32[]{:S(2)}, u32[]{:S(2)}) collective-permute-start(bf16[528,1024]{1,0:T(8,128)(2,1)S(1)} %get-tuple-element.28), channel_id=1, source_target_pairs={{0,32},{1,97},{2,34},{3,99},{4,36},{5,101},{6,38},{7,103},{8,40},{... | collective-permute-start | bytes 3244040 | tf_op jit(solution)/shard_map/ppermute | solution.py:31
  33.1 11.1 %collective-permute-start.10 = (bf16[264,1024]{1,0:T(8,128)(2,1)S(1)}, bf16[264,1024]{1,0:T(8,128)(2,1)S(1)}, u32[]{:S(2)}, u32[]{:S(2)}) collective-permute-start(bf16[264,1024]{1,0:T(8,128)(2,1)S(1)} %get-tuple-element.27), channel_id=1, source_target_pairs={{0,2},{1,7},{2,4},{3,1},{4,6},{5,3},{6,0},{7,5},{8,10},{9,15},{10,... | collective-permute-start | bytes 1622024 | tf_op jit(solution)/shard_map/ppermute | solution.py:31
  35.6 11.4 %collective-permute-start.6 = (bf16[2,128,1024]{2,1,0:T(8,128)(2,1)S(1)}, bf16[2,128,1024]{2,1,0:T(8,128)(2,1)S(1)}, u32[]{:S(2)}, u32[]{:S(2)}) collective-permute-start(bf16[2,128,1024]{2,1,0:T(8,128)(2,1)S(1)} %fusion.right_own.refs_0_), channel_id=1, source_target_pairs={{0,1},{1,0},{2,3},{3,2},{4,5},{5,4},{6,7},{7,6},{8,9},{9,8},{10,11... | collective-permute-start | bytes 1572872 | tf_op jit(solution)/shard_map/ppermute | solution.py:31
  41.7 6.6 %collective-permute-start.9 = (bf16[2,128,1024]{2,1,0:T(8,128)(2,1)S(1)}, bf16[2,128,1024]{2,1,0:T(8,128)(2,1)S(1)}, u32[]{:S(2)}, u32[]{:S(2)}) collective-permute-start(bf16[2,128,1024]{2,1,0:T(8,128)(2,1)S(1)} %collective-permute-done.8.refs_0_.refs_2_), channel_id=1, source_target_pairs={{0,1},{1,0},{2,3},{3,2},{4,5},{5,4},{6,7},{7,6},{8,9},{9,8},{10,11... | collective-permute-start | bytes 1572872 | tf_op jit(solution)/shard_map/ppermute | solution.py:31
  44.2 10.5 %collective-permute-start.11 = (bf16[264,1024]{1,0:T(8,128)(2,1)S(1)}, bf16[264,1024]{1,0:T(8,128)(2,1)S(1)}, u32[]{:S(2)}, u32[]{:S(2)}) collective-permute-start(bf16[264,1024]{1,0:T(8,128)(2,1)S(1)} %collective-permute-done.10.refs_5_), channel_id=1, source_target_pairs={{0,32},{1,97},{2,34},{3,99},{4,36},{5,101},{6,38},{7,103},{8,40},{... | collective-permute-start | bytes 1622024 | tf_op jit(solution)/shard_map/ppermute | solution.py:31
  56.0 2.0 %collective-permute-start.13 = (bf16[2,128,1024]{2,1,0:T(8,128)(2,1)S(1)}, bf16[2,128,1024]{2,1,0:T(8,128)(2,1)S(1)}, u32[]{:S(2)}, u32[]{:S(2)}) collective-permute-start(bf16[2,128,1024]{2,1,0:T(8,128)(2,1)S(1)} %get-tuple-element.35), channel_id=1, source_target_pairs={{0,1},{1,0},{2,3},{3,2},{4,5},{5,4},{6,7},{7,6},{8,9},{9,8},{10,11... | collective-permute-start | bytes 1572872 | tf_op jit(solution)/shard_map/ppermute | solution.py:31
  80.4 3.0 %collective-permute-start.14 = (bf16[2,32,1024]{2,1,0:T(8,128)(2,1)S(1)}, bf16[2,32,1024]{2,1,0:T(8,128)(2,1)S(1)}, u32[]{:S(2)}, u32[]{:S(2)}) collective-permute-start(bf16[2,32,1024]{2,1,0:T(8,128)(2,1)S(1)} %get-tuple-element.38), channel_id=1, source_target_pairs={{0,1},{1,0},{2,3},{3,2},{4,5},{5,4},{6,7},{7,6},{8,9},{9,8},{10,11... | collective-permute-start | bytes 393224 | tf_op jit(solution)/shard_map/ppermute | solution.py:31

commit v12 on v11

--- a/solution.py
+++ b/solution.py
@@ -138,22 +138,6 @@
     )(west, east)
 
 
-def after_kernel(value_ref, *refs):
-    pltpu.touch(value_ref)
-    pltpu.touch(refs[-1])
-
-
-def after(value, *first):
-    return pl.pallas_call(
-        after_kernel,
-        out_shape=jax.ShapeDtypeStruct(value.shape, value.dtype),
-        in_specs=[VMEM] * (1 + len(first)),
-        out_specs=VMEM,
-        input_output_aliases={0: 0},
-        compiler_params=params(8),
-    )(value, *first)
-
-
 def weight_of(ref, row):
     parts = [ref[pl.ds(row, 1), pl.ds(k * BLOCK, BLOCK)].astype(F32) for k in range(3)]
     return parts[0] + (parts[1] + parts[2])
@@ -172,40 +156,10 @@
     return refs[at][pl.ds(start, size), :], weights_of(refs[at], start + size, size // HALF)
 
 
-def square_kernel(pieces, right_own, right_other, *refs):
-    rows, out = refs[:-1], refs[-1]
-    for t in range(right_own.shape[0]):
-        right = jnp.concatenate([right_own[t], right_other[t]], axis=0)
-        offset = 0
-        for piece in pieces:
-            part, weight = rows_of(rows, piece)
-            a = lax.dot_general(right, part, NT, preferred_element_type=F32)
-            out[t, :, pl.ds(offset, piece[2])] = a * a * weight
-            offset += piece[2]
-
-
-def squares(right, right_other, rows, pieces):
-    times, own, orb = right.shape
-    n = sum(piece[2] for piece in pieces)
-    return pl.pallas_call(
-        functools.partial(square_kernel, tuple(pieces)),
-        out_shape=jax.ShapeDtypeStruct((times, 2 * own, n), F32),
-        in_specs=[VMEM] * (2 + len(rows)),
-        out_specs=VMEM,
-        compiler_params=params(12),
-        cost_estimate=pl.CostEstimate(
-            flops=times * 2 * (2 * own) * n * orb, bytes_accessed=2 << 20, transcendentals=0
-        ),
-    )(right, right_other, *rows)
-
-
-def chunk_kernel(pieces, sides, count, given, first, *refs):
+def chunk_kernel(pieces, sides, count, first, *refs):
     left_own, left_other = refs[sides - 2 : sides]
     rows = refs[sides : sides + count]
     rest = refs[sides + count :]
-    if given:
-        squared = rest[0]
-        rest = rest[1:]
     if not first:
         acc_own, acc_other = rest[:2]
         rest = rest[2:]
@@ -213,21 +167,14 @@
     own = out_own.shape[1]
     for t in range(out_own.shape[0]):
         left = jnp.concatenate([left_own[t], left_other[t]], axis=0)
-        total = None
-        offset = 0
-        for piece in pieces:
-            part, weight = rows_of(rows, piece)
-            if given:
-                square = squared[t, :, pl.ds(offset, piece[2])]
-            else:
-                right = jnp.concatenate([refs[0][t], refs[1][t]], axis=0)
-                a = lax.dot_general(right, part, NT, preferred_element_type=F32)
-                square = a * a * weight
-            offset += piece[2]
-            m = lax.dot_general(left, part, NT, preferred_element_type=F32)
-            k = (square * m).astype(BF16)
-            d = lax.dot_general(k, part, NN, preferred_element_type=F32)
-            total = d if total is None else total + d
+        right = jnp.concatenate([refs[0][t], refs[1][t]], axis=0)
+        pairs = [rows_of(rows, piece) for piece in pieces]
+        part = jnp.concatenate([pair[0] for pair in pairs], axis=0)
+        weight = jnp.concatenate([pair[1] for pair in pairs], axis=1)
+        a = lax.dot_general(right, part, NT, preferred_element_type=F32)
+        m = lax.dot_general(left, part, NT, preferred_element_type=F32)
+        k = (a * a * weight * m).astype(BF16)
+        total = lax.dot_general(k, part, NN, preferred_element_type=F32)
         mine, theirs = total[:own], total[own:]
         if not first:
             mine, theirs = acc_own[t] + mine, acc_other[t] + theirs
@@ -235,11 +182,11 @@
         out_other[t] = theirs.astype(out_other.dtype)
 
 
-def chunk(sides, rows, pieces, given=(), acc=(), last=False):
+def chunk(sides, rows, pieces, acc=(), last=False):
     times, own, orb = sides[0].shape
     shape = jax.ShapeDtypeStruct((times, own, orb), F32)
     theirs = jax.ShapeDtypeStruct((times, own, orb), BF16 if last else F32)
-    at = len(sides) + len(rows) + len(given)
+    at = len(sides) + len(rows)
     aliases = {}
     if acc:
         aliases[at] = 0
@@ -249,7 +196,7 @@
     flops = times * 2 * 2 * (2 * own) * n * orb // 2
     return pl.pallas_call(
         functools.partial(
-            chunk_kernel, tuple(pieces), len(sides), len(rows), bool(given), not acc
+            chunk_kernel, tuple(pieces), len(sides), len(rows), not acc
         ),
         out_shape=(shape, theirs),
         in_specs=[VMEM] * (at + len(acc)),
@@ -257,7 +204,7 @@
         input_output_aliases=aliases,
         compiler_params=params(16),
         cost_estimate=pl.CostEstimate(flops=flops, bytes_accessed=2 << 20, transcendentals=0),
-    )(*sides, *rows, *given, *acc)
+    )(*sides, *rows, *acc)
 
 
 def finish_kernel(own_ref, got_ref, coulomb_ref, out_ref):
@@ -338,13 +285,13 @@
     far_q = other_parity(far)
     left = two_along_z(left)
     rights = (right, right_other)
-    squared = squares(*rights, (here, here_q, west, east), [(k, 0, n) for k in range(4)])
     left_other = other_core(left)
 
     lefts = (left, left_other)
-    four = [(k, 0, n) for k in range(4)]
-    acc = chunk(lefts, (here, here_q, west, east), four, given=(squared,))
+    two = [(0, 0, n), (1, 0, n)]
     sides = rights + lefts
+    acc = chunk(sides, (here, here_q), two)
+    acc = chunk(sides, (west, east), two, acc=acc)
     acc = chunk(sides, (sides_q, far), [(0, 0, n), (0, n + 8, n), (1, 0, n)], acc=acc)
     keep, theirs = chunk(sides, (far_q,), [(0, 0, n)], acc=acc, last=True)
 

time: 84.4 us -> 83.5 us (0.989)
  Pallas kernels: 12.1 us -> 11.2 us
    pallas_call x1 -> x0, Pallas kernels: 1.31 us -> none  [squares(): pl.pallas_call(functools.partial(square_kernel, tuple(pieces)), out_shape...]
    pallas_call x3 -> x4, Pallas kernels: 7.67 us -> 8.1 us  [chunk(): pl.pallas_call(functools.partial(chunk_kernel, tuple(pieces), len(sides),...]
  transfers between devices with their start and end apart: 15 -> 15, of which waited for: 4 -> 4; matrix products, arithmetic and copies ran while one was open for 8% -> 8% of each run, Pallas kernels for 9% -> 8%
where the time goes in v12:
time: 83.5 us; the launch traced here: 83.3 us
  starting transfers between devices  31.9 us (38%)
  blocking collectives  21.3 us (26%)
  waiting for transfers between devices  11.9 us (14%)
  Pallas kernels  11.2 us (13%)
  matrix products  6.61 us (8%)
    ppermute x15, starting transfers between devices, send(): return lax.ppermute(value, BOTH, sorted(pairs))  31.9 us
    all_to_all x1, blocking collectives, local(): lax.all_to_all(part, 'aux', 0, 0, axis_index_groups=groups, tiled=True)  21.3 us
    ppermute x15, waiting for transfers between devices, send(): return lax.ppermute(value, BOTH, sorted(pairs))  11.9 us
    pallas_call x4, Pallas kernels, chunk(): pl.pallas_call(functools.partial(chunk_kernel, tuple(pieces), len(sides),...  8.1 us
    dot_general x1, matrix products, local(): jnp.einsum('qo,tko->tqk', masked, green, preferred_element_type=F32)  3.69 us
    dot_general x1, matrix products, local(): jnp.einsum('qo,tok->tqk', masked, green, preferred_element_type=F32)  2.92 us
  transfers between devices with their start and end apart: 15, of which 4 were waited for; matrix products, arithmetic and copies ran while one was open for 8% of the time, Pallas kernels for 8%

profile of v12, /device:TPU:1, one launch (start us, length us, event | category | flops | bytes accessed | tf_op | source)
XLA Modules:
  0.0 83.3 jit_solution(12010703005259015359)
XLA Ops:
  0.0 1.1 %shard_map.46 = (bf16[128,1024]{1,0:T(8,128)(2,1)S(1)}, bf16[72,1024]{1,0:T(8,128)(2,1)S(1)}, f32[1,128]{1,0:T(1,128)S(1)}) custom-call(bf16[128,1024]{1,0:T(8,128)(2,1)} %factors_in.1, s32[1,8]{1,0:T(1,128)} %pattern_in.1, f32[1,128]{1,0:T(1,128)} %bitcast.12), custom_call_target="tpu_custom_call" | custom-call | tf_op jit(solution)/shard_map/pallas_call | solution.py:102
  1.2 2.5 %collective-permute-start = (bf16[72,1024]{1,0:T(8,128)(2,1)S(1)}, bf16[72,1024]{1,0:T(8,128)(2,1)S(1)}, u32[]{:S(2)}, u32[]{:S(2)}) collective-permute-start(bf16[72,1024]{1,0:T(8,128)(2,1)S(1)} %get-tuple-element.24), channel_id=1, source_target_pairs={{0,8},{1,9},{2,10},{3,11},{4,12},{5,13},{6,14},{7,15},{8,16},{9,17... | collective-permute-start | bytes 442376 | tf_op jit(solution)/shard_map/ppermute | solution.py:31
  3.7 4.0 %collective-permute-start.1 = (bf16[72,1024]{1,0:T(8,128)(2,1)S(1)}, bf16[72,1024]{1,0:T(8,128)(2,1)S(1)}, u32[]{:S(2)}, u32[]{:S(2)}) collective-permute-start(bf16[72,1024]{1,0:T(8,128)(2,1)S(1)} %get-tuple-element.24), channel_id=1, source_target_pairs={{0,152},{1,153},{2,154},{3,155},{4,156},{5,157},{6,158},{7,159},{8... | collective-permute-start | bytes 442376 | tf_op jit(solution)/shard_map/ppermute | solution.py:31
  7.7 1.8 %collective-permute-start.2 = (bf16[72,1024]{1,0:T(8,128)(2,1)S(1)}, bf16[72,1024]{1,0:T(8,128)(2,1)S(1)}, u32[]{:S(2)}, u32[]{:S(2)}) collective-permute-start(bf16[72,1024]{1,0:T(8,128)(2,1)S(1)} %get-tuple-element.24), channel_id=1, source_target_pairs={{0,16},{1,145},{2,18},{3,147},{4,20},{5,149},{6,22},{7,151},{8,24}... | collective-permute-start | bytes 442376 | tf_op jit(solution)/shard_map/ppermute | solution.py:31
  9.5 2.9 %fusion.1 = bf16[2,128,1024]{2,1,0:T(8,128)(2,1)S(1)} fusion(bf16[2,1024,1024]{2,1,0:T(8,128)(2,1)} %param.4, bf16[128,1024]{1,0:T(8,128)(2,1)S(1)} %get-tuple-element.25), kind=kOutput, calls=%fused_computation.3 | convolution fusion | flops 537133056 | bytes 4980736 | tf_op jit(solution)/shard_map/qo,tok->tqk/dot_general | solution.py:267
  12.5 2.5 %collective-permute-start.7 = (bf16[2,128,1024]{2,1,0:T(8,128)(2,1)S(1)}, bf16[2,128,1024]{2,1,0:T(8,128)(2,1)S(1)}, u32[]{:S(2)}, u32[]{:S(2)}) collective-permute-start(bf16[2,128,1024]{2,1,0:T(8,128)(2,1)S(1)} %fusion.1), channel_id=1, source_target_pairs={{0,16},{1,145},{2,18},{3,147},{4,20},{5,149},{6,22},{7,151},{8,24}... | collective-permute-start | bytes 1572872 | tf_op jit(solution)/shard_map/ppermute | solution.py:31
  15.0 0.0 collective-permute-done
  15.0 0.0 collective-permute-done.1
  15.0 0.0 collective-permute-done.2
  15.1 0.1 concatenate.6.refs_4_.refs_0_
  15.2 1.3 %collective-permute-start.3 = (bf16[264,1024]{1,0:T(8,128)(2,1)S(1)}, bf16[264,1024]{1,0:T(8,128)(2,1)S(1)}, u32[]{:S(2)}, u32[]{:S(2)}) collective-permute-start(bf16[264,1024]{1,0:T(8,128)(2,1)S(1)} %concatenate.6.refs_4_.refs_0_), channel_id=1, source_target_pairs={{0,2},{1,3},{2,4},{3,5},{4,6},{5,7},{6,0},{7,1},{8,10},{9,11},{10,... | collective-permute-start | bytes 1622024 | tf_op jit(solution)/shard_map/ppermute | solution.py:31
  16.5 1.5 %collective-permute-start.4 = (bf16[264,1024]{1,0:T(8,128)(2,1)S(1)}, bf16[264,1024]{1,0:T(8,128)(2,1)S(1)}, u32[]{:S(2)}, u32[]{:S(2)}) collective-permute-start(bf16[264,1024]{1,0:T(8,128)(2,1)S(1)} %concatenate.6.refs_4_.refs_0_), channel_id=1, source_target_pairs={{0,6},{1,7},{2,0},{3,1},{4,2},{5,3},{6,4},{7,5},{8,14},{9,15},{10,... | collective-permute-start | bytes 1622024 | tf_op jit(solution)/shard_map/ppermute | solution.py:31
  18.0 2.8 %collective-permute-start.5 = (bf16[200,1024]{1,0:T(8,128)(2,1)S(1)}, bf16[200,1024]{1,0:T(8,128)(2,1)S(1)}, u32[]{:S(2)}, u32[]{:S(2)}) collective-permute-start(bf16[200,1024]{1,0:T(8,128)(2,1)S(1)} %slice.46), channel_id=1, source_target_pairs={{0,32},{1,97},{2,34},{3,99},{4,36},{5,101},{6,38},{7,103},{8,40},{... | collective-permute-start | bytes 1228808 | tf_op jit(solution)/shard_map/ppermute | solution.py:31
  20.8 3.7 %fusion.refs_0_ = bf16[2,128,1024]{2,1,0:T(8,128)(2,1)S(1)} fusion(bf16[2,1024,1024]{2,1,0:T(8,128)(2,1)} %param.4, bf16[128,1024]{1,0:T(8,128)(2,1)S(1)} %get-tuple-element.25), kind=kOutput, calls=%fused_computation.2 | convolution fusion | flops 537133056 | bytes 4980736 | tf_op jit(solution)/shard_map/qo,tko->tqk/dot_general | solution.py:279
  24.5 2.9 %collective-permute-done.7 = bf16[2,128,1024]{2,1,0:T(8,128)(2,1)S(1)} collective-permute-done((bf16[2,128,1024]{2,1,0:T(8,128)(2,1)S(1)}, bf16[2,128,1024]{2,1,0:T(8,128)(2,1)S(1)}, u32[]{:S(2)}, u32[]{:S(2)}) %collective-permute-start.7) | collective-permute-done | bytes 524320 | tf_op jit(solution)/shard_map/ppermute | solution.py:31
  27.4 2.7 %collective-permute-start.8 = (bf16[2,128,1024]{2,1,0:T(8,128)(2,1)S(1)}, bf16[2,128,1024]{2,1,0:T(8,128)(2,1)S(1)}, u32[]{:S(2)}, u32[]{:S(2)}) collective-permute-start(bf16[2,128,1024]{2,1,0:T(8,128)(2,1)S(1)} %collective-permute-done.7), channel_id=1, source_target_pairs={{0,16},{1,145},{2,18},{3,147},{4,20},{5,149},{6,22},{7,151},{8,24}... | collective-permute-start | bytes 1572872 | tf_op jit(solution)/shard_map/ppermute | solution.py:31
  30.1 0.0 collective-permute-done.5
  30.2 0.0 collective-permute-done.3.west_ref.refs_4_.refs_2_
  30.2 0.0 collective-permute-done.4.east_ref.refs_5_.refs_3_
  30.2 0.1 shard_map.47
  30.3 2.8 %collective-permute-start.12 = (bf16[528,1024]{1,0:T(8,128)(2,1)S(1)}, bf16[528,1024]{1,0:T(8,128)(2,1)S(1)}, u32[]{:S(2)}, u32[]{:S(2)}) collective-permute-start(bf16[528,1024]{1,0:T(8,128)(2,1)S(1)} %get-tuple-element.30), channel_id=1, source_target_pairs={{0,32},{1,97},{2,34},{3,99},{4,36},{5,101},{6,38},{7,103},{8,40},{... | collective-permute-start | bytes 3244040 | tf_op jit(solution)/shard_map/ppermute | solution.py:31
  33.1 2.5 %collective-permute-start.10 = (bf16[264,1024]{1,0:T(8,128)(2,1)S(1)}, bf16[264,1024]{1,0:T(8,128)(2,1)S(1)}, u32[]{:S(2)}, u32[]{:S(2)}) collective-permute-start(bf16[264,1024]{1,0:T(8,128)(2,1)S(1)} %get-tuple-element.29), channel_id=1, source_target_pairs={{0,2},{1,7},{2,4},{3,1},{4,6},{5,3},{6,0},{7,5},{8,10},{9,15},{10,... | collective-permute-start | bytes 1622024 | tf_op jit(solution)/shard_map/ppermute | solution.py:31
  35.6 0.0 collective-permute-start.6
  35.6 6.1 %collective-permute-done.8.refs_2_ = bf16[2,128,1024]{2,1,0:T(8,128)(2,1)S(1)} collective-permute-done((bf16[2,128,1024]{2,1,0:T(8,128)(2,1)S(1)}, bf16[2,128,1024]{2,1,0:T(8,128)(2,1)S(1)}, u32[]{:S(2)}, u32[]{:S(2)}) %collective-permute-start.8) | collective-permute-done | bytes 524320 | tf_op jit(solution)/shard_map/ppermute | solution.py:31
  41.7 2.5 %collective-permute-start.9 = (bf16[2,128,1024]{2,1,0:T(8,128)(2,1)S(1)}, bf16[2,128,1024]{2,1,0:T(8,128)(2,1)S(1)}, u32[]{:S(2)}, u32[]{:S(2)}) collective-permute-start(bf16[2,128,1024]{2,1,0:T(8,128)(2,1)S(1)} %collective-permute-done.8.refs_2_), channel_id=1, source_target_pairs={{0,1},{1,0},{2,3},{3,2},{4,5},{5,4},{6,7},{7,6},{8,9},{9,8},{10,11... | collective-permute-start | bytes 1572872 | tf_op jit(solution)/shard_map/ppermute | solution.py:31
  44.2 0.0 collective-permute-done.10.refs_5_
  44.2 2.7 %collective-permute-start.11 = (bf16[264,1024]{1,0:T(8,128)(2,1)S(1)}, bf16[264,1024]{1,0:T(8,128)(2,1)S(1)}, u32[]{:S(2)}, u32[]{:S(2)}) collective-permute-start(bf16[264,1024]{1,0:T(8,128)(2,1)S(1)} %collective-permute-done.10.refs_5_), channel_id=1, source_target_pairs={{0,32},{1,97},{2,34},{3,99},{4,36},{5,101},{6,38},{7,103},{8,40},{... | collective-permute-start | bytes 1622024 | tf_op jit(solution)/shard_map/ppermute | solution.py:31
  47.0 0.0 collective-permute-done.6.refs_1_
  47.0 0.0 collective-permute-done.9.refs_3_
  47.0 2.0 %shard_map.48 = (f32[2,128,1024]{2,1,0:T(8,128)S(1)}, f32[2,128,1024]{2,1,0:T(8,128)S(1)}) custom-call(bf16[2,128,1024]{2,1,0:T(8,128)(2,1)S(1)} %fusion.refs_0_, bf16[2,128,1024]{2,1,0:T(8,128)(2,1)S(1)} %collective-permute-done.6.refs_1_, bf16[2,128,1024]{2,1,0:T(8,128)(2,1)S(1)} %collective-permute-done.8.refs_2_, ...), custom_call_target="tpu_custom_call" | custom-call | flops 536870912 | bytes 2097152 | tf_op jit(solution)/shard_map/pallas_call | solution.py:197
  49.0 2.1 %shard_map.49 = (f32[2,128,1024]{2,1,0:T(8,128)S(1)}, f32[2,128,1024]{2,1,0:T(8,128)S(1)}) custom-call(bf16[2,128,1024]{2,1,0:T(8,128)(2,1)S(1)} %fusion.refs_0_, bf16[2,128,1024]{2,1,0:T(8,128)(2,1)S(1)} %collective-permute-done.6.refs_1_, bf16[2,128,1024]{2,1,0:T(8,128)(2,1)S(1)} %collective-permute-done.8.refs_2_, ...), custom_call_target="tpu_custom_call", output_to_operand_aliasing={{0}: (6, {}), {1}: (7, {})} | custom-call | flops 536870912 | bytes 2097152 | tf_op jit(solution)/shard_map/pallas_call | solution.py:197
  51.1 0.0 collective-permute-done.12.refs_4_
  51.1 2.8 %shard_map.50 = (f32[2,128,1024]{2,1,0:T(8,128)S(1)}, f32[2,128,1024]{2,1,0:T(8,128)S(1)}) custom-call(bf16[2,128,1024]{2,1,0:T(8,128)(2,1)S(1)} %fusion.refs_0_, bf16[2,128,1024]{2,1,0:T(8,128)(2,1)S(1)} %collective-permute-done.6.refs_1_, bf16[2,128,1024]{2,1,0:T(8,128)(2,1)S(1)} %collective-permute-done.8.refs_2_, ...), custom_call_target="tpu_custom_call", output_to_operand_aliasing={{0}: (6, {}), {1}: (7, {})} | custom-call | flops 805306368 | bytes 2097152 | tf_op jit(solution)/shard_map/pallas_call | solution.py:197
  53.9 0.0 collective-permute-done.11.refs_4_.refs_6_
  53.9 1.2 %shard_map.51 = (f32[2,128,1024]{2,1,0:T(8,128)S(1)}, bf16[2,128,1024]{2,1,0:T(8,128)(2,1)S(1)}) custom-call(bf16[2,128,1024]{2,1,0:T(8,128)(2,1)S(1)} %fusion.refs_0_, bf16[2,128,1024]{2,1,0:T(8,128)(2,1)S(1)} %collective-permute-done.6.refs_1_, bf16[2,128,1024]{2,1,0:T(8,128)(2,1)S(1)} %collective-permute-done.8.refs_2_, ...), custom_call_target="tpu_custom_call", output_to_operand_aliasing={{0}: (5, {})} | custom-call | flops 268435456 | bytes 2097152 | tf_op jit(solution)/shard_map/pallas_call | solution.py:197
  55.1 0.1 collective-permute-start.13
  55.2 1.9 %collective-permute-done.13.got_ref = bf16[2,128,1024]{2,1,0:T(8,128)(2,1)S(1)} collective-permute-done((bf16[2,128,1024]{2,1,0:T(8,128)(2,1)S(1)}, bf16[2,128,1024]{2,1,0:T(8,128)(2,1)S(1)}, u32[]{:S(2)}, u32[]{:S(2)}) %collective-permute-start.13) | collective-permute-done | bytes 524320 | tf_op jit(solution)/shard_map/ppermute | solution.py:31
  57.1 0.3 shard_map.52
  57.5 21.3 %all_to_all.5.part_ref = bf16[16,2,64,128]{3,2,1,0:T(8,128)(2,1)S(1)} all-to-all(bf16[16,2,64,128]{3,2,1,0:T(8,128)(2,1)S(1)} %shard_map.52), channel_id=1, replica_groups={{0,2,4,6,8,10,12,14,16,18,20,22,24,26,28,30},{1,3,5,7,9,11,13,15,17,19,..., dimensions={0} | all-to-all | bytes 1048576 | tf_op jit(solution)/shard_map/all_to_all | solution.py:308
  78.7 0.8 shard_map.53
  79.5 2.0 %collective-permute-start.14 = (bf16[2,32,1024]{2,1,0:T(8,128)(2,1)S(1)}, bf16[2,32,1024]{2,1,0:T(8,128)(2,1)S(1)}, u32[]{:S(2)}, u32[]{:S(2)}) collective-permute-start(bf16[2,32,1024]{2,1,0:T(8,128)(2,1)S(1)} %get-tuple-element.42), channel_id=1, source_target_pairs={{0,1},{1,0},{2,3},{3,2},{4,5},{5,4},{6,7},{7,6},{8,9},{9,8},{10,11... | collective-permute-start | bytes 393224 | tf_op jit(solution)/shard_map/ppermute | solution.py:31
  81.5 1.0 %collective-permute-done.14.got_ref = bf16[2,32,1024]{2,1,0:T(8,128)(2,1)S(1)} collective-permute-done((bf16[2,32,1024]{2,1,0:T(8,128)(2,1)S(1)}, bf16[2,32,1024]{2,1,0:T(8,128)(2,1)S(1)}, u32[]{:S(2)}, u32[]{:S(2)}) %collective-permute-start.14) | collective-permute-done | bytes 131104 | tf_op jit(solution)/shard_map/ppermute | solution.py:31
  82.5 0.8 shard_map.54
  (12 shorter events, 0.1 us)
Async XLA Ops:
  1.2 13.8 %collective-permute-start = (bf16[72,1024]{1,0:T(8,128)(2,1)S(1)}, bf16[72,1024]{1,0:T(8,128)(2,1)S(1)}, u32[]{:S(2)}, u32[]{:S(2)}) collective-permute-start(bf16[72,1024]{1,0:T(8,128)(2,1)S(1)} %get-tuple-element.24), channel_id=1, source_target_pairs={{0,8},{1,9},{2,10},{3,11},{4,12},{5,13},{6,14},{7,15},{8,16},{9,17... | collective-permute-start | bytes 442376 | tf_op jit(solution)/shard_map/ppermute | solution.py:31
  3.7 11.3 %collective-permute-start.1 = (bf16[72,1024]{1,0:T(8,128)(2,1)S(1)}, bf16[72,1024]{1,0:T(8,128)(2,1)S(1)}, u32[]{:S(2)}, u32[]{:S(2)}) collective-permute-start(bf16[72,1024]{1,0:T(8,128)(2,1)S(1)} %get-tuple-element.24), channel_id=1, source_target_pairs={{0,152},{1,153},{2,154},{3,155},{4,156},{5,157},{6,158},{7,159},{8... | collective-permute-start | bytes 442376 | tf_op jit(solution)/shard_map/ppermute | solution.py:31
  7.7 7.3 %collective-permute-start.2 = (bf16[72,1024]{1,0:T(8,128)(2,1)S(1)}, bf16[72,1024]{1,0:T(8,128)(2,1)S(1)}, u32[]{:S(2)}, u32[]{:S(2)}) collective-permute-start(bf16[72,1024]{1,0:T(8,128)(2,1)S(1)} %get-tuple-element.24), channel_id=1, source_target_pairs={{0,16},{1,145},{2,18},{3,147},{4,20},{5,149},{6,22},{7,151},{8,24}... | collective-permute-start | bytes 442376 | tf_op jit(solution)/shard_map/ppermute | solution.py:31
  12.5 14.9 %collective-permute-start.7 = (bf16[2,128,1024]{2,1,0:T(8,128)(2,1)S(1)}, bf16[2,128,1024]{2,1,0:T(8,128)(2,1)S(1)}, u32[]{:S(2)}, u32[]{:S(2)}) collective-permute-start(bf16[2,128,1024]{2,1,0:T(8,128)(2,1)S(1)} %fusion.1), channel_id=1, source_target_pairs={{0,16},{1,145},{2,18},{3,147},{4,20},{5,149},{6,22},{7,151},{8,24}... | collective-permute-start | bytes 1572872 | tf_op jit(solution)/shard_map/ppermute | solution.py:31
  15.2 15.0 %collective-permute-start.3 = (bf16[264,1024]{1,0:T(8,128)(2,1)S(1)}, bf16[264,1024]{1,0:T(8,128)(2,1)S(1)}, u32[]{:S(2)}, u32[]{:S(2)}) collective-permute-start(bf16[264,1024]{1,0:T(8,128)(2,1)S(1)} %concatenate.6.refs_4_.refs_0_), channel_id=1, source_target_pairs={{0,2},{1,3},{2,4},{3,5},{4,6},{5,7},{6,0},{7,1},{8,10},{9,11},{10,... | collective-permute-start | bytes 1622024 | tf_op jit(solution)/shard_map/ppermute | solution.py:31
  16.5 13.7 %collective-permute-start.4 = (bf16[264,1024]{1,0:T(8,128)(2,1)S(1)}, bf16[264,1024]{1,0:T(8,128)(2,1)S(1)}, u32[]{:S(2)}, u32[]{:S(2)}) collective-permute-start(bf16[264,1024]{1,0:T(8,128)(2,1)S(1)} %concatenate.6.refs_4_.refs_0_), channel_id=1, source_target_pairs={{0,6},{1,7},{2,0},{3,1},{4,2},{5,3},{6,4},{7,5},{8,14},{9,15},{10,... | collective-permute-start | bytes 1622024 | tf_op jit(solution)/shard_map/ppermute | solution.py:31
  18.0 12.2 %collective-permute-start.5 = (bf16[200,1024]{1,0:T(8,128)(2,1)S(1)}, bf16[200,1024]{1,0:T(8,128)(2,1)S(1)}, u32[]{:S(2)}, u32[]{:S(2)}) collective-permute-start(bf16[200,1024]{1,0:T(8,128)(2,1)S(1)} %slice.46), channel_id=1, source_target_pairs={{0,32},{1,97},{2,34},{3,99},{4,36},{5,101},{6,38},{7,103},{8,40},{... | collective-permute-start | bytes 1228808 | tf_op jit(solution)/shard_map/ppermute | solution.py:31
  27.4 14.3 %collective-permute-start.8 = (bf16[2,128,1024]{2,1,0:T(8,128)(2,1)S(1)}, bf16[2,128,1024]{2,1,0:T(8,128)(2,1)S(1)}, u32[]{:S(2)}, u32[]{:S(2)}) collective-permute-start(bf16[2,128,1024]{2,1,0:T(8,128)(2,1)S(1)} %collective-permute-done.7), channel_id=1, source_target_pairs={{0,16},{1,145},{2,18},{3,147},{4,20},{5,149},{6,22},{7,151},{8,24}... | collective-permute-start | bytes 1572872 | tf_op jit(solution)/shard_map/ppermute | solution.py:31
  30.3 20.8 %collective-permute-start.12 = (bf16[528,1024]{1,0:T(8,128)(2,1)S(1)}, bf16[528,1024]{1,0:T(8,128)(2,1)S(1)}, u32[]{:S(2)}, u32[]{:S(2)}) collective-permute-start(bf16[528,1024]{1,0:T(8,128)(2,1)S(1)} %get-tuple-element.30), channel_id=1, source_target_pairs={{0,32},{1,97},{2,34},{3,99},{4,36},{5,101},{6,38},{7,103},{8,40},{... | collective-permute-start | bytes 3244040 | tf_op jit(solution)/shard_map/ppermute | solution.py:31
  33.1 11.1 %collective-permute-start.10 = (bf16[264,1024]{1,0:T(8,128)(2,1)S(1)}, bf16[264,1024]{1,0:T(8,128)(2,1)S(1)}, u32[]{:S(2)}, u32[]{:S(2)}) collective-permute-start(bf16[264,1024]{1,0:T(8,128)(2,1)S(1)} %get-tuple-element.29), channel_id=1, source_target_pairs={{0,2},{1,7},{2,4},{3,1},{4,6},{5,3},{6,0},{7,5},{8,10},{9,15},{10,... | collective-permute-start | bytes 1622024 | tf_op jit(solution)/shard_map/ppermute | solution.py:31
  35.6 11.4 %collective-permute-start.6 = (bf16[2,128,1024]{2,1,0:T(8,128)(2,1)S(1)}, bf16[2,128,1024]{2,1,0:T(8,128)(2,1)S(1)}, u32[]{:S(2)}, u32[]{:S(2)}) collective-permute-start(bf16[2,128,1024]{2,1,0:T(8,128)(2,1)S(1)} %fusion.refs_0_), channel_id=1, source_target_pairs={{0,1},{1,0},{2,3},{3,2},{4,5},{5,4},{6,7},{7,6},{8,9},{9,8},{10,11... | collective-permute-start | bytes 1572872 | tf_op jit(solution)/shard_map/ppermute | solution.py:31
  41.7 5.3 %collective-permute-start.9 = (bf16[2,128,1024]{2,1,0:T(8,128)(2,1)S(1)}, bf16[2,128,1024]{2,1,0:T(8,128)(2,1)S(1)}, u32[]{:S(2)}, u32[]{:S(2)}) collective-permute-start(bf16[2,128,1024]{2,1,0:T(8,128)(2,1)S(1)} %collective-permute-done.8.refs_2_), channel_id=1, source_target_pairs={{0,1},{1,0},{2,3},{3,2},{4,5},{5,4},{6,7},{7,6},{8,9},{9,8},{10,11... | collective-permute-start | bytes 1572872 | tf_op jit(solution)/shard_map/ppermute | solution.py:31
  44.2 9.7 %collective-permute-start.11 = (bf16[264,1024]{1,0:T(8,128)(2,1)S(1)}, bf16[264,1024]{1,0:T(8,128)(2,1)S(1)}, u32[]{:S(2)}, u32[]{:S(2)}) collective-permute-start(bf16[264,1024]{1,0:T(8,128)(2,1)S(1)} %collective-permute-done.10.refs_5_), channel_id=1, source_target_pairs={{0,32},{1,97},{2,34},{3,99},{4,36},{5,101},{6,38},{7,103},{8,40},{... | collective-permute-start | bytes 1622024 | tf_op jit(solution)/shard_map/ppermute | solution.py:31
  55.1 2.0 %collective-permute-start.13 = (bf16[2,128,1024]{2,1,0:T(8,128)(2,1)S(1)}, bf16[2,128,1024]{2,1,0:T(8,128)(2,1)S(1)}, u32[]{:S(2)}, u32[]{:S(2)}) collective-permute-start(bf16[2,128,1024]{2,1,0:T(8,128)(2,1)S(1)} %get-tuple-element.39), channel_id=1, source_target_pairs={{0,1},{1,0},{2,3},{3,2},{4,5},{5,4},{6,7},{7,6},{8,9},{9,8},{10,11... | collective-permute-start | bytes 1572872 | tf_op jit(solution)/shard_map/ppermute | solution.py:31
  79.5 3.0 %collective-permute-start.14 = (bf16[2,32,1024]{2,1,0:T(8,128)(2,1)S(1)}, bf16[2,32,1024]{2,1,0:T(8,128)(2,1)S(1)}, u32[]{:S(2)}, u32[]{:S(2)}) collective-permute-start(bf16[2,32,1024]{2,1,0:T(8,128)(2,1)S(1)} %get-tuple-element.42), channel_id=1, source_target_pairs={{0,1},{1,0},{2,3},{3,2},{4,5},{5,4},{6,7},{7,6},{8,9},{9,8},{10,11... | collective-permute-start | bytes 393224 | tf_op jit(solution)/shard_map/ppermute | solution.py:31

commit v13 on v12

--- a/solution.py
+++ b/solution.py
@@ -118,6 +118,27 @@
     )(*[pltpu.with_memory_space_constraint(v, pltpu.HBM) for v in (factors, pattern, coulomb[None, :])])
 
 
+def project_kernel(dims, masked_ref, green_ref, out_ref):
+    for t in range(green_ref.shape[0]):
+        out_ref[t] = lax.dot_general(
+            masked_ref[...], green_ref[t], dims, preferred_element_type=F32
+        ).astype(BF16)
+
+
+def project(masked, green, dims):
+    own, orb = masked.shape
+    return pl.pallas_call(
+        functools.partial(project_kernel, dims),
+        out_shape=jax.ShapeDtypeStruct((green.shape[0], own, orb), BF16),
+        in_specs=[VMEM] * 2,
+        out_specs=VMEM,
+        compiler_params=params(12),
+        cost_estimate=pl.CostEstimate(
+            flops=2 * green.shape[0] * own * orb * orb, bytes_accessed=4 << 20, transcendentals=0
+        ),
+    )(masked, green)
+
+
 def mix_kernel(west_ref, east_ref, onward_ref, both_ref):
     core = lax.axis_index("aux") & 1
     n = west_ref.shape[0]
@@ -264,7 +285,7 @@
     beyond = two_along_z(whole)
     below = along_z(whole, 1)
     above = along_z(whole, -1)
-    left = jnp.einsum("qo,tok->tqk", masked, green, preferred_element_type=F32).astype(BF16)
+    left = project(masked, green, NN)
     left = two_along_z(left)
 
     blocks = [whole, below, above, beyond]
@@ -276,7 +297,7 @@
     east = along_x(here, -1)
     rest = other_parity(here[HALF:])
     here_q = jnp.concatenate([masked[HALF:], rest], axis=0)
-    right = jnp.einsum("qo,tko->tqk", masked, green, preferred_element_type=F32).astype(BF16)
+    right = project(masked, green, NT)
     west, east, right, here_q = barrier((west, east, right, here_q))
     right_other = other_core(right)
     onward, both = mix(west, east)
@@ -288,10 +309,9 @@
     left_other = other_core(left)
 
     lefts = (left, left_other)
-    two = [(0, 0, n), (1, 0, n)]
+    four = [(k, 0, n) for k in range(4)]
     sides = rights + lefts
-    acc = chunk(sides, (here, here_q), two)
-    acc = chunk(sides, (west, east), two, acc=acc)
+    acc = chunk(sides, (here, here_q, west, east), four)
     acc = chunk(sides, (sides_q, far), [(0, 0, n), (0, n + 8, n), (1, 0, n)], acc=acc)
     keep, theirs = chunk(sides, (far_q,), [(0, 0, n)], acc=acc, last=True)
 

time: 83.5 us -> 83.3 us (level)
  matrix products: 6.61 us -> 0 us
  local copies, waits for them, and re-layouts: 0.19 us -> 4.56 us
  Pallas kernels: 11.2 us -> 12.8 us
    dot_general x2 -> x0, matrix products: 6.61 us -> none  [the longest x1 3.69 us: local(): jnp.einsum('qo,tko->tqk', masked, green, preferred_element_type=F32)]
    unnamed x0 -> x4, local copies, waits for them, and re-layouts: none -> 4.37 us
    pallas_call x0 -> x2, Pallas kernels: none -> 2.22 us  [project(): pl.pallas_call(functools.partial(project_kernel, dims), out_shape=jax.Sha...]
    pallas_call x4 -> x3, Pallas kernels: 8.1 us -> 7.41 us  [chunk(): pl.pallas_call(functools.partial(chunk_kernel, tuple(pieces), len(sides),...]
  transfers between devices with their start and end apart: 15 -> 15, of which waited for: 4 -> 5; matrix products, arithmetic and copies ran while one was open for 8% -> 0% of each run, Pallas kernels for 8% -> 10%
where the time goes in v13:
time: 83.3 us; the launch traced here: 83.1 us
  starting transfers between devices  31.9 us (38%)
  blocking collectives  21.3 us (26%)
  Pallas kernels  12.8 us (15%)
  waiting for transfers between devices  12.4 us (15%)
  local copies, waits for them, and re-layouts  4.56 us (5%)
    ppermute x15, starting transfers between devices, send(): return lax.ppermute(value, BOTH, sorted(pairs))  31.9 us
    all_to_all x1, blocking collectives, local(): lax.all_to_all(part, 'aux', 0, 0, axis_index_groups=groups, tiled=True)  21.3 us
    ppermute x15, waiting for transfers between devices, send(): return lax.ppermute(value, BOTH, sorted(pairs))  12.4 us
    pallas_call x3, Pallas kernels, chunk(): pl.pallas_call(functools.partial(chunk_kernel, tuple(pieces), len(sides),...  7.41 us
    unnamed x4, local copies, waits for them, and re-layouts  4.37 us
    pallas_call x2, Pallas kernels, project(): pl.pallas_call(functools.partial(project_kernel, dims), out_shape=jax.Sha...  2.22 us
  transfers between devices with their start and end apart: 15, of which 5 were waited for; matrix products, arithmetic and copies ran while one was open for 0% of the time, Pallas kernels for 10%

profile of v13, /device:TPU:1, one launch (start us, length us, event | category | flops | bytes accessed | tf_op | source)
XLA Modules:
  0.0 83.1 jit_solution(6196650782714751443)
XLA Ops:
  0.0 1.1 %shard_map.46 = (bf16[128,1024]{1,0:T(8,128)(2,1)S(1)}, bf16[72,1024]{1,0:T(8,128)(2,1)S(1)}, f32[1,128]{1,0:T(1,128)S(1)}) custom-call(bf16[128,1024]{1,0:T(8,128)(2,1)} %factors_in.1, s32[1,8]{1,0:T(1,128)} %pattern_in.1, f32[1,128]{1,0:T(1,128)} %bitcast.1), custom_call_target="tpu_custom_call" | custom-call | tf_op jit(solution)/shard_map/pallas_call | solution.py:102
  1.2 2.5 %collective-permute-start = (bf16[72,1024]{1,0:T(8,128)(2,1)S(1)}, bf16[72,1024]{1,0:T(8,128)(2,1)S(1)}, u32[]{:S(2)}, u32[]{:S(2)}) collective-permute-start(bf16[72,1024]{1,0:T(8,128)(2,1)S(1)} %get-tuple-element.22), channel_id=1, source_target_pairs={{0,8},{1,9},{2,10},{3,11},{4,12},{5,13},{6,14},{7,15},{8,16},{9,17... | collective-permute-start | bytes 442376 | tf_op jit(solution)/shard_map/ppermute | solution.py:31
  3.7 4.0 %collective-permute-start.1 = (bf16[72,1024]{1,0:T(8,128)(2,1)S(1)}, bf16[72,1024]{1,0:T(8,128)(2,1)S(1)}, u32[]{:S(2)}, u32[]{:S(2)}) collective-permute-start(bf16[72,1024]{1,0:T(8,128)(2,1)S(1)} %get-tuple-element.22), channel_id=1, source_target_pairs={{0,152},{1,153},{2,154},{3,155},{4,156},{5,157},{6,158},{7,159},{8... | collective-permute-start | bytes 442376 | tf_op jit(solution)/shard_map/ppermute | solution.py:31
  7.7 1.8 %collective-permute-start.2 = (bf16[72,1024]{1,0:T(8,128)(2,1)S(1)}, bf16[72,1024]{1,0:T(8,128)(2,1)S(1)}, u32[]{:S(2)}, u32[]{:S(2)}) collective-permute-start(bf16[72,1024]{1,0:T(8,128)(2,1)S(1)} %get-tuple-element.22), channel_id=1, source_target_pairs={{0,16},{1,145},{2,18},{3,147},{4,20},{5,149},{6,22},{7,151},{8,24}... | collective-permute-start | bytes 442376 | tf_op jit(solution)/shard_map/ppermute | solution.py:31
  9.5 0.0 copy-start
  9.5 2.2 %copy-done = bf16[2,1024,1024]{2,1,0:T(8,128)(2,1)S(1)} copy-done((bf16[2,1024,1024]{2,1,0:T(8,128)(2,1)S(1)}, bf16[2,1024,1024]{2,1,0:T(8,128)(2,1)}, u32[]{:S(2)}) %copy-start) | copy-done | bytes 4194328
  11.7 0.7 shard_map.48
  12.5 2.5 %collective-permute-start.7 = (bf16[2,128,1024]{2,1,0:T(8,128)(2,1)S(1)}, bf16[2,128,1024]{2,1,0:T(8,128)(2,1)S(1)}, u32[]{:S(2)}, u32[]{:S(2)}) collective-permute-start(bf16[2,128,1024]{2,1,0:T(8,128)(2,1)S(1)} %shard_map.48), channel_id=1, source_target_pairs={{0,16},{1,145},{2,18},{3,147},{4,20},{5,149},{6,22},{7,151},{8,24}... | collective-permute-start | bytes 1572872 | tf_op jit(solution)/shard_map/ppermute | solution.py:31
  14.9 0.0 collective-permute-done
  15.0 0.0 collective-permute-done.1
  15.0 0.0 collective-permute-done.2
  15.1 0.1 concatenate.6.refs_4_.refs_0_
  15.2 1.3 %collective-permute-start.3 = (bf16[264,1024]{1,0:T(8,128)(2,1)S(1)}, bf16[264,1024]{1,0:T(8,128)(2,1)S(1)}, u32[]{:S(2)}, u32[]{:S(2)}) collective-permute-start(bf16[264,1024]{1,0:T(8,128)(2,1)S(1)} %concatenate.6.refs_4_.refs_0_), channel_id=1, source_target_pairs={{0,2},{1,3},{2,4},{3,5},{4,6},{5,7},{6,0},{7,1},{8,10},{9,11},{10,... | collective-permute-start | bytes 1622024 | tf_op jit(solution)/shard_map/ppermute | solution.py:31
  16.5 1.5 %collective-permute-start.4 = (bf16[264,1024]{1,0:T(8,128)(2,1)S(1)}, bf16[264,1024]{1,0:T(8,128)(2,1)S(1)}, u32[]{:S(2)}, u32[]{:S(2)}) collective-permute-start(bf16[264,1024]{1,0:T(8,128)(2,1)S(1)} %concatenate.6.refs_4_.refs_0_), channel_id=1, source_target_pairs={{0,6},{1,7},{2,0},{3,1},{4,2},{5,3},{6,4},{7,5},{8,14},{9,15},{10,... | collective-permute-start | bytes 1622024 | tf_op jit(solution)/shard_map/ppermute | solution.py:31
  18.0 2.8 %collective-permute-start.5 = (bf16[200,1024]{1,0:T(8,128)(2,1)S(1)}, bf16[200,1024]{1,0:T(8,128)(2,1)S(1)}, u32[]{:S(2)}, u32[]{:S(2)}) collective-permute-start(bf16[200,1024]{1,0:T(8,128)(2,1)S(1)} %slice.46), channel_id=1, source_target_pairs={{0,32},{1,97},{2,34},{3,99},{4,36},{5,101},{6,38},{7,103},{8,40},{... | collective-permute-start | bytes 1228808 | tf_op jit(solution)/shard_map/ppermute | solution.py:31
  20.8 0.0 copy-start.1
  20.8 2.2 %copy-done.1 = bf16[2,1024,1024]{2,1,0:T(8,128)(2,1)S(1)} copy-done((bf16[2,1024,1024]{2,1,0:T(8,128)(2,1)S(1)}, bf16[2,1024,1024]{2,1,0:T(8,128)(2,1)}, u32[]{:S(2)}) %copy-start.1) | copy-done | bytes 4194328
  23.0 1.5 %shard_map.47.refs_0_ = bf16[2,128,1024]{2,1,0:T(8,128)(2,1)S(1)} custom-call(bf16[128,1024]{1,0:T(8,128)(2,1)S(1)} %get-tuple-element.23.masked_ref, bf16[2,1024,1024]{2,1,0:T(8,128)(2,1)S(1)} %copy-done.1), custom_call_target="tpu_custom_call" | custom-call | flops 536870912 | bytes 4194304 | tf_op jit(solution)/shard_map/pallas_call | solution.py:130
  24.5 2.9 %collective-permute-done.7 = bf16[2,128,1024]{2,1,0:T(8,128)(2,1)S(1)} collective-permute-done((bf16[2,128,1024]{2,1,0:T(8,128)(2,1)S(1)}, bf16[2,128,1024]{2,1,0:T(8,128)(2,1)S(1)}, u32[]{:S(2)}, u32[]{:S(2)}) %collective-permute-start.7) | collective-permute-done | bytes 524320 | tf_op jit(solution)/shard_map/ppermute | solution.py:31
  27.4 2.7 %collective-permute-start.8 = (bf16[2,128,1024]{2,1,0:T(8,128)(2,1)S(1)}, bf16[2,128,1024]{2,1,0:T(8,128)(2,1)S(1)}, u32[]{:S(2)}, u32[]{:S(2)}) collective-permute-start(bf16[2,128,1024]{2,1,0:T(8,128)(2,1)S(1)} %collective-permute-done.7), channel_id=1, source_target_pairs={{0,16},{1,145},{2,18},{3,147},{4,20},{5,149},{6,22},{7,151},{8,24}... | collective-permute-start | bytes 1572872 | tf_op jit(solution)/shard_map/ppermute | solution.py:31
  30.1 0.0 collective-permute-done.5
  30.2 0.0 collective-permute-done.3.west_ref.refs_6_.refs_2_
  30.2 0.0 collective-permute-done.4.east_ref.refs_7_.refs_3_
  30.2 0.1 shard_map.49
  30.3 2.8 %collective-permute-start.12 = (bf16[528,1024]{1,0:T(8,128)(2,1)S(1)}, bf16[528,1024]{1,0:T(8,128)(2,1)S(1)}, u32[]{:S(2)}, u32[]{:S(2)}) collective-permute-start(bf16[528,1024]{1,0:T(8,128)(2,1)S(1)} %get-tuple-element.28), channel_id=1, source_target_pairs={{0,32},{1,97},{2,34},{3,99},{4,36},{5,101},{6,38},{7,103},{8,40},{... | collective-permute-start | bytes 3244040 | tf_op jit(solution)/shard_map/ppermute | solution.py:31
  33.1 2.5 %collective-permute-start.10 = (bf16[264,1024]{1,0:T(8,128)(2,1)S(1)}, bf16[264,1024]{1,0:T(8,128)(2,1)S(1)}, u32[]{:S(2)}, u32[]{:S(2)}) collective-permute-start(bf16[264,1024]{1,0:T(8,128)(2,1)S(1)} %get-tuple-element.27), channel_id=1, source_target_pairs={{0,2},{1,7},{2,4},{3,1},{4,6},{5,3},{6,0},{7,5},{8,10},{9,15},{10,... | collective-permute-start | bytes 1622024 | tf_op jit(solution)/shard_map/ppermute | solution.py:31
  35.6 0.0 collective-permute-start.6
  35.6 6.1 %collective-permute-done.8.refs_2_ = bf16[2,128,1024]{2,1,0:T(8,128)(2,1)S(1)} collective-permute-done((bf16[2,128,1024]{2,1,0:T(8,128)(2,1)S(1)}, bf16[2,128,1024]{2,1,0:T(8,128)(2,1)S(1)}, u32[]{:S(2)}, u32[]{:S(2)}) %collective-permute-start.8) | collective-permute-done | bytes 524320 | tf_op jit(solution)/shard_map/ppermute | solution.py:31
  41.7 2.5 %collective-permute-start.9 = (bf16[2,128,1024]{2,1,0:T(8,128)(2,1)S(1)}, bf16[2,128,1024]{2,1,0:T(8,128)(2,1)S(1)}, u32[]{:S(2)}, u32[]{:S(2)}) collective-permute-start(bf16[2,128,1024]{2,1,0:T(8,128)(2,1)S(1)} %collective-permute-done.8.refs_2_), channel_id=1, source_target_pairs={{0,1},{1,0},{2,3},{3,2},{4,5},{5,4},{6,7},{7,6},{8,9},{9,8},{10,11... | collective-permute-start | bytes 1572872 | tf_op jit(solution)/shard_map/ppermute | solution.py:31
  44.2 0.0 collective-permute-done.10.refs_5_
  44.2 2.7 %collective-permute-start.11 = (bf16[264,1024]{1,0:T(8,128)(2,1)S(1)}, bf16[264,1024]{1,0:T(8,128)(2,1)S(1)}, u32[]{:S(2)}, u32[]{:S(2)}) collective-permute-start(bf16[264,1024]{1,0:T(8,128)(2,1)S(1)} %collective-permute-done.10.refs_5_), channel_id=1, source_target_pairs={{0,32},{1,97},{2,34},{3,99},{4,36},{5,101},{6,38},{7,103},{8,40},{... | collective-permute-start | bytes 1622024 | tf_op jit(solution)/shard_map/ppermute | solution.py:31
  47.0 0.0 collective-permute-done.6.refs_1_
  47.0 0.0 collective-permute-done.9.refs_3_
  47.0 3.5 %shard_map.50 = (f32[2,128,1024]{2,1,0:T(8,128)S(1)}, f32[2,128,1024]{2,1,0:T(8,128)S(1)}) custom-call(bf16[2,128,1024]{2,1,0:T(8,128)(2,1)S(1)} %shard_map.47.refs_0_, bf16[2,128,1024]{2,1,0:T(8,128)(2,1)S(1)} %collective-permute-done.6.refs_1_, bf16[2,128,1024]{2,1,0:T(8,128)(2,1)S(1)} %collective-permute-done.8.refs_2_, ...), custom_call_target="tpu_custom_call" | custom-call | flops 1073741824 | bytes 2097152 | tf_op jit(solution)/shard_map/pallas_call | solution.py:218
  50.4 0.0 collective-permute-done.12.refs_4_
  50.4 2.8 %shard_map.51 = (f32[2,128,1024]{2,1,0:T(8,128)S(1)}, f32[2,128,1024]{2,1,0:T(8,128)S(1)}) custom-call(bf16[2,128,1024]{2,1,0:T(8,128)(2,1)S(1)} %shard_map.47.refs_0_, bf16[2,128,1024]{2,1,0:T(8,128)(2,1)S(1)} %collective-permute-done.6.refs_1_, ...), custom_call_target="tpu_custom_call", output_to_operand_aliasing={{0}: (6, {}), {1}: (7, {})} | custom-call | flops 805306368 | bytes 2097152 | tf_op jit(solution)/shard_map/pallas_call | solution.py:218
  53.2 0.5 collective-permute-done.11.refs_4_.refs_6_
  53.7 1.2 %shard_map.52 = (f32[2,128,1024]{2,1,0:T(8,128)S(1)}, bf16[2,128,1024]{2,1,0:T(8,128)(2,1)S(1)}) custom-call(bf16[2,128,1024]{2,1,0:T(8,128)(2,1)S(1)} %shard_map.47.refs_0_, bf16[2,128,1024]{2,1,0:T(8,128)(2,1)S(1)} %collective-permute-done.6.refs_1_, bf16[2,128,1024]{2,1,0:T(8,128)(2,1)S(1)} %collective-permute-done.8.refs_2_, ...), custom_call_target="tpu_custom_call", output_to_operand_aliasing={{0}: (5, {})} | custom-call | flops 268435456 | bytes 2097152 | tf_op jit(solution)/shard_map/pallas_call | solution.py:218
  54.9 0.1 collective-permute-start.13
  55.0 1.9 %collective-permute-done.13.got_ref = bf16[2,128,1024]{2,1,0:T(8,128)(2,1)S(1)} collective-permute-done((bf16[2,128,1024]{2,1,0:T(8,128)(2,1)S(1)}, bf16[2,128,1024]{2,1,0:T(8,128)(2,1)S(1)}, u32[]{:S(2)}, u32[]{:S(2)}) %collective-permute-start.13) | collective-permute-done | bytes 524320 | tf_op jit(solution)/shard_map/ppermute | solution.py:31
  56.9 0.3 shard_map.53
  57.3 21.3 %all_to_all.5.part_ref = bf16[16,2,64,128]{3,2,1,0:T(8,128)(2,1)S(1)} all-to-all(bf16[16,2,64,128]{3,2,1,0:T(8,128)(2,1)S(1)} %shard_map.53), channel_id=1, replica_groups={{0,2,4,6,8,10,12,14,16,18,20,22,24,26,28,30},{1,3,5,7,9,11,13,15,17,19,..., dimensions={0} | all-to-all | bytes 1048576 | tf_op jit(solution)/shard_map/all_to_all | solution.py:328
  78.5 0.8 shard_map.54
  79.3 2.0 %collective-permute-start.14 = (bf16[2,32,1024]{2,1,0:T(8,128)(2,1)S(1)}, bf16[2,32,1024]{2,1,0:T(8,128)(2,1)S(1)}, u32[]{:S(2)}, u32[]{:S(2)}) collective-permute-start(bf16[2,32,1024]{2,1,0:T(8,128)(2,1)S(1)} %get-tuple-element.38), channel_id=1, source_target_pairs={{0,1},{1,0},{2,3},{3,2},{4,5},{5,4},{6,7},{7,6},{8,9},{9,8},{10,11... | collective-permute-start | bytes 393224 | tf_op jit(solution)/shard_map/ppermute | solution.py:31
  81.3 1.0 %collective-permute-done.14.got_ref = bf16[2,32,1024]{2,1,0:T(8,128)(2,1)S(1)} collective-permute-done((bf16[2,32,1024]{2,1,0:T(8,128)(2,1)S(1)}, bf16[2,32,1024]{2,1,0:T(8,128)(2,1)S(1)}, u32[]{:S(2)}, u32[]{:S(2)}) %collective-permute-start.14) | collective-permute-done | bytes 131104 | tf_op jit(solution)/shard_map/ppermute | solution.py:31
  82.3 0.8 shard_map.55
  (12 shorter events, 0.1 us)
Async XLA Ops:
  1.2 13.8 %collective-permute-start = (bf16[72,1024]{1,0:T(8,128)(2,1)S(1)}, bf16[72,1024]{1,0:T(8,128)(2,1)S(1)}, u32[]{:S(2)}, u32[]{:S(2)}) collective-permute-start(bf16[72,1024]{1,0:T(8,128)(2,1)S(1)} %get-tuple-element.22), channel_id=1, source_target_pairs={{0,8},{1,9},{2,10},{3,11},{4,12},{5,13},{6,14},{7,15},{8,16},{9,17... | collective-permute-start | bytes 442376 | tf_op jit(solution)/shard_map/ppermute | solution.py:31
  3.7 11.3 %collective-permute-start.1 = (bf16[72,1024]{1,0:T(8,128)(2,1)S(1)}, bf16[72,1024]{1,0:T(8,128)(2,1)S(1)}, u32[]{:S(2)}, u32[]{:S(2)}) collective-permute-start(bf16[72,1024]{1,0:T(8,128)(2,1)S(1)} %get-tuple-element.22), channel_id=1, source_target_pairs={{0,152},{1,153},{2,154},{3,155},{4,156},{5,157},{6,158},{7,159},{8... | collective-permute-start | bytes 442376 | tf_op jit(solution)/shard_map/ppermute | solution.py:31
  7.7 7.3 %collective-permute-start.2 = (bf16[72,1024]{1,0:T(8,128)(2,1)S(1)}, bf16[72,1024]{1,0:T(8,128)(2,1)S(1)}, u32[]{:S(2)}, u32[]{:S(2)}) collective-permute-start(bf16[72,1024]{1,0:T(8,128)(2,1)S(1)} %get-tuple-element.22), channel_id=1, source_target_pairs={{0,16},{1,145},{2,18},{3,147},{4,20},{5,149},{6,22},{7,151},{8,24}... | collective-permute-start | bytes 442376 | tf_op jit(solution)/shard_map/ppermute | solution.py:31
  9.5 2.2 %copy-start = (bf16[2,1024,1024]{2,1,0:T(8,128)(2,1)S(1)}, bf16[2,1024,1024]{2,1,0:T(8,128)(2,1)}, u32[]{:S(2)}) copy-start(bf16[2,1024,1024]{2,1,0:T(8,128)(2,1)} %green_ref.3) | copy-start | bytes 12582916
  12.5 14.9 %collective-permute-start.7 = (bf16[2,128,1024]{2,1,0:T(8,128)(2,1)S(1)}, bf16[2,128,1024]{2,1,0:T(8,128)(2,1)S(1)}, u32[]{:S(2)}, u32[]{:S(2)}) collective-permute-start(bf16[2,128,1024]{2,1,0:T(8,128)(2,1)S(1)} %shard_map.48), channel_id=1, source_target_pairs={{0,16},{1,145},{2,18},{3,147},{4,20},{5,149},{6,22},{7,151},{8,24}... | collective-permute-start | bytes 1572872 | tf_op jit(solution)/shard_map/ppermute | solution.py:31
  15.2 15.0 %collective-permute-start.3 = (bf16[264,1024]{1,0:T(8,128)(2,1)S(1)}, bf16[264,1024]{1,0:T(8,128)(2,1)S(1)}, u32[]{:S(2)}, u32[]{:S(2)}) collective-permute-start(bf16[264,1024]{1,0:T(8,128)(2,1)S(1)} %concatenate.6.refs_4_.refs_0_), channel_id=1, source_target_pairs={{0,2},{1,3},{2,4},{3,5},{4,6},{5,7},{6,0},{7,1},{8,10},{9,11},{10,... | collective-permute-start | bytes 1622024 | tf_op jit(solution)/shard_map/ppermute | solution.py:31
  16.5 13.7 %collective-permute-start.4 = (bf16[264,1024]{1,0:T(8,128)(2,1)S(1)}, bf16[264,1024]{1,0:T(8,128)(2,1)S(1)}, u32[]{:S(2)}, u32[]{:S(2)}) collective-permute-start(bf16[264,1024]{1,0:T(8,128)(2,1)S(1)} %concatenate.6.refs_4_.refs_0_), channel_id=1, source_target_pairs={{0,6},{1,7},{2,0},{3,1},{4,2},{5,3},{6,4},{7,5},{8,14},{9,15},{10,... | collective-permute-start | bytes 1622024 | tf_op jit(solution)/shard_map/ppermute | solution.py:31
  18.0 12.2 %collective-permute-start.5 = (bf16[200,1024]{1,0:T(8,128)(2,1)S(1)}, bf16[200,1024]{1,0:T(8,128)(2,1)S(1)}, u32[]{:S(2)}, u32[]{:S(2)}) collective-permute-start(bf16[200,1024]{1,0:T(8,128)(2,1)S(1)} %slice.46), channel_id=1, source_target_pairs={{0,32},{1,97},{2,34},{3,99},{4,36},{5,101},{6,38},{7,103},{8,40},{... | collective-permute-start | bytes 1228808 | tf_op jit(solution)/shard_map/ppermute | solution.py:31
  20.8 2.2 %copy-start.1 = (bf16[2,1024,1024]{2,1,0:T(8,128)(2,1)S(1)}, bf16[2,1024,1024]{2,1,0:T(8,128)(2,1)}, u32[]{:S(2)}) copy-start(bf16[2,1024,1024]{2,1,0:T(8,128)(2,1)} %green_ref.3) | copy-start | bytes 12582916
  27.4 14.3 %collective-permute-start.8 = (bf16[2,128,1024]{2,1,0:T(8,128)(2,1)S(1)}, bf16[2,128,1024]{2,1,0:T(8,128)(2,1)S(1)}, u32[]{:S(2)}, u32[]{:S(2)}) collective-permute-start(bf16[2,128,1024]{2,1,0:T(8,128)(2,1)S(1)} %collective-permute-done.7), channel_id=1, source_target_pairs={{0,16},{1,145},{2,18},{3,147},{4,20},{5,149},{6,22},{7,151},{8,24}... | collective-permute-start | bytes 1572872 | tf_op jit(solution)/shard_map/ppermute | solution.py:31
  30.3 20.1 %collective-permute-start.12 = (bf16[528,1024]{1,0:T(8,128)(2,1)S(1)}, bf16[528,1024]{1,0:T(8,128)(2,1)S(1)}, u32[]{:S(2)}, u32[]{:S(2)}) collective-permute-start(bf16[528,1024]{1,0:T(8,128)(2,1)S(1)} %get-tuple-element.28), channel_id=1, source_target_pairs={{0,32},{1,97},{2,34},{3,99},{4,36},{5,101},{6,38},{7,103},{8,40},{... | collective-permute-start | bytes 3244040 | tf_op jit(solution)/shard_map/ppermute | solution.py:31
  33.1 11.1 %collective-permute-start.10 = (bf16[264,1024]{1,0:T(8,128)(2,1)S(1)}, bf16[264,1024]{1,0:T(8,128)(2,1)S(1)}, u32[]{:S(2)}, u32[]{:S(2)}) collective-permute-start(bf16[264,1024]{1,0:T(8,128)(2,1)S(1)} %get-tuple-element.27), channel_id=1, source_target_pairs={{0,2},{1,7},{2,4},{3,1},{4,6},{5,3},{6,0},{7,5},{8,10},{9,15},{10,... | collective-permute-start | bytes 1622024 | tf_op jit(solution)/shard_map/ppermute | solution.py:31
  35.6 11.4 %collective-permute-start.6 = (bf16[2,128,1024]{2,1,0:T(8,128)(2,1)S(1)}, bf16[2,128,1024]{2,1,0:T(8,128)(2,1)S(1)}, u32[]{:S(2)}, u32[]{:S(2)}) collective-permute-start(bf16[2,128,1024]{2,1,0:T(8,128)(2,1)S(1)} %shard_map.47.refs_0_), channel_id=1, source_target_pairs={{0,1},{1,0},{2,3},{3,2},{4,5},{5,4},{6,7},{7,6},{8,9},{9,8},{10,11... | collective-permute-start | bytes 1572872 | tf_op jit(solution)/shard_map/ppermute | solution.py:31
  41.7 5.3 %collective-permute-start.9 = (bf16[2,128,1024]{2,1,0:T(8,128)(2,1)S(1)}, bf16[2,128,1024]{2,1,0:T(8,128)(2,1)S(1)}, u32[]{:S(2)}, u32[]{:S(2)}) collective-permute-start(bf16[2,128,1024]{2,1,0:T(8,128)(2,1)S(1)} %collective-permute-done.8.refs_2_), channel_id=1, source_target_pairs={{0,1},{1,0},{2,3},{3,2},{4,5},{5,4},{6,7},{7,6},{8,9},{9,8},{10,11... | collective-permute-start | bytes 1572872 | tf_op jit(solution)/shard_map/ppermute | solution.py:31
  44.2 9.5 %collective-permute-start.11 = (bf16[264,1024]{1,0:T(8,128)(2,1)S(1)}, bf16[264,1024]{1,0:T(8,128)(2,1)S(1)}, u32[]{:S(2)}, u32[]{:S(2)}) collective-permute-start(bf16[264,1024]{1,0:T(8,128)(2,1)S(1)} %collective-permute-done.10.refs_5_), channel_id=1, source_target_pairs={{0,32},{1,97},{2,34},{3,99},{4,36},{5,101},{6,38},{7,103},{8,40},{... | collective-permute-start | bytes 1622024 | tf_op jit(solution)/shard_map/ppermute | solution.py:31
  54.9 2.0 %collective-permute-start.13 = (bf16[2,128,1024]{2,1,0:T(8,128)(2,1)S(1)}, bf16[2,128,1024]{2,1,0:T(8,128)(2,1)S(1)}, u32[]{:S(2)}, u32[]{:S(2)}) collective-permute-start(bf16[2,128,1024]{2,1,0:T(8,128)(2,1)S(1)} %get-tuple-element.35), channel_id=1, source_target_pairs={{0,1},{1,0},{2,3},{3,2},{4,5},{5,4},{6,7},{7,6},{8,9},{9,8},{10,11... | collective-permute-start | bytes 1572872 | tf_op jit(solution)/shard_map/ppermute | solution.py:31
  79.3 3.0 %collective-permute-start.14 = (bf16[2,32,1024]{2,1,0:T(8,128)(2,1)S(1)}, bf16[2,32,1024]{2,1,0:T(8,128)(2,1)S(1)}, u32[]{:S(2)}, u32[]{:S(2)}) collective-permute-start(bf16[2,32,1024]{2,1,0:T(8,128)(2,1)S(1)} %get-tuple-element.38), channel_id=1, source_target_pairs={{0,1},{1,0},{2,3},{3,2},{4,5},{5,4},{6,7},{7,6},{8,9},{9,8},{10,11... | collective-permute-start | bytes 393224 | tf_op jit(solution)/shard_map/ppermute | solution.py:31

commit v14 on v13

--- a/solution.py
+++ b/solution.py
@@ -139,24 +139,26 @@
     )(masked, green)
 
 
-def mix_kernel(west_ref, east_ref, onward_ref, both_ref):
+def pick_kernel(west_ref, east_ref, out_ref):
     core = lax.axis_index("aux") & 1
+    out_ref[...] = jnp.where(core == 0, west_ref[...], east_ref[...])
+
+
+def pair_kernel(west_ref, east_ref, first_ref, out_ref):
+    del first_ref
     n = west_ref.shape[0]
-    west, east = west_ref[...], east_ref[...]
-    onward_ref[...] = jnp.where(core == 0, west, east)
-    both_ref[pl.ds(0, n), :] = west
-    both_ref[pl.ds(n, n), :] = east
-
-
-def mix(west, east):
-    n, orb = west.shape
-    return pl.pallas_call(
-        mix_kernel,
-        out_shape=(jax.ShapeDtypeStruct((n, orb), BF16), jax.ShapeDtypeStruct((2 * n, orb), BF16)),
-        in_specs=[VMEM] * 2,
-        out_specs=[VMEM] * 2,
+    out_ref[pl.ds(0, n), :] = west_ref[...]
+    out_ref[pl.ds(n, n), :] = east_ref[...]
+
+
+def small(kernel, rows, *values):
+    return pl.pallas_call(
+        kernel,
+        out_shape=jax.ShapeDtypeStruct((rows, values[0].shape[1]), BF16),
+        in_specs=[VMEM] * len(values),
+        out_specs=VMEM,
         compiler_params=params(8),
-    )(west, east)
+    )(*values)
 
 
 def weight_of(ref, row):
@@ -298,9 +300,10 @@
     rest = other_parity(here[HALF:])
     here_q = jnp.concatenate([masked[HALF:], rest], axis=0)
     right = project(masked, green, NT)
+    right_other = other_core(right)
     west, east, right, here_q = barrier((west, east, right, here_q))
-    right_other = other_core(right)
-    onward, both = mix(west, east)
+    onward = small(pick_kernel, n + 8, west, east)
+    both = small(pair_kernel, 2 * (n + 8), west, east, right_other)
     far = split_x(onward)
     sides_q = other_parity(both)
     far_q = other_parity(far)

time: 83.3 us -> 83.3 us (level)
  no operation moved by 1% of the time
where the time goes in v14:
time: 83.3 us; the launch traced here: 83.1 us
  starting transfers between devices  32.5 us (39%)
  blocking collectives  21.3 us (26%)
  Pallas kernels  12.8 us (15%)
  waiting for transfers between devices  11.7 us (14%)
  local copies, waits for them, and re-layouts  4.56 us (5%)
    ppermute x15, starting transfers between devices, send(): return lax.ppermute(value, BOTH, sorted(pairs))  32.5 us
    all_to_all x1, blocking collectives, local(): lax.all_to_all(part, 'aux', 0, 0, axis_index_groups=groups, tiled=True)  21.3 us
    ppermute x15, waiting for transfers between devices, send(): return lax.ppermute(value, BOTH, sorted(pairs))  11.7 us
    pallas_call x3, Pallas kernels, chunk(): pl.pallas_call(functools.partial(chunk_kernel, tuple(pieces), len(sides),...  7.41 us
    unnamed x4, local copies, waits for them, and re-layouts  4.37 us
    pallas_call x2, Pallas kernels, project(): pl.pallas_call(functools.partial(project_kernel, dims), out_shape=jax.Sha...  2.21 us
  transfers between devices with their start and end apart: 15, of which 5 were waited for; matrix products, arithmetic and copies ran while one was open for 0% of the time, Pallas kernels for 10%

profile of v14, /device:TPU:1, one launch (start us, length us, event | category | flops | bytes accessed | tf_op | source)
XLA Modules:
  0.0 83.1 jit_solution(13005421526620491494)
XLA Ops:
  0.0 1.1 %shard_map.46 = (bf16[128,1024]{1,0:T(8,128)(2,1)S(1)}, bf16[72,1024]{1,0:T(8,128)(2,1)S(1)}, f32[1,128]{1,0:T(1,128)S(1)}) custom-call(bf16[128,1024]{1,0:T(8,128)(2,1)} %factors_in.1, s32[1,8]{1,0:T(1,128)} %pattern_in.1, f32[1,128]{1,0:T(1,128)} %bitcast.1), custom_call_target="tpu_custom_call" | custom-call | tf_op jit(solution)/shard_map/pallas_call | solution.py:102
  1.2 2.5 %collective-permute-start = (bf16[72,1024]{1,0:T(8,128)(2,1)S(1)}, bf16[72,1024]{1,0:T(8,128)(2,1)S(1)}, u32[]{:S(2)}, u32[]{:S(2)}) collective-permute-start(bf16[72,1024]{1,0:T(8,128)(2,1)S(1)} %get-tuple-element.20), channel_id=1, source_target_pairs={{0,8},{1,9},{2,10},{3,11},{4,12},{5,13},{6,14},{7,15},{8,16},{9,17... | collective-permute-start | bytes 442376 | tf_op jit(solution)/shard_map/ppermute | solution.py:31
  3.7 4.0 %collective-permute-start.1 = (bf16[72,1024]{1,0:T(8,128)(2,1)S(1)}, bf16[72,1024]{1,0:T(8,128)(2,1)S(1)}, u32[]{:S(2)}, u32[]{:S(2)}) collective-permute-start(bf16[72,1024]{1,0:T(8,128)(2,1)S(1)} %get-tuple-element.20), channel_id=1, source_target_pairs={{0,152},{1,153},{2,154},{3,155},{4,156},{5,157},{6,158},{7,159},{8... | collective-permute-start | bytes 442376 | tf_op jit(solution)/shard_map/ppermute | solution.py:31
  7.7 1.8 %collective-permute-start.2 = (bf16[72,1024]{1,0:T(8,128)(2,1)S(1)}, bf16[72,1024]{1,0:T(8,128)(2,1)S(1)}, u32[]{:S(2)}, u32[]{:S(2)}) collective-permute-start(bf16[72,1024]{1,0:T(8,128)(2,1)S(1)} %get-tuple-element.20), channel_id=1, source_target_pairs={{0,16},{1,145},{2,18},{3,147},{4,20},{5,149},{6,22},{7,151},{8,24}... | collective-permute-start | bytes 442376 | tf_op jit(solution)/shard_map/ppermute | solution.py:31
  9.5 0.0 copy-start
  9.5 2.2 %copy-done = bf16[2,1024,1024]{2,1,0:T(8,128)(2,1)S(1)} copy-done((bf16[2,1024,1024]{2,1,0:T(8,128)(2,1)S(1)}, bf16[2,1024,1024]{2,1,0:T(8,128)(2,1)}, u32[]{:S(2)}) %copy-start) | copy-done | bytes 4194328
  11.7 0.7 shard_map.48
  12.5 2.5 %collective-permute-start.7 = (bf16[2,128,1024]{2,1,0:T(8,128)(2,1)S(1)}, bf16[2,128,1024]{2,1,0:T(8,128)(2,1)S(1)}, u32[]{:S(2)}, u32[]{:S(2)}) collective-permute-start(bf16[2,128,1024]{2,1,0:T(8,128)(2,1)S(1)} %shard_map.48), channel_id=1, source_target_pairs={{0,16},{1,145},{2,18},{3,147},{4,20},{5,149},{6,22},{7,151},{8,24}... | collective-permute-start | bytes 1572872 | tf_op jit(solution)/shard_map/ppermute | solution.py:31
  14.9 0.0 collective-permute-done
  15.0 0.0 collective-permute-done.1
  15.0 0.0 collective-permute-done.2
  15.1 0.1 concatenate.6.refs_4_.refs_0_
  15.2 1.3 %collective-permute-start.3 = (bf16[264,1024]{1,0:T(8,128)(2,1)S(1)}, bf16[264,1024]{1,0:T(8,128)(2,1)S(1)}, u32[]{:S(2)}, u32[]{:S(2)}) collective-permute-start(bf16[264,1024]{1,0:T(8,128)(2,1)S(1)} %concatenate.6.refs_4_.refs_0_), channel_id=1, source_target_pairs={{0,2},{1,3},{2,4},{3,5},{4,6},{5,7},{6,0},{7,1},{8,10},{9,11},{10,... | collective-permute-start | bytes 1622024 | tf_op jit(solution)/shard_map/ppermute | solution.py:31
  16.5 1.5 %collective-permute-start.4 = (bf16[264,1024]{1,0:T(8,128)(2,1)S(1)}, bf16[264,1024]{1,0:T(8,128)(2,1)S(1)}, u32[]{:S(2)}, u32[]{:S(2)}) collective-permute-start(bf16[264,1024]{1,0:T(8,128)(2,1)S(1)} %concatenate.6.refs_4_.refs_0_), channel_id=1, source_target_pairs={{0,6},{1,7},{2,0},{3,1},{4,2},{5,3},{6,4},{7,5},{8,14},{9,15},{10,... | collective-permute-start | bytes 1622024 | tf_op jit(solution)/shard_map/ppermute | solution.py:31
  18.0 2.7 %collective-permute-start.5 = (bf16[200,1024]{1,0:T(8,128)(2,1)S(1)}, bf16[200,1024]{1,0:T(8,128)(2,1)S(1)}, u32[]{:S(2)}, u32[]{:S(2)}) collective-permute-start(bf16[200,1024]{1,0:T(8,128)(2,1)S(1)} %slice.46), channel_id=1, source_target_pairs={{0,32},{1,97},{2,34},{3,99},{4,36},{5,101},{6,38},{7,103},{8,40},{... | collective-permute-start | bytes 1228808 | tf_op jit(solution)/shard_map/ppermute | solution.py:31
  20.7 0.0 copy-start.1
  20.7 2.2 %copy-done.1 = bf16[2,1024,1024]{2,1,0:T(8,128)(2,1)S(1)} copy-done((bf16[2,1024,1024]{2,1,0:T(8,128)(2,1)S(1)}, bf16[2,1024,1024]{2,1,0:T(8,128)(2,1)}, u32[]{:S(2)}) %copy-start.1) | copy-done | bytes 4194328
  22.9 1.5 %shard_map.47.refs_0_ = bf16[2,128,1024]{2,1,0:T(8,128)(2,1)S(1)} custom-call(bf16[128,1024]{1,0:T(8,128)(2,1)S(1)} %get-tuple-element.21.masked_ref, bf16[2,1024,1024]{2,1,0:T(8,128)(2,1)S(1)} %copy-done.1), custom_call_target="tpu_custom_call" | custom-call | flops 536870912 | bytes 4194304 | tf_op jit(solution)/shard_map/pallas_call | solution.py:130
  24.4 1.3 %collective-permute-start.6 = (bf16[2,128,1024]{2,1,0:T(8,128)(2,1)S(1)}, bf16[2,128,1024]{2,1,0:T(8,128)(2,1)S(1)}, u32[]{:S(2)}, u32[]{:S(2)}) collective-permute-start(bf16[2,128,1024]{2,1,0:T(8,128)(2,1)S(1)} %shard_map.47.refs_0_), channel_id=1, source_target_pairs={{0,1},{1,0},{2,3},{3,2},{4,5},{5,4},{6,7},{7,6},{8,9},{9,8},{10,11... | collective-permute-start | bytes 1572872 | tf_op jit(solution)/shard_map/ppermute | solution.py:31
  25.7 1.7 %collective-permute-done.7 = bf16[2,128,1024]{2,1,0:T(8,128)(2,1)S(1)} collective-permute-done((bf16[2,128,1024]{2,1,0:T(8,128)(2,1)S(1)}, bf16[2,128,1024]{2,1,0:T(8,128)(2,1)S(1)}, u32[]{:S(2)}, u32[]{:S(2)}) %collective-permute-start.7) | collective-permute-done | bytes 524320 | tf_op jit(solution)/shard_map/ppermute | solution.py:31
  27.4 2.7 %collective-permute-start.8 = (bf16[2,128,1024]{2,1,0:T(8,128)(2,1)S(1)}, bf16[2,128,1024]{2,1,0:T(8,128)(2,1)S(1)}, u32[]{:S(2)}, u32[]{:S(2)}) collective-permute-start(bf16[2,128,1024]{2,1,0:T(8,128)(2,1)S(1)} %collective-permute-done.7), channel_id=1, source_target_pairs={{0,16},{1,145},{2,18},{3,147},{4,20},{5,149},{6,22},{7,151},{8,24}... | collective-permute-start | bytes 1572872 | tf_op jit(solution)/shard_map/ppermute | solution.py:31
  30.1 0.0 collective-permute-done.5
  30.2 0.0 collective-permute-done.3.west_ref.refs_6_.refs_2_
  30.2 0.0 collective-permute-done.4.east_ref.refs_7_.refs_3_
  30.2 0.0 collective-permute-done.6.first_ref.refs_1_
  30.2 0.1 shard_map.50
  30.3 2.8 %collective-permute-start.12 = (bf16[528,1024]{1,0:T(8,128)(2,1)S(1)}, bf16[528,1024]{1,0:T(8,128)(2,1)S(1)}, u32[]{:S(2)}, u32[]{:S(2)}) collective-permute-start(bf16[528,1024]{1,0:T(8,128)(2,1)S(1)} %shard_map.50), channel_id=1, source_target_pairs={{0,32},{1,97},{2,34},{3,99},{4,36},{5,101},{6,38},{7,103},{8,40},{... | collective-permute-start | bytes 3244040 | tf_op jit(solution)/shard_map/ppermute | solution.py:31
  33.1 0.1 shard_map.49
  33.2 2.6 %collective-permute-start.10 = (bf16[264,1024]{1,0:T(8,128)(2,1)S(1)}, bf16[264,1024]{1,0:T(8,128)(2,1)S(1)}, u32[]{:S(2)}, u32[]{:S(2)}) collective-permute-start(bf16[264,1024]{1,0:T(8,128)(2,1)S(1)} %shard_map.49), channel_id=1, source_target_pairs={{0,2},{1,7},{2,4},{3,1},{4,6},{5,3},{6,0},{7,5},{8,10},{9,15},{10,... | collective-permute-start | bytes 1622024 | tf_op jit(solution)/shard_map/ppermute | solution.py:31
  35.7 6.6 %collective-permute-done.8.refs_2_ = bf16[2,128,1024]{2,1,0:T(8,128)(2,1)S(1)} collective-permute-done((bf16[2,128,1024]{2,1,0:T(8,128)(2,1)S(1)}, bf16[2,128,1024]{2,1,0:T(8,128)(2,1)S(1)}, u32[]{:S(2)}, u32[]{:S(2)}) %collective-permute-start.8) | collective-permute-done | bytes 524320 | tf_op jit(solution)/shard_map/ppermute | solution.py:31
  42.4 1.9 %collective-permute-start.9 = (bf16[2,128,1024]{2,1,0:T(8,128)(2,1)S(1)}, bf16[2,128,1024]{2,1,0:T(8,128)(2,1)S(1)}, u32[]{:S(2)}, u32[]{:S(2)}) collective-permute-start(bf16[2,128,1024]{2,1,0:T(8,128)(2,1)S(1)} %collective-permute-done.8.refs_2_), channel_id=1, source_target_pairs={{0,1},{1,0},{2,3},{3,2},{4,5},{5,4},{6,7},{7,6},{8,9},{9,8},{10,11... | collective-permute-start | bytes 1572872 | tf_op jit(solution)/shard_map/ppermute | solution.py:31
  44.2 0.0 collective-permute-done.10.refs_5_
  44.2 2.7 %collective-permute-start.11 = (bf16[264,1024]{1,0:T(8,128)(2,1)S(1)}, bf16[264,1024]{1,0:T(8,128)(2,1)S(1)}, u32[]{:S(2)}, u32[]{:S(2)}) collective-permute-start(bf16[264,1024]{1,0:T(8,128)(2,1)S(1)} %collective-permute-done.10.refs_5_), channel_id=1, source_target_pairs={{0,32},{1,97},{2,34},{3,99},{4,36},{5,101},{6,38},{7,103},{8,40},{... | collective-permute-start | bytes 1622024 | tf_op jit(solution)/shard_map/ppermute | solution.py:31
  47.0 0.0 collective-permute-done.9.refs_3_
  47.0 3.5 %shard_map.51 = (f32[2,128,1024]{2,1,0:T(8,128)S(1)}, f32[2,128,1024]{2,1,0:T(8,128)S(1)}) custom-call(bf16[2,128,1024]{2,1,0:T(8,128)(2,1)S(1)} %shard_map.47.refs_0_, bf16[2,128,1024]{2,1,0:T(8,128)(2,1)S(1)} %collective-permute-done.6.first_ref.refs_1_, bf16[2,128,1024]{2,1,0:T(8,128)(2,1)S(1)} %collective-permute-done.8.refs_2_, ...), custom_call_target="tpu_custom_call" | custom-call | flops 1073741824 | bytes 2097152 | tf_op jit(solution)/shard_map/pallas_call | solution.py:220
  50.4 0.0 collective-permute-done.12.refs_4_
  50.4 2.8 %shard_map.52 = (f32[2,128,1024]{2,1,0:T(8,128)S(1)}, f32[2,128,1024]{2,1,0:T(8,128)S(1)}) custom-call(bf16[2,128,1024]{2,1,0:T(8,128)(2,1)S(1)} %shard_map.47.refs_0_, bf16[2,128,1024]{2,1,0:T(8,128)(2,1)S(1)} %collective-permute-done.6.first_ref.refs_1_, ...), custom_call_target="tpu_custom_call", output_to_operand_aliasing={{0}: (6, {}), {1}: (7, {})} | custom-call | flops 805306368 | bytes 2097152 | tf_op jit(solution)/shard_map/pallas_call | solution.py:220
  53.2 0.5 collective-permute-done.11.refs_4_.refs_6_
  53.7 1.2 %shard_map.53 = (f32[2,128,1024]{2,1,0:T(8,128)S(1)}, bf16[2,128,1024]{2,1,0:T(8,128)(2,1)S(1)}) custom-call(bf16[2,128,1024]{2,1,0:T(8,128)(2,1)S(1)} %shard_map.47.refs_0_, bf16[2,128,1024]{2,1,0:T(8,128)(2,1)S(1)} %collective-permute-done.6.first_ref.refs_1_, ...), custom_call_target="tpu_custom_call", output_to_operand_aliasing={{0}: (5, {})} | custom-call | flops 268435456 | bytes 2097152 | tf_op jit(solution)/shard_map/pallas_call | solution.py:220
  54.9 0.2 collective-permute-start.13
  55.1 1.8 %collective-permute-done.13.got_ref = bf16[2,128,1024]{2,1,0:T(8,128)(2,1)S(1)} collective-permute-done((bf16[2,128,1024]{2,1,0:T(8,128)(2,1)S(1)}, bf16[2,128,1024]{2,1,0:T(8,128)(2,1)S(1)}, u32[]{:S(2)}, u32[]{:S(2)}) %collective-permute-start.13) | collective-permute-done | bytes 524320 | tf_op jit(solution)/shard_map/ppermute | solution.py:31
  56.9 0.3 shard_map.54
  57.3 21.3 %all_to_all.5.part_ref = bf16[16,2,64,128]{3,2,1,0:T(8,128)(2,1)S(1)} all-to-all(bf16[16,2,64,128]{3,2,1,0:T(8,128)(2,1)S(1)} %shard_map.54), channel_id=1, replica_groups={{0,2,4,6,8,10,12,14,16,18,20,22,24,26,28,30},{1,3,5,7,9,11,13,15,17,19,..., dimensions={0} | all-to-all | bytes 1048576 | tf_op jit(solution)/shard_map/all_to_all | solution.py:331
  78.5 0.8 shard_map.55
  79.3 2.0 %collective-permute-start.14 = (bf16[2,32,1024]{2,1,0:T(8,128)(2,1)S(1)}, bf16[2,32,1024]{2,1,0:T(8,128)(2,1)S(1)}, u32[]{:S(2)}, u32[]{:S(2)}) collective-permute-start(bf16[2,32,1024]{2,1,0:T(8,128)(2,1)S(1)} %get-tuple-element.34), channel_id=1, source_target_pairs={{0,1},{1,0},{2,3},{3,2},{4,5},{5,4},{6,7},{7,6},{8,9},{9,8},{10,11... | collective-permute-start | bytes 393224 | tf_op jit(solution)/shard_map/ppermute | solution.py:31
  81.3 1.0 %collective-permute-done.14.got_ref = bf16[2,32,1024]{2,1,0:T(8,128)(2,1)S(1)} collective-permute-done((bf16[2,32,1024]{2,1,0:T(8,128)(2,1)S(1)}, bf16[2,32,1024]{2,1,0:T(8,128)(2,1)S(1)}, u32[]{:S(2)}, u32[]{:S(2)}) %collective-permute-start.14) | collective-permute-done | bytes 131104 | tf_op jit(solution)/shard_map/ppermute | solution.py:31
  82.3 0.8 shard_map.56
  (12 shorter events, 0.1 us)
Async XLA Ops:
  1.2 13.8 %collective-permute-start = (bf16[72,1024]{1,0:T(8,128)(2,1)S(1)}, bf16[72,1024]{1,0:T(8,128)(2,1)S(1)}, u32[]{:S(2)}, u32[]{:S(2)}) collective-permute-start(bf16[72,1024]{1,0:T(8,128)(2,1)S(1)} %get-tuple-element.20), channel_id=1, source_target_pairs={{0,8},{1,9},{2,10},{3,11},{4,12},{5,13},{6,14},{7,15},{8,16},{9,17... | collective-permute-start | bytes 442376 | tf_op jit(solution)/shard_map/ppermute | solution.py:31
  3.7 11.3 %collective-permute-start.1 = (bf16[72,1024]{1,0:T(8,128)(2,1)S(1)}, bf16[72,1024]{1,0:T(8,128)(2,1)S(1)}, u32[]{:S(2)}, u32[]{:S(2)}) collective-permute-start(bf16[72,1024]{1,0:T(8,128)(2,1)S(1)} %get-tuple-element.20), channel_id=1, source_target_pairs={{0,152},{1,153},{2,154},{3,155},{4,156},{5,157},{6,158},{7,159},{8... | collective-permute-start | bytes 442376 | tf_op jit(solution)/shard_map/ppermute | solution.py:31
  7.7 7.3 %collective-permute-start.2 = (bf16[72,1024]{1,0:T(8,128)(2,1)S(1)}, bf16[72,1024]{1,0:T(8,128)(2,1)S(1)}, u32[]{:S(2)}, u32[]{:S(2)}) collective-permute-start(bf16[72,1024]{1,0:T(8,128)(2,1)S(1)} %get-tuple-element.20), channel_id=1, source_target_pairs={{0,16},{1,145},{2,18},{3,147},{4,20},{5,149},{6,22},{7,151},{8,24}... | collective-permute-start | bytes 442376 | tf_op jit(solution)/shard_map/ppermute | solution.py:31
  9.5 2.2 %copy-start = (bf16[2,1024,1024]{2,1,0:T(8,128)(2,1)S(1)}, bf16[2,1024,1024]{2,1,0:T(8,128)(2,1)}, u32[]{:S(2)}) copy-start(bf16[2,1024,1024]{2,1,0:T(8,128)(2,1)} %green_ref.3) | copy-start | bytes 12582916
  12.5 14.9 %collective-permute-start.7 = (bf16[2,128,1024]{2,1,0:T(8,128)(2,1)S(1)}, bf16[2,128,1024]{2,1,0:T(8,128)(2,1)S(1)}, u32[]{:S(2)}, u32[]{:S(2)}) collective-permute-start(bf16[2,128,1024]{2,1,0:T(8,128)(2,1)S(1)} %shard_map.48), channel_id=1, source_target_pairs={{0,16},{1,145},{2,18},{3,147},{4,20},{5,149},{6,22},{7,151},{8,24}... | collective-permute-start | bytes 1572872 | tf_op jit(solution)/shard_map/ppermute | solution.py:31
  15.2 15.0 %collective-permute-start.3 = (bf16[264,1024]{1,0:T(8,128)(2,1)S(1)}, bf16[264,1024]{1,0:T(8,128)(2,1)S(1)}, u32[]{:S(2)}, u32[]{:S(2)}) collective-permute-start(bf16[264,1024]{1,0:T(8,128)(2,1)S(1)} %concatenate.6.refs_4_.refs_0_), channel_id=1, source_target_pairs={{0,2},{1,3},{2,4},{3,5},{4,6},{5,7},{6,0},{7,1},{8,10},{9,11},{10,... | collective-permute-start | bytes 1622024 | tf_op jit(solution)/shard_map/ppermute | solution.py:31
  16.5 13.7 %collective-permute-start.4 = (bf16[264,1024]{1,0:T(8,128)(2,1)S(1)}, bf16[264,1024]{1,0:T(8,128)(2,1)S(1)}, u32[]{:S(2)}, u32[]{:S(2)}) collective-permute-start(bf16[264,1024]{1,0:T(8,128)(2,1)S(1)} %concatenate.6.refs_4_.refs_0_), channel_id=1, source_target_pairs={{0,6},{1,7},{2,0},{3,1},{4,2},{5,3},{6,4},{7,5},{8,14},{9,15},{10,... | collective-permute-start | bytes 1622024 | tf_op jit(solution)/shard_map/ppermute | solution.py:31
  18.0 12.2 %collective-permute-start.5 = (bf16[200,1024]{1,0:T(8,128)(2,1)S(1)}, bf16[200,1024]{1,0:T(8,128)(2,1)S(1)}, u32[]{:S(2)}, u32[]{:S(2)}) collective-permute-start(bf16[200,1024]{1,0:T(8,128)(2,1)S(1)} %slice.46), channel_id=1, source_target_pairs={{0,32},{1,97},{2,34},{3,99},{4,36},{5,101},{6,38},{7,103},{8,40},{... | collective-permute-start | bytes 1228808 | tf_op jit(solution)/shard_map/ppermute | solution.py:31
  20.7 2.2 %copy-start.1 = (bf16[2,1024,1024]{2,1,0:T(8,128)(2,1)S(1)}, bf16[2,1024,1024]{2,1,0:T(8,128)(2,1)}, u32[]{:S(2)}) copy-start(bf16[2,1024,1024]{2,1,0:T(8,128)(2,1)} %green_ref.3) | copy-start | bytes 12582916
  24.4 5.8 %collective-permute-start.6 = (bf16[2,128,1024]{2,1,0:T(8,128)(2,1)S(1)}, bf16[2,128,1024]{2,1,0:T(8,128)(2,1)S(1)}, u32[]{:S(2)}, u32[]{:S(2)}) collective-permute-start(bf16[2,128,1024]{2,1,0:T(8,128)(2,1)S(1)} %shard_map.47.refs_0_), channel_id=1, source_target_pairs={{0,1},{1,0},{2,3},{3,2},{4,5},{5,4},{6,7},{7,6},{8,9},{9,8},{10,11... | collective-permute-start | bytes 1572872 | tf_op jit(solution)/shard_map/ppermute | solution.py:31
  27.4 15.0 %collective-permute-start.8 = (bf16[2,128,1024]{2,1,0:T(8,128)(2,1)S(1)}, bf16[2,128,1024]{2,1,0:T(8,128)(2,1)S(1)}, u32[]{:S(2)}, u32[]{:S(2)}) collective-permute-start(bf16[2,128,1024]{2,1,0:T(8,128)(2,1)S(1)} %collective-permute-done.7), channel_id=1, source_target_pairs={{0,16},{1,145},{2,18},{3,147},{4,20},{5,149},{6,22},{7,151},{8,24}... | collective-permute-start | bytes 1572872 | tf_op jit(solution)/shard_map/ppermute | solution.py:31
  30.3 20.1 %collective-permute-start.12 = (bf16[528,1024]{1,0:T(8,128)(2,1)S(1)}, bf16[528,1024]{1,0:T(8,128)(2,1)S(1)}, u32[]{:S(2)}, u32[]{:S(2)}) collective-permute-start(bf16[528,1024]{1,0:T(8,128)(2,1)S(1)} %shard_map.50), channel_id=1, source_target_pairs={{0,32},{1,97},{2,34},{3,99},{4,36},{5,101},{6,38},{7,103},{8,40},{... | collective-permute-start | bytes 3244040 | tf_op jit(solution)/shard_map/ppermute | solution.py:31
  33.2 11.1 %collective-permute-start.10 = (bf16[264,1024]{1,0:T(8,128)(2,1)S(1)}, bf16[264,1024]{1,0:T(8,128)(2,1)S(1)}, u32[]{:S(2)}, u32[]{:S(2)}) collective-permute-start(bf16[264,1024]{1,0:T(8,128)(2,1)S(1)} %shard_map.49), channel_id=1, source_target_pairs={{0,2},{1,7},{2,4},{3,1},{4,6},{5,3},{6,0},{7,5},{8,10},{9,15},{10,... | collective-permute-start | bytes 1622024 | tf_op jit(solution)/shard_map/ppermute | solution.py:31
  42.4 4.6 %collective-permute-start.9 = (bf16[2,128,1024]{2,1,0:T(8,128)(2,1)S(1)}, bf16[2,128,1024]{2,1,0:T(8,128)(2,1)S(1)}, u32[]{:S(2)}, u32[]{:S(2)}) collective-permute-start(bf16[2,128,1024]{2,1,0:T(8,128)(2,1)S(1)} %collective-permute-done.8.refs_2_), channel_id=1, source_target_pairs={{0,1},{1,0},{2,3},{3,2},{4,5},{5,4},{6,7},{7,6},{8,9},{9,8},{10,11... | collective-permute-start | bytes 1572872 | tf_op jit(solution)/shard_map/ppermute | solution.py:31
  44.2 9.5 %collective-permute-start.11 = (bf16[264,1024]{1,0:T(8,128)(2,1)S(1)}, bf16[264,1024]{1,0:T(8,128)(2,1)S(1)}, u32[]{:S(2)}, u32[]{:S(2)}) collective-permute-start(bf16[264,1024]{1,0:T(8,128)(2,1)S(1)} %collective-permute-done.10.refs_5_), channel_id=1, source_target_pairs={{0,32},{1,97},{2,34},{3,99},{4,36},{5,101},{6,38},{7,103},{8,40},{... | collective-permute-start | bytes 1622024 | tf_op jit(solution)/shard_map/ppermute | solution.py:31
  54.9 2.0 %collective-permute-start.13 = (bf16[2,128,1024]{2,1,0:T(8,128)(2,1)S(1)}, bf16[2,128,1024]{2,1,0:T(8,128)(2,1)S(1)}, u32[]{:S(2)}, u32[]{:S(2)}) collective-permute-start(bf16[2,128,1024]{2,1,0:T(8,128)(2,1)S(1)} %get-tuple-element.31), channel_id=1, source_target_pairs={{0,1},{1,0},{2,3},{3,2},{4,5},{5,4},{6,7},{7,6},{8,9},{9,8},{10,11... | collective-permute-start | bytes 1572872 | tf_op jit(solution)/shard_map/ppermute | solution.py:31
  79.3 3.0 %collective-permute-start.14 = (bf16[2,32,1024]{2,1,0:T(8,128)(2,1)S(1)}, bf16[2,32,1024]{2,1,0:T(8,128)(2,1)S(1)}, u32[]{:S(2)}, u32[]{:S(2)}) collective-permute-start(bf16[2,32,1024]{2,1,0:T(8,128)(2,1)S(1)} %get-tuple-element.34), channel_id=1, source_target_pairs={{0,1},{1,0},{2,3},{3,2},{4,5},{5,4},{6,7},{7,6},{8,9},{9,8},{10,11... | collective-permute-start | bytes 393224 | tf_op jit(solution)/shard_map/ppermute | solution.py:31

commit v15 on v12

--- a/solution.py
+++ b/solution.py
@@ -288,10 +288,9 @@
     left_other = other_core(left)
 
     lefts = (left, left_other)
-    two = [(0, 0, n), (1, 0, n)]
+    four = [(k, 0, n) for k in range(4)]
     sides = rights + lefts
-    acc = chunk(sides, (here, here_q), two)
-    acc = chunk(sides, (west, east), two, acc=acc)
+    acc = chunk(sides, (here, here_q, west, east), four)
     acc = chunk(sides, (sides_q, far), [(0, 0, n), (0, n + 8, n), (1, 0, n)], acc=acc)
     keep, theirs = chunk(sides, (far_q,), [(0, 0, n)], acc=acc, last=True)
 

time: 83.5 us -> 83.3 us (level)
    pallas_call x4 -> x3, Pallas kernels: 8.1 us -> 7.47 us  [chunk(): pl.pallas_call(functools.partial(chunk_kernel, tuple(pieces), len(sides),...]
  transfers between devices with their start and end apart: 15 -> 15, of which waited for: 4 -> 5; matrix products, arithmetic and copies ran while one was open for 8% -> 8% of each run, Pallas kernels for 8% -> 8%
where the time goes in v15:
time: 83.3 us; the launch traced here: 83.1 us
  starting transfers between devices  31.9 us (38%)
  blocking collectives  21.3 us (26%)
  waiting for transfers between devices  12.3 us (15%)
  Pallas kernels  10.6 us (13%)
  matrix products  6.61 us (8%)
    ppermute x15, starting transfers between devices, send(): return lax.ppermute(value, BOTH, sorted(pairs))  31.9 us
    all_to_all x1, blocking collectives, local(): lax.all_to_all(part, 'aux', 0, 0, axis_index_groups=groups, tiled=True)  21.3 us
    ppermute x15, waiting for transfers between devices, send(): return lax.ppermute(value, BOTH, sorted(pairs))  12.3 us
    pallas_call x3, Pallas kernels, chunk(): pl.pallas_call(functools.partial(chunk_kernel, tuple(pieces), len(sides),...  7.47 us
    dot_general x1, matrix products, local(): jnp.einsum('qo,tko->tqk', masked, green, preferred_element_type=F32)  3.69 us
    dot_general x1, matrix products, local(): jnp.einsum('qo,tok->tqk', masked, green, preferred_element_type=F32)  2.92 us
  transfers between devices with their start and end apart: 15, of which 5 were waited for; matrix products, arithmetic and copies ran while one was open for 8% of the time, Pallas kernels for 8%

profile of v15, /device:TPU:1, one launch (start us, length us, event | category | flops | bytes accessed | tf_op | source)
XLA Modules:
  0.0 83.1 jit_solution(1841953028181950785)
XLA Ops:
  0.0 1.1 %shard_map.46 = (bf16[128,1024]{1,0:T(8,128)(2,1)S(1)}, bf16[72,1024]{1,0:T(8,128)(2,1)S(1)}, f32[1,128]{1,0:T(1,128)S(1)}) custom-call(bf16[128,1024]{1,0:T(8,128)(2,1)} %factors_in.1, s32[1,8]{1,0:T(1,128)} %pattern_in.1, f32[1,128]{1,0:T(1,128)} %bitcast.12), custom_call_target="tpu_custom_call" | custom-call | tf_op jit(solution)/shard_map/pallas_call | solution.py:102
  1.2 2.5 %collective-permute-start = (bf16[72,1024]{1,0:T(8,128)(2,1)S(1)}, bf16[72,1024]{1,0:T(8,128)(2,1)S(1)}, u32[]{:S(2)}, u32[]{:S(2)}) collective-permute-start(bf16[72,1024]{1,0:T(8,128)(2,1)S(1)} %get-tuple-element.22), channel_id=1, source_target_pairs={{0,8},{1,9},{2,10},{3,11},{4,12},{5,13},{6,14},{7,15},{8,16},{9,17... | collective-permute-start | bytes 442376 | tf_op jit(solution)/shard_map/ppermute | solution.py:31
  3.7 4.0 %collective-permute-start.1 = (bf16[72,1024]{1,0:T(8,128)(2,1)S(1)}, bf16[72,1024]{1,0:T(8,128)(2,1)S(1)}, u32[]{:S(2)}, u32[]{:S(2)}) collective-permute-start(bf16[72,1024]{1,0:T(8,128)(2,1)S(1)} %get-tuple-element.22), channel_id=1, source_target_pairs={{0,152},{1,153},{2,154},{3,155},{4,156},{5,157},{6,158},{7,159},{8... | collective-permute-start | bytes 442376 | tf_op jit(solution)/shard_map/ppermute | solution.py:31
  7.7 1.8 %collective-permute-start.2 = (bf16[72,1024]{1,0:T(8,128)(2,1)S(1)}, bf16[72,1024]{1,0:T(8,128)(2,1)S(1)}, u32[]{:S(2)}, u32[]{:S(2)}) collective-permute-start(bf16[72,1024]{1,0:T(8,128)(2,1)S(1)} %get-tuple-element.22), channel_id=1, source_target_pairs={{0,16},{1,145},{2,18},{3,147},{4,20},{5,149},{6,22},{7,151},{8,24}... | collective-permute-start | bytes 442376 | tf_op jit(solution)/shard_map/ppermute | solution.py:31
  9.5 2.9 %fusion.1 = bf16[2,128,1024]{2,1,0:T(8,128)(2,1)S(1)} fusion(bf16[2,1024,1024]{2,1,0:T(8,128)(2,1)} %param.4, bf16[128,1024]{1,0:T(8,128)(2,1)S(1)} %get-tuple-element.23), kind=kOutput, calls=%fused_computation.3 | convolution fusion | flops 537133056 | bytes 4980736 | tf_op jit(solution)/shard_map/qo,tok->tqk/dot_general | solution.py:267
  12.5 2.5 %collective-permute-start.7 = (bf16[2,128,1024]{2,1,0:T(8,128)(2,1)S(1)}, bf16[2,128,1024]{2,1,0:T(8,128)(2,1)S(1)}, u32[]{:S(2)}, u32[]{:S(2)}) collective-permute-start(bf16[2,128,1024]{2,1,0:T(8,128)(2,1)S(1)} %fusion.1), channel_id=1, source_target_pairs={{0,16},{1,145},{2,18},{3,147},{4,20},{5,149},{6,22},{7,151},{8,24}... | collective-permute-start | bytes 1572872 | tf_op jit(solution)/shard_map/ppermute | solution.py:31
  15.0 0.0 collective-permute-done
  15.0 0.0 collective-permute-done.1
  15.0 0.0 collective-permute-done.2
  15.1 0.1 concatenate.6.refs_4_.refs_0_
  15.2 1.3 %collective-permute-start.3 = (bf16[264,1024]{1,0:T(8,128)(2,1)S(1)}, bf16[264,1024]{1,0:T(8,128)(2,1)S(1)}, u32[]{:S(2)}, u32[]{:S(2)}) collective-permute-start(bf16[264,1024]{1,0:T(8,128)(2,1)S(1)} %concatenate.6.refs_4_.refs_0_), channel_id=1, source_target_pairs={{0,2},{1,3},{2,4},{3,5},{4,6},{5,7},{6,0},{7,1},{8,10},{9,11},{10,... | collective-permute-start | bytes 1622024 | tf_op jit(solution)/shard_map/ppermute | solution.py:31
  16.5 1.5 %collective-permute-start.4 = (bf16[264,1024]{1,0:T(8,128)(2,1)S(1)}, bf16[264,1024]{1,0:T(8,128)(2,1)S(1)}, u32[]{:S(2)}, u32[]{:S(2)}) collective-permute-start(bf16[264,1024]{1,0:T(8,128)(2,1)S(1)} %concatenate.6.refs_4_.refs_0_), channel_id=1, source_target_pairs={{0,6},{1,7},{2,0},{3,1},{4,2},{5,3},{6,4},{7,5},{8,14},{9,15},{10,... | collective-permute-start | bytes 1622024 | tf_op jit(solution)/shard_map/ppermute | solution.py:31
  18.0 2.8 %collective-permute-start.5 = (bf16[200,1024]{1,0:T(8,128)(2,1)S(1)}, bf16[200,1024]{1,0:T(8,128)(2,1)S(1)}, u32[]{:S(2)}, u32[]{:S(2)}) collective-permute-start(bf16[200,1024]{1,0:T(8,128)(2,1)S(1)} %slice.46), channel_id=1, source_target_pairs={{0,32},{1,97},{2,34},{3,99},{4,36},{5,101},{6,38},{7,103},{8,40},{... | collective-permute-start | bytes 1228808 | tf_op jit(solution)/shard_map/ppermute | solution.py:31
  20.8 3.7 %fusion.refs_0_ = bf16[2,128,1024]{2,1,0:T(8,128)(2,1)S(1)} fusion(bf16[2,1024,1024]{2,1,0:T(8,128)(2,1)} %param.4, bf16[128,1024]{1,0:T(8,128)(2,1)S(1)} %get-tuple-element.23), kind=kOutput, calls=%fused_computation.2 | convolution fusion | flops 537133056 | bytes 4980736 | tf_op jit(solution)/shard_map/qo,tko->tqk/dot_general | solution.py:279
  24.5 2.9 %collective-permute-done.7 = bf16[2,128,1024]{2,1,0:T(8,128)(2,1)S(1)} collective-permute-done((bf16[2,128,1024]{2,1,0:T(8,128)(2,1)S(1)}, bf16[2,128,1024]{2,1,0:T(8,128)(2,1)S(1)}, u32[]{:S(2)}, u32[]{:S(2)}) %collective-permute-start.7) | collective-permute-done | bytes 524320 | tf_op jit(solution)/shard_map/ppermute | solution.py:31
  27.4 2.7 %collective-permute-start.8 = (bf16[2,128,1024]{2,1,0:T(8,128)(2,1)S(1)}, bf16[2,128,1024]{2,1,0:T(8,128)(2,1)S(1)}, u32[]{:S(2)}, u32[]{:S(2)}) collective-permute-start(bf16[2,128,1024]{2,1,0:T(8,128)(2,1)S(1)} %collective-permute-done.7), channel_id=1, source_target_pairs={{0,16},{1,145},{2,18},{3,147},{4,20},{5,149},{6,22},{7,151},{8,24}... | collective-permute-start | bytes 1572872 | tf_op jit(solution)/shard_map/ppermute | solution.py:31
  30.1 0.0 collective-permute-done.5
  30.2 0.0 collective-permute-done.3.west_ref.refs_6_.refs_2_
  30.2 0.0 collective-permute-done.4.east_ref.refs_7_.refs_3_
  30.2 0.1 shard_map.47
  30.3 2.8 %collective-permute-start.12 = (bf16[528,1024]{1,0:T(8,128)(2,1)S(1)}, bf16[528,1024]{1,0:T(8,128)(2,1)S(1)}, u32[]{:S(2)}, u32[]{:S(2)}) collective-permute-start(bf16[528,1024]{1,0:T(8,128)(2,1)S(1)} %get-tuple-element.28), channel_id=1, source_target_pairs={{0,32},{1,97},{2,34},{3,99},{4,36},{5,101},{6,38},{7,103},{8,40},{... | collective-permute-start | bytes 3244040 | tf_op jit(solution)/shard_map/ppermute | solution.py:31
  33.1 2.5 %collective-permute-start.10 = (bf16[264,1024]{1,0:T(8,128)(2,1)S(1)}, bf16[264,1024]{1,0:T(8,128)(2,1)S(1)}, u32[]{:S(2)}, u32[]{:S(2)}) collective-permute-start(bf16[264,1024]{1,0:T(8,128)(2,1)S(1)} %get-tuple-element.27), channel_id=1, source_target_pairs={{0,2},{1,7},{2,4},{3,1},{4,6},{5,3},{6,0},{7,5},{8,10},{9,15},{10,... | collective-permute-start | bytes 1622024 | tf_op jit(solution)/shard_map/ppermute | solution.py:31
  35.6 0.0 collective-permute-start.6
  35.6 6.1 %collective-permute-done.8.refs_2_ = bf16[2,128,1024]{2,1,0:T(8,128)(2,1)S(1)} collective-permute-done((bf16[2,128,1024]{2,1,0:T(8,128)(2,1)S(1)}, bf16[2,128,1024]{2,1,0:T(8,128)(2,1)S(1)}, u32[]{:S(2)}, u32[]{:S(2)}) %collective-permute-start.8) | collective-permute-done | bytes 524320 | tf_op jit(solution)/shard_map/ppermute | solution.py:31
  41.7 2.5 %collective-permute-start.9 = (bf16[2,128,1024]{2,1,0:T(8,128)(2,1)S(1)}, bf16[2,128,1024]{2,1,0:T(8,128)(2,1)S(1)}, u32[]{:S(2)}, u32[]{:S(2)}) collective-permute-start(bf16[2,128,1024]{2,1,0:T(8,128)(2,1)S(1)} %collective-permute-done.8.refs_2_), channel_id=1, source_target_pairs={{0,1},{1,0},{2,3},{3,2},{4,5},{5,4},{6,7},{7,6},{8,9},{9,8},{10,11... | collective-permute-start | bytes 1572872 | tf_op jit(solution)/shard_map/ppermute | solution.py:31
  44.2 0.0 collective-permute-done.10.refs_5_
  44.2 2.7 %collective-permute-start.11 = (bf16[264,1024]{1,0:T(8,128)(2,1)S(1)}, bf16[264,1024]{1,0:T(8,128)(2,1)S(1)}, u32[]{:S(2)}, u32[]{:S(2)}) collective-permute-start(bf16[264,1024]{1,0:T(8,128)(2,1)S(1)} %collective-permute-done.10.refs_5_), channel_id=1, source_target_pairs={{0,32},{1,97},{2,34},{3,99},{4,36},{5,101},{6,38},{7,103},{8,40},{... | collective-permute-start | bytes 1622024 | tf_op jit(solution)/shard_map/ppermute | solution.py:31
  47.0 0.0 collective-permute-done.6.refs_1_
  47.0 0.0 collective-permute-done.9.refs_3_
  47.0 3.5 %shard_map.48 = (f32[2,128,1024]{2,1,0:T(8,128)S(1)}, f32[2,128,1024]{2,1,0:T(8,128)S(1)}) custom-call(bf16[2,128,1024]{2,1,0:T(8,128)(2,1)S(1)} %fusion.refs_0_, bf16[2,128,1024]{2,1,0:T(8,128)(2,1)S(1)} %collective-permute-done.6.refs_1_, bf16[2,128,1024]{2,1,0:T(8,128)(2,1)S(1)} %collective-permute-done.8.refs_2_, ...), custom_call_target="tpu_custom_call" | custom-call | flops 1073741824 | bytes 2097152 | tf_op jit(solution)/shard_map/pallas_call | solution.py:197
  50.5 0.0 collective-permute-done.12.refs_4_
  50.5 2.8 %shard_map.49 = (f32[2,128,1024]{2,1,0:T(8,128)S(1)}, f32[2,128,1024]{2,1,0:T(8,128)S(1)}) custom-call(bf16[2,128,1024]{2,1,0:T(8,128)(2,1)S(1)} %fusion.refs_0_, bf16[2,128,1024]{2,1,0:T(8,128)(2,1)S(1)} %collective-permute-done.6.refs_1_, bf16[2,128,1024]{2,1,0:T(8,128)(2,1)S(1)} %collective-permute-done.8.refs_2_, ...), custom_call_target="tpu_custom_call", output_to_operand_aliasing={{0}: (6, {}), {1}: (7, {})} | custom-call | flops 805306368 | bytes 2097152 | tf_op jit(solution)/shard_map/pallas_call | solution.py:197
  53.3 0.4 collective-permute-done.11.refs_4_.refs_6_
  53.7 1.2 %shard_map.50 = (f32[2,128,1024]{2,1,0:T(8,128)S(1)}, bf16[2,128,1024]{2,1,0:T(8,128)(2,1)S(1)}) custom-call(bf16[2,128,1024]{2,1,0:T(8,128)(2,1)S(1)} %fusion.refs_0_, bf16[2,128,1024]{2,1,0:T(8,128)(2,1)S(1)} %collective-permute-done.6.refs_1_, bf16[2,128,1024]{2,1,0:T(8,128)(2,1)S(1)} %collective-permute-done.8.refs_2_, ...), custom_call_target="tpu_custom_call", output_to_operand_aliasing={{0}: (5, {})} | custom-call | flops 268435456 | bytes 2097152 | tf_op jit(solution)/shard_map/pallas_call | solution.py:197
  54.9 0.1 collective-permute-start.13
  55.0 1.9 %collective-permute-done.13.got_ref = bf16[2,128,1024]{2,1,0:T(8,128)(2,1)S(1)} collective-permute-done((bf16[2,128,1024]{2,1,0:T(8,128)(2,1)S(1)}, bf16[2,128,1024]{2,1,0:T(8,128)(2,1)S(1)}, u32[]{:S(2)}, u32[]{:S(2)}) %collective-permute-start.13) | collective-permute-done | bytes 524320 | tf_op jit(solution)/shard_map/ppermute | solution.py:31
  56.9 0.3 shard_map.51
  57.3 21.3 %all_to_all.5.part_ref = bf16[16,2,64,128]{3,2,1,0:T(8,128)(2,1)S(1)} all-to-all(bf16[16,2,64,128]{3,2,1,0:T(8,128)(2,1)S(1)} %shard_map.51), channel_id=1, replica_groups={{0,2,4,6,8,10,12,14,16,18,20,22,24,26,28,30},{1,3,5,7,9,11,13,15,17,19,..., dimensions={0} | all-to-all | bytes 1048576 | tf_op jit(solution)/shard_map/all_to_all | solution.py:307
  78.5 0.8 shard_map.52
  79.3 2.0 %collective-permute-start.14 = (bf16[2,32,1024]{2,1,0:T(8,128)(2,1)S(1)}, bf16[2,32,1024]{2,1,0:T(8,128)(2,1)S(1)}, u32[]{:S(2)}, u32[]{:S(2)}) collective-permute-start(bf16[2,32,1024]{2,1,0:T(8,128)(2,1)S(1)} %get-tuple-element.38), channel_id=1, source_target_pairs={{0,1},{1,0},{2,3},{3,2},{4,5},{5,4},{6,7},{7,6},{8,9},{9,8},{10,11... | collective-permute-start | bytes 393224 | tf_op jit(solution)/shard_map/ppermute | solution.py:31
  81.3 1.0 %collective-permute-done.14.got_ref = bf16[2,32,1024]{2,1,0:T(8,128)(2,1)S(1)} collective-permute-done((bf16[2,32,1024]{2,1,0:T(8,128)(2,1)S(1)}, bf16[2,32,1024]{2,1,0:T(8,128)(2,1)S(1)}, u32[]{:S(2)}, u32[]{:S(2)}) %collective-permute-start.14) | collective-permute-done | bytes 131104 | tf_op jit(solution)/shard_map/ppermute | solution.py:31
  82.3 0.8 shard_map.53
  (12 shorter events, 0.1 us)
Async XLA Ops:
  1.2 13.8 %collective-permute-start = (bf16[72,1024]{1,0:T(8,128)(2,1)S(1)}, bf16[72,1024]{1,0:T(8,128)(2,1)S(1)}, u32[]{:S(2)}, u32[]{:S(2)}) collective-permute-start(bf16[72,1024]{1,0:T(8,128)(2,1)S(1)} %get-tuple-element.22), channel_id=1, source_target_pairs={{0,8},{1,9},{2,10},{3,11},{4,12},{5,13},{6,14},{7,15},{8,16},{9,17... | collective-permute-start | bytes 442376 | tf_op jit(solution)/shard_map/ppermute | solution.py:31
  3.7 11.3 %collective-permute-start.1 = (bf16[72,1024]{1,0:T(8,128)(2,1)S(1)}, bf16[72,1024]{1,0:T(8,128)(2,1)S(1)}, u32[]{:S(2)}, u32[]{:S(2)}) collective-permute-start(bf16[72,1024]{1,0:T(8,128)(2,1)S(1)} %get-tuple-element.22), channel_id=1, source_target_pairs={{0,152},{1,153},{2,154},{3,155},{4,156},{5,157},{6,158},{7,159},{8... | collective-permute-start | bytes 442376 | tf_op jit(solution)/shard_map/ppermute | solution.py:31
  7.7 7.3 %collective-permute-start.2 = (bf16[72,1024]{1,0:T(8,128)(2,1)S(1)}, bf16[72,1024]{1,0:T(8,128)(2,1)S(1)}, u32[]{:S(2)}, u32[]{:S(2)}) collective-permute-start(bf16[72,1024]{1,0:T(8,128)(2,1)S(1)} %get-tuple-element.22), channel_id=1, source_target_pairs={{0,16},{1,145},{2,18},{3,147},{4,20},{5,149},{6,22},{7,151},{8,24}... | collective-permute-start | bytes 442376 | tf_op jit(solution)/shard_map/ppermute | solution.py:31
  12.5 14.9 %collective-permute-start.7 = (bf16[2,128,1024]{2,1,0:T(8,128)(2,1)S(1)}, bf16[2,128,1024]{2,1,0:T(8,128)(2,1)S(1)}, u32[]{:S(2)}, u32[]{:S(2)}) collective-permute-start(bf16[2,128,1024]{2,1,0:T(8,128)(2,1)S(1)} %fusion.1), channel_id=1, source_target_pairs={{0,16},{1,145},{2,18},{3,147},{4,20},{5,149},{6,22},{7,151},{8,24}... | collective-permute-start | bytes 1572872 | tf_op jit(solution)/shard_map/ppermute | solution.py:31
  15.2 15.0 %collective-permute-start.3 = (bf16[264,1024]{1,0:T(8,128)(2,1)S(1)}, bf16[264,1024]{1,0:T(8,128)(2,1)S(1)}, u32[]{:S(2)}, u32[]{:S(2)}) collective-permute-start(bf16[264,1024]{1,0:T(8,128)(2,1)S(1)} %concatenate.6.refs_4_.refs_0_), channel_id=1, source_target_pairs={{0,2},{1,3},{2,4},{3,5},{4,6},{5,7},{6,0},{7,1},{8,10},{9,11},{10,... | collective-permute-start | bytes 1622024 | tf_op jit(solution)/shard_map/ppermute | solution.py:31
  16.5 13.7 %collective-permute-start.4 = (bf16[264,1024]{1,0:T(8,128)(2,1)S(1)}, bf16[264,1024]{1,0:T(8,128)(2,1)S(1)}, u32[]{:S(2)}, u32[]{:S(2)}) collective-permute-start(bf16[264,1024]{1,0:T(8,128)(2,1)S(1)} %concatenate.6.refs_4_.refs_0_), channel_id=1, source_target_pairs={{0,6},{1,7},{2,0},{3,1},{4,2},{5,3},{6,4},{7,5},{8,14},{9,15},{10,... | collective-permute-start | bytes 1622024 | tf_op jit(solution)/shard_map/ppermute | solution.py:31
  18.0 12.2 %collective-permute-start.5 = (bf16[200,1024]{1,0:T(8,128)(2,1)S(1)}, bf16[200,1024]{1,0:T(8,128)(2,1)S(1)}, u32[]{:S(2)}, u32[]{:S(2)}) collective-permute-start(bf16[200,1024]{1,0:T(8,128)(2,1)S(1)} %slice.46), channel_id=1, source_target_pairs={{0,32},{1,97},{2,34},{3,99},{4,36},{5,101},{6,38},{7,103},{8,40},{... | collective-permute-start | bytes 1228808 | tf_op jit(solution)/shard_map/ppermute | solution.py:31
  27.4 14.3 %collective-permute-start.8 = (bf16[2,128,1024]{2,1,0:T(8,128)(2,1)S(1)}, bf16[2,128,1024]{2,1,0:T(8,128)(2,1)S(1)}, u32[]{:S(2)}, u32[]{:S(2)}) collective-permute-start(bf16[2,128,1024]{2,1,0:T(8,128)(2,1)S(1)} %collective-permute-done.7), channel_id=1, source_target_pairs={{0,16},{1,145},{2,18},{3,147},{4,20},{5,149},{6,22},{7,151},{8,24}... | collective-permute-start | bytes 1572872 | tf_op jit(solution)/shard_map/ppermute | solution.py:31
  30.3 20.2 %collective-permute-start.12 = (bf16[528,1024]{1,0:T(8,128)(2,1)S(1)}, bf16[528,1024]{1,0:T(8,128)(2,1)S(1)}, u32[]{:S(2)}, u32[]{:S(2)}) collective-permute-start(bf16[528,1024]{1,0:T(8,128)(2,1)S(1)} %get-tuple-element.28), channel_id=1, source_target_pairs={{0,32},{1,97},{2,34},{3,99},{4,36},{5,101},{6,38},{7,103},{8,40},{... | collective-permute-start | bytes 3244040 | tf_op jit(solution)/shard_map/ppermute | solution.py:31
  33.1 11.1 %collective-permute-start.10 = (bf16[264,1024]{1,0:T(8,128)(2,1)S(1)}, bf16[264,1024]{1,0:T(8,128)(2,1)S(1)}, u32[]{:S(2)}, u32[]{:S(2)}) collective-permute-start(bf16[264,1024]{1,0:T(8,128)(2,1)S(1)} %get-tuple-element.27), channel_id=1, source_target_pairs={{0,2},{1,7},{2,4},{3,1},{4,6},{5,3},{6,0},{7,5},{8,10},{9,15},{10,... | collective-permute-start | bytes 1622024 | tf_op jit(solution)/shard_map/ppermute | solution.py:31
  35.6 11.4 %collective-permute-start.6 = (bf16[2,128,1024]{2,1,0:T(8,128)(2,1)S(1)}, bf16[2,128,1024]{2,1,0:T(8,128)(2,1)S(1)}, u32[]{:S(2)}, u32[]{:S(2)}) collective-permute-start(bf16[2,128,1024]{2,1,0:T(8,128)(2,1)S(1)} %fusion.refs_0_), channel_id=1, source_target_pairs={{0,1},{1,0},{2,3},{3,2},{4,5},{5,4},{6,7},{7,6},{8,9},{9,8},{10,11... | collective-permute-start | bytes 1572872 | tf_op jit(solution)/shard_map/ppermute | solution.py:31
  41.7 5.3 %collective-permute-start.9 = (bf16[2,128,1024]{2,1,0:T(8,128)(2,1)S(1)}, bf16[2,128,1024]{2,1,0:T(8,128)(2,1)S(1)}, u32[]{:S(2)}, u32[]{:S(2)}) collective-permute-start(bf16[2,128,1024]{2,1,0:T(8,128)(2,1)S(1)} %collective-permute-done.8.refs_2_), channel_id=1, source_target_pairs={{0,1},{1,0},{2,3},{3,2},{4,5},{5,4},{6,7},{7,6},{8,9},{9,8},{10,11... | collective-permute-start | bytes 1572872 | tf_op jit(solution)/shard_map/ppermute | solution.py:31
  44.2 9.5 %collective-permute-start.11 = (bf16[264,1024]{1,0:T(8,128)(2,1)S(1)}, bf16[264,1024]{1,0:T(8,128)(2,1)S(1)}, u32[]{:S(2)}, u32[]{:S(2)}) collective-permute-start(bf16[264,1024]{1,0:T(8,128)(2,1)S(1)} %collective-permute-done.10.refs_5_), channel_id=1, source_target_pairs={{0,32},{1,97},{2,34},{3,99},{4,36},{5,101},{6,38},{7,103},{8,40},{... | collective-permute-start | bytes 1622024 | tf_op jit(solution)/shard_map/ppermute | solution.py:31
  54.9 2.0 %collective-permute-start.13 = (bf16[2,128,1024]{2,1,0:T(8,128)(2,1)S(1)}, bf16[2,128,1024]{2,1,0:T(8,128)(2,1)S(1)}, u32[]{:S(2)}, u32[]{:S(2)}) collective-permute-start(bf16[2,128,1024]{2,1,0:T(8,128)(2,1)S(1)} %get-tuple-element.35), channel_id=1, source_target_pairs={{0,1},{1,0},{2,3},{3,2},{4,5},{5,4},{6,7},{7,6},{8,9},{9,8},{10,11... | collective-permute-start | bytes 1572872 | tf_op jit(solution)/shard_map/ppermute | solution.py:31
  79.3 3.0 %collective-permute-start.14 = (bf16[2,32,1024]{2,1,0:T(8,128)(2,1)S(1)}, bf16[2,32,1024]{2,1,0:T(8,128)(2,1)S(1)}, u32[]{:S(2)}, u32[]{:S(2)}) collective-permute-start(bf16[2,32,1024]{2,1,0:T(8,128)(2,1)S(1)} %get-tuple-element.38), channel_id=1, source_target_pairs={{0,1},{1,0},{2,3},{3,2},{4,5},{5,4},{6,7},{7,6},{8,9},{9,8},{10,11... | collective-permute-start | bytes 393224 | tf_op jit(solution)/shard_map/ppermute | solution.py:31
